TPU v7x, 128 devices: a whole 4x4x4 slice. The times are simulated.
128 devices in a mesh: row: 8 (over z, core), col: 16 (over y, x).
Axes of the slice: x: 4, y: 4, z: 4, core: 2. Of those that a mesh axis runs over, the one named last changes fastest.
Arguments:
- a_blocks: bfloat16 [1024, 16, 4, 4096], P('row', 'col'), may hold values from -0.125 to 0.125
- a_index: int32 [1024, 16, 4], P('row', 'col'), may hold values from 0 to 63, as said below
- p_blocks: bfloat16 [64, 16, 4, 4096], P('row', 'col'), may hold values from -2 to 2
- p_index: int32 [64, 16, 4], P('row', 'col'), may hold values from 0 to 127, as said below
- ap_index: int32 [1024, 8], P('row'), may hold values from 0 to 127, as said below
- coarse_index: int32 [128, 8], replicated, may hold values from 0 to 127, as said below
Outputs:
- ap_out: bfloat16 [64, 16, 8, 4096], P('row', 'col')
- coarse_out: float32 [128, 8, 4096], P(('row', 'col'))
Inputs may be any that keep to these rules, and one draw needn't show every extreme that they name: `a_index`: within one (i, c) the 4 entries are distinct. `p_index`: within one row the 4 entries are distinct. `ap_index`: within one row the 8 entries are distinct. `coarse_index`: within one row the 8 entries are distinct.
All inputs are finite; a program needn't handle non-finite values.
Results may differ from a plain program's by a relative error of at most 0.0029.
Values may be sent and summed in bfloat16 or wider, within the bound.
No kernel may reach another device: no remote copies, remote signals or barrier semaphores. Data moves between devices by JAX's collectives and lax.ppermute only.
A program may use at most 320 MiB of HBM per device.

v0:
```python
import jax
import jax.numpy as jnp
from jax import lax
from jax.experimental import pallas as pl
from jax.experimental.pallas import tpu as pltpu
from jax.sharding import PartitionSpec as P


B = 64
KA = 4
KP = 4
KAP = 8
KC = 8
NCOL = 16
NK = 64
NCB = 128
FULL = 14.0
TINY = 1e-30


def along_row(v, dz, flip):
    pairs = [(r, ((r // 2 + dz) % 4) * 2 + (r % 2 + flip) % 2) for r in range(8)]
    return lax.ppermute(v, "row", pairs)


def along_col(v, dx, dy):
    pairs = [(c, ((c // 4 + dy) % 4) * 4 + (c % 4 + dx) % 4) for c in range(16)]
    return lax.ppermute(v, "col", pairs)


def low_lanes(rows):
    return lax.broadcasted_iota(jnp.int32, (rows, 128), 1) < B


def spread_kernel(a_ref, out_ref, buf_ref):
    low = low_lanes(32)

    def some(g, carry):
        for u in range(4):
            i = g * 4 + u
            v = a_ref[i].astype(jnp.float32)
            for h in range(32):
                buf_ref[u, h * 4:(h + 1) * 4, :] = v[:, h * 128:(h + 1) * 128]
        for u in range(4):
            i = g * 4 + u
            for ep in range(2):
                v0 = buf_ref[u, pl.ds(2 * ep, 32, stride=4), :]
                v1 = buf_ref[u, pl.ds(2 * ep + 1, 32, stride=4), :]
                top = jnp.where(low, v0, pltpu.roll(v1, B, 1))
                bottom = jnp.where(low, pltpu.roll(v0, B, 1), v1)
                out_ref[i, 0:32, ep * 128:(ep + 1) * 128] = top.astype(jnp.bfloat16)
                out_ref[i, 32:64, ep * 128:(ep + 1) * 128] = bottom.astype(jnp.bfloat16)
        return carry

    lax.fori_loop(0, 4, some, 0)


def spread(a):
    return pl.pallas_call(
        spread_kernel,
        grid=(8,),
        in_specs=[pl.BlockSpec((16, KA, B * B), lambda g: (g, 0, 0))],
        out_specs=pl.BlockSpec((16, B, KA * B), lambda g: (g, 0, 0)),
        scratch_shapes=[pltpu.VMEM((4, 128, 128), jnp.float32)],
        out_shape=jax.ShapeDtypeStruct((128, B, KA * B), jnp.bfloat16),
        name="spread",
    )(a)


def table_kernel(*refs):
    parts, out_ref = refs[:8], refs[8]
    low = low_lanes(B)
    for n, part in enumerate(parts):
        def fill(q, carry):
            for mh in range(2):
                v = part[q, :, mh * 128:(mh + 1) * 128]
                turned = jnp.concatenate([v[:, B:], v[:, :B]], axis=1)
                at = (n * 8 + q) * 4 + 2 * mh
                out_ref[at] = jnp.where(low, v, turned)
                out_ref[at + 1] = jnp.where(low, turned, v)
            return carry

        lax.fori_loop(0, 8, fill, 0)
    out_ref[NK * KP] = jnp.zeros((B, 128), jnp.bfloat16)


def table(parts):
    whole = pl.BlockSpec(memory_space=pltpu.VMEM)
    return pl.pallas_call(
        table_kernel,
        in_specs=[whole] * 8,
        out_specs=whole,
        out_shape=jax.ShapeDtypeStruct((NK * KP + 1, B, 128), jnp.bfloat16),
        name="table",
    )(*parts)


def nt_dot(a, b):
    return lax.dot_general(a, b, (((1,), (1,)), ((), ())), preferred_element_type=jnp.float32)


def exponent(most):
    return jnp.ceil(jnp.log2(jnp.maximum(most, TINY)))


def coded(v, mul):
    return jnp.round(v * mul).astype(jnp.int32).astype(jnp.int16)


def product_kernel(color, idx_ref, at_ref, a_ref, dup_ref, out_ref, exp_ref):
    ih = pl.program_id(0)
    cblk = pl.program_id(1)
    low = low_lanes(B)
    mine = at_ref[color]
    count = a_ref.shape[2]
    zero = jnp.zeros((B, KA * B), jnp.bfloat16)

    def one(cc, carry):
        rows = []
        for s in range(KAP):
            pieces = []
            for lo in range(2):
                base = (((ih * 4 + color * 2 + lo) * NCOL) + cblk * count + cc) * (KA * KAP)
                for ep in range(2):
                    first = dup_ref[idx_ref[base + (2 * ep) * KAP + s]]
                    second = dup_ref[idx_ref[base + (2 * ep + 1) * KAP + s]]
                    pieces.append(jnp.where(low, first, second))
            rows.append(jnp.concatenate(pieces, axis=1))
        stacked = jnp.concatenate(
            [
                jnp.concatenate([a_ref[0, 0, cc], zero], axis=1),
                jnp.concatenate([zero, a_ref[0, 1, cc]], axis=1),
            ],
            axis=0,
        )
        res = nt_dot(jnp.concatenate(rows, axis=0), stacked)
        most = jnp.max(jnp.abs(res), axis=0, keepdims=True)
        e = exponent(most)
        q = jnp.round(res * jnp.exp2(FULL - e)).astype(jnp.int32)
        c = cblk * count + cc
        exp_ref[ih, pl.ds(c, 1), :] = e
        for bg in range(8):
            g = bg % 2
            if color == 0:
                d = lax.rem(2 * g + ih - mine + 4, 4)
                u = bg // 2
            else:
                d = lax.rem(bg // 2 - mine + 4, 4)
                u = 2 * g + ih
            for sp in range(4):
                r0 = 2 * sp * B + bg * 8
                pair = jnp.concatenate([q[r0:r0 + 8], q[r0 + B:r0 + B + 8]], axis=0)
                out_ref[d, (u * NCOL + c) * 4 + sp] = pair.astype(jnp.int16)

        return carry

    lax.fori_loop(0, count, one, 0)

    @pl.when((ih == 1) & (cblk == pl.num_programs(1) - 1))
    def _():
        for d in range(4):
            for t in range(2):
                source = lax.rem(mine + d, 2) if color == 0 else t
                out_ref[d, 256 + t] = exp_ref[source].astype(jnp.int32).astype(jnp.int16)


def products(color, idx, at, a, dup):
    block = 8
    return pl.pallas_call(
        lambda *refs: product_kernel(color, *refs),
        grid_spec=pltpu.PrefetchScalarGridSpec(
            num_scalar_prefetch=2,
            grid=(2, NCOL // block),
            in_specs=[
                pl.BlockSpec(
                    (1, 2, block, B, KA * B), lambda ih, c, idx, at: (ih * 2 + color, 0, c, 0, 0)
                ),
                pl.BlockSpec((NK * KP + 1, B, 128), lambda ih, c, idx, at: (0, 0, 0)),
            ],
            out_specs=pl.BlockSpec((4, 258, 16, 128), lambda ih, c, idx, at: (0, 0, 0, 0)),
            scratch_shapes=[
                pltpu.VMEM((2, NCOL, 128), jnp.float32),
            ],
        ),
        out_shape=jax.ShapeDtypeStruct((4, 258, 16, 128), jnp.int16),
    )(idx, at, a, dup)


def middle_kernel(color, at_ref, own_ref, m1_ref, m2_ref, m3_ref, out_ref, scale_ref, exp_ref):
    other = at_ref[1 - color]
    for d, m in enumerate((own_ref, m1_ref, m2_ref, m3_ref)):
        for t in range(2):
            scale_ref[d, t] = jnp.exp2(m[256 + t].astype(jnp.float32) - FULL)

    for u in range(4):
        d2 = lax.rem(u - other + 4, 4)

        def one(c, carry):
            t = 0 if color == 0 else u % 2
            scales = [scale_ref[d, t, pl.ds(c, 1), :] for d in range(4)]
            sums = []
            for sp in range(4):
                total = None
                for d, m in enumerate((own_ref, m1_ref, m2_ref, m3_ref)):
                    term = m[(u * NCOL + c) * 4 + sp].astype(jnp.float32) * scales[d]
                    total = term if total is None else total + term
                sums.append(total)
            most = sums[0]
            most = jnp.maximum(
                jnp.maximum(jnp.abs(sums[0]), jnp.abs(sums[1])),
                jnp.maximum(jnp.abs(sums[2]), jnp.abs(sums[3])),
            )
            e = exponent(jnp.max(most, axis=0, keepdims=True))
            mul = jnp.exp2(FULL - e)
            exp_ref[u, pl.ds(c, 1), :] = e
            for sp in range(4):
                out_ref[d2, c * 4 + sp] = coded(sums[sp], mul)
            return carry

        lax.fori_loop(0, NCOL, one, 0)
        out_ref[d2, 64] = exp_ref[u].astype(jnp.int32).astype(jnp.int16)


def middle(color, at, own, m1, m2, m3):
    vmem = pl.BlockSpec(memory_space=pltpu.VMEM)
    return pl.pallas_call(
        lambda *refs: middle_kernel(color, *refs),
        in_specs=[
            pl.BlockSpec(memory_space=pltpu.SMEM),
            vmem, vmem, vmem, vmem,
        ],
        out_specs=vmem,
        scratch_shapes=[
            pltpu.VMEM((4, 2, NCOL, 128), jnp.float32),
            pltpu.VMEM((4, NCOL, 128), jnp.float32),
        ],
        out_shape=jax.ShapeDtypeStruct((4, 65, 16, 128), jnp.int16),
    )(at, own, m1, m2, m3)


def final_kernel(*refs):
    parts, out_ref, scale_ref = refs[:8], refs[8], refs[9]
    for n, m in enumerate(parts):
        scale_ref[n] = jnp.exp2(m[64].astype(jnp.float32) - FULL)

    def one(c, carry):
        for qh in range(2):
            scales = [scale_ref[qh * 4 + d, pl.ds(c, 1), :] for d in range(4)]
            for sp in range(4):
                total = None
                for d in range(4):
                    m = parts[qh * 4 + d]
                    term = m[c * 4 + sp].astype(jnp.float32) * scales[d]
                    total = term if total is None else total + term
                out_ref[c, qh, sp * 16:(sp + 1) * 16, :] = total.astype(jnp.bfloat16)
        return carry

    lax.fori_loop(0, NCOL, one, 0)


def final(parts):
    vmem = pl.BlockSpec(memory_space=pltpu.VMEM)
    return pl.pallas_call(
        final_kernel,
        in_specs=[vmem] * 8,
        out_specs=vmem,
        scratch_shapes=[pltpu.VMEM((8, NCOL, 128), jnp.float32)],
        out_shape=jax.ShapeDtypeStruct((NCOL, 2, B, 128), jnp.bfloat16),
        name="final",
    )(*parts)


def coarse_kernel(tgt_ref, at_ref, x_ref, p0_ref, p1_ref, p2_ref, p3_ref, keep_ref, send_ref, acc_ref):
    dx = pl.program_id(0)
    low = low_lanes(8)
    low_x = low_lanes(B)
    my_x, my_y, my_z, my_core = at_ref[0], at_ref[1], at_ref[2], at_ref[3]

    @pl.when(dx == 0)
    def _():
        acc_ref[...] = jnp.zeros_like(acc_ref)

    for dy, p_ref in enumerate((p0_ref, p1_ref, p2_ref, p3_ref)):
        c = lax.rem(my_y - dy + 4, 4) * 4 + lax.rem(my_x - dx + 4, 4)
        for qh in range(2):
            x = x_ref[c, qh]
            none = jnp.zeros_like(x)
            lhs = jnp.concatenate([jnp.where(low_x, x, none), jnp.where(low_x, none, x)], axis=0)
            rhs = p_ref[0, 2 * qh:2 * qh + 2].reshape(2 * B, KP * B)
            res = lax.dot_general(
                lhs, rhs, (((1,), (0,)), ((), ())), preferred_element_type=jnp.float32
            )
            for lo in range(2):
                ats, sums = [], []
                for m in range(KP):
                    for s in range(KAP):
                        at = tgt_ref[(((c * 2 + qh) * 2 + lo) * KP + m) * KAP + s]
                        rows = (lo * KAP + s) * 8
                        tile = res[rows:rows + 8, (m // 2) * 128:(m // 2) * 128 + 128]
                        keep = low if m % 2 == 0 else jnp.logical_not(low)
                        ats.append(at)
                        sums.append(acc_ref[at] + jnp.where(keep, tile, 0.0))
                for at, total in zip(ats, sums):
                    acc_ref[at] = total

    @pl.when(dx == 3)
    def _():
        for flip, out_ref in ((1, send_ref), (0, keep_ref)):
            core = lax.rem(my_core + flip, 2)
            for d in range(4):
                first = (lax.rem(my_z + d, 4) * 2 + core) * NCOL

                def fold(col, carry):
                    for tp in range(KC // 2):
                        t0 = acc_ref[(first + col) * KC + 2 * tp]
                        t1 = acc_ref[(first + col) * KC + 2 * tp + 1]
                        t0 = t0 + pltpu.roll(t0, B, 1)
                        t1 = t1 + pltpu.roll(t1, B, 1)
                        out_ref[d, col, tp] = jnp.where(low, t0, t1)
                    return carry

                lax.fori_loop(0, NCOL, fold, 0, unroll=4)


def coarse_terms(tgt, at, x, ps):
    shape = (4, NCOL, KC // 2, 8, 128)
    out = pl.BlockSpec(shape, lambda dx, tgt, at: (0, 0, 0, 0, 0))
    return pl.pallas_call(
        coarse_kernel,
        grid_spec=pltpu.PrefetchScalarGridSpec(
            num_scalar_prefetch=2,
            grid=(4,),
            in_specs=[pl.BlockSpec((NCOL, 2, B, 128), lambda dx, tgt, at: (0, 0, 0, 0))]
            + [pl.BlockSpec((1, 5, B, KP * B), lambda dx, tgt, at: (dx, 0, 0, 0))] * 4,
            out_specs=[out, out],
            scratch_shapes=[pltpu.VMEM((NCB * KC + 1, 8, 128), jnp.float32)],
        ),
        out_shape=[jax.ShapeDtypeStruct(shape, jnp.float32)] * 2,
        name="coarse_terms",
    )(tgt, at, x, *ps)


def ap_out_kernel(x_ref, out_ref, turn_ref):
    for ih in range(2):
        for qh in range(2):
            for s in range(KAP):
                m = jnp.concatenate(
                    [x_ref[bg * 2 + ih, qh, s * 8:(s + 1) * 8, :] for bg in range(8)], axis=0
                )
                t = m.astype(jnp.float32).T
                for lo in range(2):
                    top, bottom = t[lo * B:lo * B + 32], t[lo * B + 32:lo * B + B]
                    turn_ref[lo, pl.ds(s, 32, stride=8), :] = jnp.concatenate([top, bottom], axis=1)
            for lo in range(2):
                for h in range(32):
                    tile = turn_ref[lo, h * 8:(h + 1) * 8, :]
                    out_ref[ih * 4 + qh * 2 + lo, :, h * 128:(h + 1) * 128] = tile.astype(jnp.bfloat16)


def ap_layout(x):
    vmem = pl.BlockSpec(memory_space=pltpu.VMEM)
    return pl.pallas_call(
        ap_out_kernel,
        in_specs=[vmem],
        out_specs=vmem,
        scratch_shapes=[pltpu.VMEM((2, 256, 128), jnp.float32)],
        out_shape=jax.ShapeDtypeStruct((8, KAP, B * B), jnp.bfloat16),
        name="ap_layout",
    )(x)


def coarse_out_kernel(x_ref, out_ref, turn_ref, flat_ref):
    for tp in range(KC // 2):
        m = jnp.concatenate([x_ref[bg * 2, tp] + x_ref[bg * 2 + 1, tp] for bg in range(8)], axis=0)
        turn_ref[...] = m.T
        for lo in range(2):
            even = turn_ref[pl.ds(lo * B, 32, stride=2), :]
            odd = turn_ref[pl.ds(lo * B + 1, 32, stride=2), :]
            flat_ref[pl.ds(tp * 2 + lo, 32, stride=8), :] = jnp.concatenate([even, odd], axis=1)
    for h in range(32):
        out_ref[:, h * 128:(h + 1) * 128] = flat_ref[h * 8:(h + 1) * 8, :]


def coarse_layout(x):
    vmem = pl.BlockSpec(memory_space=pltpu.VMEM)
    return pl.pallas_call(
        coarse_out_kernel,
        in_specs=[vmem],
        out_specs=vmem,
        scratch_shapes=[pltpu.VMEM((128, B), jnp.float32), pltpu.VMEM((256, 128), jnp.float32)],
        out_shape=jax.ShapeDtypeStruct((KC, B * B), jnp.float32),
        name="coarse_layout",
    )(x)


def pick_rows(table, index):
    hot = (index[..., None] == jnp.arange(table.shape[0], dtype=jnp.int32)).astype(jnp.bfloat16)
    rows = jnp.einsum(
        "...k,km->...m", hot, table.astype(jnp.bfloat16), preferred_element_type=jnp.float32
    )
    return rows.astype(jnp.int32)


def index_slab(index):
    wide = jnp.pad(index.astype(jnp.bfloat16), ((0, B - index.shape[0]), (0, KP * B - KP)))
    return wide[None]


def step(a_blocks, a_index, p_blocks, p_index, ap_index, coarse_index):
    row = lax.axis_index("row")
    col = lax.axis_index("col")
    z, core = row // 2, row % 2
    y, x = col // 4, col % 4
    at = jnp.stack([x, y, z, core]).astype(jnp.int32)
    half = x % 2

    own = p_blocks[:, 0].reshape(8, KP, B, B)
    pt = own.transpose(0, 3, 1, 2).reshape(8, B, KP * B)
    pt = jnp.concatenate([pt, index_slab(p_index[:, 0])], axis=0)
    by_z = [pt] + [along_row(pt, d, 0) for d in (1, 2, 3)]
    parts = []
    for part in by_z:
        parts += [part, along_row(part, 0, 1)]

    pn = own.reshape(8, KP, 32, 2, B).transpose(0, 3, 2, 1, 4).reshape(2, 4, B, KP * B)
    halves = jnp.stack(
        [
            jnp.concatenate([pn[h], index_slab(p_index[4 * h:4 * h + 4, 0])], axis=0)
            for h in range(2)
        ]
    )
    same = lax.dynamic_index_in_dim(halves, half, 0, keepdims=False)
    diff = lax.dynamic_index_in_dim(halves, 1 - half, 0, keepdims=False)
    by_x = jnp.stack(
        [same, along_col(diff, 1, 0), along_col(same, 2, 0), along_col(diff, 3, 0)]
    )
    ps = [by_x] + [along_col(by_x, 0, d) for d in (1, 2, 3)]

    a = spread(a_blocks[:, 0]).reshape(4, 2, NCOL, B, KA * B)

    a_idx = a_index[:, 0]
    from_row = a_idx // 8
    place = ((z - from_row // 2) % 4) * 2 + (core + from_row) % 2
    place = place * 8 + a_idx % 8
    cols_k = jnp.concatenate([part[8, :8, :KP] for part in parts], axis=0)
    picked = pick_rows(cols_k, place)
    equal = picked[:, :, None, :] == ap_index[:, None, :, None]
    ids = place[:, :, None, None] * KP + jnp.arange(KP, dtype=jnp.int32)
    idx = jnp.min(jnp.where(equal, ids, NK * KP), axis=3).reshape(-1)

    dup = table(parts)
    q0 = products(0, idx, at, a, dup)
    x_sent = [along_col(q0[d], d, 0) for d in (1, 2, 3)]
    q1 = products(1, idx, at, a, dup)
    y_sent = [along_col(q1[d], 0, d) for d in (1, 2, 3)]
    s0 = middle(0, at, q0[0], *x_sent)
    y_last = [along_col(s0[d], 0, d) for d in (1, 2, 3)]
    s1 = middle(1, at, q1[0], *y_sent)
    x_last = [along_col(s1[d], d, 0) for d in (1, 2, 3)]
    apt = final([s0[0], *y_last, s1[0], *x_last])

    back = lax.all_to_all(apt, "col", 0, 0, tiled=True)
    ap_out = ap_layout(back).reshape(8, 1, KAP, B * B)

    cols_p = jnp.stack([p[:, 4, :4, :KP] for p in ps]).reshape(NCOL, 16)
    cc = jnp.arange(NCOL, dtype=jnp.int32)
    where = ((y - cc // 4) % 4) * 4 + (x - cc % 4) % 4
    cols_i = pick_rows(cols_p, where).reshape(NCOL, 4, KP)
    slots = lax.dynamic_index_in_dim(
        ap_index.reshape(2, 4, NCOL, KAP), half, 0, keepdims=False
    ).transpose(1, 0, 2)
    targets = pick_rows(coarse_index, cols_i)
    hit = targets[:, :, :, None, :] == slots[:, :, None, :, None]
    slot = cols_i[:, :, :, None, None] * KC + jnp.arange(KC, dtype=jnp.int32)
    tgt = jnp.min(jnp.where(hit, slot, NCB * KC), axis=4).reshape(-1)

    keep, send = coarse_terms(tgt, at, apt, ps)
    got = along_row(send, 0, 1)
    sums = [keep[d] + got[d] for d in range(4)]
    coarse = sums[0]
    moved = [along_row(sums[d], d, 0) for d in (1, 2, 3)]
    for part in moved:
        coarse = coarse + part
    coarse = lax.all_to_all(coarse, "col", 0, 0, tiled=True)
    coarse_out = coarse_layout(coarse).reshape(1, KC, B * B)
    return ap_out, coarse_out


def solution(mesh):
    placed = (
        P("row", "col", None, None),
        P("row", "col", None),
        P("row", "col", None, None),
        P("row", "col", None),
        P("row", None),
        P(),
    )
    return jax.shard_map(
        step,
        mesh=mesh,
        in_specs=placed,
        out_specs=(P("row", "col", None, None), P(("row", "col"), None, None)),
        check_vma=False,
    )
```

profile of v0, /device:TPU:0, one launch (start us, length us, event | category | flops | bytes accessed | tf_op | source)
XLA Modules:
  0.0 229.7 jit_solution(14048391677670276752)
XLA Ops:
  0.6 0.7 convert_bitcast_fusion
  1.4 1.4 reshape_squeeze.3
  3.6 2.1 collective-permute-start.1
  5.7 3.6 %collective-permute-start.3 = (bf16[9,64,256]{2,1,0:T(8,128)(2,1)S(1)}, bf16[9,64,256]{2,1,0:T(8,128)(2,1)S(1)}, u32[]{:S(2)}, u32[]{:S(2)}) collective-permute-start(bf16[9,64,256]{2,1,0:T(8,128)(2,1)S(1)} %pad_maximum_fusion.1.refs_0_), channel_id=1, source_target_pairs={{0,64},{16,80},{32,96},{48,112},{64,0},{80,16},{96,32},{112,48},{1... | collective-permute-start | bytes 884744 | tf_op jit(solution)/shard_map/ppermute | solution.py:23
  9.3 1.0 collective-permute-start.5
  12.3 2.8 %collective-permute-start.21 = (bf16[5,64,256]{2,1,0:T(8,128)(2,1)S(1)}, bf16[5,64,256]{2,1,0:T(8,128)(2,1)S(1)}, u32[]{:S(2)}, u32[]{:S(2)}) collective-permute-start(bf16[5,64,256]{2,1,0:T(8,128)(2,1)S(1)} %get-tuple-element.38), channel_id=1, source_target_pairs={{0,3},{1,0},{2,1},{3,2},{4,7},{5,4},{6,5},{7,6},{8,11},{9,8},{10,9... | collective-permute-start | bytes 491528 | tf_op jit(solution)/shard_map/ppermute | solution.py:28
  15.1 0.8 collective-permute-start.20
  16.0 5.3 %collective-permute-done.21 = bf16[5,64,256]{2,1,0:T(8,128)(2,1)S(1)} collective-permute-done((bf16[5,64,256]{2,1,0:T(8,128)(2,1)S(1)}, bf16[5,64,256]{2,1,0:T(8,128)(2,1)S(1)}, u32[]{:S(2)}, u32[]{:S(2)}) %collective-permute-start.21) | collective-permute-done | bytes 163872 | tf_op jit(solution)/shard_map/ppermute | solution.py:28
  21.3 0.7 collective-permute-done.20
  21.9 1.4 collective-permute-start.19
  24.7 8.4 %spread.1 = bf16[128,64,256]{2,1,0:T(8,128)(2,1)} custom-call(bf16[128,4,4096]{2,1,0:T(4,128)(2,1)} %bitcast.134), custom_call_target="tpu_custom_call" | custom-call | tf_op jit(solution)/shard_map/spread/pallas_call | solution.py:59
  33.3 3.1 %collective-permute-start.24 = (bf16[4,5,64,256]{3,2,1,0:T(8,128)(2,1)S(1)}, bf16[4,5,64,256]{3,2,1,0:T(8,128)(2,1)S(1)}, u32[]{:S(2)}, u32[]{:S(2)}) collective-permute-start(bf16[4,5,64,256]{3,2,1,0:T(8,128)(2,1)S(1)} %pad_maximum_fusion.p0_ref), channel_id=1, source_target_pairs={{0,12},{1,13},{2,14},{3,15},{4,0},{5,1},{6,2},{7,3},{8,4},{9,5},{1... | collective-permute-start | bytes 1966088 | tf_op jit(solution)/shard_map/ppermute | solution.py:28
  36.8 0.7 slice.167
  37.5 0.7 slice.169
  38.3 0.7 slice.171
  39.5 0.8 reshape.297.refs_0_
  40.4 8.7 %table.1.refs_3_ = bf16[257,64,128]{2,1,0:T(8,128)(2,1)} custom-call(bf16[9,64,256]{2,1,0:T(8,128)(2,1)} %copy-done.2, bf16[9,64,256]{2,1,0:T(8,128)(2,1)} %copy-done.9, bf16[9,64,256]{2,1,0:T(8,128)(2,1)} %copy-done.6, bf16[9,64,256]{2,1,0:T(8,128)(2,1)} %collective-permute-done.2.refs_3_, bf16[9,64,256]{2,1,0:T(8,128)(2,1)} %copy-done.7, ...), custom_call_target="tpu_custom_call" | custom-call | tf_op jit(solution)/shard_map/table/pallas_call | solution.py:89
  49.0 17.0 %shard_map.77 = s16[4,258,16,128]{3,2,1,0:T(8,128)(2,1)} custom-call(s32[4096]{0:T(1024)} %reshape.297.refs_0_, s32[4]{0:T(128)} %pad_add_fusion.refs_1_.refs_0_.at_ref, bf16[4,2,16,64,256]{4,3,2,1,0:T(8,128)(2,1)} %bitcast.132, bf16[257,64,128]{2,1,0:T(8,128)(2,1)} %table.1.refs_3_), custom_call_target="tpu_custom_call" | custom-call | tf_op jit(solution)/shard_map/pallas_call | solution.py:169
  66.1 4.6 %slice_bitcast_fusion.4 = (s16[258,16,128]{2,1,0:T(8,128)(2,1)}, s16[258,16,128]{2,1,0:T(8,128)(2,1)}, s16[258,16,128]{2,1,0:T(8,128)(2,1)}, s16[258,16,128]{2,1,0:T(8,128)(2,1)}) fusion(s16[4,258,16,128]{3,2,1,0:T(8,128)(2,1)} %shard_map.77), kind=kLoop, calls=%fused_computation.7 | loop fusion | bytes 8454144 | tf_op jit(solution)/shard_map/squeeze | solution.py:453
  71.0 0.7 collective-permute-start.23
  71.7 1.0 collective-permute-start.22
  72.7 17.1 %shard_map.79 = s16[4,258,16,128]{3,2,1,0:T(8,128)(2,1)} custom-call(s32[4096]{0:T(1024)} %reshape.297.refs_0_, s32[4]{0:T(128)} %pad_add_fusion.refs_1_.refs_0_.at_ref, bf16[4,2,16,64,256]{4,3,2,1,0:T(8,128)(2,1)} %bitcast.133, bf16[257,64,128]{2,1,0:T(8,128)(2,1)} %table.1.refs_3_), custom_call_target="tpu_custom_call" | custom-call | tf_op jit(solution)/shard_map/pallas_call | solution.py:169
  89.8 3.2 %collective-permute-start.8 = (s16[258,16,128]{2,1,0:T(8,128)(2,1)}, s16[258,16,128]{2,1,0:T(8,128)(2,1)}, u32[]{:S(2)}, u32[]{:S(2)}) collective-permute-start(s16[258,16,128]{2,1,0:T(8,128)(2,1)} %get-tuple-element.21), channel_id=1, source_target_pairs={{0,2},{1,3},{2,0},{3,1},{4,6},{5,7},{6,4},{7,5},{8,10},{9,11},{10,... | collective-permute-start | bytes 3170312 | tf_op jit(solution)/shard_map/ppermute | solution.py:28
  93.0 4.2 %slice_bitcast_fusion = (s16[258,16,128]{2,1,0:T(8,128)(2,1)S(1)}, s16[258,16,128]{2,1,0:T(8,128)(2,1)S(1)}, s16[258,16,128]{2,1,0:T(8,128)(2,1)}, s16[258,16,128]{2,1,0:T(8,128)(2,1)}) fusion(s16[4,258,16,128]{3,2,1,0:T(8,128)(2,1)} %shard_map.79), kind=kLoop, calls=%fused_computation.3 | loop fusion | bytes 8454144 | tf_op jit(solution)/shard_map/squeeze | solution.py:455
  97.3 2.3 collective-permute-start.9
  99.5 2.0 collective-permute-start.13
  101.5 0.7 slice_bitcast_fusion.17
  102.2 1.1 collective-permute-done.22.p1_ref
  103.3 0.7 collective-permute-start.14
  104.0 1.0 collective-permute-start.15
  105.1 0.7 slice_bitcast_fusion.18
  106.5 13.9 %collective-permute-done.8.refs_3_ = s16[258,16,128]{2,1,0:T(8,128)(2,1)} collective-permute-done((s16[258,16,128]{2,1,0:T(8,128)(2,1)}, s16[258,16,128]{2,1,0:T(8,128)(2,1)}, u32[]{:S(2)}, u32[]{:S(2)}) %collective-permute-start.8) | collective-permute-done | bytes 1056800 | tf_op jit(solution)/shard_map/ppermute | solution.py:28
  120.4 18.7 %collective-permute-done.9.refs_4_ = s16[258,16,128]{2,1,0:T(8,128)(2,1)} collective-permute-done((s16[258,16,128]{2,1,0:T(8,128)(2,1)}, s16[258,16,128]{2,1,0:T(8,128)(2,1)}, u32[]{:S(2)}, u32[]{:S(2)}) %collective-permute-start.9) | collective-permute-done | bytes 1056800 | tf_op jit(solution)/shard_map/ppermute | solution.py:28
  139.1 6.3 %shard_map.78 = s16[4,65,16,128]{3,2,1,0:T(8,128)(2,1)} custom-call(s32[4]{0:T(128)} %pad_add_fusion.refs_1_.refs_0_.at_ref, s16[258,16,128]{2,1,0:T(8,128)(2,1)} %get-tuple-element.23.refs_1_, s16[258,16,128]{2,1,0:T(8,128)(2,1)} %collective-permute-done.7.refs_2_, s16[258,16,128]{2,1,0:T(8,128)(2,1)} %collective-permute-done.8.refs_3_, ...), custom_call_target="tpu_custom_call" | custom-call | tf_op jit(solution)/shard_map/pallas_call | solution.py:226
  145.4 2.2 slice_bitcast_fusion.12
  147.7 1.9 collective-permute-start.10
  149.6 1.8 collective-permute-start.11
  151.4 1.1 collective-permute-start.12
  152.5 6.4 %shard_map.80 = s16[4,65,16,128]{3,2,1,0:T(8,128)(2,1)} custom-call(s32[4]{0:T(128)} %pad_add_fusion.refs_1_.refs_0_.at_ref, s16[258,16,128]{2,1,0:T(8,128)(2,1)} %get-tuple-element.19.refs_1_, s16[258,16,128]{2,1,0:T(8,128)(2,1)} %collective-permute-done.13.refs_2_, s16[258,16,128]{2,1,0:T(8,128)(2,1)} %collective-permute-done.14.refs_3_, ...), custom_call_target="tpu_custom_call" | custom-call | tf_op jit(solution)/shard_map/pallas_call | solution.py:226
  158.9 2.1 slice_bitcast_fusion.8
  161.0 2.5 %collective-permute-start.16 = (s16[65,16,128]{2,1,0:T(8,128)(2,1)S(1)}, s16[65,16,128]{2,1,0:T(8,128)(2,1)S(1)}, u32[]{:S(2)}, u32[]{:S(2)}) collective-permute-start(s16[65,16,128]{2,1,0:T(8,128)(2,1)S(1)} %get-tuple-element.29), channel_id=1, source_target_pairs={{0,1},{1,2},{2,3},{3,0},{4,5},{5,6},{6,7},{7,4},{8,9},{9,10},{10,1... | collective-permute-start | bytes 798728 | tf_op jit(solution)/shard_map/ppermute | solution.py:28
  163.4 1.6 collective-permute-start.17
  165.1 1.6 collective-permute-start.18
  167.1 0.8 reshape.302.tgt_ref
  167.9 2.3 %collective-permute-done.16.refs_5_ = s16[65,16,128]{2,1,0:T(8,128)(2,1)S(1)} collective-permute-done((s16[65,16,128]{2,1,0:T(8,128)(2,1)S(1)}, s16[65,16,128]{2,1,0:T(8,128)(2,1)S(1)}, u32[]{:S(2)}, u32[]{:S(2)}) %collective-permute-start.16) | collective-permute-done | bytes 266272 | tf_op jit(solution)/shard_map/ppermute | solution.py:28
  170.2 6.1 %collective-permute-done.17.refs_6_ = s16[65,16,128]{2,1,0:T(8,128)(2,1)S(1)} collective-permute-done((s16[65,16,128]{2,1,0:T(8,128)(2,1)S(1)}, s16[65,16,128]{2,1,0:T(8,128)(2,1)S(1)}, u32[]{:S(2)}, u32[]{:S(2)}) %collective-permute-start.17) | collective-permute-done | bytes 266272 | tf_op jit(solution)/shard_map/ppermute | solution.py:28
  176.4 0.7 copy-done.14
  177.1 2.9 %final.1.x_ref = bf16[16,2,64,128]{3,2,1,0:T(8,128)(2,1)} custom-call(s16[65,16,128]{2,1,0:T(8,128)(2,1)} %get-tuple-element.34.refs_0_, s16[65,16,128]{2,1,0:T(8,128)(2,1)} %copy-done.10, s16[65,16,128]{2,1,0:T(8,128)(2,1)} %copy-done.11, s16[65,16,128]{2,1,0:T(8,128)(2,1)} %copy-done.12, s16[65,16,128]{2,1,0:T(8,128)(2,1)} %get-tuple-element.30.refs_4_, ...), custom_call_target="tpu_custom_call" | custom-call | tf_op jit(solution)/shard_map/final/pallas_call | solution.py:263
  180.1 11.5 %coarse_terms.1 = (f32[4,16,4,8,128]{4,3,2,1,0:T(8,128)}, f32[4,16,4,8,128]{4,3,2,1,0:T(8,128)}) custom-call(s32[2048]{0:T(1024)} %reshape.302.tgt_ref, s32[4]{0:T(128)} %pad_add_fusion.refs_1_.refs_0_.at_ref, bf16[16,2,64,128]{3,2,1,0:T(8,128)(2,1)} %final.1.x_ref, bf16[4,5,64,256]{3,2,1,0:T(8,128)(2,1)} %copy-done, ...), custom_call_target="tpu_custom_call" | custom-call | tf_op jit(solution)/shard_map/coarse_terms/pallas_call | solution.py:328
  191.6 2.9 %collective-permute-done.25 = f32[4,16,4,8,128]{4,3,2,1,0:T(8,128)S(1)} collective-permute-done((f32[4,16,4,8,128]{4,3,2,1,0:T(8,128)}, f32[4,16,4,8,128]{4,3,2,1,0:T(8,128)S(1)}, u32[]{:S(2)}, u32[]{:S(2)}) %collective-permute-start.25) | collective-permute-done | bytes 1048608 | tf_op jit(solution)/shard_map/ppermute | solution.py:23
  194.4 1.2 fusion.2
  195.7 0.6 collective-permute-start.28
  196.3 2.5 %collective-permute-start.27 = (f32[16,4,8,128]{3,2,1,0:T(8,128)S(1)}, f32[16,4,8,128]{3,2,1,0:T(8,128)S(1)}, u32[]{:S(2)}, u32[]{:S(2)}) collective-permute-start(f32[16,4,8,128]{3,2,1,0:T(8,128)S(1)} %get-tuple-element.26), channel_id=1, source_target_pairs={{0,64},{16,80},{32,96},{48,112},{64,0},{80,16},{96,32},{112,48},{1... | collective-permute-start | bytes 786440 | tf_op jit(solution)/shard_map/ppermute | solution.py:23
  198.8 4.5 %all-to-all-start = ((bf16[16,2,64,128]{3,2,1,0:T(8,128)(2,1)}), bf16[16,2,64,128]{3,2,1,0:T(8,128)(2,1)S(1)}, u32[]{:S(2)}, u32[]{:S(2)}) async-start(bf16[16,2,64,128]{3,2,1,0:T(8,128)(2,1)} %final.1.x_ref), calls=%async_computation | async-start | bytes 1048576 | tf_op jit(solution)/shard_map/all_to_all | solution.py:462
  203.3 1.6 collective-permute-done.28
  204.9 2.1 collective-permute-done.27
  207.0 4.5 %collective-permute-done.26 = f32[16,4,8,128]{3,2,1,0:T(8,128)S(1)} collective-permute-done((f32[16,4,8,128]{3,2,1,0:T(8,128)S(1)}, f32[16,4,8,128]{3,2,1,0:T(8,128)S(1)}, u32[]{:S(2)}, u32[]{:S(2)}) %collective-permute-start.26) | collective-permute-done | bytes 262176 | tf_op jit(solution)/shard_map/ppermute | solution.py:23
  211.5 1.8 fusion.6
  213.3 1.3 all-to-all-done.x_ref
  214.6 3.7 %all-to-all-start.1 = ((f32[16,4,8,128]{3,2,1,0:T(8,128)}), f32[16,4,8,128]{3,2,1,0:T(8,128)S(1)}, u32[]{:S(2)}, u32[]{:S(2)}) async-start(f32[16,4,8,128]{3,2,1,0:T(8,128)} %fusion.6), calls=%async_computation.1 | async-start | bytes 524288 | tf_op jit(solution)/shard_map/all_to_all | solution.py:484
  218.3 2.4 %ap_layout.1 = bf16[8,8,4096]{2,1,0:T(8,128)(2,1)} custom-call(bf16[16,2,64,128]{3,2,1,0:T(8,128)(2,1)} %copy-done.1), custom_call_target="tpu_custom_call" | custom-call | tf_op jit(solution)/shard_map/ap_layout/pallas_call | solution.py:362
  220.7 6.4 %all-to-all-done.1.x_ref = f32[16,4,8,128]{3,2,1,0:T(8,128)S(1)} async-done(((f32[16,4,8,128]{3,2,1,0:T(8,128)}), f32[16,4,8,128]{3,2,1,0:T(8,128)S(1)}, u32[]{:S(2)}, u32[]{:S(2)}) %all-to-all-start.1) | async-done | bytes 262176 | tf_op jit(solution)/shard_map/all_to_all | solution.py:484
  227.2 0.7 copy-done.4
  227.9 1.9 coarse_layout.1
  (117 shorter events, 6.9 us)
Async XLA Ops:
  2.8 7.4 %copy-start.17 = (s32[8,1,4]{0,2,1:T(4,128)S(1)}, s32[8,1,4]{0,2,1:T(4,128)}, u32[]{:S(2)}) copy-start(s32[8,1,4]{0,2,1:T(4,128)} %param.9) | copy-start | bytes 388
  2.9 7.4 %copy-start.3 = (bf16[8,1,4,4096]{3,2,1,0:T(4,128)(2,1)S(1)}, bf16[8,1,4,4096]{3,2,1,0:T(4,128)(2,1)}, u32[]{:S(2)}) copy-start(bf16[8,1,4,4096]{3,2,1,0:T(4,128)(2,1)} %param.8) | copy-start | bytes 786436
  3.6 17.7 %copy-start.2 = (bf16[9,64,256]{2,1,0:T(8,128)(2,1)}, bf16[9,64,256]{2,1,0:T(8,128)(2,1)S(1)}, u32[]{:S(2)}) copy-start(bf16[9,64,256]{2,1,0:T(8,128)(2,1)S(1)} %pad_maximum_fusion.1.refs_0_) | copy-start | bytes 884740
  3.6 19.8 %collective-permute-start.1 = (bf16[9,64,256]{2,1,0:T(8,128)(2,1)S(1)}, bf16[9,64,256]{2,1,0:T(8,128)(2,1)S(1)}, u32[]{:S(2)}, u32[]{:S(2)}) collective-permute-start(bf16[9,64,256]{2,1,0:T(8,128)(2,1)S(1)} %pad_maximum_fusion.1.refs_0_), channel_id=1, source_target_pairs={{0,32},{16,48},{32,64},{48,80},{64,96},{80,112},{96,0},{112,16},{1... | collective-permute-start | bytes 884744 | tf_op jit(solution)/shard_map/ppermute | solution.py:23
  5.7 17.7 %collective-permute-start.3 = (bf16[9,64,256]{2,1,0:T(8,128)(2,1)S(1)}, bf16[9,64,256]{2,1,0:T(8,128)(2,1)S(1)}, u32[]{:S(2)}, u32[]{:S(2)}) collective-permute-start(bf16[9,64,256]{2,1,0:T(8,128)(2,1)S(1)} %pad_maximum_fusion.1.refs_0_), channel_id=1, source_target_pairs={{0,64},{16,80},{32,96},{48,112},{64,0},{80,16},{96,32},{112,48},{1... | collective-permute-start | bytes 884744 | tf_op jit(solution)/shard_map/ppermute | solution.py:23
  9.3 14.7 %collective-permute-start.5 = (bf16[9,64,256]{2,1,0:T(8,128)(2,1)S(1)}, bf16[9,64,256]{2,1,0:T(8,128)(2,1)S(1)}, u32[]{:S(2)}, u32[]{:S(2)}) collective-permute-start(bf16[9,64,256]{2,1,0:T(8,128)(2,1)S(1)} %pad_maximum_fusion.1.refs_0_), channel_id=1, source_target_pairs={{0,96},{16,112},{32,0},{48,16},{64,32},{80,48},{96,64},{112,80},{1... | collective-permute-start | bytes 884744 | tf_op jit(solution)/shard_map/ppermute | solution.py:23
  11.5 4.4 %copy-start.18 = (s32[128,1,4]{0,2,1:T(4,128)S(1)}, s32[128,1,4]{0,2,1:T(4,128)}, u32[]{:S(2)}) copy-start(s32[128,1,4]{0,2,1:T(4,128)} %param.7) | copy-start | bytes 6148
  12.3 9.0 %collective-permute-start.21 = (bf16[5,64,256]{2,1,0:T(8,128)(2,1)S(1)}, bf16[5,64,256]{2,1,0:T(8,128)(2,1)S(1)}, u32[]{:S(2)}, u32[]{:S(2)}) collective-permute-start(bf16[5,64,256]{2,1,0:T(8,128)(2,1)S(1)} %get-tuple-element.38), channel_id=1, source_target_pairs={{0,3},{1,0},{2,1},{3,2},{4,7},{5,4},{6,5},{7,6},{8,11},{9,8},{10,9... | collective-permute-start | bytes 491528 | tf_op jit(solution)/shard_map/ppermute | solution.py:28
  15.1 6.8 %collective-permute-start.20 = (bf16[5,64,256]{2,1,0:T(8,128)(2,1)S(1)}, bf16[5,64,256]{2,1,0:T(8,128)(2,1)S(1)}, u32[]{:S(2)}, u32[]{:S(2)}) collective-permute-start(bf16[5,64,256]{2,1,0:T(8,128)(2,1)S(1)} %bitcast.137), channel_id=1, source_target_pairs={{0,2},{1,3},{2,0},{3,1},{4,6},{5,7},{6,4},{7,5},{8,10},{9,11},{10,... | collective-permute-start | bytes 491528 | tf_op jit(solution)/shard_map/ppermute | solution.py:28
  21.3 15.1 %collective-permute-start = (bf16[9,64,256]{2,1,0:T(8,128)(2,1)S(1)}, bf16[9,64,256]{2,1,0:T(8,128)(2,1)S(1)}, u32[]{:S(2)}, u32[]{:S(2)}) collective-permute-start(bf16[9,64,256]{2,1,0:T(8,128)(2,1)S(1)} %pad_maximum_fusion.1.refs_0_), channel_id=1, source_target_pairs={{0,16},{16,0},{32,48},{48,32},{64,80},{80,64},{96,112},{112,96},{1... | collective-permute-start | bytes 884744 | tf_op jit(solution)/shard_map/ppermute | solution.py:23
  21.9 11.2 %collective-permute-start.19 = (bf16[5,64,256]{2,1,0:T(8,128)(2,1)S(1)}, bf16[5,64,256]{2,1,0:T(8,128)(2,1)S(1)}, u32[]{:S(2)}, u32[]{:S(2)}) collective-permute-start(bf16[5,64,256]{2,1,0:T(8,128)(2,1)S(1)} %get-tuple-element.38), channel_id=1, source_target_pairs={{0,1},{1,2},{2,3},{3,0},{4,5},{5,6},{6,7},{7,4},{8,9},{9,10},{10,1... | collective-permute-start | bytes 491528 | tf_op jit(solution)/shard_map/ppermute | solution.py:28
  23.4 13.1 %copy-start.6 = (bf16[9,64,256]{2,1,0:T(8,128)(2,1)}, bf16[9,64,256]{2,1,0:T(8,128)(2,1)S(1)}, u32[]{:S(2)}) copy-start(bf16[9,64,256]{2,1,0:T(8,128)(2,1)S(1)} %collective-permute-done.1.refs_2_) | copy-start | bytes 884740
  23.4 13.4 %collective-permute-start.2 = (bf16[9,64,256]{2,1,0:T(8,128)(2,1)S(1)}, bf16[9,64,256]{2,1,0:T(8,128)(2,1)}, u32[]{:S(2)}, u32[]{:S(2)}) collective-permute-start(bf16[9,64,256]{2,1,0:T(8,128)(2,1)S(1)} %collective-permute-done.1.refs_2_), channel_id=1, source_target_pairs={{0,16},{16,0},{32,48},{48,32},{64,80},{80,64},{96,112},{112,96},{1... | collective-permute-start | bytes 884744 | tf_op jit(solution)/shard_map/ppermute | solution.py:23
  23.4 13.1 %copy-start.7 = (bf16[9,64,256]{2,1,0:T(8,128)(2,1)}, bf16[9,64,256]{2,1,0:T(8,128)(2,1)S(1)}, u32[]{:S(2)}) copy-start(bf16[9,64,256]{2,1,0:T(8,128)(2,1)S(1)} %collective-permute-done.3.refs_4_) | copy-start | bytes 884740
  23.4 14.1 %collective-permute-start.4 = (bf16[9,64,256]{2,1,0:T(8,128)(2,1)S(1)}, bf16[9,64,256]{2,1,0:T(8,128)(2,1)}, u32[]{:S(2)}, u32[]{:S(2)}) collective-permute-start(bf16[9,64,256]{2,1,0:T(8,128)(2,1)S(1)} %collective-permute-done.3.refs_4_), channel_id=1, source_target_pairs={{0,16},{16,0},{32,48},{48,32},{64,80},{80,64},{96,112},{112,96},{1... | collective-permute-start | bytes 884744 | tf_op jit(solution)/shard_map/ppermute | solution.py:23
  23.9 12.7 %copy-start.8 = (bf16[9,64,256]{2,1,0:T(8,128)(2,1)}, bf16[9,64,256]{2,1,0:T(8,128)(2,1)S(1)}, u32[]{:S(2)}) copy-start(bf16[9,64,256]{2,1,0:T(8,128)(2,1)S(1)} %collective-permute-done.5.refs_6_) | copy-start | bytes 884740
  23.9 14.4 %collective-permute-start.6 = (bf16[9,64,256]{2,1,0:T(8,128)(2,1)S(1)}, bf16[9,64,256]{2,1,0:T(8,128)(2,1)}, u32[]{:S(2)}, u32[]{:S(2)}) collective-permute-start(bf16[9,64,256]{2,1,0:T(8,128)(2,1)S(1)} %collective-permute-done.5.refs_6_), channel_id=1, source_target_pairs={{0,16},{16,0},{32,48},{48,32},{64,80},{80,64},{96,112},{112,96},{1... | collective-permute-start | bytes 884744 | tf_op jit(solution)/shard_map/ppermute | solution.py:23
  24.7 8.4 %copy-start.16 = (s32[128,8]{0,1:T(8,128)S(1)}, s32[128,8]{0,1:T(8,128)}, u32[]{:S(2)}) copy-start(s32[128,8]{0,1:T(8,128)} %param.10) | copy-start | bytes 12292
  33.3 39.4 %copy-start = (bf16[4,5,64,256]{3,2,1,0:T(8,128)(2,1)}, bf16[4,5,64,256]{3,2,1,0:T(8,128)(2,1)S(1)}, u32[]{:S(2)}) copy-start(bf16[4,5,64,256]{3,2,1,0:T(8,128)(2,1)S(1)} %pad_maximum_fusion.p0_ref) | copy-start | bytes 1966084
  33.3 64.0 %collective-permute-start.24 = (bf16[4,5,64,256]{3,2,1,0:T(8,128)(2,1)S(1)}, bf16[4,5,64,256]{3,2,1,0:T(8,128)(2,1)S(1)}, u32[]{:S(2)}, u32[]{:S(2)}) collective-permute-start(bf16[4,5,64,256]{3,2,1,0:T(8,128)(2,1)S(1)} %pad_maximum_fusion.p0_ref), channel_id=1, source_target_pairs={{0,12},{1,13},{2,14},{3,15},{4,0},{5,1},{6,2},{7,3},{8,4},{9,5},{1... | collective-permute-start | bytes 1966088 | tf_op jit(solution)/shard_map/ppermute | solution.py:28
  36.3 4.0 %copy-start.9 = (bf16[9,64,256]{2,1,0:T(8,128)(2,1)}, bf16[9,64,256]{2,1,0:T(8,128)(2,1)S(1)}, u32[]{:S(2)}) copy-start(bf16[9,64,256]{2,1,0:T(8,128)(2,1)S(1)} %collective-permute-done.refs_1_) | copy-start | bytes 884740
  70.7 33.3 %collective-permute-start.7 = (s16[258,16,128]{2,1,0:T(8,128)(2,1)}, s16[258,16,128]{2,1,0:T(8,128)(2,1)}, u32[]{:S(2)}, u32[]{:S(2)}) collective-permute-start(s16[258,16,128]{2,1,0:T(8,128)(2,1)} %get-tuple-element.22), channel_id=1, source_target_pairs={{0,1},{1,2},{2,3},{3,0},{4,5},{5,6},{6,7},{7,4},{8,9},{9,10},{10,1... | collective-permute-start | bytes 3170312 | tf_op jit(solution)/shard_map/ppermute | solution.py:28
  71.0 28.5 %collective-permute-start.23 = (bf16[4,5,64,256]{3,2,1,0:T(8,128)(2,1)S(1)}, bf16[4,5,64,256]{3,2,1,0:T(8,128)(2,1)}, u32[]{:S(2)}, u32[]{:S(2)}) collective-permute-start(bf16[4,5,64,256]{3,2,1,0:T(8,128)(2,1)S(1)} %pad_maximum_fusion.p0_ref), channel_id=1, source_target_pairs={{0,8},{1,9},{2,10},{3,11},{4,12},{5,13},{6,14},{7,15},{8,0},{9,1},... | collective-permute-start | bytes 1966088 | tf_op jit(solution)/shard_map/ppermute | solution.py:28
  71.7 31.6 %collective-permute-start.22 = (bf16[4,5,64,256]{3,2,1,0:T(8,128)(2,1)S(1)}, bf16[4,5,64,256]{3,2,1,0:T(8,128)(2,1)}, u32[]{:S(2)}, u32[]{:S(2)}) collective-permute-start(bf16[4,5,64,256]{3,2,1,0:T(8,128)(2,1)S(1)} %pad_maximum_fusion.p0_ref), channel_id=1, source_target_pairs={{0,4},{1,5},{2,6},{3,7},{4,8},{5,9},{6,10},{7,11},{8,12},{9,13},{1... | collective-permute-start | bytes 1966088 | tf_op jit(solution)/shard_map/ppermute | solution.py:28
  89.8 16.4 %copy-start.19 = (s32[128,8]{0,1:T(8,128)S(1)}, s32[128,8]{0,1:T(8,128)}, u32[]{:S(2)}) copy-start(s32[128,8]{0,1:T(8,128)} %param.11) | copy-start | bytes 12292
  89.8 30.6 %collective-permute-start.8 = (s16[258,16,128]{2,1,0:T(8,128)(2,1)}, s16[258,16,128]{2,1,0:T(8,128)(2,1)}, u32[]{:S(2)}, u32[]{:S(2)}) collective-permute-start(s16[258,16,128]{2,1,0:T(8,128)(2,1)} %get-tuple-element.21), channel_id=1, source_target_pairs={{0,2},{1,3},{2,0},{3,1},{4,6},{5,7},{6,4},{7,5},{8,10},{9,11},{10,... | collective-permute-start | bytes 3170312 | tf_op jit(solution)/shard_map/ppermute | solution.py:28
  97.2 48.2 %copy-start.5 = (bf16[4,5,64,256]{3,2,1,0:T(8,128)(2,1)}, bf16[4,5,64,256]{3,2,1,0:T(8,128)(2,1)S(1)}, u32[]{:S(2)}) copy-start(bf16[4,5,64,256]{3,2,1,0:T(8,128)(2,1)S(1)} %collective-permute-done.24.p3_ref) | copy-start | bytes 1966084
  97.3 41.8 %collective-permute-start.9 = (s16[258,16,128]{2,1,0:T(8,128)(2,1)}, s16[258,16,128]{2,1,0:T(8,128)(2,1)}, u32[]{:S(2)}, u32[]{:S(2)}) collective-permute-start(s16[258,16,128]{2,1,0:T(8,128)(2,1)} %get-tuple-element.20), channel_id=1, source_target_pairs={{0,3},{1,0},{2,1},{3,2},{4,7},{5,4},{6,5},{7,6},{8,11},{9,8},{10,9... | collective-permute-start | bytes 3170312 | tf_op jit(solution)/shard_map/ppermute | solution.py:28
  99.5 51.9 %collective-permute-start.13 = (s16[258,16,128]{2,1,0:T(8,128)(2,1)}, s16[258,16,128]{2,1,0:T(8,128)(2,1)}, u32[]{:S(2)}, u32[]{:S(2)}) collective-permute-start(s16[258,16,128]{2,1,0:T(8,128)(2,1)} %get-tuple-element.18), channel_id=1, source_target_pairs={{0,4},{1,5},{2,6},{3,7},{4,8},{5,9},{6,10},{7,11},{8,12},{9,13},{1... | collective-permute-start | bytes 3170312 | tf_op jit(solution)/shard_map/ppermute | solution.py:28
  103.3 49.2 %collective-permute-start.14 = (s16[258,16,128]{2,1,0:T(8,128)(2,1)S(1)}, s16[258,16,128]{2,1,0:T(8,128)(2,1)}, u32[]{:S(2)}, u32[]{:S(2)}) collective-permute-start(s16[258,16,128]{2,1,0:T(8,128)(2,1)S(1)} %get-tuple-element.17), channel_id=1, source_target_pairs={{0,8},{1,9},{2,10},{3,11},{4,12},{5,13},{6,14},{7,15},{8,0},{9,1},... | collective-permute-start | bytes 3170312 | tf_op jit(solution)/shard_map/ppermute | solution.py:28
  104.0 48.5 %collective-permute-start.15 = (s16[258,16,128]{2,1,0:T(8,128)(2,1)S(1)}, s16[258,16,128]{2,1,0:T(8,128)(2,1)}, u32[]{:S(2)}, u32[]{:S(2)}) collective-permute-start(s16[258,16,128]{2,1,0:T(8,128)(2,1)S(1)} %get-tuple-element.16), channel_id=1, source_target_pairs={{0,12},{1,13},{2,14},{3,15},{4,0},{5,1},{6,2},{7,3},{8,4},{9,5},{1... | collective-permute-start | bytes 3170312 | tf_op jit(solution)/shard_map/ppermute | solution.py:28
  147.7 17.4 %collective-permute-start.10 = (s16[65,16,128]{2,1,0:T(8,128)(2,1)}, s16[65,16,128]{2,1,0:T(8,128)(2,1)S(1)}, u32[]{:S(2)}, u32[]{:S(2)}) collective-permute-start(s16[65,16,128]{2,1,0:T(8,128)(2,1)} %get-tuple-element.33), channel_id=1, source_target_pairs={{0,4},{1,5},{2,6},{3,7},{4,8},{5,9},{6,10},{7,11},{8,12},{9,13},{1... | collective-permute-start | bytes 798728 | tf_op jit(solution)/shard_map/ppermute | solution.py:28
  149.6 18.3 %collective-permute-start.11 = (s16[65,16,128]{2,1,0:T(8,128)(2,1)}, s16[65,16,128]{2,1,0:T(8,128)(2,1)S(1)}, u32[]{:S(2)}, u32[]{:S(2)}) collective-permute-start(s16[65,16,128]{2,1,0:T(8,128)(2,1)} %get-tuple-element.32), channel_id=1, source_target_pairs={{0,8},{1,9},{2,10},{3,11},{4,12},{5,13},{6,14},{7,15},{8,0},{9,1},... | collective-permute-start | bytes 798728 | tf_op jit(solution)/shard_map/ppermute | solution.py:28
  151.4 16.5 %collective-permute-start.12 = (s16[65,16,128]{2,1,0:T(8,128)(2,1)}, s16[65,16,128]{2,1,0:T(8,128)(2,1)S(1)}, u32[]{:S(2)}, u32[]{:S(2)}) collective-permute-start(s16[65,16,128]{2,1,0:T(8,128)(2,1)} %get-tuple-element.31), channel_id=1, source_target_pairs={{0,12},{1,13},{2,14},{3,15},{4,0},{5,1},{6,2},{7,3},{8,4},{9,5},{1... | collective-permute-start | bytes 798728 | tf_op jit(solution)/shard_map/ppermute | solution.py:28
  161.0 9.2 %collective-permute-start.16 = (s16[65,16,128]{2,1,0:T(8,128)(2,1)S(1)}, s16[65,16,128]{2,1,0:T(8,128)(2,1)S(1)}, u32[]{:S(2)}, u32[]{:S(2)}) collective-permute-start(s16[65,16,128]{2,1,0:T(8,128)(2,1)S(1)} %get-tuple-element.29), channel_id=1, source_target_pairs={{0,1},{1,2},{2,3},{3,0},{4,5},{5,6},{6,7},{7,4},{8,9},{9,10},{10,1... | collective-permute-start | bytes 798728 | tf_op jit(solution)/shard_map/ppermute | solution.py:28
  163.4 12.9 %collective-permute-start.17 = (s16[65,16,128]{2,1,0:T(8,128)(2,1)S(1)}, s16[65,16,128]{2,1,0:T(8,128)(2,1)S(1)}, u32[]{:S(2)}, u32[]{:S(2)}) collective-permute-start(s16[65,16,128]{2,1,0:T(8,128)(2,1)S(1)} %get-tuple-element.28), channel_id=1, source_target_pairs={{0,2},{1,3},{2,0},{3,1},{4,6},{5,7},{6,4},{7,5},{8,10},{9,11},{10,... | collective-permute-start | bytes 798728 | tf_op jit(solution)/shard_map/ppermute | solution.py:28
  165.1 11.3 %copy-start.10 = (s16[65,16,128]{2,1,0:T(8,128)(2,1)}, s16[65,16,128]{2,1,0:T(8,128)(2,1)S(1)}, u32[]{:S(2)}) copy-start(s16[65,16,128]{2,1,0:T(8,128)(2,1)S(1)} %collective-permute-done.10.refs_1_) | copy-start | bytes 798724
  165.1 11.2 %collective-permute-start.18 = (s16[65,16,128]{2,1,0:T(8,128)(2,1)S(1)}, s16[65,16,128]{2,1,0:T(8,128)(2,1)S(1)}, u32[]{:S(2)}, u32[]{:S(2)}) collective-permute-start(s16[65,16,128]{2,1,0:T(8,128)(2,1)S(1)} %get-tuple-element.27), channel_id=1, source_target_pairs={{0,3},{1,0},{2,1},{3,2},{4,7},{5,4},{6,5},{7,6},{8,11},{9,8},{10,9... | collective-permute-start | bytes 798728 | tf_op jit(solution)/shard_map/ppermute | solution.py:28
  167.9 8.4 %copy-start.11 = (s16[65,16,128]{2,1,0:T(8,128)(2,1)}, s16[65,16,128]{2,1,0:T(8,128)(2,1)S(1)}, u32[]{:S(2)}) copy-start(s16[65,16,128]{2,1,0:T(8,128)(2,1)S(1)} %collective-permute-done.11.refs_2_) | copy-start | bytes 798724
  167.9 8.5 %copy-start.12 = (s16[65,16,128]{2,1,0:T(8,128)(2,1)}, s16[65,16,128]{2,1,0:T(8,128)(2,1)S(1)}, u32[]{:S(2)}) copy-start(s16[65,16,128]{2,1,0:T(8,128)(2,1)S(1)} %collective-permute-done.12.refs_3_) | copy-start | bytes 798724
  170.2 6.1 %copy-start.13 = (s16[65,16,128]{2,1,0:T(8,128)(2,1)}, s16[65,16,128]{2,1,0:T(8,128)(2,1)S(1)}, u32[]{:S(2)}) copy-start(s16[65,16,128]{2,1,0:T(8,128)(2,1)S(1)} %collective-permute-done.16.refs_5_) | copy-start | bytes 798724
  176.3 0.7 copy-start.14
  176.3 0.8 copy-start.15
  191.6 2.9 %collective-permute-start.25 = (f32[4,16,4,8,128]{4,3,2,1,0:T(8,128)}, f32[4,16,4,8,128]{4,3,2,1,0:T(8,128)S(1)}, u32[]{:S(2)}, u32[]{:S(2)}) collective-permute-start(f32[4,16,4,8,128]{4,3,2,1,0:T(8,128)} %get-tuple-element.5), channel_id=1, source_target_pairs={{0,16},{16,0},{32,48},{48,32},{64,80},{80,64},{96,112},{112,96},{1... | collective-permute-start | bytes 3145736 | tf_op jit(solution)/shard_map/ppermute | solution.py:23
  195.7 9.2 %collective-permute-start.28 = (f32[16,4,8,128]{3,2,1,0:T(8,128)S(1)}, f32[16,4,8,128]{3,2,1,0:T(8,128)S(1)}, u32[]{:S(2)}, u32[]{:S(2)}) collective-permute-start(f32[16,4,8,128]{3,2,1,0:T(8,128)S(1)} %get-tuple-element.25), channel_id=1, source_target_pairs={{0,96},{16,112},{32,0},{48,16},{64,32},{80,48},{96,64},{112,80},{1... | collective-permute-start | bytes 786440 | tf_op jit(solution)/shard_map/ppermute | solution.py:23
  196.3 10.7 %collective-permute-start.27 = (f32[16,4,8,128]{3,2,1,0:T(8,128)S(1)}, f32[16,4,8,128]{3,2,1,0:T(8,128)S(1)}, u32[]{:S(2)}, u32[]{:S(2)}) collective-permute-start(f32[16,4,8,128]{3,2,1,0:T(8,128)S(1)} %get-tuple-element.26), channel_id=1, source_target_pairs={{0,64},{16,80},{32,96},{48,112},{64,0},{80,16},{96,32},{112,48},{1... | collective-permute-start | bytes 786440 | tf_op jit(solution)/shard_map/ppermute | solution.py:23
  198.8 12.6 %collective-permute-start.26 = (f32[16,4,8,128]{3,2,1,0:T(8,128)S(1)}, f32[16,4,8,128]{3,2,1,0:T(8,128)S(1)}, u32[]{:S(2)}, u32[]{:S(2)}) collective-permute-start(f32[16,4,8,128]{3,2,1,0:T(8,128)S(1)} %get-tuple-element.24), channel_id=1, source_target_pairs={{0,32},{16,48},{32,64},{48,80},{64,96},{80,112},{96,0},{112,16},{1... | collective-permute-start | bytes 786440 | tf_op jit(solution)/shard_map/ppermute | solution.py:23
  198.8 15.8 %all-to-all-start = ((bf16[16,2,64,128]{3,2,1,0:T(8,128)(2,1)}), bf16[16,2,64,128]{3,2,1,0:T(8,128)(2,1)S(1)}, u32[]{:S(2)}, u32[]{:S(2)}) async-start(bf16[16,2,64,128]{3,2,1,0:T(8,128)(2,1)} %final.1.x_ref), calls=%async_computation | async-start | bytes 1048576 | tf_op jit(solution)/shard_map/all_to_all | solution.py:462
  214.6 3.7 %copy-start.1 = (bf16[16,2,64,128]{3,2,1,0:T(8,128)(2,1)}, bf16[16,2,64,128]{3,2,1,0:T(8,128)(2,1)S(1)}, u32[]{:S(2)}) copy-start(bf16[16,2,64,128]{3,2,1,0:T(8,128)(2,1)S(1)} %all-to-all-done.x_ref) | copy-start | bytes 1572868
  214.6 12.6 %all-to-all-start.1 = ((f32[16,4,8,128]{3,2,1,0:T(8,128)}), f32[16,4,8,128]{3,2,1,0:T(8,128)S(1)}, u32[]{:S(2)}, u32[]{:S(2)}) async-start(f32[16,4,8,128]{3,2,1,0:T(8,128)} %fusion.6), calls=%async_computation.1 | async-start | bytes 524288 | tf_op jit(solution)/shard_map/all_to_all | solution.py:484
  227.2 0.7 copy-start.4
where the time goes:
time: 231 us; the launch traced here: 230 us
  Pallas kernels  82.6 us (36%)
  waiting for transfers between devices  66.9 us (29%)
  starting transfers between devices  48.5 us (21%)
  local copies, waits for them, and re-layouts  25.2 us (11%)
  other arithmetic  4.92 us (2%)
    ppermute x18, waiting for transfers between devices, along_col(): return lax.ppermute(v, 'col', pairs)  48.1 us
    pallas_call x2, Pallas kernels, products(): pl.pallas_call(lambda *refs: product_kernel(color, *refs), grid_spec=pltp...  34.1 us
    ppermute x18, starting transfers between devices, along_col(): return lax.ppermute(v, 'col', pairs)  29.9 us
    pallas_call x2, Pallas kernels, middle(): pl.pallas_call(lambda *refs: middle_kernel(color, *refs), in_specs=[pl.Bl...  12.7 us
    pallas_call x1, Pallas kernels, coarse_terms(): pl.pallas_call(coarse_kernel, grid_spec=pltpu.PrefetchScalarGridSpec(num_...  11.5 us
    ppermute x11, waiting for transfers between devices, along_row(): return lax.ppermute(v, 'row', pairs)  11 us
    ppermute x11, starting transfers between devices, along_row(): return lax.ppermute(v, 'row', pairs)  10.4 us
    pallas_call x1, Pallas kernels, table(): pl.pallas_call(table_kernel, in_specs=[whole] * 8, out_specs=whole, out_s...  8.69 us
  transfers between devices with their start and end apart: 31, of which 13 were waited for; matrix products, arithmetic and copies ran while one was open for 11% of the time, Pallas kernels for 29%

commit v1 on v0

--- a/solution.py
+++ b/solution.py
@@ -68,9 +68,11 @@
 
 
 def table_kernel(*refs):
-    parts, out_ref = refs[:8], refs[8]
+    parts, out_ref, cols_ref = refs[:8], refs[8], refs[9]
     low = low_lanes(B)
     for n, part in enumerate(parts):
+        cols_ref[n * 8:(n + 1) * 8, :] = part[8, 0:8, 0:128].astype(jnp.float32)
+
         def fill(q, carry):
             for mh in range(2):
                 v = part[q, :, mh * 128:(mh + 1) * 128]
@@ -80,7 +82,7 @@
                 out_ref[at + 1] = jnp.where(low, turned, v)
             return carry
 
-        lax.fori_loop(0, 8, fill, 0)
+        lax.fori_loop(0, 8, fill, 0, unroll=2)
     out_ref[NK * KP] = jnp.zeros((B, 128), jnp.bfloat16)
 
 
@@ -89,8 +91,11 @@
     return pl.pallas_call(
         table_kernel,
         in_specs=[whole] * 8,
-        out_specs=whole,
-        out_shape=jax.ShapeDtypeStruct((NK * KP + 1, B, 128), jnp.bfloat16),
+        out_specs=[whole, whole],
+        out_shape=[
+            jax.ShapeDtypeStruct((NK * KP + 1, B, 128), jnp.bfloat16),
+            jax.ShapeDtypeStruct((NK, 128), jnp.float32),
+        ],
         name="table",
     )(*parts)
 
@@ -107,139 +112,226 @@
     return jnp.round(v * mul).astype(jnp.int32).astype(jnp.int16)
 
 
-def product_kernel(color, idx_ref, at_ref, a_ref, dup_ref, out_ref, exp_ref):
-    ih = pl.program_id(0)
-    cblk = pl.program_id(1)
+def row_pair(lhs, rhs_top, rhs_bottom):
+    zero = jnp.zeros((B, KA * B), jnp.bfloat16)
+    stacked = jnp.concatenate(
+        [
+            jnp.concatenate([rhs_top, zero], axis=1),
+            jnp.concatenate([zero, rhs_bottom], axis=1),
+        ],
+        axis=0,
+    )
+    return nt_dot(lhs, stacked)
+
+
+def chosen_blocks(idx_ref, dup_ref, low, first_row):
+    rows = []
+    for s in range(KAP):
+        pieces = []
+        for lo in range(2):
+            base = (first_row + lo * NCOL) * (KA * KAP)
+            for ep in range(2):
+                first = dup_ref[idx_ref[base + (2 * ep) * KAP + s]]
+                second = dup_ref[idx_ref[base + (2 * ep + 1) * KAP + s]]
+                pieces.append(jnp.where(low, first, second))
+        rows.append(jnp.concatenate(pieces, axis=1))
+    return jnp.concatenate(rows, axis=0)
+
+
+def coded_products(res):
+    e = exponent(jnp.max(jnp.abs(res), axis=0, keepdims=True))
+    q = jnp.round(res * jnp.exp2(FULL - e)).astype(jnp.int32)
+
+    def tile(bg, sp):
+        r0 = 2 * sp * B + bg * 8
+        return jnp.concatenate([q[r0:r0 + 8], q[r0 + B:r0 + B + 8]], axis=0)
+
+    return e, tile
+
+
+def x_product_kernel(j, idx_ref, at_ref, a_ref, dup_ref, near_ref, far_ref, exp_ref):
+    cblk = pl.program_id(0)
     low = low_lanes(B)
-    mine = at_ref[color]
+    goal = lax.rem(at_ref[0] + j, 4)
+    ih = lax.rem(goal, 2)
     count = a_ref.shape[2]
-    zero = jnp.zeros((B, KA * B), jnp.bfloat16)
+    is_low = goal < 2
 
     def one(cc, carry):
-        rows = []
-        for s in range(KAP):
-            pieces = []
-            for lo in range(2):
-                base = (((ih * 4 + color * 2 + lo) * NCOL) + cblk * count + cc) * (KA * KAP)
-                for ep in range(2):
-                    first = dup_ref[idx_ref[base + (2 * ep) * KAP + s]]
-                    second = dup_ref[idx_ref[base + (2 * ep + 1) * KAP + s]]
-                    pieces.append(jnp.where(low, first, second))
-            rows.append(jnp.concatenate(pieces, axis=1))
-        stacked = jnp.concatenate(
-            [
-                jnp.concatenate([a_ref[0, 0, cc], zero], axis=1),
-                jnp.concatenate([zero, a_ref[0, 1, cc]], axis=1),
-            ],
-            axis=0,
-        )
-        res = nt_dot(jnp.concatenate(rows, axis=0), stacked)
-        most = jnp.max(jnp.abs(res), axis=0, keepdims=True)
-        e = exponent(most)
-        q = jnp.round(res * jnp.exp2(FULL - e)).astype(jnp.int32)
         c = cblk * count + cc
-        exp_ref[ih, pl.ds(c, 1), :] = e
-        for bg in range(8):
-            g = bg % 2
-            if color == 0:
-                d = lax.rem(2 * g + ih - mine + 4, 4)
-                u = bg // 2
-            else:
-                d = lax.rem(bg // 2 - mine + 4, 4)
-                u = 2 * g + ih
+        lhs = chosen_blocks(idx_ref, dup_ref, low, ih * 4 * NCOL + c)
+        res = row_pair(lhs, a_ref[0, 0, cc], a_ref[0, 1, cc])
+        e, tile = coded_products(res)
+        exp_ref[pl.ds(c, 1), :] = e
+        for u in range(4):
             for sp in range(4):
-                r0 = 2 * sp * B + bg * 8
-                pair = jnp.concatenate([q[r0:r0 + 8], q[r0 + B:r0 + B + 8]], axis=0)
-                out_ref[d, (u * NCOL + c) * 4 + sp] = pair.astype(jnp.int16)
-
+                t0, t1 = tile(2 * u, sp), tile(2 * u + 1, sp)
+                at = (u * NCOL + c) * 4 + sp
+                near_ref[at] = jnp.where(is_low, t0, t1).astype(jnp.int16)
+                far_ref[at] = jnp.where(is_low, t1, t0).astype(jnp.int16)
         return carry
 
     lax.fori_loop(0, count, one, 0)
 
-    @pl.when((ih == 1) & (cblk == pl.num_programs(1) - 1))
+    @pl.when(cblk == pl.num_programs(0) - 1)
     def _():
-        for d in range(4):
-            for t in range(2):
-                source = lax.rem(mine + d, 2) if color == 0 else t
-                out_ref[d, 256 + t] = exp_ref[source].astype(jnp.int32).astype(jnp.int16)
-
-
-def products(color, idx, at, a, dup):
+        e = exp_ref[...].astype(jnp.int32).astype(jnp.int16)
+        near_ref[256] = e
+        far_ref[256] = e
+
+
+def x_products(j, idx, at, a, dup):
     block = 8
-    return pl.pallas_call(
-        lambda *refs: product_kernel(color, *refs),
+    out = pl.BlockSpec((257, 16, 128), lambda c, idx, at: (0, 0, 0))
+    return pl.pallas_call(
+        lambda *refs: x_product_kernel(j, *refs),
         grid_spec=pltpu.PrefetchScalarGridSpec(
             num_scalar_prefetch=2,
-            grid=(2, NCOL // block),
+            grid=(NCOL // block,),
             in_specs=[
                 pl.BlockSpec(
-                    (1, 2, block, B, KA * B), lambda ih, c, idx, at: (ih * 2 + color, 0, c, 0, 0)
+                    (1, 2, block, B, KA * B),
+                    lambda c, idx, at: (lax.rem(at[0] + j, 2) * 2, 0, c, 0, 0),
                 ),
-                pl.BlockSpec((NK * KP + 1, B, 128), lambda ih, c, idx, at: (0, 0, 0)),
+                pl.BlockSpec((NK * KP + 1, B, 128), lambda c, idx, at: (0, 0, 0)),
             ],
-            out_specs=pl.BlockSpec((4, 258, 16, 128), lambda ih, c, idx, at: (0, 0, 0, 0)),
-            scratch_shapes=[
-                pltpu.VMEM((2, NCOL, 128), jnp.float32),
+            out_specs=[out, out],
+            scratch_shapes=[pltpu.VMEM((NCOL, 128), jnp.float32)],
+        ),
+        out_shape=[jax.ShapeDtypeStruct((257, 16, 128), jnp.int16)] * 2,
+    )(idx, at, a, dup)
+
+
+def y_product_kernel(part, idx_ref, at_ref, a_ref, dup_ref, o0_ref, o1_ref, o2_ref, o3_ref, exp_ref):
+    ih = pl.program_id(0)
+    low = low_lanes(B)
+    y = at_ref[1]
+    count = a_ref.shape[2]
+    outs = (o0_ref, o1_ref, o2_ref, o3_ref)
+    turn1 = lax.rem(y, 2) == 1
+    turn2 = y >= 2
+
+    def one(cc, carry):
+        lhs = chosen_blocks(idx_ref, dup_ref, low, (ih * 4 + 2) * NCOL + part * count + cc)
+        res = row_pair(lhs, a_ref[0, 0, cc], a_ref[0, 1, cc])
+        e, tile = coded_products(res)
+        exp_ref[pl.ds(ih * 8 + cc, 1), :] = e
+        for g in range(2):
+            for sp in range(4):
+                t = [tile(2 * k + g, sp) for k in range(4)]
+                t = [jnp.where(turn1, t[(k + 1) % 4], t[k]) for k in range(4)]
+                t = [jnp.where(turn2, t[(k + 2) % 4], t[k]) for k in range(4)]
+                for d in range(4):
+                    outs[d][((2 * g + ih) * 8 + cc) * 4 + sp] = t[d].astype(jnp.int16)
+        return carry
+
+    lax.fori_loop(0, count, one, 0)
+
+    @pl.when(ih == 1)
+    def _():
+        e = exp_ref[...].astype(jnp.int32).astype(jnp.int16)
+        for o_ref in outs:
+            o_ref[128] = e
+
+
+def y_products(part, idx, at, a, dup):
+    block = 8
+    out = pl.BlockSpec((129, 16, 128), lambda ih, idx, at: (0, 0, 0))
+    return pl.pallas_call(
+        lambda *refs: y_product_kernel(part, *refs),
+        grid_spec=pltpu.PrefetchScalarGridSpec(
+            num_scalar_prefetch=2,
+            grid=(2,),
+            in_specs=[
+                pl.BlockSpec(
+                    (1, 2, block, B, KA * B), lambda ih, idx, at: (ih * 2 + 1, 0, part, 0, 0)
+                ),
+                pl.BlockSpec((NK * KP + 1, B, 128), lambda ih, idx, at: (0, 0, 0)),
             ],
+            out_specs=[out] * 4,
+            scratch_shapes=[pltpu.VMEM((NCOL, 128), jnp.float32)],
         ),
-        out_shape=jax.ShapeDtypeStruct((4, 258, 16, 128), jnp.int16),
+        out_shape=[jax.ShapeDtypeStruct((129, 16, 128), jnp.int16)] * 4,
     )(idx, at, a, dup)
 
 
-def middle_kernel(color, at_ref, own_ref, m1_ref, m2_ref, m3_ref, out_ref, scale_ref, exp_ref):
-    other = at_ref[1 - color]
-    for d, m in enumerate((own_ref, m1_ref, m2_ref, m3_ref)):
-        for t in range(2):
-            scale_ref[d, t] = jnp.exp2(m[256 + t].astype(jnp.float32) - FULL)
-
-    for u in range(4):
-        d2 = lax.rem(u - other + 4, 4)
+def sum_and_code(tiles, out_ref, c):
+    most = jnp.maximum(
+        jnp.maximum(jnp.abs(tiles[0]), jnp.abs(tiles[1])),
+        jnp.maximum(jnp.abs(tiles[2]), jnp.abs(tiles[3])),
+    )
+    e = exponent(jnp.max(most, axis=0, keepdims=True))
+    mul = jnp.exp2(FULL - e)
+    for sp in range(4):
+        out_ref[c * 4 + sp] = coded(tiles[sp], mul)
+    return e
+
+
+def x_middle_kernel(at_ref, m0, m1, m2, m3, o0, o1, o2, o3, scale_ref, exp_ref):
+    parts = (m0, m1, m2, m3)
+    for d, m in enumerate(parts):
+        scale_ref[d] = jnp.exp2(m[256].astype(jnp.float32) - FULL)
+    for d2, out_ref in enumerate((o0, o1, o2, o3)):
+        u = lax.rem(at_ref[1] + d2, 4)
 
         def one(c, carry):
-            t = 0 if color == 0 else u % 2
-            scales = [scale_ref[d, t, pl.ds(c, 1), :] for d in range(4)]
-            sums = []
+            scales = [scale_ref[d, pl.ds(c, 1), :] for d in range(4)]
+            tiles = []
             for sp in range(4):
-                total = None
-                for d, m in enumerate((own_ref, m1_ref, m2_ref, m3_ref)):
-                    term = m[(u * NCOL + c) * 4 + sp].astype(jnp.float32) * scales[d]
-                    total = term if total is None else total + term
-                sums.append(total)
-            most = sums[0]
-            most = jnp.maximum(
-                jnp.maximum(jnp.abs(sums[0]), jnp.abs(sums[1])),
-                jnp.maximum(jnp.abs(sums[2]), jnp.abs(sums[3])),
-            )
-            e = exponent(jnp.max(most, axis=0, keepdims=True))
-            mul = jnp.exp2(FULL - e)
-            exp_ref[u, pl.ds(c, 1), :] = e
-            for sp in range(4):
-                out_ref[d2, c * 4 + sp] = coded(sums[sp], mul)
+                terms = [
+                    m[(u * NCOL + c) * 4 + sp].astype(jnp.float32) * scale
+                    for m, scale in zip(parts, scales)
+                ]
+                tiles.append((terms[0] + terms[1]) + (terms[2] + terms[3]))
+            exp_ref[pl.ds(c, 1), :] = sum_and_code(tiles, out_ref, c)
             return carry
 
-        lax.fori_loop(0, NCOL, one, 0)
-        out_ref[d2, 64] = exp_ref[u].astype(jnp.int32).astype(jnp.int16)
-
-
-def middle(color, at, own, m1, m2, m3):
+        lax.fori_loop(0, NCOL, one, 0, unroll=2)
+        out_ref[64] = exp_ref[...].astype(jnp.int32).astype(jnp.int16)
+
+
+def y_middle_kernel(at_ref, *refs):
+    parts, outs, scale_ref, exp_ref = refs[:8], refs[8:12], refs[12], refs[13]
+    for n, m in enumerate(parts):
+        scale_ref[n] = jnp.exp2(m[128].astype(jnp.float32) - FULL)
+    for d2, out_ref in enumerate(outs):
+        u = lax.rem(at_ref[0] + d2, 4)
+        ih = lax.rem(u, 2)
+        for half in range(2):
+            own = parts[half * 4:half * 4 + 4]
+
+            def one(cc, carry):
+                scales = [scale_ref[half * 4 + d, pl.ds(ih * 8 + cc, 1), :] for d in range(4)]
+                tiles = []
+                for sp in range(4):
+                    terms = [
+                        m[(u * 8 + cc) * 4 + sp].astype(jnp.float32) * scale
+                        for m, scale in zip(own, scales)
+                    ]
+                    tiles.append((terms[0] + terms[1]) + (terms[2] + terms[3]))
+                c = half * 8 + cc
+                exp_ref[pl.ds(c, 1), :] = sum_and_code(tiles, out_ref, c)
+                return carry
+
+            lax.fori_loop(0, 8, one, 0, unroll=2)
+        out_ref[64] = exp_ref[...].astype(jnp.int32).astype(jnp.int16)
+
+
+def middle(kernel, at, parts):
     vmem = pl.BlockSpec(memory_space=pltpu.VMEM)
     return pl.pallas_call(
-        lambda *refs: middle_kernel(color, *refs),
-        in_specs=[
-            pl.BlockSpec(memory_space=pltpu.SMEM),
-            vmem, vmem, vmem, vmem,
+        kernel,
+        in_specs=[pl.BlockSpec(memory_space=pltpu.SMEM)] + [vmem] * len(parts),
+        out_specs=[vmem] * 4,
+        scratch_shapes=[
+            pltpu.VMEM((len(parts), NCOL, 128), jnp.float32),
+            pltpu.VMEM((NCOL, 128), jnp.float32),
         ],
-        out_specs=vmem,
-        scratch_shapes=[
-            pltpu.VMEM((4, 2, NCOL, 128), jnp.float32),
-            pltpu.VMEM((4, NCOL, 128), jnp.float32),
-        ],
-        out_shape=jax.ShapeDtypeStruct((4, 65, 16, 128), jnp.int16),
-    )(at, own, m1, m2, m3)
-
-
-def final_kernel(*refs):
-    parts, out_ref, scale_ref = refs[:8], refs[8], refs[9]
+        out_shape=[jax.ShapeDtypeStruct((65, 16, 128), jnp.int16)] * 4,
+    )(at, *parts)
+
+
+def decode(parts, out_ref, scale_ref):
     for n, m in enumerate(parts):
         scale_ref[n] = jnp.exp2(m[64].astype(jnp.float32) - FULL)
 
@@ -247,30 +339,19 @@
         for qh in range(2):
             scales = [scale_ref[qh * 4 + d, pl.ds(c, 1), :] for d in range(4)]
             for sp in range(4):
-                total = None
-                for d in range(4):
-                    m = parts[qh * 4 + d]
-                    term = m[c * 4 + sp].astype(jnp.float32) * scales[d]
-                    total = term if total is None else total + term
+                terms = [
+                    parts[qh * 4 + d][c * 4 + sp].astype(jnp.float32) * scales[d] for d in range(4)
+                ]
+                total = (terms[0] + terms[1]) + (terms[2] + terms[3])
                 out_ref[c, qh, sp * 16:(sp + 1) * 16, :] = total.astype(jnp.bfloat16)
         return carry
 
     lax.fori_loop(0, NCOL, one, 0)
 
 
-def final(parts):
-    vmem = pl.BlockSpec(memory_space=pltpu.VMEM)
-    return pl.pallas_call(
-        final_kernel,
-        in_specs=[vmem] * 8,
-        out_specs=vmem,
-        scratch_shapes=[pltpu.VMEM((8, NCOL, 128), jnp.float32)],
-        out_shape=jax.ShapeDtypeStruct((NCOL, 2, B, 128), jnp.bfloat16),
-        name="final",
-    )(*parts)
-
-
-def coarse_kernel(tgt_ref, at_ref, x_ref, p0_ref, p1_ref, p2_ref, p3_ref, keep_ref, send_ref, acc_ref):
+def coarse_kernel(tgt_ref, at_ref, *refs):
+    parts, (p0_ref, p1_ref, p2_ref, p3_ref) = refs[:8], refs[8:12]
+    x_ref, keep_ref, send_ref, acc_ref, scale_ref = refs[12:]
     dx = pl.program_id(0)
     low = low_lanes(8)
     low_x = low_lanes(B)
@@ -279,6 +360,7 @@
     @pl.when(dx == 0)
     def _():
         acc_ref[...] = jnp.zeros_like(acc_ref)
+        decode(parts, x_ref, scale_ref)
 
     for dy, p_ref in enumerate((p0_ref, p1_ref, p2_ref, p3_ref)):
         c = lax.rem(my_y - dy + 4, 4) * 4 + lax.rem(my_x - dx + 4, 4)
@@ -322,7 +404,7 @@
                 lax.fori_loop(0, NCOL, fold, 0, unroll=4)
 
 
-def coarse_terms(tgt, at, x, ps):
+def coarse_terms(tgt, at, parts, ps):
     shape = (4, NCOL, KC // 2, 8, 128)
     out = pl.BlockSpec(shape, lambda dx, tgt, at: (0, 0, 0, 0, 0))
     return pl.pallas_call(
@@ -330,14 +412,23 @@
         grid_spec=pltpu.PrefetchScalarGridSpec(
             num_scalar_prefetch=2,
             grid=(4,),
-            in_specs=[pl.BlockSpec((NCOL, 2, B, 128), lambda dx, tgt, at: (0, 0, 0, 0))]
+            in_specs=[pl.BlockSpec((65, 16, 128), lambda dx, tgt, at: (0, 0, 0))] * 8
             + [pl.BlockSpec((1, 5, B, KP * B), lambda dx, tgt, at: (dx, 0, 0, 0))] * 4,
-            out_specs=[out, out],
-            scratch_shapes=[pltpu.VMEM((NCB * KC + 1, 8, 128), jnp.float32)],
+            out_specs=[
+                pl.BlockSpec((NCOL, 2, B, 128), lambda dx, tgt, at: (0, 0, 0, 0)), out, out
+            ],
+            scratch_shapes=[
+                pltpu.VMEM((NCB * KC + 1, 8, 128), jnp.float32),
+                pltpu.VMEM((8, NCOL, 128), jnp.float32),
+            ],
         ),
-        out_shape=[jax.ShapeDtypeStruct(shape, jnp.float32)] * 2,
+        out_shape=[
+            jax.ShapeDtypeStruct((NCOL, 2, B, 128), jnp.bfloat16),
+            jax.ShapeDtypeStruct(shape, jnp.float32),
+            jax.ShapeDtypeStruct(shape, jnp.float32),
+        ],
         name="coarse_terms",
-    )(tgt, at, x, *ps)
+    )(tgt, at, *parts, *ps)
 
 
 def ap_out_kernel(x_ref, out_ref, turn_ref):
@@ -418,9 +509,7 @@
     pt = own.transpose(0, 3, 1, 2).reshape(8, B, KP * B)
     pt = jnp.concatenate([pt, index_slab(p_index[:, 0])], axis=0)
     by_z = [pt] + [along_row(pt, d, 0) for d in (1, 2, 3)]
-    parts = []
-    for part in by_z:
-        parts += [part, along_row(part, 0, 1)]
+    partner = along_row(pt, 0, 1)
 
     pn = own.reshape(8, KP, 32, 2, B).transpose(0, 3, 2, 1, 4).reshape(2, 4, B, KP * B)
     halves = jnp.stack(
@@ -429,11 +518,14 @@
             for h in range(2)
         ]
     )
+    *by_z, halves = lax.optimization_barrier((*by_z, halves))
+    parts = [by_z[0], partner]
+    for part in by_z[1:]:
+        parts += [part, along_row(part, 0, 1)]
     same = lax.dynamic_index_in_dim(halves, half, 0, keepdims=False)
     diff = lax.dynamic_index_in_dim(halves, 1 - half, 0, keepdims=False)
-    by_x = jnp.stack(
-        [same, along_col(diff, 1, 0), along_col(same, 2, 0), along_col(diff, 3, 0)]
-    )
+    by_x = [same, along_col(diff, 1, 0), along_col(same, 2, 0), along_col(diff, 3, 0)]
+    by_x = jnp.stack(by_x)
     ps = [by_x] + [along_col(by_x, 0, d) for d in (1, 2, 3)]
 
     a = spread(a_blocks[:, 0]).reshape(4, 2, NCOL, B, KA * B)
@@ -442,25 +534,11 @@
     from_row = a_idx // 8
     place = ((z - from_row // 2) % 4) * 2 + (core + from_row) % 2
     place = place * 8 + a_idx % 8
-    cols_k = jnp.concatenate([part[8, :8, :KP] for part in parts], axis=0)
-    picked = pick_rows(cols_k, place)
+    dup, cols_k = table(parts)
+    picked = pick_rows(cols_k[:, :KP], place)
     equal = picked[:, :, None, :] == ap_index[:, None, :, None]
     ids = place[:, :, None, None] * KP + jnp.arange(KP, dtype=jnp.int32)
     idx = jnp.min(jnp.where(equal, ids, NK * KP), axis=3).reshape(-1)
-
-    dup = table(parts)
-    q0 = products(0, idx, at, a, dup)
-    x_sent = [along_col(q0[d], d, 0) for d in (1, 2, 3)]
-    q1 = products(1, idx, at, a, dup)
-    y_sent = [along_col(q1[d], 0, d) for d in (1, 2, 3)]
-    s0 = middle(0, at, q0[0], *x_sent)
-    y_last = [along_col(s0[d], 0, d) for d in (1, 2, 3)]
-    s1 = middle(1, at, q1[0], *y_sent)
-    x_last = [along_col(s1[d], d, 0) for d in (1, 2, 3)]
-    apt = final([s0[0], *y_last, s1[0], *x_last])
-
-    back = lax.all_to_all(apt, "col", 0, 0, tiled=True)
-    ap_out = ap_layout(back).reshape(8, 1, KAP, B * B)
 
     cols_p = jnp.stack([p[:, 4, :4, :KP] for p in ps]).reshape(NCOL, 16)
     cc = jnp.arange(NCOL, dtype=jnp.int32)
@@ -474,13 +552,28 @@
     slot = cols_i[:, :, :, None, None] * KC + jnp.arange(KC, dtype=jnp.int32)
     tgt = jnp.min(jnp.where(hit, slot, NCB * KC), axis=4).reshape(-1)
 
-    keep, send = coarse_terms(tgt, at, apt, ps)
+    x1, x3 = x_products(1, idx, at, a, dup)
+    got_x1, got_x3 = along_col(x1, 1, 0), along_col(x3, 3, 0)
+    ya = y_products(0, idx, at, a, dup)
+    got_ya = [along_col(ya[d], 0, d) for d in (1, 2, 3)]
+    x0, x2 = x_products(0, idx, at, a, dup)
+    got_x2 = along_col(x2, 2, 0)
+    yb = y_products(1, idx, at, a, dup)
+    got_yb = [along_col(yb[d], 0, d) for d in (1, 2, 3)]
+    s0 = middle(x_middle_kernel, at, [x0, got_x1, got_x2, got_x3])
+    y_last = [along_col(s0[d], 0, d) for d in (1, 2, 3)]
+    s1 = middle(y_middle_kernel, at, [ya[0], *got_ya, yb[0], *got_yb])
+    x_last = [along_col(s1[d], d, 0) for d in (1, 2, 3)]
+
+    apt, keep, send = coarse_terms(tgt, at, [s0[0], *y_last, s1[0], *x_last], ps)
     got = along_row(send, 0, 1)
     sums = [keep[d] + got[d] for d in range(4)]
     coarse = sums[0]
     moved = [along_row(sums[d], d, 0) for d in (1, 2, 3)]
     for part in moved:
         coarse = coarse + part
+    back = lax.all_to_all(apt, "col", 0, 0, tiled=True)
+    ap_out = ap_layout(back).reshape(8, 1, KAP, B * B)
     coarse = lax.all_to_all(coarse, "col", 0, 0, tiled=True)
     coarse_out = coarse_layout(coarse).reshape(1, KC, B * B)
     return ap_out, coarse_out

time: 231 us -> 234 us (1.013)
  local copies, waits for them, and re-layouts: 25.2 us -> 11.1 us
  waiting for transfers between devices: 66.9 us -> 74.9 us
  starting transfers between devices: 48.5 us -> 54.9 us
  Pallas kernels: 82.6 us -> 85.2 us
    squeeze x4 -> x0, local copies, waits for them, and re-layouts: 13.2 us -> none  [the longest x1 4.62 us: step(): x_sent = [along_col(q0[d], d, 0) for d in (1, 2, 3)]]
    ppermute x11, waiting for transfers between devices: 11 us -> 16.3 us  [along_row(): return lax.ppermute(v, 'row', pairs)]
    all_to_all x1, waiting for transfers between devices: 1.33 us -> 5.61 us  [step(): back = lax.all_to_all(apt, 'col', 0, 0, tiled=True)]
    slice x16 -> x0, local copies, waits for them, and re-layouts: 2.81 us -> none  [step(): cols_k = jnp.concatenate([part[8, :8, :KP] for part in parts], axis=0)]
    all_to_all x1, starting transfers between devices: 4.47 us -> 7.21 us  [step(): back = lax.all_to_all(apt, 'col', 0, 0, tiled=True)]
    ppermute x18 -> x21, starting transfers between devices: 29.9 us -> 31.8 us  [along_col(): return lax.ppermute(v, 'col', pairs)]
    ppermute x18 -> x21, waiting for transfers between devices: 48.1 us -> 46.7 us  [along_col(): return lax.ppermute(v, 'col', pairs)]
    pallas_call x6 -> x7, Pallas kernels: 58.4 us -> 59.8 us  [the longest x2 21.6 us: y_products(): pl.pallas_call(lambda *refs: y_product_kernel(part, *refs), grid_spec=plt...]
  transfers between devices with their start and end apart: 31 -> 34, of which waited for: 13 -> 14; matrix products, arithmetic and copies ran while one was open for 11% -> 4% of each run, Pallas kernels for 29% -> 30%
where the time goes in v1:
time: 234 us; the launch traced here: 233 us
  Pallas kernels  85.2 us (36%)
  waiting for transfers between devices  74.9 us (32%)
  starting transfers between devices  54.9 us (23%)
  local copies, waits for them, and re-layouts  11.1 us (5%)
  other arithmetic  4.23 us (2%)
    ppermute x21, waiting for transfers between devices, along_col(): return lax.ppermute(v, 'col', pairs)  46.7 us
    ppermute x21, starting transfers between devices, along_col(): return lax.ppermute(v, 'col', pairs)  31.8 us
    pallas_call x2, Pallas kernels, y_products(): pl.pallas_call(lambda *refs: y_product_kernel(part, *refs), grid_spec=plt...  21.6 us
    pallas_call x2, Pallas kernels, x_products(): pl.pallas_call(lambda *refs: x_product_kernel(j, *refs), grid_spec=pltpu....  21.3 us
    ppermute x11, waiting for transfers between devices, along_row(): return lax.ppermute(v, 'row', pairs)  16.3 us
    pallas_call x1, Pallas kernels, coarse_terms(): pl.pallas_call(coarse_kernel, grid_spec=pltpu.PrefetchScalarGridSpec(num_...  12.7 us
    ppermute x11, starting transfers between devices, along_row(): return lax.ppermute(v, 'row', pairs)  12.3 us
    pallas_call x2, Pallas kernels, middle(): pl.pallas_call(kernel, in_specs=[pl.BlockSpec(memory_space=pltpu.SMEM)] +...  10.5 us
  transfers between devices with their start and end apart: 34, of which 14 were waited for; matrix products, arithmetic and copies ran while one was open for 4% of the time, Pallas kernels for 30%

profile of v1, /device:TPU:0, one launch (start us, length us, event | category | flops | bytes accessed | tf_op | source)
XLA Modules:
  0.0 232.8 jit_solution(1541212967687735868)
XLA Ops:
  0.6 1.4 reshape_squeeze.3
  2.9 2.1 collective-permute-start
  5.0 3.6 %collective-permute-start.1 = (bf16[9,64,256]{2,1,0:T(8,128)(2,1)S(1)}, bf16[9,64,256]{2,1,0:T(8,128)(2,1)S(1)}, u32[]{:S(2)}, u32[]{:S(2)}) collective-permute-start(bf16[9,64,256]{2,1,0:T(8,128)(2,1)S(1)} %pad_maximum_fusion.2.refs_0_), channel_id=1, source_target_pairs={{0,64},{16,80},{32,96},{48,112},{64,0},{80,16},{96,32},{112,48},{1... | collective-permute-start | bytes 884744 | tf_op jit(solution)/shard_map/ppermute | solution.py:23
  8.6 1.0 collective-permute-start.2
  9.6 0.4 reshape_reshape_squeeze.3
  11.7 2.4 %collective-permute-done.refs_2_ = bf16[9,64,256]{2,1,0:T(8,128)(2,1)S(1)} collective-permute-done((bf16[9,64,256]{2,1,0:T(8,128)(2,1)S(1)}, bf16[9,64,256]{2,1,0:T(8,128)(2,1)S(1)}, u32[]{:S(2)}, u32[]{:S(2)}) %collective-permute-start) | collective-permute-done | bytes 294944 | tf_op jit(solution)/shard_map/ppermute | solution.py:23
  14.1 7.5 %collective-permute-done.1.refs_4_ = bf16[9,64,256]{2,1,0:T(8,128)(2,1)S(1)} collective-permute-done((bf16[9,64,256]{2,1,0:T(8,128)(2,1)S(1)}, bf16[9,64,256]{2,1,0:T(8,128)(2,1)S(1)}, u32[]{:S(2)}, u32[]{:S(2)}) %collective-permute-start.1) | collective-permute-done | bytes 294944 | tf_op jit(solution)/shard_map/ppermute | solution.py:23
  21.7 1.6 collective-permute-start.3
  23.2 1.7 collective-permute-start.5
  25.0 1.8 collective-permute-start.4
  26.8 8.4 %spread.1 = bf16[128,64,256]{2,1,0:T(8,128)(2,1)} custom-call(bf16[128,4,4096]{2,1,0:T(4,128)(2,1)} %bitcast.96), custom_call_target="tpu_custom_call" | custom-call | tf_op jit(solution)/shard_map/spread/pallas_call | solution.py:59
  35.1 0.7 pad_add_fusion.refs_1_.at_ref
  35.8 0.5 collective-permute-start.11
  36.5 3.1 %collective-permute-start.8 = (bf16[4,5,64,256]{3,2,1,0:T(8,128)(2,1)S(1)}, bf16[4,5,64,256]{3,2,1,0:T(8,128)(2,1)S(1)}, u32[]{:S(2)}, u32[]{:S(2)}) collective-permute-start(bf16[4,5,64,256]{3,2,1,0:T(8,128)(2,1)S(1)} %pad_maximum_fusion.refs_8_), channel_id=1, source_target_pairs={{0,12},{1,13},{2,14},{3,15},{4,0},{5,1},{6,2},{7,3},{8,4},{9,5},{1... | collective-permute-start | bytes 1966088 | tf_op jit(solution)/shard_map/ppermute | solution.py:28
  39.6 0.6 collective-permute-start.7
  40.2 1.0 collective-permute-start.6
  41.2 0.7 copy-done.14
  41.9 6.4 %table.1 = (bf16[257,64,128]{2,1,0:T(8,128)(2,1)}, f32[64,128]{1,0:T(8,128)}) custom-call(bf16[9,64,256]{2,1,0:T(8,128)(2,1)} %copy-done.2, bf16[9,64,256]{2,1,0:T(8,128)(2,1)} %collective-permute-done.9.refs_1_, bf16[9,64,256]{2,1,0:T(8,128)(2,1)} %copy-done.12, bf16[9,64,256]{2,1,0:T(8,128)(2,1)} %collective-permute-done.10.refs_3_, ...), custom_call_target="tpu_custom_call" | custom-call | tf_op jit(solution)/shard_map/table/pallas_call | solution.py:91
  48.4 0.9 convolution_convert_fusion.1
  49.5 0.8 reshape.300.refs_0_
  50.3 10.8 %shard_map.81 = (s16[129,16,128]{2,1,0:T(8,128)(2,1)}, s16[129,16,128]{2,1,0:T(8,128)(2,1)}, s16[129,16,128]{2,1,0:T(8,128)(2,1)}, s16[129,16,128]{2,1,0:T(8,128)(2,1)}) custom-call(s32[4096]{0:T(1024)} %reshape.300.refs_0_, s32[4]{0:T(128)} %pad_add_fusion.refs_1_.at_ref, bf16[4,2,16,64,256]{4,3,2,1,0:T(8,128)(2,1)} %bitcast.92, ...), custom_call_target="tpu_custom_call" | custom-call | tf_op jit(solution)/shard_map/pallas_call | solution.py:240
  61.1 1.9 collective-permute-start.22
  63.0 1.8 collective-permute-start.23
  64.9 10.8 %shard_map.80 = (s16[129,16,128]{2,1,0:T(8,128)(2,1)}, s16[129,16,128]{2,1,0:T(8,128)(2,1)}, s16[129,16,128]{2,1,0:T(8,128)(2,1)}, s16[129,16,128]{2,1,0:T(8,128)(2,1)}) custom-call(s32[4096]{0:T(1024)} %reshape.300.refs_0_, s32[4]{0:T(128)} %pad_add_fusion.refs_1_.at_ref, bf16[4,2,16,64,256]{4,3,2,1,0:T(8,128)(2,1)} %bitcast.93, ...), custom_call_target="tpu_custom_call" | custom-call | tf_op jit(solution)/shard_map/pallas_call | solution.py:240
  75.6 3.9 %collective-permute-done.8.refs_11_ = bf16[4,5,64,256]{3,2,1,0:T(8,128)(2,1)S(1)} collective-permute-done((bf16[4,5,64,256]{3,2,1,0:T(8,128)(2,1)S(1)}, bf16[4,5,64,256]{3,2,1,0:T(8,128)(2,1)S(1)}, u32[]{:S(2)}, u32[]{:S(2)}) %collective-permute-start.8) | collective-permute-done | bytes 655392 | tf_op jit(solution)/shard_map/ppermute | solution.py:28
  79.5 3.7 %collective-permute-start.24 = (s16[129,16,128]{2,1,0:T(8,128)(2,1)}, s16[129,16,128]{2,1,0:T(8,128)(2,1)}, u32[]{:S(2)}, u32[]{:S(2)}) collective-permute-start(s16[129,16,128]{2,1,0:T(8,128)(2,1)} %get-tuple-element.54), channel_id=1, source_target_pairs={{0,12},{1,13},{2,14},{3,15},{4,0},{5,1},{6,2},{7,3},{8,4},{9,5},{1... | collective-permute-start | bytes 1585160 | tf_op jit(solution)/shard_map/ppermute | solution.py:28
  83.3 10.7 %shard_map.78 = (s16[257,16,128]{2,1,0:T(8,128)(2,1)}, s16[257,16,128]{2,1,0:T(8,128)(2,1)}) custom-call(s32[4096]{0:T(1024)} %reshape.300.refs_0_, s32[4]{0:T(128)} %pad_add_fusion.refs_1_.at_ref, bf16[4,2,16,64,256]{4,3,2,1,0:T(8,128)(2,1)} %bitcast.94, bf16[257,64,128]{2,1,0:T(8,128)(2,1)} %get-tuple-element.38.refs_3_), custom_call_target="tpu_custom_call" | custom-call | tf_op jit(solution)/shard_map/pallas_call | solution.py:186
  94.0 10.6 %shard_map.77 = (s16[257,16,128]{2,1,0:T(8,128)(2,1)}, s16[257,16,128]{2,1,0:T(8,128)(2,1)}) custom-call(s32[4096]{0:T(1024)} %reshape.300.refs_0_, s32[4]{0:T(128)} %pad_add_fusion.refs_1_.at_ref, bf16[4,2,16,64,256]{4,3,2,1,0:T(8,128)(2,1)} %bitcast.95, bf16[257,64,128]{2,1,0:T(8,128)(2,1)} %get-tuple-element.38.refs_3_), custom_call_target="tpu_custom_call" | custom-call | tf_op jit(solution)/shard_map/pallas_call | solution.py:186
  104.6 0.7 collective-permute-start.13
  105.3 2.6 %collective-permute-start.15 = (s16[257,16,128]{2,1,0:T(8,128)(2,1)}, s16[257,16,128]{2,1,0:T(8,128)(2,1)S(1)}, u32[]{:S(2)}, u32[]{:S(2)}) collective-permute-start(s16[257,16,128]{2,1,0:T(8,128)(2,1)} %get-tuple-element.42), channel_id=1, source_target_pairs={{0,3},{1,0},{2,1},{3,2},{4,7},{5,4},{6,5},{7,6},{8,11},{9,8},{10,9... | collective-permute-start | bytes 3158024 | tf_op jit(solution)/shard_map/ppermute | solution.py:28
  107.9 0.8 collective-permute-start.14
  108.7 0.7 slice_bitcast_fusion.1
  109.4 1.5 collective-permute-start.20
  110.9 1.8 collective-permute-start.21
  112.7 0.7 slice_bitcast_fusion.2
  113.8 9.8 %collective-permute-done.20.refs_2_ = s16[129,16,128]{2,1,0:T(8,128)(2,1)} collective-permute-done((s16[129,16,128]{2,1,0:T(8,128)(2,1)}, s16[129,16,128]{2,1,0:T(8,128)(2,1)}, u32[]{:S(2)}, u32[]{:S(2)}) %collective-permute-start.20) | collective-permute-done | bytes 528416 | tf_op jit(solution)/shard_map/ppermute | solution.py:28
  123.6 11.6 %collective-permute-done.21.refs_3_ = s16[129,16,128]{2,1,0:T(8,128)(2,1)} collective-permute-done((s16[129,16,128]{2,1,0:T(8,128)(2,1)}, s16[129,16,128]{2,1,0:T(8,128)(2,1)}, u32[]{:S(2)}, u32[]{:S(2)}) %collective-permute-start.21) | collective-permute-done | bytes 528416 | tf_op jit(solution)/shard_map/ppermute | solution.py:28
  135.2 5.3 %shard_map.82 = (s16[65,16,128]{2,1,0:T(8,128)(2,1)}, s16[65,16,128]{2,1,0:T(8,128)(2,1)}, s16[65,16,128]{2,1,0:T(8,128)(2,1)}, s16[65,16,128]{2,1,0:T(8,128)(2,1)}) custom-call(s32[4]{0:T(128)} %pad_add_fusion.refs_1_.at_ref, s16[129,16,128]{2,1,0:T(8,128)(2,1)} %get-tuple-element.47.refs_0_, s16[129,16,128]{2,1,0:T(8,128)(2,1)} %collective-permute-done.19.refs_1_, ...), custom_call_target="tpu_custom_call" | custom-call | tf_op jit(solution)/shard_map/pallas_call | solution.py:322
  140.5 1.2 collective-permute-start.25
  142.0 1.9 collective-permute-start.26
  143.9 9.2 %collective-permute-done.13.m1 = s16[257,16,128]{2,1,0:T(8,128)(2,1)S(1)} collective-permute-done((s16[257,16,128]{2,1,0:T(8,128)(2,1)}, s16[257,16,128]{2,1,0:T(8,128)(2,1)S(1)}, u32[]{:S(2)}, u32[]{:S(2)}) %collective-permute-start.13) | collective-permute-done | bytes 1052704 | tf_op jit(solution)/shard_map/ppermute | solution.py:28
  153.1 5.9 %collective-permute-done.15.m3 = s16[257,16,128]{2,1,0:T(8,128)(2,1)S(1)} collective-permute-done((s16[257,16,128]{2,1,0:T(8,128)(2,1)}, s16[257,16,128]{2,1,0:T(8,128)(2,1)S(1)}, u32[]{:S(2)}, u32[]{:S(2)}) %collective-permute-start.15) | collective-permute-done | bytes 1052704 | tf_op jit(solution)/shard_map/ppermute | solution.py:28
  159.0 1.0 copy-done.4
  160.3 5.2 %shard_map.79 = (s16[65,16,128]{2,1,0:T(8,128)(2,1)}, s16[65,16,128]{2,1,0:T(8,128)(2,1)}, s16[65,16,128]{2,1,0:T(8,128)(2,1)}, s16[65,16,128]{2,1,0:T(8,128)(2,1)}) custom-call(s32[4]{0:T(128)} %pad_add_fusion.refs_1_.at_ref, s16[257,16,128]{2,1,0:T(8,128)(2,1)} %get-tuple-element.39.m0, s16[257,16,128]{2,1,0:T(8,128)(2,1)} %copy-done.3, ...), custom_call_target="tpu_custom_call" | custom-call | tf_op jit(solution)/shard_map/pallas_call | solution.py:322
  165.5 4.1 %collective-permute-start.17 = (s16[65,16,128]{2,1,0:T(8,128)(2,1)}, s16[65,16,128]{2,1,0:T(8,128)(2,1)S(1)}, u32[]{:S(2)}, u32[]{:S(2)}) collective-permute-start(s16[65,16,128]{2,1,0:T(8,128)(2,1)} %get-tuple-element.45), channel_id=1, source_target_pairs={{0,8},{1,9},{2,10},{3,11},{4,12},{5,13},{6,14},{7,15},{8,0},{9,1},... | collective-permute-start | bytes 798728 | tf_op jit(solution)/shard_map/ppermute | solution.py:28
  170.1 0.8 reshape.299.tgt_ref
  170.9 2.5 %collective-permute-done.16.refs_1_ = s16[65,16,128]{2,1,0:T(8,128)(2,1)S(1)} collective-permute-done((s16[65,16,128]{2,1,0:T(8,128)(2,1)}, s16[65,16,128]{2,1,0:T(8,128)(2,1)S(1)}, u32[]{:S(2)}, u32[]{:S(2)}) %collective-permute-start.16) | collective-permute-done | bytes 266272 | tf_op jit(solution)/shard_map/ppermute | solution.py:28
  173.4 3.7 %collective-permute-done.17.refs_2_ = s16[65,16,128]{2,1,0:T(8,128)(2,1)S(1)} collective-permute-done((s16[65,16,128]{2,1,0:T(8,128)(2,1)}, s16[65,16,128]{2,1,0:T(8,128)(2,1)S(1)}, u32[]{:S(2)}, u32[]{:S(2)}) %collective-permute-start.17) | collective-permute-done | bytes 266272 | tf_op jit(solution)/shard_map/ppermute | solution.py:28
  177.1 0.7 copy-done.17
  177.9 12.7 %coarse_terms.1 = (bf16[16,2,64,128]{3,2,1,0:T(8,128)(2,1)}, f32[4,16,4,8,128]{4,3,2,1,0:T(8,128)}, f32[4,16,4,8,128]{4,3,2,1,0:T(8,128)}) custom-call(s32[2048]{0:T(1024)} %reshape.299.tgt_ref, s32[4]{0:T(128)} %pad_add_fusion.refs_1_.at_ref, s16[65,16,128]{2,1,0:T(8,128)(2,1)} %get-tuple-element.43.refs_0_, s16[65,16,128]{2,1,0:T(8,128)(2,1)} %copy-done.16, ...), custom_call_target="tpu_custom_call" | custom-call | tf_op jit(solution)/shard_map/coarse_terms/pallas_call | solution.py:410
  190.6 2.9 %collective-permute-done.28 = f32[4,16,4,8,128]{4,3,2,1,0:T(8,128)S(1)} collective-permute-done((f32[4,16,4,8,128]{4,3,2,1,0:T(8,128)}, f32[4,16,4,8,128]{4,3,2,1,0:T(8,128)S(1)}, u32[]{:S(2)}, u32[]{:S(2)}) %collective-permute-start.28) | collective-permute-done | bytes 1048608 | tf_op jit(solution)/shard_map/ppermute | solution.py:23
  193.5 1.2 fusion.2
  194.7 1.4 collective-permute-start.29
  196.1 2.4 %collective-permute-start.30 = (f32[16,4,8,128]{3,2,1,0:T(8,128)S(1)}, f32[16,4,8,128]{3,2,1,0:T(8,128)S(1)}, u32[]{:S(2)}, u32[]{:S(2)}) collective-permute-start(f32[16,4,8,128]{3,2,1,0:T(8,128)S(1)} %get-tuple-element.74), channel_id=1, source_target_pairs={{0,64},{16,80},{32,96},{48,112},{64,0},{80,16},{96,32},{112,48},{1... | collective-permute-start | bytes 786440 | tf_op jit(solution)/shard_map/ppermute | solution.py:23
  198.5 1.2 collective-permute-start.31
  199.8 7.2 %all-to-all-start = ((bf16[16,2,64,128]{3,2,1,0:T(8,128)(2,1)}), bf16[16,2,64,128]{3,2,1,0:T(8,128)(2,1)S(1)}, u32[]{:S(2)}, u32[]{:S(2)}) async-start(bf16[16,2,64,128]{3,2,1,0:T(8,128)(2,1)} %get-tuple-element.59), calls=%async_computation | async-start | bytes 1048576 | tf_op jit(solution)/shard_map/all_to_all | solution.py:575
  207.0 3.5 %collective-permute-done.30 = f32[16,4,8,128]{3,2,1,0:T(8,128)S(1)} collective-permute-done((f32[16,4,8,128]{3,2,1,0:T(8,128)S(1)}, f32[16,4,8,128]{3,2,1,0:T(8,128)S(1)}, u32[]{:S(2)}, u32[]{:S(2)}) %collective-permute-start.30) | collective-permute-done | bytes 262176 | tf_op jit(solution)/shard_map/ppermute | solution.py:23
  210.6 1.8 fusion.6
  212.4 5.6 %all-to-all-done.x_ref = bf16[16,2,64,128]{3,2,1,0:T(8,128)(2,1)S(1)} async-done(((bf16[16,2,64,128]{3,2,1,0:T(8,128)(2,1)}), bf16[16,2,64,128]{3,2,1,0:T(8,128)(2,1)S(1)}, u32[]{:S(2)}, u32[]{:S(2)}) %all-to-all-start) | async-done | bytes 524320 | tf_op jit(solution)/shard_map/all_to_all | solution.py:575
  218.0 3.5 %all-to-all-start.1 = ((f32[16,4,8,128]{3,2,1,0:T(8,128)}), f32[16,4,8,128]{3,2,1,0:T(8,128)S(1)}, u32[]{:S(2)}, u32[]{:S(2)}) async-start(f32[16,4,8,128]{3,2,1,0:T(8,128)} %fusion.6), calls=%async_computation.1 | async-start | bytes 524288 | tf_op jit(solution)/shard_map/all_to_all | solution.py:577
  221.5 2.4 %ap_layout.1 = bf16[8,8,4096]{2,1,0:T(8,128)(2,1)} custom-call(bf16[16,2,64,128]{3,2,1,0:T(8,128)(2,1)} %copy-done.1), custom_call_target="tpu_custom_call" | custom-call | tf_op jit(solution)/shard_map/ap_layout/pallas_call | solution.py:453
  224.0 6.2 %all-to-all-done.1.x_ref = f32[16,4,8,128]{3,2,1,0:T(8,128)S(1)} async-done(((f32[16,4,8,128]{3,2,1,0:T(8,128)}), f32[16,4,8,128]{3,2,1,0:T(8,128)S(1)}, u32[]{:S(2)}, u32[]{:S(2)}) %all-to-all-start.1) | async-done | bytes 262176 | tf_op jit(solution)/shard_map/all_to_all | solution.py:577
  230.2 0.7 copy-done.7
  230.9 1.9 coarse_layout.1
  (110 shorter events, 4.5 us)
Async XLA Ops:
  2.1 0.7 copy-start.20
  2.1 7.5 %copy-start.6 = (bf16[8,1,4,4096]{3,2,1,0:T(4,128)(2,1)S(1)}, bf16[8,1,4,4096]{3,2,1,0:T(4,128)(2,1)}, u32[]{:S(2)}) copy-start(bf16[8,1,4,4096]{3,2,1,0:T(4,128)(2,1)} %param.8) | copy-start | bytes 786436
  2.9 7.9 %copy-start.2 = (bf16[9,64,256]{2,1,0:T(8,128)(2,1)}, bf16[9,64,256]{2,1,0:T(8,128)(2,1)S(1)}, u32[]{:S(2)}) copy-start(bf16[9,64,256]{2,1,0:T(8,128)(2,1)S(1)} %pad_maximum_fusion.2.refs_0_) | copy-start | bytes 884740
  2.9 11.2 %collective-permute-start = (bf16[9,64,256]{2,1,0:T(8,128)(2,1)S(1)}, bf16[9,64,256]{2,1,0:T(8,128)(2,1)S(1)}, u32[]{:S(2)}, u32[]{:S(2)}) collective-permute-start(bf16[9,64,256]{2,1,0:T(8,128)(2,1)S(1)} %pad_maximum_fusion.2.refs_0_), channel_id=1, source_target_pairs={{0,32},{16,48},{32,64},{48,80},{64,96},{80,112},{96,0},{112,16},{1... | collective-permute-start | bytes 884744 | tf_op jit(solution)/shard_map/ppermute | solution.py:23
  5.0 16.6 %collective-permute-start.1 = (bf16[9,64,256]{2,1,0:T(8,128)(2,1)S(1)}, bf16[9,64,256]{2,1,0:T(8,128)(2,1)S(1)}, u32[]{:S(2)}, u32[]{:S(2)}) collective-permute-start(bf16[9,64,256]{2,1,0:T(8,128)(2,1)S(1)} %pad_maximum_fusion.2.refs_0_), channel_id=1, source_target_pairs={{0,64},{16,80},{32,96},{48,112},{64,0},{80,16},{96,32},{112,48},{1... | collective-permute-start | bytes 884744 | tf_op jit(solution)/shard_map/ppermute | solution.py:23
  8.6 13.0 %collective-permute-start.2 = (bf16[9,64,256]{2,1,0:T(8,128)(2,1)S(1)}, bf16[9,64,256]{2,1,0:T(8,128)(2,1)}, u32[]{:S(2)}, u32[]{:S(2)}) collective-permute-start(bf16[9,64,256]{2,1,0:T(8,128)(2,1)S(1)} %pad_maximum_fusion.2.refs_0_), channel_id=1, source_target_pairs={{0,96},{16,112},{32,0},{48,16},{64,32},{80,48},{96,64},{112,80},{1... | collective-permute-start | bytes 884744 | tf_op jit(solution)/shard_map/ppermute | solution.py:23
  9.6 30.0 %collective-permute-start.9 = (bf16[9,64,256]{2,1,0:T(8,128)(2,1)S(1)}, bf16[9,64,256]{2,1,0:T(8,128)(2,1)}, u32[]{:S(2)}, u32[]{:S(2)}) collective-permute-start(bf16[9,64,256]{2,1,0:T(8,128)(2,1)S(1)} %pad_maximum_fusion.2.refs_0_), channel_id=1, source_target_pairs={{0,16},{16,0},{32,48},{48,32},{64,80},{80,64},{96,112},{112,96},{1... | collective-permute-start | bytes 884744 | tf_op jit(solution)/shard_map/ppermute | solution.py:23
  10.5 1.0 copy-start.19
  10.7 1.0 copy-start.21
  14.1 21.7 %copy-start.12 = (bf16[9,64,256]{2,1,0:T(8,128)(2,1)}, bf16[9,64,256]{2,1,0:T(8,128)(2,1)S(1)}, u32[]{:S(2)}) copy-start(bf16[9,64,256]{2,1,0:T(8,128)(2,1)S(1)} %collective-permute-done.refs_2_) | copy-start | bytes 884740
  21.6 14.2 %copy-start.13 = (bf16[9,64,256]{2,1,0:T(8,128)(2,1)}, bf16[9,64,256]{2,1,0:T(8,128)(2,1)S(1)}, u32[]{:S(2)}) copy-start(bf16[9,64,256]{2,1,0:T(8,128)(2,1)S(1)} %collective-permute-done.1.refs_4_) | copy-start | bytes 884740
  21.7 14.2 %collective-permute-start.3 = (bf16[5,64,256]{2,1,0:T(8,128)(2,1)S(1)}, bf16[5,64,256]{2,1,0:T(8,128)(2,1)S(1)}, u32[]{:S(2)}, u32[]{:S(2)}) collective-permute-start(bf16[5,64,256]{2,1,0:T(8,128)(2,1)S(1)} %get-tuple-element.78), channel_id=1, source_target_pairs={{0,1},{1,2},{2,3},{3,0},{4,5},{5,6},{6,7},{7,4},{8,9},{9,10},{10,1... | collective-permute-start | bytes 491528 | tf_op jit(solution)/shard_map/ppermute | solution.py:28
  23.2 13.2 %collective-permute-start.5 = (bf16[5,64,256]{2,1,0:T(8,128)(2,1)S(1)}, bf16[5,64,256]{2,1,0:T(8,128)(2,1)S(1)}, u32[]{:S(2)}, u32[]{:S(2)}) collective-permute-start(bf16[5,64,256]{2,1,0:T(8,128)(2,1)S(1)} %get-tuple-element.78), channel_id=1, source_target_pairs={{0,3},{1,0},{2,1},{3,2},{4,7},{5,4},{6,5},{7,6},{8,11},{9,8},{10,9... | collective-permute-start | bytes 491528 | tf_op jit(solution)/shard_map/ppermute | solution.py:28
  25.0 11.4 %collective-permute-start.4 = (bf16[5,64,256]{2,1,0:T(8,128)(2,1)S(1)}, bf16[5,64,256]{2,1,0:T(8,128)(2,1)S(1)}, u32[]{:S(2)}, u32[]{:S(2)}) collective-permute-start(bf16[5,64,256]{2,1,0:T(8,128)(2,1)S(1)} %bitcast.99), channel_id=1, source_target_pairs={{0,2},{1,3},{2,0},{3,1},{4,6},{5,7},{6,4},{7,5},{8,10},{9,11},{10,... | collective-permute-start | bytes 491528 | tf_op jit(solution)/shard_map/ppermute | solution.py:28
  35.8 4.4 %collective-permute-start.10 = (bf16[9,64,256]{2,1,0:T(8,128)(2,1)S(1)}, bf16[9,64,256]{2,1,0:T(8,128)(2,1)}, u32[]{:S(2)}, u32[]{:S(2)}) collective-permute-start(bf16[9,64,256]{2,1,0:T(8,128)(2,1)S(1)} %collective-permute-done.refs_2_), channel_id=1, source_target_pairs={{0,16},{16,0},{32,48},{48,32},{64,80},{80,64},{96,112},{112,96},{1... | collective-permute-start | bytes 884744 | tf_op jit(solution)/shard_map/ppermute | solution.py:23
  35.8 5.4 %collective-permute-start.11 = (bf16[9,64,256]{2,1,0:T(8,128)(2,1)S(1)}, bf16[9,64,256]{2,1,0:T(8,128)(2,1)S(1)}, u32[]{:S(2)}, u32[]{:S(2)}) collective-permute-start(bf16[9,64,256]{2,1,0:T(8,128)(2,1)S(1)} %collective-permute-done.1.refs_4_), channel_id=1, source_target_pairs={{0,16},{16,0},{32,48},{48,32},{64,80},{80,64},{96,112},{112,96},{1... | collective-permute-start | bytes 884744 | tf_op jit(solution)/shard_map/ppermute | solution.py:23
  36.3 5.6 %collective-permute-start.12 = (bf16[9,64,256]{2,1,0:T(8,128)(2,1)}, bf16[9,64,256]{2,1,0:T(8,128)(2,1)}, u32[]{:S(2)}, u32[]{:S(2)}) collective-permute-start(bf16[9,64,256]{2,1,0:T(8,128)(2,1)} %collective-permute-done.2.refs_6_), channel_id=1, source_target_pairs={{0,16},{16,0},{32,48},{48,32},{64,80},{80,64},{96,112},{112,96},{1... | collective-permute-start | bytes 884744 | tf_op jit(solution)/shard_map/ppermute | solution.py:23
  36.5 46.7 %copy-start = (bf16[4,5,64,256]{3,2,1,0:T(8,128)(2,1)}, bf16[4,5,64,256]{3,2,1,0:T(8,128)(2,1)S(1)}, u32[]{:S(2)}) copy-start(bf16[4,5,64,256]{3,2,1,0:T(8,128)(2,1)S(1)} %pad_maximum_fusion.refs_8_) | copy-start | bytes 1966084
  36.5 43.0 %collective-permute-start.8 = (bf16[4,5,64,256]{3,2,1,0:T(8,128)(2,1)S(1)}, bf16[4,5,64,256]{3,2,1,0:T(8,128)(2,1)S(1)}, u32[]{:S(2)}, u32[]{:S(2)}) collective-permute-start(bf16[4,5,64,256]{3,2,1,0:T(8,128)(2,1)S(1)} %pad_maximum_fusion.refs_8_), channel_id=1, source_target_pairs={{0,12},{1,13},{2,14},{3,15},{4,0},{5,1},{6,2},{7,3},{8,4},{9,5},{1... | collective-permute-start | bytes 1966088 | tf_op jit(solution)/shard_map/ppermute | solution.py:28
  39.6 43.6 %collective-permute-start.7 = (bf16[4,5,64,256]{3,2,1,0:T(8,128)(2,1)S(1)}, bf16[4,5,64,256]{3,2,1,0:T(8,128)(2,1)S(1)}, u32[]{:S(2)}, u32[]{:S(2)}) collective-permute-start(bf16[4,5,64,256]{3,2,1,0:T(8,128)(2,1)S(1)} %pad_maximum_fusion.refs_8_), channel_id=1, source_target_pairs={{0,8},{1,9},{2,10},{3,11},{4,12},{5,13},{6,14},{7,15},{8,0},{9,1},... | collective-permute-start | bytes 1966088 | tf_op jit(solution)/shard_map/ppermute | solution.py:28
  40.2 64.3 %collective-permute-start.6 = (bf16[4,5,64,256]{3,2,1,0:T(8,128)(2,1)S(1)}, bf16[4,5,64,256]{3,2,1,0:T(8,128)(2,1)S(1)}, u32[]{:S(2)}, u32[]{:S(2)}) collective-permute-start(bf16[4,5,64,256]{3,2,1,0:T(8,128)(2,1)S(1)} %pad_maximum_fusion.refs_8_), channel_id=1, source_target_pairs={{0,4},{1,5},{2,6},{3,7},{4,8},{5,9},{6,10},{7,11},{8,12},{9,13},{1... | collective-permute-start | bytes 1966088 | tf_op jit(solution)/shard_map/ppermute | solution.py:28
  41.2 0.7 copy-start.14
  61.1 44.2 %collective-permute-start.22 = (s16[129,16,128]{2,1,0:T(8,128)(2,1)}, s16[129,16,128]{2,1,0:T(8,128)(2,1)S(1)}, u32[]{:S(2)}, u32[]{:S(2)}) collective-permute-start(s16[129,16,128]{2,1,0:T(8,128)(2,1)} %get-tuple-element.52), channel_id=1, source_target_pairs={{0,4},{1,5},{2,6},{3,7},{4,8},{5,9},{6,10},{7,11},{8,12},{9,13},{1... | collective-permute-start | bytes 1585160 | tf_op jit(solution)/shard_map/ppermute | solution.py:28
  63.0 44.9 %collective-permute-start.23 = (s16[129,16,128]{2,1,0:T(8,128)(2,1)}, s16[129,16,128]{2,1,0:T(8,128)(2,1)}, u32[]{:S(2)}, u32[]{:S(2)}) collective-permute-start(s16[129,16,128]{2,1,0:T(8,128)(2,1)} %get-tuple-element.53), channel_id=1, source_target_pairs={{0,8},{1,9},{2,10},{3,11},{4,12},{5,13},{6,14},{7,15},{8,0},{9,1},... | collective-permute-start | bytes 1585160 | tf_op jit(solution)/shard_map/ppermute | solution.py:28
  79.5 25.0 %copy-start.8 = (bf16[4,5,64,256]{3,2,1,0:T(8,128)(2,1)}, bf16[4,5,64,256]{3,2,1,0:T(8,128)(2,1)S(1)}, u32[]{:S(2)}) copy-start(bf16[4,5,64,256]{3,2,1,0:T(8,128)(2,1)S(1)} %collective-permute-done.8.refs_11_) | copy-start | bytes 1966084
  79.5 29.9 %collective-permute-start.24 = (s16[129,16,128]{2,1,0:T(8,128)(2,1)}, s16[129,16,128]{2,1,0:T(8,128)(2,1)}, u32[]{:S(2)}, u32[]{:S(2)}) collective-permute-start(s16[129,16,128]{2,1,0:T(8,128)(2,1)} %get-tuple-element.54), channel_id=1, source_target_pairs={{0,12},{1,13},{2,14},{3,15},{4,0},{5,1},{6,2},{7,3},{8,4},{9,5},{1... | collective-permute-start | bytes 1585160 | tf_op jit(solution)/shard_map/ppermute | solution.py:28
  83.2 10.7 %copy-start.9 = (bf16[4,5,64,256]{3,2,1,0:T(8,128)(2,1)}, bf16[4,5,64,256]{3,2,1,0:T(8,128)(2,1)S(1)}, u32[]{:S(2)}) copy-start(bf16[4,5,64,256]{3,2,1,0:T(8,128)(2,1)S(1)} %collective-permute-done.7.refs_10_) | copy-start | bytes 1966084
  83.2 27.7 %collective-permute-start.19 = (s16[129,16,128]{2,1,0:T(8,128)(2,1)}, s16[129,16,128]{2,1,0:T(8,128)(2,1)}, u32[]{:S(2)}, u32[]{:S(2)}) collective-permute-start(s16[129,16,128]{2,1,0:T(8,128)(2,1)} %get-tuple-element.48), channel_id=1, source_target_pairs={{0,4},{1,5},{2,6},{3,7},{4,8},{5,9},{6,10},{7,11},{8,12},{9,13},{1... | collective-permute-start | bytes 1585160 | tf_op jit(solution)/shard_map/ppermute | solution.py:28
  104.6 3.3 %copy-start.10 = (bf16[4,5,64,256]{3,2,1,0:T(8,128)(2,1)}, bf16[4,5,64,256]{3,2,1,0:T(8,128)(2,1)S(1)}, u32[]{:S(2)}) copy-start(bf16[4,5,64,256]{3,2,1,0:T(8,128)(2,1)S(1)} %collective-permute-done.6.refs_9_) | copy-start | bytes 1966084
  104.6 48.4 %collective-permute-start.13 = (s16[257,16,128]{2,1,0:T(8,128)(2,1)}, s16[257,16,128]{2,1,0:T(8,128)(2,1)S(1)}, u32[]{:S(2)}, u32[]{:S(2)}) collective-permute-start(s16[257,16,128]{2,1,0:T(8,128)(2,1)} %get-tuple-element.40), channel_id=1, source_target_pairs={{0,1},{1,2},{2,3},{3,0},{4,5},{5,6},{6,7},{7,4},{8,9},{9,10},{10,1... | collective-permute-start | bytes 3158024 | tf_op jit(solution)/shard_map/ppermute | solution.py:28
  105.3 2.7 %copy-start.11 = (s16[129,16,128]{2,1,0:T(8,128)(2,1)}, s16[129,16,128]{2,1,0:T(8,128)(2,1)S(1)}, u32[]{:S(2)}) copy-start(s16[129,16,128]{2,1,0:T(8,128)(2,1)S(1)} %collective-permute-done.22.refs_5_) | copy-start | bytes 1585156
  105.3 53.7 %collective-permute-start.15 = (s16[257,16,128]{2,1,0:T(8,128)(2,1)}, s16[257,16,128]{2,1,0:T(8,128)(2,1)S(1)}, u32[]{:S(2)}, u32[]{:S(2)}) collective-permute-start(s16[257,16,128]{2,1,0:T(8,128)(2,1)} %get-tuple-element.42), channel_id=1, source_target_pairs={{0,3},{1,0},{2,1},{3,2},{4,7},{5,4},{6,5},{7,6},{8,11},{9,8},{10,9... | collective-permute-start | bytes 3158024 | tf_op jit(solution)/shard_map/ppermute | solution.py:28
  107.9 51.1 %collective-permute-start.14 = (s16[257,16,128]{2,1,0:T(8,128)(2,1)}, s16[257,16,128]{2,1,0:T(8,128)(2,1)S(1)}, u32[]{:S(2)}, u32[]{:S(2)}) collective-permute-start(s16[257,16,128]{2,1,0:T(8,128)(2,1)} %get-tuple-element.41), channel_id=1, source_target_pairs={{0,2},{1,3},{2,0},{3,1},{4,6},{5,7},{6,4},{7,5},{8,10},{9,11},{10,... | collective-permute-start | bytes 3158024 | tf_op jit(solution)/shard_map/ppermute | solution.py:28
  109.4 14.2 %collective-permute-start.20 = (s16[129,16,128]{2,1,0:T(8,128)(2,1)}, s16[129,16,128]{2,1,0:T(8,128)(2,1)}, u32[]{:S(2)}, u32[]{:S(2)}) collective-permute-start(s16[129,16,128]{2,1,0:T(8,128)(2,1)} %get-tuple-element.49), channel_id=1, source_target_pairs={{0,8},{1,9},{2,10},{3,11},{4,12},{5,13},{6,14},{7,15},{8,0},{9,1},... | collective-permute-start | bytes 1585160 | tf_op jit(solution)/shard_map/ppermute | solution.py:28
  110.9 24.3 %collective-permute-start.21 = (s16[129,16,128]{2,1,0:T(8,128)(2,1)}, s16[129,16,128]{2,1,0:T(8,128)(2,1)}, u32[]{:S(2)}, u32[]{:S(2)}) collective-permute-start(s16[129,16,128]{2,1,0:T(8,128)(2,1)} %get-tuple-element.50), channel_id=1, source_target_pairs={{0,12},{1,13},{2,14},{3,15},{4,0},{5,1},{6,2},{7,3},{8,4},{9,5},{1... | collective-permute-start | bytes 1585160 | tf_op jit(solution)/shard_map/ppermute | solution.py:28
  135.2 6.4 %copy-start.22 = (s32[128,8]{0,1:T(8,128)S(1)}, s32[128,8]{0,1:T(8,128)}, u32[]{:S(2)}) copy-start(s32[128,8]{0,1:T(8,128)} %param.11) | copy-start | bytes 12292
  140.5 29.2 %collective-permute-start.25 = (s16[65,16,128]{2,1,0:T(8,128)(2,1)}, s16[65,16,128]{2,1,0:T(8,128)(2,1)S(1)}, u32[]{:S(2)}, u32[]{:S(2)}) collective-permute-start(s16[65,16,128]{2,1,0:T(8,128)(2,1)} %get-tuple-element.56), channel_id=1, source_target_pairs={{0,1},{1,2},{2,3},{3,0},{4,5},{5,6},{6,7},{7,4},{8,9},{9,10},{10,1... | collective-permute-start | bytes 798728 | tf_op jit(solution)/shard_map/ppermute | solution.py:28
  142.0 28.9 %collective-permute-start.26 = (s16[65,16,128]{2,1,0:T(8,128)(2,1)}, s16[65,16,128]{2,1,0:T(8,128)(2,1)}, u32[]{:S(2)}, u32[]{:S(2)}) collective-permute-start(s16[65,16,128]{2,1,0:T(8,128)(2,1)} %get-tuple-element.57), channel_id=1, source_target_pairs={{0,2},{1,3},{2,0},{3,1},{4,6},{5,7},{6,4},{7,5},{8,10},{9,11},{10,... | collective-permute-start | bytes 798728 | tf_op jit(solution)/shard_map/ppermute | solution.py:28
  153.1 6.0 %copy-start.3 = (s16[257,16,128]{2,1,0:T(8,128)(2,1)}, s16[257,16,128]{2,1,0:T(8,128)(2,1)S(1)}, u32[]{:S(2)}) copy-start(s16[257,16,128]{2,1,0:T(8,128)(2,1)S(1)} %collective-permute-done.13.m1) | copy-start | bytes 3158020
  153.1 17.8 %collective-permute-start.27 = (s16[65,16,128]{2,1,0:T(8,128)(2,1)}, s16[65,16,128]{2,1,0:T(8,128)(2,1)}, u32[]{:S(2)}, u32[]{:S(2)}) collective-permute-start(s16[65,16,128]{2,1,0:T(8,128)(2,1)} %get-tuple-element.58), channel_id=1, source_target_pairs={{0,3},{1,0},{2,1},{3,2},{4,7},{5,4},{6,5},{7,6},{8,11},{9,8},{10,9... | collective-permute-start | bytes 798728 | tf_op jit(solution)/shard_map/ppermute | solution.py:28
  159.0 1.0 copy-start.4
  159.0 1.3 copy-start.5
  165.5 7.8 %collective-permute-start.16 = (s16[65,16,128]{2,1,0:T(8,128)(2,1)}, s16[65,16,128]{2,1,0:T(8,128)(2,1)S(1)}, u32[]{:S(2)}, u32[]{:S(2)}) collective-permute-start(s16[65,16,128]{2,1,0:T(8,128)(2,1)} %get-tuple-element.44), channel_id=1, source_target_pairs={{0,4},{1,5},{2,6},{3,7},{4,8},{5,9},{6,10},{7,11},{8,12},{9,13},{1... | collective-permute-start | bytes 798728 | tf_op jit(solution)/shard_map/ppermute | solution.py:28
  165.5 11.6 %collective-permute-start.17 = (s16[65,16,128]{2,1,0:T(8,128)(2,1)}, s16[65,16,128]{2,1,0:T(8,128)(2,1)S(1)}, u32[]{:S(2)}, u32[]{:S(2)}) collective-permute-start(s16[65,16,128]{2,1,0:T(8,128)(2,1)} %get-tuple-element.45), channel_id=1, source_target_pairs={{0,8},{1,9},{2,10},{3,11},{4,12},{5,13},{6,14},{7,15},{8,0},{9,1},... | collective-permute-start | bytes 798728 | tf_op jit(solution)/shard_map/ppermute | solution.py:28
  169.6 7.5 %copy-start.15 = (s16[65,16,128]{2,1,0:T(8,128)(2,1)}, s16[65,16,128]{2,1,0:T(8,128)(2,1)S(1)}, u32[]{:S(2)}) copy-start(s16[65,16,128]{2,1,0:T(8,128)(2,1)S(1)} %collective-permute-done.25.refs_5_) | copy-start | bytes 798724
  169.7 7.5 %collective-permute-start.18 = (s16[65,16,128]{2,1,0:T(8,128)(2,1)}, s16[65,16,128]{2,1,0:T(8,128)(2,1)S(1)}, u32[]{:S(2)}, u32[]{:S(2)}) collective-permute-start(s16[65,16,128]{2,1,0:T(8,128)(2,1)} %get-tuple-element.46), channel_id=1, source_target_pairs={{0,12},{1,13},{2,14},{3,15},{4,0},{5,1},{6,2},{7,3},{8,4},{9,5},{1... | collective-permute-start | bytes 798728 | tf_op jit(solution)/shard_map/ppermute | solution.py:28
  173.4 3.8 %copy-start.16 = (s16[65,16,128]{2,1,0:T(8,128)(2,1)}, s16[65,16,128]{2,1,0:T(8,128)(2,1)S(1)}, u32[]{:S(2)}) copy-start(s16[65,16,128]{2,1,0:T(8,128)(2,1)S(1)} %collective-permute-done.16.refs_1_) | copy-start | bytes 798724
  177.1 0.7 copy-start.17
  177.1 0.8 copy-start.18
  190.6 2.9 %collective-permute-start.28 = (f32[4,16,4,8,128]{4,3,2,1,0:T(8,128)}, f32[4,16,4,8,128]{4,3,2,1,0:T(8,128)S(1)}, u32[]{:S(2)}, u32[]{:S(2)}) collective-permute-start(f32[4,16,4,8,128]{4,3,2,1,0:T(8,128)} %get-tuple-element.61), channel_id=1, source_target_pairs={{0,16},{16,0},{32,48},{48,32},{64,80},{80,64},{96,112},{112,96},{1... | collective-permute-start | bytes 3145736 | tf_op jit(solution)/shard_map/ppermute | solution.py:23
  194.7 12.3 %collective-permute-start.29 = (f32[16,4,8,128]{3,2,1,0:T(8,128)S(1)}, f32[16,4,8,128]{3,2,1,0:T(8,128)S(1)}, u32[]{:S(2)}, u32[]{:S(2)}) collective-permute-start(f32[16,4,8,128]{3,2,1,0:T(8,128)S(1)} %get-tuple-element.72), channel_id=1, source_target_pairs={{0,32},{16,48},{32,64},{48,80},{64,96},{80,112},{96,0},{112,16},{1... | collective-permute-start | bytes 786440 | tf_op jit(solution)/shard_map/ppermute | solution.py:23
  196.1 14.3 %collective-permute-start.30 = (f32[16,4,8,128]{3,2,1,0:T(8,128)S(1)}, f32[16,4,8,128]{3,2,1,0:T(8,128)S(1)}, u32[]{:S(2)}, u32[]{:S(2)}) collective-permute-start(f32[16,4,8,128]{3,2,1,0:T(8,128)S(1)} %get-tuple-element.74), channel_id=1, source_target_pairs={{0,64},{16,80},{32,96},{48,112},{64,0},{80,16},{96,32},{112,48},{1... | collective-permute-start | bytes 786440 | tf_op jit(solution)/shard_map/ppermute | solution.py:23
  198.5 12.1 %collective-permute-start.31 = (f32[16,4,8,128]{3,2,1,0:T(8,128)S(1)}, f32[16,4,8,128]{3,2,1,0:T(8,128)S(1)}, u32[]{:S(2)}, u32[]{:S(2)}) collective-permute-start(f32[16,4,8,128]{3,2,1,0:T(8,128)S(1)} %get-tuple-element.73), channel_id=1, source_target_pairs={{0,96},{16,112},{32,0},{48,16},{64,32},{80,48},{96,64},{112,80},{1... | collective-permute-start | bytes 786440 | tf_op jit(solution)/shard_map/ppermute | solution.py:23
  199.8 18.2 %all-to-all-start = ((bf16[16,2,64,128]{3,2,1,0:T(8,128)(2,1)}), bf16[16,2,64,128]{3,2,1,0:T(8,128)(2,1)S(1)}, u32[]{:S(2)}, u32[]{:S(2)}) async-start(bf16[16,2,64,128]{3,2,1,0:T(8,128)(2,1)} %get-tuple-element.59), calls=%async_computation | async-start | bytes 1048576 | tf_op jit(solution)/shard_map/all_to_all | solution.py:575
  218.0 3.5 %copy-start.1 = (bf16[16,2,64,128]{3,2,1,0:T(8,128)(2,1)}, bf16[16,2,64,128]{3,2,1,0:T(8,128)(2,1)S(1)}, u32[]{:S(2)}) copy-start(bf16[16,2,64,128]{3,2,1,0:T(8,128)(2,1)S(1)} %all-to-all-done.x_ref) | copy-start | bytes 1572868
  218.0 12.2 %all-to-all-start.1 = ((f32[16,4,8,128]{3,2,1,0:T(8,128)}), f32[16,4,8,128]{3,2,1,0:T(8,128)S(1)}, u32[]{:S(2)}, u32[]{:S(2)}) async-start(f32[16,4,8,128]{3,2,1,0:T(8,128)} %fusion.6), calls=%async_computation.1 | async-start | bytes 524288 | tf_op jit(solution)/shard_map/all_to_all | solution.py:577
  230.2 0.7 copy-start.7

commit v2 on v1

--- a/solution.py
+++ b/solution.py
@@ -64,6 +64,7 @@
         scratch_shapes=[pltpu.VMEM((4, 128, 128), jnp.float32)],
         out_shape=jax.ShapeDtypeStruct((128, B, KA * B), jnp.bfloat16),
         name="spread",
+        compiler_params=pltpu.CompilerParams(vmem_limit_bytes=8 * 1024 * 1024),
     )(a)
 
 
@@ -97,6 +98,7 @@
             jax.ShapeDtypeStruct((NK, 128), jnp.float32),
         ],
         name="table",
+        compiler_params=pltpu.CompilerParams(vmem_limit_bytes=12 * 1024 * 1024),
     )(*parts)
 
 
@@ -149,7 +151,23 @@
     return e, tile
 
 
-def x_product_kernel(j, idx_ref, at_ref, a_ref, dup_ref, near_ref, far_ref, exp_ref):
+def pipelined(count, multiply, encode, r0_ref, r1_ref):
+    r1_ref[...] = jnp.zeros_like(r1_ref)
+
+    def two(k, carry):
+        r0_ref[...] = multiply(2 * k)
+        encode(jnp.maximum(2 * k - 1, 0), r1_ref[...])
+        r1_ref[...] = multiply(2 * k + 1)
+        encode(2 * k, r0_ref[...])
+        return carry
+
+    lax.fori_loop(0, count // 2, two, 0)
+    encode(count - 1, r1_ref[...])
+
+
+def x_product_kernel(
+    j, idx_ref, at_ref, a_ref, dup_ref, near_ref, far_ref, exp_ref, r0_ref, r1_ref
+):
     cblk = pl.program_id(0)
     low = low_lanes(B)
     goal = lax.rem(at_ref[0] + j, 4)
@@ -157,10 +175,12 @@
     count = a_ref.shape[2]
     is_low = goal < 2
 
-    def one(cc, carry):
+    def multiply(cc):
+        lhs = chosen_blocks(idx_ref, dup_ref, low, ih * 4 * NCOL + cblk * count + cc)
+        return row_pair(lhs, a_ref[0, 0, cc], a_ref[0, 1, cc])
+
+    def encode(cc, res):
         c = cblk * count + cc
-        lhs = chosen_blocks(idx_ref, dup_ref, low, ih * 4 * NCOL + c)
-        res = row_pair(lhs, a_ref[0, 0, cc], a_ref[0, 1, cc])
         e, tile = coded_products(res)
         exp_ref[pl.ds(c, 1), :] = e
         for u in range(4):
@@ -169,9 +189,8 @@
                 at = (u * NCOL + c) * 4 + sp
                 near_ref[at] = jnp.where(is_low, t0, t1).astype(jnp.int16)
                 far_ref[at] = jnp.where(is_low, t1, t0).astype(jnp.int16)
-        return carry
-
-    lax.fori_loop(0, count, one, 0)
+
+    pipelined(count, multiply, encode, r0_ref, r1_ref)
 
     @pl.when(cblk == pl.num_programs(0) - 1)
     def _():
@@ -193,16 +212,20 @@
                     (1, 2, block, B, KA * B),
                     lambda c, idx, at: (lax.rem(at[0] + j, 2) * 2, 0, c, 0, 0),
                 ),
-                pl.BlockSpec((NK * KP + 1, B, 128), lambda c, idx, at: (0, 0, 0)),
+                pl.BlockSpec(memory_space=pltpu.VMEM),
             ],
             out_specs=[out, out],
-            scratch_shapes=[pltpu.VMEM((NCOL, 128), jnp.float32)],
+            scratch_shapes=[pltpu.VMEM((NCOL, 128), jnp.float32)]
+            + [pltpu.VMEM((KAP * B, 128), jnp.float32)] * 2,
         ),
         out_shape=[jax.ShapeDtypeStruct((257, 16, 128), jnp.int16)] * 2,
-    )(idx, at, a, dup)
-
-
-def y_product_kernel(part, idx_ref, at_ref, a_ref, dup_ref, o0_ref, o1_ref, o2_ref, o3_ref, exp_ref):
+        compiler_params=pltpu.CompilerParams(vmem_limit_bytes=20 * 1024 * 1024),
+    )(idx, at, a, pltpu.with_memory_space_constraint(dup, pltpu.VMEM))
+
+
+def y_product_kernel(
+    part, idx_ref, at_ref, a_ref, dup_ref, o0_ref, o1_ref, o2_ref, o3_ref, exp_ref, r0_ref, r1_ref
+):
     ih = pl.program_id(0)
     low = low_lanes(B)
     y = at_ref[1]
@@ -211,9 +234,11 @@
     turn1 = lax.rem(y, 2) == 1
     turn2 = y >= 2
 
-    def one(cc, carry):
+    def multiply(cc):
         lhs = chosen_blocks(idx_ref, dup_ref, low, (ih * 4 + 2) * NCOL + part * count + cc)
-        res = row_pair(lhs, a_ref[0, 0, cc], a_ref[0, 1, cc])
+        return row_pair(lhs, a_ref[0, 0, cc], a_ref[0, 1, cc])
+
+    def encode(cc, res):
         e, tile = coded_products(res)
         exp_ref[pl.ds(ih * 8 + cc, 1), :] = e
         for g in range(2):
@@ -223,9 +248,8 @@
                 t = [jnp.where(turn2, t[(k + 2) % 4], t[k]) for k in range(4)]
                 for d in range(4):
                     outs[d][((2 * g + ih) * 8 + cc) * 4 + sp] = t[d].astype(jnp.int16)
-        return carry
-
-    lax.fori_loop(0, count, one, 0)
+
+    pipelined(count, multiply, encode, r0_ref, r1_ref)
 
     @pl.when(ih == 1)
     def _():
@@ -246,13 +270,15 @@
                 pl.BlockSpec(
                     (1, 2, block, B, KA * B), lambda ih, idx, at: (ih * 2 + 1, 0, part, 0, 0)
                 ),
-                pl.BlockSpec((NK * KP + 1, B, 128), lambda ih, idx, at: (0, 0, 0)),
+                pl.BlockSpec(memory_space=pltpu.VMEM),
             ],
             out_specs=[out] * 4,
-            scratch_shapes=[pltpu.VMEM((NCOL, 128), jnp.float32)],
+            scratch_shapes=[pltpu.VMEM((NCOL, 128), jnp.float32)]
+            + [pltpu.VMEM((KAP * B, 128), jnp.float32)] * 2,
         ),
         out_shape=[jax.ShapeDtypeStruct((129, 16, 128), jnp.int16)] * 4,
-    )(idx, at, a, dup)
+        compiler_params=pltpu.CompilerParams(vmem_limit_bytes=20 * 1024 * 1024),
+    )(idx, at, a, pltpu.with_memory_space_constraint(dup, pltpu.VMEM))
 
 
 def sum_and_code(tiles, out_ref, c):

time: 234 us -> 225 us (0.962)
  Pallas kernels: 85.2 us -> 57.4 us
  local copies, waits for them, and re-layouts: 11.1 us -> 23 us
  waiting for transfers between devices: 74.9 us -> 83.4 us
    unnamed x46 -> x54, local copies, waits for them, and re-layouts: 3.55 us -> 14.7 us
    pallas_call x2, Pallas kernels: 21.6 us -> 11.6 us  [y_products(): pl.pallas_call(lambda *refs: y_product_kernel(part, *refs), grid_spec=plt...]
    pallas_call x2, Pallas kernels: 21.3 us -> 11.4 us  [x_products(): pl.pallas_call(lambda *refs: x_product_kernel(j, *refs), grid_spec=pltpu....]
    ppermute x21, waiting for transfers between devices: 46.7 us -> 55.3 us  [along_col(): return lax.ppermute(v, 'col', pairs)]
    pallas_call x1, Pallas kernels: 8.35 us -> 4.1 us  [spread(): pl.pallas_call(spread_kernel, grid=(8,), in_specs=[pl.BlockSpec((16, KA,...]
    pallas_call x1, Pallas kernels: 6.44 us -> 2.86 us  [table(): pl.pallas_call(table_kernel, in_specs=[whole] * 8, out_specs=[whole, whol...]
  transfers between devices with their start and end apart: 34 -> 34, of which waited for: 14 -> 15; matrix products, arithmetic and copies ran while one was open for 4% -> 4% of each run, Pallas kernels for 30% -> 19%
where the time goes in v2:
time: 225 us; the launch traced here: 224 us
  waiting for transfers between devices  83.4 us (37%)
  Pallas kernels  57.4 us (26%)
  starting transfers between devices  53.8 us (24%)
  local copies, waits for them, and re-layouts  23 us (10%)
  other arithmetic  4.51 us (2%)
    ppermute x21, waiting for transfers between devices, along_col(): return lax.ppermute(v, 'col', pairs)  55.3 us
    ppermute x21, starting transfers between devices, along_col(): return lax.ppermute(v, 'col', pairs)  30.7 us
    ppermute x11, waiting for transfers between devices, along_row(): return lax.ppermute(v, 'row', pairs)  16.3 us
    unnamed x54, local copies, waits for them, and re-layouts  14.7 us
    pallas_call x1, Pallas kernels, coarse_terms(): pl.pallas_call(coarse_kernel, grid_spec=pltpu.PrefetchScalarGridSpec(num_...  12.7 us
    ppermute x11, starting transfers between devices, along_row(): return lax.ppermute(v, 'row', pairs)  12.3 us
    pallas_call x2, Pallas kernels, y_products(): pl.pallas_call(lambda *refs: y_product_kernel(part, *refs), grid_spec=plt...  11.6 us
    pallas_call x2, Pallas kernels, x_products(): pl.pallas_call(lambda *refs: x_product_kernel(j, *refs), grid_spec=pltpu....  11.4 us
  transfers between devices with their start and end apart: 34, of which 15 were waited for; matrix products, arithmetic and copies ran while one was open for 4% of the time, Pallas kernels for 19%

profile of v2, /device:TPU:0, one launch (start us, length us, event | category | flops | bytes accessed | tf_op | source)
XLA Modules:
  0.0 224.1 jit_solution(11618708707026021122)
XLA Ops:
  0.6 1.4 reshape_squeeze.3
  2.9 2.1 collective-permute-start
  5.0 3.6 %collective-permute-start.1 = (bf16[9,64,256]{2,1,0:T(8,128)(2,1)S(1)}, bf16[9,64,256]{2,1,0:T(8,128)(2,1)S(1)}, u32[]{:S(2)}, u32[]{:S(2)}) collective-permute-start(bf16[9,64,256]{2,1,0:T(8,128)(2,1)S(1)} %pad_maximum_fusion.2.refs_0_), channel_id=1, source_target_pairs={{0,64},{16,80},{32,96},{48,112},{64,0},{80,16},{96,32},{112,48},{1... | collective-permute-start | bytes 884744 | tf_op jit(solution)/shard_map/ppermute | solution.py:23
  8.6 1.0 collective-permute-start.2
  11.7 2.4 %collective-permute-done.refs_2_ = bf16[9,64,256]{2,1,0:T(8,128)(2,1)S(1)} collective-permute-done((bf16[9,64,256]{2,1,0:T(8,128)(2,1)S(1)}, bf16[9,64,256]{2,1,0:T(8,128)(2,1)S(1)}, u32[]{:S(2)}, u32[]{:S(2)}) %collective-permute-start) | collective-permute-done | bytes 294944 | tf_op jit(solution)/shard_map/ppermute | solution.py:23
  14.1 7.5 %collective-permute-done.1.refs_4_ = bf16[9,64,256]{2,1,0:T(8,128)(2,1)S(1)} collective-permute-done((bf16[9,64,256]{2,1,0:T(8,128)(2,1)S(1)}, bf16[9,64,256]{2,1,0:T(8,128)(2,1)S(1)}, u32[]{:S(2)}, u32[]{:S(2)}) %collective-permute-start.1) | collective-permute-done | bytes 294944 | tf_op jit(solution)/shard_map/ppermute | solution.py:23
  21.6 1.6 collective-permute-start.3
  23.2 1.7 collective-permute-start.5
  24.9 1.8 collective-permute-start.4
  26.8 2.2 copy-done.4
  29.0 4.1 %spread.1 = bf16[128,64,256]{2,1,0:T(8,128)(2,1)S(1)} custom-call(bf16[128,4,4096]{2,1,0:T(4,128)(2,1)S(1)} %bitcast.96), custom_call_target="tpu_custom_call" | custom-call | tf_op jit(solution)/shard_map/spread/pallas_call | solution.py:59
  33.1 2.0 copy-done
  35.8 1.0 pad_maximum_fusion.refs_8_
  36.8 3.0 %collective-permute-start.8 = (bf16[4,5,64,256]{3,2,1,0:T(8,128)(2,1)}, bf16[4,5,64,256]{3,2,1,0:T(8,128)(2,1)S(1)}, u32[]{:S(2)}, u32[]{:S(2)}) collective-permute-start(bf16[4,5,64,256]{3,2,1,0:T(8,128)(2,1)} %pad_maximum_fusion.refs_8_), channel_id=1, source_target_pairs={{0,12},{1,13},{2,14},{3,15},{4,0},{5,1},{6,2},{7,3},{8,4},{9,5},{1... | collective-permute-start | bytes 1966088 | tf_op jit(solution)/shard_map/ppermute | solution.py:28
  40.4 1.0 collective-permute-start.6
  41.4 2.9 %table.1 = (bf16[257,64,128]{2,1,0:T(8,128)(2,1)S(1)}, f32[64,128]{1,0:T(8,128)S(1)}) custom-call(bf16[9,64,256]{2,1,0:T(8,128)(2,1)S(1)} %pad_maximum_fusion.2.refs_0_, bf16[9,64,256]{2,1,0:T(8,128)(2,1)S(1)} %collective-permute-done.9.refs_1_, bf16[9,64,256]{2,1,0:T(8,128)(2,1)S(1)} %collective-permute-done.refs_2_, ...), custom_call_target="tpu_custom_call" | custom-call | tf_op jit(solution)/shard_map/table/pallas_call | solution.py:92
  44.3 2.1 copy-done.2
  47.0 2.2 copy-done.1
  49.2 2.2 copy-done.3
  51.4 5.4 %shard_map.81 = (s16[129,16,128]{2,1,0:T(8,128)(2,1)S(1)}, s16[129,16,128]{2,1,0:T(8,128)(2,1)S(1)}, s16[129,16,128]{2,1,0:T(8,128)(2,1)S(1)}, s16[129,16,128]{2,1,0:T(8,128)(2,1)S(1)}) custom-call(s32[4096]{0:T(1024)S(1)} %reshape.300.refs_0_, s32[4]{0:T(128)S(1)} %pad_add_fusion.refs_1_.at_ref, bf16[4,2,16,64,256]{4,3,2,1,0:T(8,128)(2,1)S(1)} %bitcast.92, ...), custom_call_target="tpu_custom_call" | custom-call | tf_op jit(solution)/shard_map/pallas_call | solution.py:264
  56.7 0.8 copy-done.6
  57.5 1.9 collective-permute-start.22
  59.4 1.8 collective-permute-start.23
  61.2 6.2 %shard_map.80 = (s16[129,16,128]{2,1,0:T(8,128)(2,1)S(1)}, s16[129,16,128]{2,1,0:T(8,128)(2,1)S(1)}, s16[129,16,128]{2,1,0:T(8,128)(2,1)}, s16[129,16,128]{2,1,0:T(8,128)(2,1)S(1)}) custom-call(s32[4096]{0:T(1024)S(1)} %reshape.300.refs_0_, s32[4]{0:T(128)S(1)} %pad_add_fusion.refs_1_.at_ref, bf16[4,2,16,64,256]{4,3,2,1,0:T(8,128)(2,1)S(1)} %bitcast.93, ...), custom_call_target="tpu_custom_call" | custom-call | tf_op jit(solution)/shard_map/pallas_call | solution.py:264
  67.5 0.8 copy-done.7
  68.3 11.8 %collective-permute-done.8.refs_11_ = bf16[4,5,64,256]{3,2,1,0:T(8,128)(2,1)S(1)} collective-permute-done((bf16[4,5,64,256]{3,2,1,0:T(8,128)(2,1)}, bf16[4,5,64,256]{3,2,1,0:T(8,128)(2,1)S(1)}, u32[]{:S(2)}, u32[]{:S(2)}) %collective-permute-start.8) | collective-permute-done | bytes 655392 | tf_op jit(solution)/shard_map/ppermute | solution.py:28
  80.0 3.6 %collective-permute-start.24 = (s16[129,16,128]{2,1,0:T(8,128)(2,1)S(1)}, s16[129,16,128]{2,1,0:T(8,128)(2,1)S(1)}, u32[]{:S(2)}, u32[]{:S(2)}) collective-permute-start(s16[129,16,128]{2,1,0:T(8,128)(2,1)S(1)} %get-tuple-element.54), channel_id=1, source_target_pairs={{0,12},{1,13},{2,14},{3,15},{4,0},{5,1},{6,2},{7,3},{8,4},{9,5},{1... | collective-permute-start | bytes 1585160 | tf_op jit(solution)/shard_map/ppermute | solution.py:28
  83.6 0.7 slice_bitcast_fusion.3
  84.3 6.2 %shard_map.78 = (s16[257,16,128]{2,1,0:T(8,128)(2,1)}, s16[257,16,128]{2,1,0:T(8,128)(2,1)S(1)}) custom-call(s32[4096]{0:T(1024)S(1)} %reshape.300.refs_0_, s32[4]{0:T(128)S(1)} %pad_add_fusion.refs_1_.at_ref, bf16[4,2,16,64,256]{4,3,2,1,0:T(8,128)(2,1)S(1)} %bitcast.94, bf16[257,64,128]{2,1,0:T(8,128)(2,1)S(1)} %copy-done.3), custom_call_target="tpu_custom_call" | custom-call | tf_op jit(solution)/shard_map/pallas_call | solution.py:205
  90.6 5.2 %shard_map.77 = (s16[257,16,128]{2,1,0:T(8,128)(2,1)S(1)}, s16[257,16,128]{2,1,0:T(8,128)(2,1)S(1)}) custom-call(s32[4096]{0:T(1024)S(1)} %reshape.300.refs_0_, s32[4]{0:T(128)S(1)} %pad_add_fusion.refs_1_.at_ref, bf16[4,2,16,64,256]{4,3,2,1,0:T(8,128)(2,1)S(1)} %bitcast.95, bf16[257,64,128]{2,1,0:T(8,128)(2,1)S(1)} %copy-done.3), custom_call_target="tpu_custom_call" | custom-call | tf_op jit(solution)/shard_map/pallas_call | solution.py:205
  95.8 1.0 copy-done.5
  96.8 0.7 slice_bitcast_fusion
  98.1 2.6 %collective-permute-start.15 = (s16[257,16,128]{2,1,0:T(8,128)(2,1)S(1)}, s16[257,16,128]{2,1,0:T(8,128)(2,1)}, u32[]{:S(2)}, u32[]{:S(2)}) collective-permute-start(s16[257,16,128]{2,1,0:T(8,128)(2,1)S(1)} %get-tuple-element.42), channel_id=1, source_target_pairs={{0,3},{1,0},{2,1},{3,2},{4,7},{5,4},{6,5},{7,6},{8,11},{9,8},{10,9... | collective-permute-start | bytes 3158024 | tf_op jit(solution)/shard_map/ppermute | solution.py:28
  101.2 0.7 slice_bitcast_fusion.1
  101.9 1.7 collective-permute-start.20
  103.7 3.5 %collective-permute-done.19.refs_1_ = s16[129,16,128]{2,1,0:T(8,128)(2,1)S(1)} collective-permute-done((s16[129,16,128]{2,1,0:T(8,128)(2,1)S(1)}, s16[129,16,128]{2,1,0:T(8,128)(2,1)S(1)}, u32[]{:S(2)}, u32[]{:S(2)}) %collective-permute-start.19) | collective-permute-done | bytes 528416 | tf_op jit(solution)/shard_map/ppermute | solution.py:28
  107.8 0.7 slice_bitcast_fusion.2
  108.9 8.9 %collective-permute-done.20.refs_2_ = s16[129,16,128]{2,1,0:T(8,128)(2,1)} collective-permute-done((s16[129,16,128]{2,1,0:T(8,128)(2,1)}, s16[129,16,128]{2,1,0:T(8,128)(2,1)}, u32[]{:S(2)}, u32[]{:S(2)}) %collective-permute-start.20) | collective-permute-done | bytes 528416 | tf_op jit(solution)/shard_map/ppermute | solution.py:28
  117.8 10.0 %collective-permute-done.21.refs_3_ = s16[129,16,128]{2,1,0:T(8,128)(2,1)} collective-permute-done((s16[129,16,128]{2,1,0:T(8,128)(2,1)S(1)}, s16[129,16,128]{2,1,0:T(8,128)(2,1)}, u32[]{:S(2)}, u32[]{:S(2)}) %collective-permute-start.21) | collective-permute-done | bytes 528416 | tf_op jit(solution)/shard_map/ppermute | solution.py:28
  127.8 5.2 %shard_map.82 = (s16[65,16,128]{2,1,0:T(8,128)(2,1)}, s16[65,16,128]{2,1,0:T(8,128)(2,1)}, s16[65,16,128]{2,1,0:T(8,128)(2,1)}, s16[65,16,128]{2,1,0:T(8,128)(2,1)}) custom-call(s32[4]{0:T(128)} %copy-done.8, s16[129,16,128]{2,1,0:T(8,128)(2,1)} %copy-done.7, s16[129,16,128]{2,1,0:T(8,128)(2,1)} %copy-done.16, ...), custom_call_target="tpu_custom_call" | custom-call | tf_op jit(solution)/shard_map/pallas_call | solution.py:348
  133.0 0.7 collective-permute-start.25
  134.0 2.4 %collective-permute-start.26 = (s16[65,16,128]{2,1,0:T(8,128)(2,1)}, s16[65,16,128]{2,1,0:T(8,128)(2,1)S(1)}, u32[]{:S(2)}, u32[]{:S(2)}) collective-permute-start(s16[65,16,128]{2,1,0:T(8,128)(2,1)} %get-tuple-element.57), channel_id=1, source_target_pairs={{0,2},{1,3},{2,0},{3,1},{4,6},{5,7},{6,4},{7,5},{8,10},{9,11},{10,... | collective-permute-start | bytes 798728 | tf_op jit(solution)/shard_map/ppermute | solution.py:28
  136.4 9.6 %collective-permute-done.13.m1 = s16[257,16,128]{2,1,0:T(8,128)(2,1)} collective-permute-done((s16[257,16,128]{2,1,0:T(8,128)(2,1)}, s16[257,16,128]{2,1,0:T(8,128)(2,1)}, u32[]{:S(2)}, u32[]{:S(2)}) %collective-permute-start.13) | collective-permute-done | bytes 1052704 | tf_op jit(solution)/shard_map/ppermute | solution.py:28
  145.9 5.5 %collective-permute-done.15.m3 = s16[257,16,128]{2,1,0:T(8,128)(2,1)} collective-permute-done((s16[257,16,128]{2,1,0:T(8,128)(2,1)S(1)}, s16[257,16,128]{2,1,0:T(8,128)(2,1)}, u32[]{:S(2)}, u32[]{:S(2)}) %collective-permute-start.15) | collective-permute-done | bytes 1052704 | tf_op jit(solution)/shard_map/ppermute | solution.py:28
  151.4 5.2 %shard_map.79 = (s16[65,16,128]{2,1,0:T(8,128)(2,1)}, s16[65,16,128]{2,1,0:T(8,128)(2,1)}, s16[65,16,128]{2,1,0:T(8,128)(2,1)}, s16[65,16,128]{2,1,0:T(8,128)(2,1)}) custom-call(s32[4]{0:T(128)} %copy-done.8, s16[257,16,128]{2,1,0:T(8,128)(2,1)} %copy-done.5, s16[257,16,128]{2,1,0:T(8,128)(2,1)} %collective-permute-done.13.m1, ...), custom_call_target="tpu_custom_call" | custom-call | tf_op jit(solution)/shard_map/pallas_call | solution.py:348
  156.7 4.2 %collective-permute-start.17 = (s16[65,16,128]{2,1,0:T(8,128)(2,1)}, s16[65,16,128]{2,1,0:T(8,128)(2,1)S(1)}, u32[]{:S(2)}, u32[]{:S(2)}) collective-permute-start(s16[65,16,128]{2,1,0:T(8,128)(2,1)} %get-tuple-element.45), channel_id=1, source_target_pairs={{0,8},{1,9},{2,10},{3,11},{4,12},{5,13},{6,14},{7,15},{8,0},{9,1},... | collective-permute-start | bytes 798728 | tf_op jit(solution)/shard_map/ppermute | solution.py:28
  161.5 0.8 reshape.299.tgt_ref
  162.3 2.2 collective-permute-done.16.refs_1_
  164.5 3.8 %collective-permute-done.17.refs_2_ = s16[65,16,128]{2,1,0:T(8,128)(2,1)S(1)} collective-permute-done((s16[65,16,128]{2,1,0:T(8,128)(2,1)}, s16[65,16,128]{2,1,0:T(8,128)(2,1)S(1)}, u32[]{:S(2)}, u32[]{:S(2)}) %collective-permute-start.17) | collective-permute-done | bytes 266272 | tf_op jit(solution)/shard_map/ppermute | solution.py:28
  169.1 12.7 %coarse_terms.1 = (bf16[16,2,64,128]{3,2,1,0:T(8,128)(2,1)}, f32[4,16,4,8,128]{4,3,2,1,0:T(8,128)}, f32[4,16,4,8,128]{4,3,2,1,0:T(8,128)}) custom-call(s32[2048]{0:T(1024)} %reshape.299.tgt_ref, s32[4]{0:T(128)} %copy-done.8, s16[65,16,128]{2,1,0:T(8,128)(2,1)} %get-tuple-element.43.refs_0_, s16[65,16,128]{2,1,0:T(8,128)(2,1)} %copy-done.20, ...), custom_call_target="tpu_custom_call" | custom-call | tf_op jit(solution)/shard_map/coarse_terms/pallas_call | solution.py:436
  181.8 2.9 %collective-permute-done.28 = f32[4,16,4,8,128]{4,3,2,1,0:T(8,128)S(1)} collective-permute-done((f32[4,16,4,8,128]{4,3,2,1,0:T(8,128)}, f32[4,16,4,8,128]{4,3,2,1,0:T(8,128)S(1)}, u32[]{:S(2)}, u32[]{:S(2)}) %collective-permute-start.28) | collective-permute-done | bytes 1048608 | tf_op jit(solution)/shard_map/ppermute | solution.py:23
  184.7 1.2 fusion.2
  185.9 1.2 collective-permute-start.29
  187.2 2.4 %collective-permute-start.30 = (f32[16,4,8,128]{3,2,1,0:T(8,128)S(1)}, f32[16,4,8,128]{3,2,1,0:T(8,128)S(1)}, u32[]{:S(2)}, u32[]{:S(2)}) collective-permute-start(f32[16,4,8,128]{3,2,1,0:T(8,128)S(1)} %get-tuple-element.74), channel_id=1, source_target_pairs={{0,64},{16,80},{32,96},{48,112},{64,0},{80,16},{96,32},{112,48},{1... | collective-permute-start | bytes 786440 | tf_op jit(solution)/shard_map/ppermute | solution.py:23
  189.6 1.3 collective-permute-start.31
  190.9 7.4 %all-to-all-start = ((bf16[16,2,64,128]{3,2,1,0:T(8,128)(2,1)}), bf16[16,2,64,128]{3,2,1,0:T(8,128)(2,1)S(1)}, u32[]{:S(2)}, u32[]{:S(2)}) async-start(bf16[16,2,64,128]{3,2,1,0:T(8,128)(2,1)} %get-tuple-element.59), calls=%async_computation | async-start | bytes 1048576 | tf_op jit(solution)/shard_map/all_to_all | solution.py:601
  198.3 3.2 %collective-permute-done.30 = f32[16,4,8,128]{3,2,1,0:T(8,128)S(1)} collective-permute-done((f32[16,4,8,128]{3,2,1,0:T(8,128)S(1)}, f32[16,4,8,128]{3,2,1,0:T(8,128)S(1)}, u32[]{:S(2)}, u32[]{:S(2)}) %collective-permute-start.30) | collective-permute-done | bytes 262176 | tf_op jit(solution)/shard_map/ppermute | solution.py:23
  201.8 1.8 fusion.6
  203.6 5.7 %all-to-all-done.x_ref = bf16[16,2,64,128]{3,2,1,0:T(8,128)(2,1)S(1)} async-done(((bf16[16,2,64,128]{3,2,1,0:T(8,128)(2,1)}), bf16[16,2,64,128]{3,2,1,0:T(8,128)(2,1)S(1)}, u32[]{:S(2)}, u32[]{:S(2)}) %all-to-all-start) | async-done | bytes 524320 | tf_op jit(solution)/shard_map/all_to_all | solution.py:601
  209.3 3.5 %all-to-all-start.1 = ((f32[16,4,8,128]{3,2,1,0:T(8,128)}), f32[16,4,8,128]{3,2,1,0:T(8,128)S(1)}, u32[]{:S(2)}, u32[]{:S(2)}) async-start(f32[16,4,8,128]{3,2,1,0:T(8,128)} %fusion.6), calls=%async_computation.1 | async-start | bytes 524288 | tf_op jit(solution)/shard_map/all_to_all | solution.py:603
  212.8 2.4 %ap_layout.1 = bf16[8,8,4096]{2,1,0:T(8,128)(2,1)} custom-call(bf16[16,2,64,128]{3,2,1,0:T(8,128)(2,1)} %copy-done.9), custom_call_target="tpu_custom_call" | custom-call | tf_op jit(solution)/shard_map/ap_layout/pallas_call | solution.py:479
  215.3 6.2 %all-to-all-done.1.x_ref = f32[16,4,8,128]{3,2,1,0:T(8,128)S(1)} async-done(((f32[16,4,8,128]{3,2,1,0:T(8,128)}), f32[16,4,8,128]{3,2,1,0:T(8,128)S(1)}, u32[]{:S(2)}, u32[]{:S(2)}) %all-to-all-start.1) | async-done | bytes 262176 | tf_op jit(solution)/shard_map/all_to_all | solution.py:603
  221.5 0.7 copy-done.11
  222.2 1.9 coarse_layout.1
  (118 shorter events, 9.0 us)
Async XLA Ops:
  2.1 0.7 copy-start.24
  2.1 7.5 %copy-start.10 = (bf16[8,1,4,4096]{3,2,1,0:T(4,128)(2,1)S(1)}, bf16[8,1,4,4096]{3,2,1,0:T(4,128)(2,1)}, u32[]{:S(2)}) copy-start(bf16[8,1,4,4096]{3,2,1,0:T(4,128)(2,1)} %param.8) | copy-start | bytes 786436
  2.9 11.2 %collective-permute-start = (bf16[9,64,256]{2,1,0:T(8,128)(2,1)S(1)}, bf16[9,64,256]{2,1,0:T(8,128)(2,1)S(1)}, u32[]{:S(2)}, u32[]{:S(2)}) collective-permute-start(bf16[9,64,256]{2,1,0:T(8,128)(2,1)S(1)} %pad_maximum_fusion.2.refs_0_), channel_id=1, source_target_pairs={{0,32},{16,48},{32,64},{48,80},{64,96},{80,112},{96,0},{112,16},{1... | collective-permute-start | bytes 884744 | tf_op jit(solution)/shard_map/ppermute | solution.py:23
  5.0 16.6 %collective-permute-start.1 = (bf16[9,64,256]{2,1,0:T(8,128)(2,1)S(1)}, bf16[9,64,256]{2,1,0:T(8,128)(2,1)S(1)}, u32[]{:S(2)}, u32[]{:S(2)}) collective-permute-start(bf16[9,64,256]{2,1,0:T(8,128)(2,1)S(1)} %pad_maximum_fusion.2.refs_0_), channel_id=1, source_target_pairs={{0,64},{16,80},{32,96},{48,112},{64,0},{80,16},{96,32},{112,48},{1... | collective-permute-start | bytes 884744 | tf_op jit(solution)/shard_map/ppermute | solution.py:23
  8.6 13.0 %collective-permute-start.2 = (bf16[9,64,256]{2,1,0:T(8,128)(2,1)S(1)}, bf16[9,64,256]{2,1,0:T(8,128)(2,1)S(1)}, u32[]{:S(2)}, u32[]{:S(2)}) collective-permute-start(bf16[9,64,256]{2,1,0:T(8,128)(2,1)S(1)} %pad_maximum_fusion.2.refs_0_), channel_id=1, source_target_pairs={{0,96},{16,112},{32,0},{48,16},{64,32},{80,48},{96,64},{112,80},{1... | collective-permute-start | bytes 884744 | tf_op jit(solution)/shard_map/ppermute | solution.py:23
  9.6 30.2 %collective-permute-start.9 = (bf16[9,64,256]{2,1,0:T(8,128)(2,1)S(1)}, bf16[9,64,256]{2,1,0:T(8,128)(2,1)S(1)}, u32[]{:S(2)}, u32[]{:S(2)}) collective-permute-start(bf16[9,64,256]{2,1,0:T(8,128)(2,1)S(1)} %pad_maximum_fusion.2.refs_0_), channel_id=1, source_target_pairs={{0,16},{16,0},{32,48},{48,32},{64,80},{80,64},{96,112},{112,96},{1... | collective-permute-start | bytes 884744 | tf_op jit(solution)/shard_map/ppermute | solution.py:23
  10.5 1.0 copy-start.23
  10.7 1.0 copy-start.25
  21.6 13.6 %collective-permute-start.3 = (bf16[5,64,256]{2,1,0:T(8,128)(2,1)S(1)}, bf16[5,64,256]{2,1,0:T(8,128)(2,1)S(1)}, u32[]{:S(2)}, u32[]{:S(2)}) collective-permute-start(bf16[5,64,256]{2,1,0:T(8,128)(2,1)S(1)} %get-tuple-element.78), channel_id=1, source_target_pairs={{0,1},{1,2},{2,3},{3,0},{4,5},{5,6},{6,7},{7,4},{8,9},{9,10},{10,1... | collective-permute-start | bytes 491528 | tf_op jit(solution)/shard_map/ppermute | solution.py:28
  23.2 12.6 %collective-permute-start.5 = (bf16[5,64,256]{2,1,0:T(8,128)(2,1)S(1)}, bf16[5,64,256]{2,1,0:T(8,128)(2,1)S(1)}, u32[]{:S(2)}, u32[]{:S(2)}) collective-permute-start(bf16[5,64,256]{2,1,0:T(8,128)(2,1)S(1)} %get-tuple-element.78), channel_id=1, source_target_pairs={{0,3},{1,0},{2,1},{3,2},{4,7},{5,4},{6,5},{7,6},{8,11},{9,8},{10,9... | collective-permute-start | bytes 491528 | tf_op jit(solution)/shard_map/ppermute | solution.py:28
  24.9 10.8 %collective-permute-start.4 = (bf16[5,64,256]{2,1,0:T(8,128)(2,1)S(1)}, bf16[5,64,256]{2,1,0:T(8,128)(2,1)S(1)}, u32[]{:S(2)}, u32[]{:S(2)}) collective-permute-start(bf16[5,64,256]{2,1,0:T(8,128)(2,1)S(1)} %bitcast.99), channel_id=1, source_target_pairs={{0,2},{1,3},{2,0},{3,1},{4,6},{5,7},{6,4},{7,5},{8,10},{9,11},{10,... | collective-permute-start | bytes 491528 | tf_op jit(solution)/shard_map/ppermute | solution.py:28
  26.8 2.2 copy-start.4
  33.1 2.0 copy-start
  35.2 55.4 %copy-start.8 = (s32[4]{0:T(128)}, s32[4]{0:T(128)S(1)}, u32[]{:S(2)}) copy-start(s32[4]{0:T(128)S(1)} %pad_add_fusion.refs_1_.at_ref) | copy-start | bytes 52
  35.2 5.3 %collective-permute-start.10 = (bf16[9,64,256]{2,1,0:T(8,128)(2,1)S(1)}, bf16[9,64,256]{2,1,0:T(8,128)(2,1)S(1)}, u32[]{:S(2)}, u32[]{:S(2)}) collective-permute-start(bf16[9,64,256]{2,1,0:T(8,128)(2,1)S(1)} %collective-permute-done.refs_2_), channel_id=1, source_target_pairs={{0,16},{16,0},{32,48},{48,32},{64,80},{80,64},{96,112},{112,96},{1... | collective-permute-start | bytes 884744 | tf_op jit(solution)/shard_map/ppermute | solution.py:23
  35.2 6.2 %collective-permute-start.11 = (bf16[9,64,256]{2,1,0:T(8,128)(2,1)S(1)}, bf16[9,64,256]{2,1,0:T(8,128)(2,1)S(1)}, u32[]{:S(2)}, u32[]{:S(2)}) collective-permute-start(bf16[9,64,256]{2,1,0:T(8,128)(2,1)S(1)} %collective-permute-done.1.refs_4_), channel_id=1, source_target_pairs={{0,16},{16,0},{32,48},{48,32},{64,80},{80,64},{96,112},{112,96},{1... | collective-permute-start | bytes 884744 | tf_op jit(solution)/shard_map/ppermute | solution.py:23
  35.7 5.7 %collective-permute-start.12 = (bf16[9,64,256]{2,1,0:T(8,128)(2,1)S(1)}, bf16[9,64,256]{2,1,0:T(8,128)(2,1)S(1)}, u32[]{:S(2)}, u32[]{:S(2)}) collective-permute-start(bf16[9,64,256]{2,1,0:T(8,128)(2,1)S(1)} %collective-permute-done.2.refs_6_), channel_id=1, source_target_pairs={{0,16},{16,0},{32,48},{48,32},{64,80},{80,64},{96,112},{112,96},{1... | collective-permute-start | bytes 884744 | tf_op jit(solution)/shard_map/ppermute | solution.py:23
  36.8 43.3 %collective-permute-start.8 = (bf16[4,5,64,256]{3,2,1,0:T(8,128)(2,1)}, bf16[4,5,64,256]{3,2,1,0:T(8,128)(2,1)S(1)}, u32[]{:S(2)}, u32[]{:S(2)}) collective-permute-start(bf16[4,5,64,256]{3,2,1,0:T(8,128)(2,1)} %pad_maximum_fusion.refs_8_), channel_id=1, source_target_pairs={{0,12},{1,13},{2,14},{3,15},{4,0},{5,1},{6,2},{7,3},{8,4},{9,5},{1... | collective-permute-start | bytes 1966088 | tf_op jit(solution)/shard_map/ppermute | solution.py:28
  39.8 43.8 %collective-permute-start.7 = (bf16[4,5,64,256]{3,2,1,0:T(8,128)(2,1)}, bf16[4,5,64,256]{3,2,1,0:T(8,128)(2,1)}, u32[]{:S(2)}, u32[]{:S(2)}) collective-permute-start(bf16[4,5,64,256]{3,2,1,0:T(8,128)(2,1)} %pad_maximum_fusion.refs_8_), channel_id=1, source_target_pairs={{0,8},{1,9},{2,10},{3,11},{4,12},{5,13},{6,14},{7,15},{8,0},{9,1},... | collective-permute-start | bytes 1966088 | tf_op jit(solution)/shard_map/ppermute | solution.py:28
  40.4 57.0 %collective-permute-start.6 = (bf16[4,5,64,256]{3,2,1,0:T(8,128)(2,1)}, bf16[4,5,64,256]{3,2,1,0:T(8,128)(2,1)}, u32[]{:S(2)}, u32[]{:S(2)}) collective-permute-start(bf16[4,5,64,256]{3,2,1,0:T(8,128)(2,1)} %pad_maximum_fusion.refs_8_), channel_id=1, source_target_pairs={{0,4},{1,5},{2,6},{3,7},{4,8},{5,9},{6,10},{7,11},{8,12},{9,13},{1... | collective-permute-start | bytes 1966088 | tf_op jit(solution)/shard_map/ppermute | solution.py:28
  44.3 2.1 copy-start.2
  47.0 2.2 copy-start.1
  49.2 2.2 copy-start.3
  56.7 0.8 copy-start.6
  57.5 40.6 %collective-permute-start.22 = (s16[129,16,128]{2,1,0:T(8,128)(2,1)S(1)}, s16[129,16,128]{2,1,0:T(8,128)(2,1)S(1)}, u32[]{:S(2)}, u32[]{:S(2)}) collective-permute-start(s16[129,16,128]{2,1,0:T(8,128)(2,1)S(1)} %get-tuple-element.52), channel_id=1, source_target_pairs={{0,4},{1,5},{2,6},{3,7},{4,8},{5,9},{6,10},{7,11},{8,12},{9,13},{1... | collective-permute-start | bytes 1585160 | tf_op jit(solution)/shard_map/ppermute | solution.py:28
  59.4 41.3 %collective-permute-start.23 = (s16[129,16,128]{2,1,0:T(8,128)(2,1)S(1)}, s16[129,16,128]{2,1,0:T(8,128)(2,1)S(1)}, u32[]{:S(2)}, u32[]{:S(2)}) collective-permute-start(s16[129,16,128]{2,1,0:T(8,128)(2,1)S(1)} %get-tuple-element.53), channel_id=1, source_target_pairs={{0,8},{1,9},{2,10},{3,11},{4,12},{5,13},{6,14},{7,15},{8,0},{9,1},... | collective-permute-start | bytes 1585160 | tf_op jit(solution)/shard_map/ppermute | solution.py:28
  67.5 0.8 copy-start.7
  80.0 3.6 %copy-start.12 = (bf16[4,5,64,256]{3,2,1,0:T(8,128)(2,1)}, bf16[4,5,64,256]{3,2,1,0:T(8,128)(2,1)S(1)}, u32[]{:S(2)}) copy-start(bf16[4,5,64,256]{3,2,1,0:T(8,128)(2,1)S(1)} %collective-permute-done.8.refs_11_) | copy-start | bytes 1966084
  80.0 21.9 %collective-permute-start.24 = (s16[129,16,128]{2,1,0:T(8,128)(2,1)S(1)}, s16[129,16,128]{2,1,0:T(8,128)(2,1)S(1)}, u32[]{:S(2)}, u32[]{:S(2)}) collective-permute-start(s16[129,16,128]{2,1,0:T(8,128)(2,1)S(1)} %get-tuple-element.54), channel_id=1, source_target_pairs={{0,12},{1,13},{2,14},{3,15},{4,0},{5,1},{6,2},{7,3},{8,4},{9,5},{1... | collective-permute-start | bytes 1585160 | tf_op jit(solution)/shard_map/ppermute | solution.py:28
  83.6 23.5 %collective-permute-start.19 = (s16[129,16,128]{2,1,0:T(8,128)(2,1)S(1)}, s16[129,16,128]{2,1,0:T(8,128)(2,1)S(1)}, u32[]{:S(2)}, u32[]{:S(2)}) collective-permute-start(s16[129,16,128]{2,1,0:T(8,128)(2,1)S(1)} %get-tuple-element.48), channel_id=1, source_target_pairs={{0,4},{1,5},{2,6},{3,7},{4,8},{5,9},{6,10},{7,11},{8,12},{9,13},{1... | collective-permute-start | bytes 1585160 | tf_op jit(solution)/shard_map/ppermute | solution.py:28
  95.8 1.0 copy-start.5
  97.5 48.5 %collective-permute-start.13 = (s16[257,16,128]{2,1,0:T(8,128)(2,1)}, s16[257,16,128]{2,1,0:T(8,128)(2,1)}, u32[]{:S(2)}, u32[]{:S(2)}) collective-permute-start(s16[257,16,128]{2,1,0:T(8,128)(2,1)} %get-tuple-element.40), channel_id=1, source_target_pairs={{0,1},{1,2},{2,3},{3,0},{4,5},{5,6},{6,7},{7,4},{8,9},{9,10},{10,1... | collective-permute-start | bytes 3158024 | tf_op jit(solution)/shard_map/ppermute | solution.py:28
  98.1 9.7 %copy-start.13 = (s16[129,16,128]{2,1,0:T(8,128)(2,1)}, s16[129,16,128]{2,1,0:T(8,128)(2,1)S(1)}, u32[]{:S(2)}) copy-start(s16[129,16,128]{2,1,0:T(8,128)(2,1)S(1)} %collective-permute-done.22.refs_5_) | copy-start | bytes 1585156
  98.1 53.4 %collective-permute-start.15 = (s16[257,16,128]{2,1,0:T(8,128)(2,1)S(1)}, s16[257,16,128]{2,1,0:T(8,128)(2,1)}, u32[]{:S(2)}, u32[]{:S(2)}) collective-permute-start(s16[257,16,128]{2,1,0:T(8,128)(2,1)S(1)} %get-tuple-element.42), channel_id=1, source_target_pairs={{0,3},{1,0},{2,1},{3,2},{4,7},{5,4},{6,5},{7,6},{8,11},{9,8},{10,9... | collective-permute-start | bytes 3158024 | tf_op jit(solution)/shard_map/ppermute | solution.py:28
  100.7 7.8 %copy-start.14 = (s16[129,16,128]{2,1,0:T(8,128)(2,1)}, s16[129,16,128]{2,1,0:T(8,128)(2,1)S(1)}, u32[]{:S(2)}) copy-start(s16[129,16,128]{2,1,0:T(8,128)(2,1)S(1)} %collective-permute-done.23.refs_6_) | copy-start | bytes 1585156
  100.7 50.7 %collective-permute-start.14 = (s16[257,16,128]{2,1,0:T(8,128)(2,1)S(1)}, s16[257,16,128]{2,1,0:T(8,128)(2,1)}, u32[]{:S(2)}, u32[]{:S(2)}) collective-permute-start(s16[257,16,128]{2,1,0:T(8,128)(2,1)S(1)} %get-tuple-element.41), channel_id=1, source_target_pairs={{0,2},{1,3},{2,0},{3,1},{4,6},{5,7},{6,4},{7,5},{8,10},{9,11},{10,... | collective-permute-start | bytes 3158024 | tf_op jit(solution)/shard_map/ppermute | solution.py:28
  101.9 6.6 %copy-start.15 = (s16[129,16,128]{2,1,0:T(8,128)(2,1)}, s16[129,16,128]{2,1,0:T(8,128)(2,1)S(1)}, u32[]{:S(2)}) copy-start(s16[129,16,128]{2,1,0:T(8,128)(2,1)S(1)} %collective-permute-done.24.refs_7_) | copy-start | bytes 1585156
  101.9 15.9 %collective-permute-start.20 = (s16[129,16,128]{2,1,0:T(8,128)(2,1)}, s16[129,16,128]{2,1,0:T(8,128)(2,1)}, u32[]{:S(2)}, u32[]{:S(2)}) collective-permute-start(s16[129,16,128]{2,1,0:T(8,128)(2,1)} %get-tuple-element.49), channel_id=1, source_target_pairs={{0,8},{1,9},{2,10},{3,11},{4,12},{5,13},{6,14},{7,15},{8,0},{9,1},... | collective-permute-start | bytes 1585160 | tf_op jit(solution)/shard_map/ppermute | solution.py:28
  107.1 1.4 copy-start.16
  107.1 20.6 %collective-permute-start.21 = (s16[129,16,128]{2,1,0:T(8,128)(2,1)S(1)}, s16[129,16,128]{2,1,0:T(8,128)(2,1)}, u32[]{:S(2)}, u32[]{:S(2)}) collective-permute-start(s16[129,16,128]{2,1,0:T(8,128)(2,1)S(1)} %get-tuple-element.50), channel_id=1, source_target_pairs={{0,12},{1,13},{2,14},{3,15},{4,0},{5,1},{6,2},{7,3},{8,4},{9,5},{1... | collective-permute-start | bytes 1585160 | tf_op jit(solution)/shard_map/ppermute | solution.py:28
  127.8 5.9 %copy-start.26 = (s32[128,8]{0,1:T(8,128)S(1)}, s32[128,8]{0,1:T(8,128)}, u32[]{:S(2)}) copy-start(s32[128,8]{0,1:T(8,128)} %param.11) | copy-start | bytes 12292
  133.0 27.9 %collective-permute-start.25 = (s16[65,16,128]{2,1,0:T(8,128)(2,1)}, s16[65,16,128]{2,1,0:T(8,128)(2,1)S(1)}, u32[]{:S(2)}, u32[]{:S(2)}) collective-permute-start(s16[65,16,128]{2,1,0:T(8,128)(2,1)} %get-tuple-element.56), channel_id=1, source_target_pairs={{0,1},{1,2},{2,3},{3,0},{4,5},{5,6},{6,7},{7,4},{8,9},{9,10},{10,1... | collective-permute-start | bytes 798728 | tf_op jit(solution)/shard_map/ppermute | solution.py:28
  134.0 28.2 %collective-permute-start.26 = (s16[65,16,128]{2,1,0:T(8,128)(2,1)}, s16[65,16,128]{2,1,0:T(8,128)(2,1)S(1)}, u32[]{:S(2)}, u32[]{:S(2)}) collective-permute-start(s16[65,16,128]{2,1,0:T(8,128)(2,1)} %get-tuple-element.57), channel_id=1, source_target_pairs={{0,2},{1,3},{2,0},{3,1},{4,6},{5,7},{6,4},{7,5},{8,10},{9,11},{10,... | collective-permute-start | bytes 798728 | tf_op jit(solution)/shard_map/ppermute | solution.py:28
  145.9 16.3 %collective-permute-start.27 = (s16[65,16,128]{2,1,0:T(8,128)(2,1)}, s16[65,16,128]{2,1,0:T(8,128)(2,1)S(1)}, u32[]{:S(2)}, u32[]{:S(2)}) collective-permute-start(s16[65,16,128]{2,1,0:T(8,128)(2,1)} %get-tuple-element.58), channel_id=1, source_target_pairs={{0,3},{1,0},{2,1},{3,2},{4,7},{5,4},{6,5},{7,6},{8,11},{9,8},{10,9... | collective-permute-start | bytes 798728 | tf_op jit(solution)/shard_map/ppermute | solution.py:28
  156.7 7.8 %collective-permute-start.16 = (s16[65,16,128]{2,1,0:T(8,128)(2,1)}, s16[65,16,128]{2,1,0:T(8,128)(2,1)S(1)}, u32[]{:S(2)}, u32[]{:S(2)}) collective-permute-start(s16[65,16,128]{2,1,0:T(8,128)(2,1)} %get-tuple-element.44), channel_id=1, source_target_pairs={{0,4},{1,5},{2,6},{3,7},{4,8},{5,9},{6,10},{7,11},{8,12},{9,13},{1... | collective-permute-start | bytes 798728 | tf_op jit(solution)/shard_map/ppermute | solution.py:28
  156.7 11.6 %collective-permute-start.17 = (s16[65,16,128]{2,1,0:T(8,128)(2,1)}, s16[65,16,128]{2,1,0:T(8,128)(2,1)S(1)}, u32[]{:S(2)}, u32[]{:S(2)}) collective-permute-start(s16[65,16,128]{2,1,0:T(8,128)(2,1)} %get-tuple-element.45), channel_id=1, source_target_pairs={{0,8},{1,9},{2,10},{3,11},{4,12},{5,13},{6,14},{7,15},{8,0},{9,1},... | collective-permute-start | bytes 798728 | tf_op jit(solution)/shard_map/ppermute | solution.py:28
  160.8 7.5 %copy-start.17 = (s16[65,16,128]{2,1,0:T(8,128)(2,1)}, s16[65,16,128]{2,1,0:T(8,128)(2,1)S(1)}, u32[]{:S(2)}) copy-start(s16[65,16,128]{2,1,0:T(8,128)(2,1)S(1)} %collective-permute-done.25.refs_5_) | copy-start | bytes 798724
  160.8 7.5 %collective-permute-start.18 = (s16[65,16,128]{2,1,0:T(8,128)(2,1)}, s16[65,16,128]{2,1,0:T(8,128)(2,1)S(1)}, u32[]{:S(2)}, u32[]{:S(2)}) collective-permute-start(s16[65,16,128]{2,1,0:T(8,128)(2,1)} %get-tuple-element.46), channel_id=1, source_target_pairs={{0,12},{1,13},{2,14},{3,15},{4,0},{5,1},{6,2},{7,3},{8,4},{9,5},{1... | collective-permute-start | bytes 798728 | tf_op jit(solution)/shard_map/ppermute | solution.py:28
  162.2 6.1 %copy-start.18 = (s16[65,16,128]{2,1,0:T(8,128)(2,1)}, s16[65,16,128]{2,1,0:T(8,128)(2,1)S(1)}, u32[]{:S(2)}) copy-start(s16[65,16,128]{2,1,0:T(8,128)(2,1)S(1)} %collective-permute-done.26.refs_6_) | copy-start | bytes 798724
  162.2 6.1 %copy-start.19 = (s16[65,16,128]{2,1,0:T(8,128)(2,1)}, s16[65,16,128]{2,1,0:T(8,128)(2,1)S(1)}, u32[]{:S(2)}) copy-start(s16[65,16,128]{2,1,0:T(8,128)(2,1)S(1)} %collective-permute-done.27.refs_7_) | copy-start | bytes 798724
  164.5 3.8 %copy-start.20 = (s16[65,16,128]{2,1,0:T(8,128)(2,1)}, s16[65,16,128]{2,1,0:T(8,128)(2,1)S(1)}, u32[]{:S(2)}) copy-start(s16[65,16,128]{2,1,0:T(8,128)(2,1)S(1)} %collective-permute-done.16.refs_1_) | copy-start | bytes 798724
  168.3 0.7 copy-start.21
  168.3 0.8 copy-start.22
  181.8 2.9 %collective-permute-start.28 = (f32[4,16,4,8,128]{4,3,2,1,0:T(8,128)}, f32[4,16,4,8,128]{4,3,2,1,0:T(8,128)S(1)}, u32[]{:S(2)}, u32[]{:S(2)}) collective-permute-start(f32[4,16,4,8,128]{4,3,2,1,0:T(8,128)} %get-tuple-element.61), channel_id=1, source_target_pairs={{0,16},{16,0},{32,48},{48,32},{64,80},{80,64},{96,112},{112,96},{1... | collective-permute-start | bytes 3145736 | tf_op jit(solution)/shard_map/ppermute | solution.py:23
  185.9 12.4 %collective-permute-start.29 = (f32[16,4,8,128]{3,2,1,0:T(8,128)S(1)}, f32[16,4,8,128]{3,2,1,0:T(8,128)S(1)}, u32[]{:S(2)}, u32[]{:S(2)}) collective-permute-start(f32[16,4,8,128]{3,2,1,0:T(8,128)S(1)} %get-tuple-element.72), channel_id=1, source_target_pairs={{0,32},{16,48},{32,64},{48,80},{64,96},{80,112},{96,0},{112,16},{1... | collective-permute-start | bytes 786440 | tf_op jit(solution)/shard_map/ppermute | solution.py:23
  187.2 14.3 %collective-permute-start.30 = (f32[16,4,8,128]{3,2,1,0:T(8,128)S(1)}, f32[16,4,8,128]{3,2,1,0:T(8,128)S(1)}, u32[]{:S(2)}, u32[]{:S(2)}) collective-permute-start(f32[16,4,8,128]{3,2,1,0:T(8,128)S(1)} %get-tuple-element.74), channel_id=1, source_target_pairs={{0,64},{16,80},{32,96},{48,112},{64,0},{80,16},{96,32},{112,48},{1... | collective-permute-start | bytes 786440 | tf_op jit(solution)/shard_map/ppermute | solution.py:23
  189.6 12.2 %collective-permute-start.31 = (f32[16,4,8,128]{3,2,1,0:T(8,128)S(1)}, f32[16,4,8,128]{3,2,1,0:T(8,128)S(1)}, u32[]{:S(2)}, u32[]{:S(2)}) collective-permute-start(f32[16,4,8,128]{3,2,1,0:T(8,128)S(1)} %get-tuple-element.73), channel_id=1, source_target_pairs={{0,96},{16,112},{32,0},{48,16},{64,32},{80,48},{96,64},{112,80},{1... | collective-permute-start | bytes 786440 | tf_op jit(solution)/shard_map/ppermute | solution.py:23
  190.9 18.4 %all-to-all-start = ((bf16[16,2,64,128]{3,2,1,0:T(8,128)(2,1)}), bf16[16,2,64,128]{3,2,1,0:T(8,128)(2,1)S(1)}, u32[]{:S(2)}, u32[]{:S(2)}) async-start(bf16[16,2,64,128]{3,2,1,0:T(8,128)(2,1)} %get-tuple-element.59), calls=%async_computation | async-start | bytes 1048576 | tf_op jit(solution)/shard_map/all_to_all | solution.py:601
  209.3 3.5 %copy-start.9 = (bf16[16,2,64,128]{3,2,1,0:T(8,128)(2,1)}, bf16[16,2,64,128]{3,2,1,0:T(8,128)(2,1)S(1)}, u32[]{:S(2)}) copy-start(bf16[16,2,64,128]{3,2,1,0:T(8,128)(2,1)S(1)} %all-to-all-done.x_ref) | copy-start | bytes 1572868
  209.3 12.2 %all-to-all-start.1 = ((f32[16,4,8,128]{3,2,1,0:T(8,128)}), f32[16,4,8,128]{3,2,1,0:T(8,128)S(1)}, u32[]{:S(2)}, u32[]{:S(2)}) async-start(f32[16,4,8,128]{3,2,1,0:T(8,128)} %fusion.6), calls=%async_computation.1 | async-start | bytes 524288 | tf_op jit(solution)/shard_map/all_to_all | solution.py:603
  221.5 0.7 copy-start.11

commit v3 on v2

--- a/solution.py
+++ b/solution.py
@@ -62,21 +62,21 @@
         in_specs=[pl.BlockSpec((16, KA, B * B), lambda g: (g, 0, 0))],
         out_specs=pl.BlockSpec((16, B, KA * B), lambda g: (g, 0, 0)),
         scratch_shapes=[pltpu.VMEM((4, 128, 128), jnp.float32)],
-        out_shape=jax.ShapeDtypeStruct((128, B, KA * B), jnp.bfloat16),
+        out_shape=pltpu.HBM((128, B, KA * B), jnp.bfloat16),
         name="spread",
         compiler_params=pltpu.CompilerParams(vmem_limit_bytes=8 * 1024 * 1024),
-    )(a)
+    )(pltpu.with_memory_space_constraint(a, pltpu.HBM))
 
 
 def table_kernel(*refs):
     parts, out_ref, cols_ref = refs[:8], refs[8], refs[9]
     low = low_lanes(B)
     for n, part in enumerate(parts):
-        cols_ref[n * 8:(n + 1) * 8, :] = part[8, 0:8, 0:128].astype(jnp.float32)
+        cols_ref[n * 8:(n + 1) * 8, :] = part[8 * B:8 * B + 8, 0:128].astype(jnp.float32)
 
         def fill(q, carry):
             for mh in range(2):
-                v = part[q, :, mh * 128:(mh + 1) * 128]
+                v = part[pl.ds(pl.multiple_of(q * B, B), B), mh * 128:(mh + 1) * 128]
                 turned = jnp.concatenate([v[:, B:], v[:, :B]], axis=1)
                 at = (n * 8 + q) * 4 + 2 * mh
                 out_ref[at] = jnp.where(low, v, turned)
@@ -94,7 +94,7 @@
         in_specs=[whole] * 8,
         out_specs=[whole, whole],
         out_shape=[
-            jax.ShapeDtypeStruct((NK * KP + 1, B, 128), jnp.bfloat16),
+            pltpu.HBM((NK * KP + 1, B, 128), jnp.bfloat16),
             jax.ShapeDtypeStruct((NK, 128), jnp.float32),
         ],
         name="table",
@@ -220,7 +220,12 @@
         ),
         out_shape=[jax.ShapeDtypeStruct((257, 16, 128), jnp.int16)] * 2,
         compiler_params=pltpu.CompilerParams(vmem_limit_bytes=20 * 1024 * 1024),
-    )(idx, at, a, pltpu.with_memory_space_constraint(dup, pltpu.VMEM))
+    )(
+        idx,
+        at,
+        pltpu.with_memory_space_constraint(a, pltpu.HBM),
+        pltpu.with_memory_space_constraint(dup, pltpu.VMEM),
+    )
 
 
 def y_product_kernel(
@@ -278,7 +283,12 @@
         ),
         out_shape=[jax.ShapeDtypeStruct((129, 16, 128), jnp.int16)] * 4,
         compiler_params=pltpu.CompilerParams(vmem_limit_bytes=20 * 1024 * 1024),
-    )(idx, at, a, pltpu.with_memory_space_constraint(dup, pltpu.VMEM))
+    )(
+        idx,
+        at,
+        pltpu.with_memory_space_constraint(a, pltpu.HBM),
+        pltpu.with_memory_space_constraint(dup, pltpu.VMEM),
+    )
 
 
 def sum_and_code(tiles, out_ref, c):
@@ -394,7 +404,7 @@
             x = x_ref[c, qh]
             none = jnp.zeros_like(x)
             lhs = jnp.concatenate([jnp.where(low_x, x, none), jnp.where(low_x, none, x)], axis=0)
-            rhs = p_ref[0, 2 * qh:2 * qh + 2].reshape(2 * B, KP * B)
+            rhs = p_ref[0, qh * 2 * B:(qh + 1) * 2 * B, :]
             res = lax.dot_general(
                 lhs, rhs, (((1,), (0,)), ((), ())), preferred_element_type=jnp.float32
             )
@@ -439,7 +449,7 @@
             num_scalar_prefetch=2,
             grid=(4,),
             in_specs=[pl.BlockSpec((65, 16, 128), lambda dx, tgt, at: (0, 0, 0))] * 8
-            + [pl.BlockSpec((1, 5, B, KP * B), lambda dx, tgt, at: (dx, 0, 0, 0))] * 4,
+            + [pl.BlockSpec((1, 4 * B + 16, KP * B), lambda dx, tgt, at: (dx, 0, 0))] * 4,
             out_specs=[
                 pl.BlockSpec((NCOL, 2, B, 128), lambda dx, tgt, at: (0, 0, 0, 0)), out, out
             ],
@@ -519,8 +529,7 @@
 
 
 def index_slab(index):
-    wide = jnp.pad(index.astype(jnp.bfloat16), ((0, B - index.shape[0]), (0, KP * B - KP)))
-    return wide[None]
+    return jnp.pad(index.astype(jnp.bfloat16), ((0, 16 - index.shape[0]), (0, KP * B - KP)))
 
 
 def step(a_blocks, a_index, p_blocks, p_index, ap_index, coarse_index):
@@ -532,12 +541,12 @@
     half = x % 2
 
     own = p_blocks[:, 0].reshape(8, KP, B, B)
-    pt = own.transpose(0, 3, 1, 2).reshape(8, B, KP * B)
+    pt = own.transpose(0, 3, 1, 2).reshape(8 * B, KP * B)
     pt = jnp.concatenate([pt, index_slab(p_index[:, 0])], axis=0)
     by_z = [pt] + [along_row(pt, d, 0) for d in (1, 2, 3)]
     partner = along_row(pt, 0, 1)
 
-    pn = own.reshape(8, KP, 32, 2, B).transpose(0, 3, 2, 1, 4).reshape(2, 4, B, KP * B)
+    pn = own.reshape(8, KP, 32, 2, B).transpose(0, 3, 2, 1, 4).reshape(2, 4 * B, KP * B)
     halves = jnp.stack(
         [
             jnp.concatenate([pn[h], index_slab(p_index[4 * h:4 * h + 4, 0])], axis=0)
@@ -566,7 +575,7 @@
     ids = place[:, :, None, None] * KP + jnp.arange(KP, dtype=jnp.int32)
     idx = jnp.min(jnp.where(equal, ids, NK * KP), axis=3).reshape(-1)
 
-    cols_p = jnp.stack([p[:, 4, :4, :KP] for p in ps]).reshape(NCOL, 16)
+    cols_p = jnp.stack([p[:, 4 * B:4 * B + 4, :KP] for p in ps]).reshape(NCOL, 16)
     cc = jnp.arange(NCOL, dtype=jnp.int32)
     where = ((y - cc // 4) % 4) * 4 + (x - cc % 4) % 4
     cols_i = pick_rows(cols_p, where).reshape(NCOL, 4, KP)

time: 225 us -> 227 us (level)
  Pallas kernels: 57.4 us -> 66.7 us
  local copies, waits for them, and re-layouts: 23 us -> 15.9 us
    unnamed x54 -> x48, local copies, waits for them, and re-layouts: 14.7 us -> 7.08 us
    pallas_call x1, Pallas kernels: 4.1 us -> 8.3 us  [spread(): pl.pallas_call(spread_kernel, grid=(8,), in_specs=[pl.BlockSpec((16, KA,...]
  transfers between devices with their start and end apart: 34 -> 34, of which waited for: 15 -> 15; matrix products, arithmetic and copies ran while one was open for 4% -> 5% of each run, Pallas kernels for 19% -> 23%
where the time goes in v3:
time: 227 us; the launch traced here: 226 us
  waiting for transfers between devices  82.6 us (36%)
  Pallas kernels  66.7 us (29%)
  starting transfers between devices  54.2 us (24%)
  local copies, waits for them, and re-layouts  15.9 us (7%)
  other arithmetic  4.4 us (2%)
    ppermute x21, waiting for transfers between devices, along_col(): return lax.ppermute(v, 'col', pairs)  55 us
    ppermute x21, starting transfers between devices, along_col(): return lax.ppermute(v, 'col', pairs)  31.2 us
    ppermute x11, waiting for transfers between devices, along_row(): return lax.ppermute(v, 'row', pairs)  16.4 us
    pallas_call x2, Pallas kernels, y_products(): pl.pallas_call(lambda *refs: y_product_kernel(part, *refs), grid_spec=plt...  13.7 us
    pallas_call x1, Pallas kernels, coarse_terms(): pl.pallas_call(coarse_kernel, grid_spec=pltpu.PrefetchScalarGridSpec(num_...  12.6 us
    pallas_call x2, Pallas kernels, x_products(): pl.pallas_call(lambda *refs: x_product_kernel(j, *refs), grid_spec=pltpu....  12.3 us
    ppermute x11, starting transfers between devices, along_row(): return lax.ppermute(v, 'row', pairs)  12.1 us
    pallas_call x2, Pallas kernels, middle(): pl.pallas_call(kernel, in_specs=[pl.BlockSpec(memory_space=pltpu.SMEM)] +...  10.5 us
  transfers between devices with their start and end apart: 34, of which 15 were waited for; matrix products, arithmetic and copies ran while one was open for 5% of the time, Pallas kernels for 23%

profile of v3, /device:TPU:0, one launch (start us, length us, event | category | flops | bytes accessed | tf_op | source)
XLA Modules:
  0.0 225.5 jit_solution(6841195333156557098)
XLA Ops:
  0.6 1.4 reshape_squeeze.3
  2.9 2.1 collective-permute-start
  5.0 3.6 %collective-permute-start.1 = (bf16[528,256]{1,0:T(8,128)(2,1)S(1)}, bf16[528,256]{1,0:T(8,128)(2,1)S(1)}, u32[]{:S(2)}, u32[]{:S(2)}) collective-permute-start(bf16[528,256]{1,0:T(8,128)(2,1)S(1)} %fusion.3.refs_0_), channel_id=1, source_target_pairs={{0,64},{16,80},{32,96},{48,112},{64,0},{80,16},{96,32},{112,48},{1... | collective-permute-start | bytes 811016 | tf_op jit(solution)/shard_map/ppermute | solution.py:23
  8.6 1.0 collective-permute-start.2
  11.6 2.0 collective-permute-done.refs_2_
  13.6 7.0 %collective-permute-done.1.refs_4_ = bf16[528,256]{1,0:T(8,128)(2,1)S(1)} collective-permute-done((bf16[528,256]{1,0:T(8,128)(2,1)S(1)}, bf16[528,256]{1,0:T(8,128)(2,1)S(1)}, u32[]{:S(2)}, u32[]{:S(2)}) %collective-permute-start.1) | collective-permute-done | bytes 270368 | tf_op jit(solution)/shard_map/ppermute | solution.py:23
  20.6 2.8 %collective-permute-start.5 = (bf16[272,256]{1,0:T(8,128)(2,1)S(1)}, bf16[272,256]{1,0:T(8,128)(2,1)S(1)}, u32[]{:S(2)}, u32[]{:S(2)}) collective-permute-start(bf16[272,256]{1,0:T(8,128)(2,1)S(1)} %get-tuple-element.78), channel_id=1, source_target_pairs={{0,3},{1,0},{2,1},{3,2},{4,7},{5,4},{6,5},{7,6},{8,11},{9,8},{10,9... | collective-permute-start | bytes 417800 | tf_op jit(solution)/shard_map/ppermute | solution.py:28
  23.4 2.3 %collective-permute-start.4 = (bf16[272,256]{1,0:T(8,128)(2,1)S(1)}, bf16[272,256]{1,0:T(8,128)(2,1)S(1)}, u32[]{:S(2)}, u32[]{:S(2)}) collective-permute-start(bf16[272,256]{1,0:T(8,128)(2,1)S(1)} %bitcast.93), channel_id=1, source_target_pairs={{0,2},{1,3},{2,0},{3,1},{4,6},{5,7},{6,4},{7,5},{8,10},{9,11},{10,... | collective-permute-start | bytes 417800 | tf_op jit(solution)/shard_map/ppermute | solution.py:28
  25.9 5.0 %collective-permute-done.4 = bf16[272,256]{1,0:T(8,128)(2,1)S(1)} collective-permute-done((bf16[272,256]{1,0:T(8,128)(2,1)S(1)}, bf16[272,256]{1,0:T(8,128)(2,1)S(1)}, u32[]{:S(2)}, u32[]{:S(2)}) %collective-permute-start.4) | collective-permute-done | bytes 139296 | tf_op jit(solution)/shard_map/ppermute | solution.py:28
  31.4 8.3 %spread.1 = bf16[128,64,256]{2,1,0:T(8,128)(2,1)} custom-call(bf16[128,4,4096]{2,1,0:T(4,128)(2,1)} %bitcast.90), custom_call_target="tpu_custom_call" | custom-call | tf_op jit(solution)/shard_map/spread/pallas_call | solution.py:59
  40.4 0.9 pad_maximum_fusion.refs_8_
  41.2 3.0 %collective-permute-start.8 = (bf16[4,272,256]{2,1,0:T(8,128)(2,1)}, bf16[4,272,256]{2,1,0:T(8,128)(2,1)S(1)}, u32[]{:S(2)}, u32[]{:S(2)}) collective-permute-start(bf16[4,272,256]{2,1,0:T(8,128)(2,1)} %pad_maximum_fusion.refs_8_), channel_id=1, source_target_pairs={{0,12},{1,13},{2,14},{3,15},{4,0},{5,1},{6,2},{7,3},{8,4},{9,5},{1... | collective-permute-start | bytes 1671176 | tf_op jit(solution)/shard_map/ppermute | solution.py:28
  44.3 0.6 collective-permute-start.7
  45.0 1.0 collective-permute-start.6
  46.0 4.9 %table.1 = (bf16[257,64,128]{2,1,0:T(8,128)(2,1)}, f32[64,128]{1,0:T(8,128)S(1)}) custom-call(bf16[528,256]{1,0:T(8,128)(2,1)S(1)} %fusion.3.refs_0_, bf16[528,256]{1,0:T(8,128)(2,1)S(1)} %collective-permute-done.9.refs_1_, bf16[528,256]{1,0:T(8,128)(2,1)S(1)} %collective-permute-done.refs_2_, bf16[528,256]{1,0:T(8,128)(2,1)S(1)} %collective-permute-done.10.refs_3_, ...), custom_call_target="tpu_custom_call" | custom-call | tf_op jit(solution)/shard_map/table/pallas_call | solution.py:92
  51.5 2.2 copy-done
  53.7 6.3 %shard_map.81 = (s16[129,16,128]{2,1,0:T(8,128)(2,1)S(1)}, s16[129,16,128]{2,1,0:T(8,128)(2,1)S(1)}, s16[129,16,128]{2,1,0:T(8,128)(2,1)S(1)}, s16[129,16,128]{2,1,0:T(8,128)(2,1)S(1)}) custom-call(s32[4096]{0:T(1024)S(1)} %reshape.300.refs_0_, s32[4]{0:T(128)S(1)} %pad_add_fusion.refs_1_.at_ref, bf16[4,2,16,64,256]{4,3,2,1,0:T(8,128)(2,1)} %bitcast.86, ...), custom_call_target="tpu_custom_call" | custom-call | tf_op jit(solution)/shard_map/pallas_call | solution.py:269
  60.0 0.8 copy-done.2
  60.9 1.9 collective-permute-start.22
  62.7 1.8 collective-permute-start.23
  64.6 7.4 %shard_map.80 = (s16[129,16,128]{2,1,0:T(8,128)(2,1)S(1)}, s16[129,16,128]{2,1,0:T(8,128)(2,1)S(1)}, s16[129,16,128]{2,1,0:T(8,128)(2,1)}, s16[129,16,128]{2,1,0:T(8,128)(2,1)}) custom-call(s32[4096]{0:T(1024)S(1)} %reshape.300.refs_0_, s32[4]{0:T(128)S(1)} %pad_add_fusion.refs_1_.at_ref, bf16[4,2,16,64,256]{4,3,2,1,0:T(8,128)(2,1)} %bitcast.87, ...), custom_call_target="tpu_custom_call" | custom-call | tf_op jit(solution)/shard_map/pallas_call | solution.py:269
  72.0 0.8 copy-done.3
  72.8 7.1 %collective-permute-done.8.refs_11_ = bf16[4,272,256]{2,1,0:T(8,128)(2,1)S(1)} collective-permute-done((bf16[4,272,256]{2,1,0:T(8,128)(2,1)}, bf16[4,272,256]{2,1,0:T(8,128)(2,1)S(1)}, u32[]{:S(2)}, u32[]{:S(2)}) %collective-permute-start.8) | collective-permute-done | bytes 557088 | tf_op jit(solution)/shard_map/ppermute | solution.py:28
  79.9 3.6 %collective-permute-start.24 = (s16[129,16,128]{2,1,0:T(8,128)(2,1)S(1)}, s16[129,16,128]{2,1,0:T(8,128)(2,1)S(1)}, u32[]{:S(2)}, u32[]{:S(2)}) collective-permute-start(s16[129,16,128]{2,1,0:T(8,128)(2,1)S(1)} %get-tuple-element.54), channel_id=1, source_target_pairs={{0,12},{1,13},{2,14},{3,15},{4,0},{5,1},{6,2},{7,3},{8,4},{9,5},{1... | collective-permute-start | bytes 1585160 | tf_op jit(solution)/shard_map/ppermute | solution.py:28
  83.5 0.8 copy-done.9
  84.3 0.7 slice_bitcast_fusion.3
  85.0 6.2 %shard_map.78 = (s16[257,16,128]{2,1,0:T(8,128)(2,1)S(1)}, s16[257,16,128]{2,1,0:T(8,128)(2,1)S(1)}) custom-call(s32[4096]{0:T(1024)S(1)} %reshape.300.refs_0_, s32[4]{0:T(128)S(1)} %pad_add_fusion.refs_1_.at_ref, bf16[4,2,16,64,256]{4,3,2,1,0:T(8,128)(2,1)} %bitcast.88, bf16[257,64,128]{2,1,0:T(8,128)(2,1)S(1)} %copy-done), custom_call_target="tpu_custom_call" | custom-call | tf_op jit(solution)/shard_map/pallas_call | solution.py:205
  91.2 6.2 %shard_map.77 = (s16[257,16,128]{2,1,0:T(8,128)(2,1)S(1)}, s16[257,16,128]{2,1,0:T(8,128)(2,1)S(1)}) custom-call(s32[4096]{0:T(1024)S(1)} %reshape.300.refs_0_, s32[4]{0:T(128)S(1)} %pad_add_fusion.refs_1_.at_ref, bf16[4,2,16,64,256]{4,3,2,1,0:T(8,128)(2,1)} %bitcast.89, bf16[257,64,128]{2,1,0:T(8,128)(2,1)S(1)} %copy-done), custom_call_target="tpu_custom_call" | custom-call | tf_op jit(solution)/shard_map/pallas_call | solution.py:205
  97.4 1.0 copy-done.1
  98.3 0.7 slice_bitcast_fusion
  99.2 3.1 %collective-permute-start.15 = (s16[257,16,128]{2,1,0:T(8,128)(2,1)S(1)}, s16[257,16,128]{2,1,0:T(8,128)(2,1)}, u32[]{:S(2)}, u32[]{:S(2)}) collective-permute-start(s16[257,16,128]{2,1,0:T(8,128)(2,1)S(1)} %get-tuple-element.42), channel_id=1, source_target_pairs={{0,3},{1,0},{2,1},{3,2},{4,7},{5,4},{6,5},{7,6},{8,11},{9,8},{10,9... | collective-permute-start | bytes 3158024 | tf_op jit(solution)/shard_map/ppermute | solution.py:28
  102.9 0.7 slice_bitcast_fusion.1
  103.6 0.8 collective-permute-start.20
  104.3 1.9 collective-permute-done.19.refs_1_
  106.2 0.7 collective-permute-start.21
  106.9 0.7 slice_bitcast_fusion.2
  108.0 9.7 %collective-permute-done.20.refs_2_ = s16[129,16,128]{2,1,0:T(8,128)(2,1)} collective-permute-done((s16[129,16,128]{2,1,0:T(8,128)(2,1)}, s16[129,16,128]{2,1,0:T(8,128)(2,1)}, u32[]{:S(2)}, u32[]{:S(2)}) %collective-permute-start.20) | collective-permute-done | bytes 528416 | tf_op jit(solution)/shard_map/ppermute | solution.py:28
  117.7 10.8 %collective-permute-done.21.refs_3_ = s16[129,16,128]{2,1,0:T(8,128)(2,1)} collective-permute-done((s16[129,16,128]{2,1,0:T(8,128)(2,1)}, s16[129,16,128]{2,1,0:T(8,128)(2,1)}, u32[]{:S(2)}, u32[]{:S(2)}) %collective-permute-start.21) | collective-permute-done | bytes 528416 | tf_op jit(solution)/shard_map/ppermute | solution.py:28
  128.5 5.3 %shard_map.82 = (s16[65,16,128]{2,1,0:T(8,128)(2,1)}, s16[65,16,128]{2,1,0:T(8,128)(2,1)}, s16[65,16,128]{2,1,0:T(8,128)(2,1)}, s16[65,16,128]{2,1,0:T(8,128)(2,1)}) custom-call(s32[4]{0:T(128)} %copy-done.4, s16[129,16,128]{2,1,0:T(8,128)(2,1)} %copy-done.3, s16[129,16,128]{2,1,0:T(8,128)(2,1)} %copy-done.13, ...), custom_call_target="tpu_custom_call" | custom-call | tf_op jit(solution)/shard_map/pallas_call | solution.py:358
  133.7 1.0 collective-permute-start.25
  135.1 1.7 collective-permute-start.26
  136.8 2.6 %collective-permute-start.27 = (s16[65,16,128]{2,1,0:T(8,128)(2,1)}, s16[65,16,128]{2,1,0:T(8,128)(2,1)S(1)}, u32[]{:S(2)}, u32[]{:S(2)}) collective-permute-start(s16[65,16,128]{2,1,0:T(8,128)(2,1)} %get-tuple-element.58), channel_id=1, source_target_pairs={{0,3},{1,0},{2,1},{3,2},{4,7},{5,4},{6,5},{7,6},{8,11},{9,8},{10,9... | collective-permute-start | bytes 798728 | tf_op jit(solution)/shard_map/ppermute | solution.py:28
  139.4 13.6 %collective-permute-done.15.m3 = s16[257,16,128]{2,1,0:T(8,128)(2,1)} collective-permute-done((s16[257,16,128]{2,1,0:T(8,128)(2,1)S(1)}, s16[257,16,128]{2,1,0:T(8,128)(2,1)}, u32[]{:S(2)}, u32[]{:S(2)}) %collective-permute-start.15) | collective-permute-done | bytes 1052704 | tf_op jit(solution)/shard_map/ppermute | solution.py:28
  153.0 5.2 %shard_map.79 = (s16[65,16,128]{2,1,0:T(8,128)(2,1)}, s16[65,16,128]{2,1,0:T(8,128)(2,1)}, s16[65,16,128]{2,1,0:T(8,128)(2,1)}, s16[65,16,128]{2,1,0:T(8,128)(2,1)}) custom-call(s32[4]{0:T(128)} %copy-done.4, s16[257,16,128]{2,1,0:T(8,128)(2,1)} %copy-done.1, s16[257,16,128]{2,1,0:T(8,128)(2,1)} %collective-permute-done.13.m1, ...), custom_call_target="tpu_custom_call" | custom-call | tf_op jit(solution)/shard_map/pallas_call | solution.py:358
  158.2 3.5 %collective-permute-start.17 = (s16[65,16,128]{2,1,0:T(8,128)(2,1)}, s16[65,16,128]{2,1,0:T(8,128)(2,1)S(1)}, u32[]{:S(2)}, u32[]{:S(2)}) collective-permute-start(s16[65,16,128]{2,1,0:T(8,128)(2,1)} %get-tuple-element.45), channel_id=1, source_target_pairs={{0,8},{1,9},{2,10},{3,11},{4,12},{5,13},{6,14},{7,15},{8,0},{9,1},... | collective-permute-start | bytes 798728 | tf_op jit(solution)/shard_map/ppermute | solution.py:28
  162.1 0.8 reshape.299.tgt_ref
  162.9 3.2 %collective-permute-done.16.refs_1_ = s16[65,16,128]{2,1,0:T(8,128)(2,1)S(1)} collective-permute-done((s16[65,16,128]{2,1,0:T(8,128)(2,1)}, s16[65,16,128]{2,1,0:T(8,128)(2,1)S(1)}, u32[]{:S(2)}, u32[]{:S(2)}) %collective-permute-start.16) | collective-permute-done | bytes 266272 | tf_op jit(solution)/shard_map/ppermute | solution.py:28
  166.0 3.1 %collective-permute-done.17.refs_2_ = s16[65,16,128]{2,1,0:T(8,128)(2,1)S(1)} collective-permute-done((s16[65,16,128]{2,1,0:T(8,128)(2,1)}, s16[65,16,128]{2,1,0:T(8,128)(2,1)S(1)}, u32[]{:S(2)}, u32[]{:S(2)}) %collective-permute-start.17) | collective-permute-done | bytes 266272 | tf_op jit(solution)/shard_map/ppermute | solution.py:28
  169.1 0.7 collective-permute-done.18.refs_3_
  169.8 0.6 copy-done.18
  170.5 12.6 %coarse_terms.1 = (bf16[16,2,64,128]{3,2,1,0:T(8,128)(2,1)}, f32[4,16,4,8,128]{4,3,2,1,0:T(8,128)}, f32[4,16,4,8,128]{4,3,2,1,0:T(8,128)}) custom-call(s32[2048]{0:T(1024)} %reshape.299.tgt_ref, s32[4]{0:T(128)} %copy-done.4, s16[65,16,128]{2,1,0:T(8,128)(2,1)} %get-tuple-element.43.refs_0_, s16[65,16,128]{2,1,0:T(8,128)(2,1)} %copy-done.16, ...), custom_call_target="tpu_custom_call" | custom-call | tf_op jit(solution)/shard_map/coarse_terms/pallas_call | solution.py:446
  183.1 2.9 %collective-permute-done.28 = f32[4,16,4,8,128]{4,3,2,1,0:T(8,128)S(1)} collective-permute-done((f32[4,16,4,8,128]{4,3,2,1,0:T(8,128)}, f32[4,16,4,8,128]{4,3,2,1,0:T(8,128)S(1)}, u32[]{:S(2)}, u32[]{:S(2)}) %collective-permute-start.28) | collective-permute-done | bytes 1048608 | tf_op jit(solution)/shard_map/ppermute | solution.py:23
  186.0 1.2 fusion.6
  187.2 2.0 collective-permute-start.29
  189.2 2.8 %collective-permute-start.30 = (f32[16,4,8,128]{3,2,1,0:T(8,128)S(1)}, f32[16,4,8,128]{3,2,1,0:T(8,128)S(1)}, u32[]{:S(2)}, u32[]{:S(2)}) collective-permute-start(f32[16,4,8,128]{3,2,1,0:T(8,128)S(1)} %get-tuple-element.74), channel_id=1, source_target_pairs={{0,64},{16,80},{32,96},{48,112},{64,0},{80,16},{96,32},{112,48},{1... | collective-permute-start | bytes 786440 | tf_op jit(solution)/shard_map/ppermute | solution.py:23
  192.1 7.4 %all-to-all-start = ((bf16[16,2,64,128]{3,2,1,0:T(8,128)(2,1)}), bf16[16,2,64,128]{3,2,1,0:T(8,128)(2,1)S(1)}, u32[]{:S(2)}, u32[]{:S(2)}) async-start(bf16[16,2,64,128]{3,2,1,0:T(8,128)(2,1)} %get-tuple-element.59), calls=%async_computation | async-start | bytes 1048576 | tf_op jit(solution)/shard_map/all_to_all | solution.py:610
  199.5 4.5 %collective-permute-done.30 = f32[16,4,8,128]{3,2,1,0:T(8,128)S(1)} collective-permute-done((f32[16,4,8,128]{3,2,1,0:T(8,128)S(1)}, f32[16,4,8,128]{3,2,1,0:T(8,128)S(1)}, u32[]{:S(2)}, u32[]{:S(2)}) %collective-permute-start.30) | collective-permute-done | bytes 262176 | tf_op jit(solution)/shard_map/ppermute | solution.py:23
  204.0 1.8 fusion.10
  205.8 5.0 %all-to-all-done.x_ref = bf16[16,2,64,128]{3,2,1,0:T(8,128)(2,1)S(1)} async-done(((bf16[16,2,64,128]{3,2,1,0:T(8,128)(2,1)}), bf16[16,2,64,128]{3,2,1,0:T(8,128)(2,1)S(1)}, u32[]{:S(2)}, u32[]{:S(2)}) %all-to-all-start) | async-done | bytes 524320 | tf_op jit(solution)/shard_map/all_to_all | solution.py:610
  210.7 3.5 %all-to-all-start.1 = ((f32[16,4,8,128]{3,2,1,0:T(8,128)}), f32[16,4,8,128]{3,2,1,0:T(8,128)S(1)}, u32[]{:S(2)}, u32[]{:S(2)}) async-start(f32[16,4,8,128]{3,2,1,0:T(8,128)} %fusion.10), calls=%async_computation.1 | async-start | bytes 524288 | tf_op jit(solution)/shard_map/all_to_all | solution.py:612
  214.3 2.4 %ap_layout.1 = bf16[8,8,4096]{2,1,0:T(8,128)(2,1)} custom-call(bf16[16,2,64,128]{3,2,1,0:T(8,128)(2,1)} %copy-done.5), custom_call_target="tpu_custom_call" | custom-call | tf_op jit(solution)/shard_map/ap_layout/pallas_call | solution.py:489
  216.7 6.2 %all-to-all-done.1.x_ref = f32[16,4,8,128]{3,2,1,0:T(8,128)S(1)} async-done(((f32[16,4,8,128]{3,2,1,0:T(8,128)}), f32[16,4,8,128]{3,2,1,0:T(8,128)S(1)}, u32[]{:S(2)}, u32[]{:S(2)}) %all-to-all-start.1) | async-done | bytes 262176 | tf_op jit(solution)/shard_map/all_to_all | solution.py:612
  222.9 0.7 copy-done.7
  223.6 1.9 coarse_layout.1
  (109 shorter events, 6.6 us)
Async XLA Ops:
  2.1 0.7 copy-start.21
  2.1 7.5 %copy-start.6 = (bf16[8,1,4,4096]{3,2,1,0:T(4,128)(2,1)S(1)}, bf16[8,1,4,4096]{3,2,1,0:T(4,128)(2,1)}, u32[]{:S(2)}) copy-start(bf16[8,1,4,4096]{3,2,1,0:T(4,128)(2,1)} %param.8) | copy-start | bytes 786436
  2.9 10.7 %collective-permute-start = (bf16[528,256]{1,0:T(8,128)(2,1)S(1)}, bf16[528,256]{1,0:T(8,128)(2,1)S(1)}, u32[]{:S(2)}, u32[]{:S(2)}) collective-permute-start(bf16[528,256]{1,0:T(8,128)(2,1)S(1)} %fusion.3.refs_0_), channel_id=1, source_target_pairs={{0,32},{16,48},{32,64},{48,80},{64,96},{80,112},{96,0},{112,16},{1... | collective-permute-start | bytes 811016 | tf_op jit(solution)/shard_map/ppermute | solution.py:23
  5.0 15.6 %collective-permute-start.1 = (bf16[528,256]{1,0:T(8,128)(2,1)S(1)}, bf16[528,256]{1,0:T(8,128)(2,1)S(1)}, u32[]{:S(2)}, u32[]{:S(2)}) collective-permute-start(bf16[528,256]{1,0:T(8,128)(2,1)S(1)} %fusion.3.refs_0_), channel_id=1, source_target_pairs={{0,64},{16,80},{32,96},{48,112},{64,0},{80,16},{96,32},{112,48},{1... | collective-permute-start | bytes 811016 | tf_op jit(solution)/shard_map/ppermute | solution.py:23
  8.6 12.0 %collective-permute-start.2 = (bf16[528,256]{1,0:T(8,128)(2,1)S(1)}, bf16[528,256]{1,0:T(8,128)(2,1)S(1)}, u32[]{:S(2)}, u32[]{:S(2)}) collective-permute-start(bf16[528,256]{1,0:T(8,128)(2,1)S(1)} %fusion.3.refs_0_), channel_id=1, source_target_pairs={{0,96},{16,112},{32,0},{48,16},{64,32},{80,48},{96,64},{112,80},{1... | collective-permute-start | bytes 811016 | tf_op jit(solution)/shard_map/ppermute | solution.py:23
  9.6 34.7 %collective-permute-start.9 = (bf16[528,256]{1,0:T(8,128)(2,1)S(1)}, bf16[528,256]{1,0:T(8,128)(2,1)S(1)}, u32[]{:S(2)}, u32[]{:S(2)}) collective-permute-start(bf16[528,256]{1,0:T(8,128)(2,1)S(1)} %fusion.3.refs_0_), channel_id=1, source_target_pairs={{0,16},{16,0},{32,48},{48,32},{64,80},{80,64},{96,112},{112,96},{1... | collective-permute-start | bytes 811016 | tf_op jit(solution)/shard_map/ppermute | solution.py:23
  10.6 0.9 copy-start.22
  10.9 14.8 %copy-start.20 = (s32[128,8]{0,1:T(8,128)S(1)}, s32[128,8]{0,1:T(8,128)}, u32[]{:S(2)}) copy-start(s32[128,8]{0,1:T(8,128)} %param.10) | copy-start | bytes 12292
  20.6 10.4 %collective-permute-start.5 = (bf16[272,256]{1,0:T(8,128)(2,1)S(1)}, bf16[272,256]{1,0:T(8,128)(2,1)S(1)}, u32[]{:S(2)}, u32[]{:S(2)}) collective-permute-start(bf16[272,256]{1,0:T(8,128)(2,1)S(1)} %get-tuple-element.78), channel_id=1, source_target_pairs={{0,3},{1,0},{2,1},{3,2},{4,7},{5,4},{6,5},{7,6},{8,11},{9,8},{10,9... | collective-permute-start | bytes 417800 | tf_op jit(solution)/shard_map/ppermute | solution.py:28
  23.4 17.0 %collective-permute-start.3 = (bf16[272,256]{1,0:T(8,128)(2,1)S(1)}, bf16[272,256]{1,0:T(8,128)(2,1)S(1)}, u32[]{:S(2)}, u32[]{:S(2)}) collective-permute-start(bf16[272,256]{1,0:T(8,128)(2,1)S(1)} %get-tuple-element.78), channel_id=1, source_target_pairs={{0,1},{1,2},{2,3},{3,0},{4,5},{5,6},{6,7},{7,4},{8,9},{9,10},{10,1... | collective-permute-start | bytes 417800 | tf_op jit(solution)/shard_map/ppermute | solution.py:28
  23.4 7.5 %collective-permute-start.4 = (bf16[272,256]{1,0:T(8,128)(2,1)S(1)}, bf16[272,256]{1,0:T(8,128)(2,1)S(1)}, u32[]{:S(2)}, u32[]{:S(2)}) collective-permute-start(bf16[272,256]{1,0:T(8,128)(2,1)S(1)} %bitcast.93), channel_id=1, source_target_pairs={{0,2},{1,3},{2,0},{3,1},{4,6},{5,7},{6,4},{7,5},{8,10},{9,11},{10,... | collective-permute-start | bytes 417800 | tf_op jit(solution)/shard_map/ppermute | solution.py:28
  25.8 19.2 %collective-permute-start.10 = (bf16[528,256]{1,0:T(8,128)(2,1)S(1)}, bf16[528,256]{1,0:T(8,128)(2,1)S(1)}, u32[]{:S(2)}, u32[]{:S(2)}) collective-permute-start(bf16[528,256]{1,0:T(8,128)(2,1)S(1)} %collective-permute-done.refs_2_), channel_id=1, source_target_pairs={{0,16},{16,0},{32,48},{48,32},{64,80},{80,64},{96,112},{112,96},{1... | collective-permute-start | bytes 811016 | tf_op jit(solution)/shard_map/ppermute | solution.py:23
  30.9 15.1 %collective-permute-start.11 = (bf16[528,256]{1,0:T(8,128)(2,1)S(1)}, bf16[528,256]{1,0:T(8,128)(2,1)S(1)}, u32[]{:S(2)}, u32[]{:S(2)}) collective-permute-start(bf16[528,256]{1,0:T(8,128)(2,1)S(1)} %collective-permute-done.1.refs_4_), channel_id=1, source_target_pairs={{0,16},{16,0},{32,48},{48,32},{64,80},{80,64},{96,112},{112,96},{1... | collective-permute-start | bytes 811016 | tf_op jit(solution)/shard_map/ppermute | solution.py:23
  30.9 15.1 %collective-permute-start.12 = (bf16[528,256]{1,0:T(8,128)(2,1)S(1)}, bf16[528,256]{1,0:T(8,128)(2,1)S(1)}, u32[]{:S(2)}, u32[]{:S(2)}) collective-permute-start(bf16[528,256]{1,0:T(8,128)(2,1)S(1)} %collective-permute-done.2.refs_6_), channel_id=1, source_target_pairs={{0,16},{16,0},{32,48},{48,32},{64,80},{80,64},{96,112},{112,96},{1... | collective-permute-start | bytes 811016 | tf_op jit(solution)/shard_map/ppermute | solution.py:23
  41.2 38.7 %collective-permute-start.8 = (bf16[4,272,256]{2,1,0:T(8,128)(2,1)}, bf16[4,272,256]{2,1,0:T(8,128)(2,1)S(1)}, u32[]{:S(2)}, u32[]{:S(2)}) collective-permute-start(bf16[4,272,256]{2,1,0:T(8,128)(2,1)} %pad_maximum_fusion.refs_8_), channel_id=1, source_target_pairs={{0,12},{1,13},{2,14},{3,15},{4,0},{5,1},{6,2},{7,3},{8,4},{9,5},{1... | collective-permute-start | bytes 1671176 | tf_op jit(solution)/shard_map/ppermute | solution.py:28
  44.3 39.2 %collective-permute-start.7 = (bf16[4,272,256]{2,1,0:T(8,128)(2,1)}, bf16[4,272,256]{2,1,0:T(8,128)(2,1)S(1)}, u32[]{:S(2)}, u32[]{:S(2)}) collective-permute-start(bf16[4,272,256]{2,1,0:T(8,128)(2,1)} %pad_maximum_fusion.refs_8_), channel_id=1, source_target_pairs={{0,8},{1,9},{2,10},{3,11},{4,12},{5,13},{6,14},{7,15},{8,0},{9,1},... | collective-permute-start | bytes 1671176 | tf_op jit(solution)/shard_map/ppermute | solution.py:28
  45.0 46.2 %copy-start.4 = (s32[4]{0:T(128)}, s32[4]{0:T(128)S(1)}, u32[]{:S(2)}) copy-start(s32[4]{0:T(128)S(1)} %pad_add_fusion.refs_1_.at_ref) | copy-start | bytes 52
  45.0 54.1 %collective-permute-start.6 = (bf16[4,272,256]{2,1,0:T(8,128)(2,1)}, bf16[4,272,256]{2,1,0:T(8,128)(2,1)}, u32[]{:S(2)}, u32[]{:S(2)}) collective-permute-start(bf16[4,272,256]{2,1,0:T(8,128)(2,1)} %pad_maximum_fusion.refs_8_), channel_id=1, source_target_pairs={{0,4},{1,5},{2,6},{3,7},{4,8},{5,9},{6,10},{7,11},{8,12},{9,13},{1... | collective-permute-start | bytes 1671176 | tf_op jit(solution)/shard_map/ppermute | solution.py:28
  51.5 2.2 copy-start
  60.0 0.8 copy-start.2
  60.9 38.3 %collective-permute-start.22 = (s16[129,16,128]{2,1,0:T(8,128)(2,1)S(1)}, s16[129,16,128]{2,1,0:T(8,128)(2,1)S(1)}, u32[]{:S(2)}, u32[]{:S(2)}) collective-permute-start(s16[129,16,128]{2,1,0:T(8,128)(2,1)S(1)} %get-tuple-element.52), channel_id=1, source_target_pairs={{0,4},{1,5},{2,6},{3,7},{4,8},{5,9},{6,10},{7,11},{8,12},{9,13},{1... | collective-permute-start | bytes 1585160 | tf_op jit(solution)/shard_map/ppermute | solution.py:28
  62.7 39.5 %collective-permute-start.23 = (s16[129,16,128]{2,1,0:T(8,128)(2,1)S(1)}, s16[129,16,128]{2,1,0:T(8,128)(2,1)S(1)}, u32[]{:S(2)}, u32[]{:S(2)}) collective-permute-start(s16[129,16,128]{2,1,0:T(8,128)(2,1)S(1)} %get-tuple-element.53), channel_id=1, source_target_pairs={{0,8},{1,9},{2,10},{3,11},{4,12},{5,13},{6,14},{7,15},{8,0},{9,1},... | collective-permute-start | bytes 1585160 | tf_op jit(solution)/shard_map/ppermute | solution.py:28
  72.0 0.8 copy-start.3
  79.9 3.6 %copy-start.8 = (bf16[4,272,256]{2,1,0:T(8,128)(2,1)}, bf16[4,272,256]{2,1,0:T(8,128)(2,1)S(1)}, u32[]{:S(2)}) copy-start(bf16[4,272,256]{2,1,0:T(8,128)(2,1)S(1)} %collective-permute-done.8.refs_11_) | copy-start | bytes 1671172
  79.9 23.7 %collective-permute-start.24 = (s16[129,16,128]{2,1,0:T(8,128)(2,1)S(1)}, s16[129,16,128]{2,1,0:T(8,128)(2,1)S(1)}, u32[]{:S(2)}, u32[]{:S(2)}) collective-permute-start(s16[129,16,128]{2,1,0:T(8,128)(2,1)S(1)} %get-tuple-element.54), channel_id=1, source_target_pairs={{0,12},{1,13},{2,14},{3,15},{4,0},{5,1},{6,2},{7,3},{8,4},{9,5},{1... | collective-permute-start | bytes 1585160 | tf_op jit(solution)/shard_map/ppermute | solution.py:28
  83.5 0.8 copy-start.9
  83.5 22.7 %collective-permute-start.19 = (s16[129,16,128]{2,1,0:T(8,128)(2,1)S(1)}, s16[129,16,128]{2,1,0:T(8,128)(2,1)S(1)}, u32[]{:S(2)}, u32[]{:S(2)}) collective-permute-start(s16[129,16,128]{2,1,0:T(8,128)(2,1)S(1)} %get-tuple-element.48), channel_id=1, source_target_pairs={{0,4},{1,5},{2,6},{3,7},{4,8},{5,9},{6,10},{7,11},{8,12},{9,13},{1... | collective-permute-start | bytes 1585160 | tf_op jit(solution)/shard_map/ppermute | solution.py:28
  97.4 1.0 copy-start.1
  99.0 37.8 %collective-permute-start.13 = (s16[257,16,128]{2,1,0:T(8,128)(2,1)S(1)}, s16[257,16,128]{2,1,0:T(8,128)(2,1)}, u32[]{:S(2)}, u32[]{:S(2)}) collective-permute-start(s16[257,16,128]{2,1,0:T(8,128)(2,1)S(1)} %get-tuple-element.40), channel_id=1, source_target_pairs={{0,1},{1,2},{2,3},{3,0},{4,5},{5,6},{6,7},{7,4},{8,9},{9,10},{10,1... | collective-permute-start | bytes 3158024 | tf_op jit(solution)/shard_map/ppermute | solution.py:28
  99.2 7.0 %copy-start.10 = (s16[129,16,128]{2,1,0:T(8,128)(2,1)}, s16[129,16,128]{2,1,0:T(8,128)(2,1)S(1)}, u32[]{:S(2)}) copy-start(s16[129,16,128]{2,1,0:T(8,128)(2,1)S(1)} %collective-permute-done.22.refs_5_) | copy-start | bytes 1585156
  99.2 53.8 %collective-permute-start.15 = (s16[257,16,128]{2,1,0:T(8,128)(2,1)S(1)}, s16[257,16,128]{2,1,0:T(8,128)(2,1)}, u32[]{:S(2)}, u32[]{:S(2)}) collective-permute-start(s16[257,16,128]{2,1,0:T(8,128)(2,1)S(1)} %get-tuple-element.42), channel_id=1, source_target_pairs={{0,3},{1,0},{2,1},{3,2},{4,7},{5,4},{6,5},{7,6},{8,11},{9,8},{10,9... | collective-permute-start | bytes 3158024 | tf_op jit(solution)/shard_map/ppermute | solution.py:28
  102.3 3.9 %copy-start.11 = (s16[129,16,128]{2,1,0:T(8,128)(2,1)}, s16[129,16,128]{2,1,0:T(8,128)(2,1)S(1)}, u32[]{:S(2)}) copy-start(s16[129,16,128]{2,1,0:T(8,128)(2,1)S(1)} %collective-permute-done.23.refs_6_) | copy-start | bytes 1585156
  102.3 50.7 %collective-permute-start.14 = (s16[257,16,128]{2,1,0:T(8,128)(2,1)S(1)}, s16[257,16,128]{2,1,0:T(8,128)(2,1)}, u32[]{:S(2)}, u32[]{:S(2)}) collective-permute-start(s16[257,16,128]{2,1,0:T(8,128)(2,1)S(1)} %get-tuple-element.41), channel_id=1, source_target_pairs={{0,2},{1,3},{2,0},{3,1},{4,6},{5,7},{6,4},{7,5},{8,10},{9,11},{10,... | collective-permute-start | bytes 3158024 | tf_op jit(solution)/shard_map/ppermute | solution.py:28
  103.6 3.4 %copy-start.12 = (s16[129,16,128]{2,1,0:T(8,128)(2,1)}, s16[129,16,128]{2,1,0:T(8,128)(2,1)S(1)}, u32[]{:S(2)}) copy-start(s16[129,16,128]{2,1,0:T(8,128)(2,1)S(1)} %collective-permute-done.24.refs_7_) | copy-start | bytes 1585156
  103.6 14.1 %collective-permute-start.20 = (s16[129,16,128]{2,1,0:T(8,128)(2,1)}, s16[129,16,128]{2,1,0:T(8,128)(2,1)}, u32[]{:S(2)}, u32[]{:S(2)}) collective-permute-start(s16[129,16,128]{2,1,0:T(8,128)(2,1)} %get-tuple-element.49), channel_id=1, source_target_pairs={{0,8},{1,9},{2,10},{3,11},{4,12},{5,13},{6,14},{7,15},{8,0},{9,1},... | collective-permute-start | bytes 1585160 | tf_op jit(solution)/shard_map/ppermute | solution.py:28
  106.2 1.4 copy-start.13
  106.2 22.3 %collective-permute-start.21 = (s16[129,16,128]{2,1,0:T(8,128)(2,1)}, s16[129,16,128]{2,1,0:T(8,128)(2,1)}, u32[]{:S(2)}, u32[]{:S(2)}) collective-permute-start(s16[129,16,128]{2,1,0:T(8,128)(2,1)} %get-tuple-element.50), channel_id=1, source_target_pairs={{0,12},{1,13},{2,14},{3,15},{4,0},{5,1},{6,2},{7,3},{8,4},{9,5},{1... | collective-permute-start | bytes 1585160 | tf_op jit(solution)/shard_map/ppermute | solution.py:28
  128.5 6.3 %copy-start.23 = (s32[128,8]{0,1:T(8,128)S(1)}, s32[128,8]{0,1:T(8,128)}, u32[]{:S(2)}) copy-start(s32[128,8]{0,1:T(8,128)} %param.11) | copy-start | bytes 12292
  133.7 27.9 %collective-permute-start.25 = (s16[65,16,128]{2,1,0:T(8,128)(2,1)}, s16[65,16,128]{2,1,0:T(8,128)(2,1)S(1)}, u32[]{:S(2)}, u32[]{:S(2)}) collective-permute-start(s16[65,16,128]{2,1,0:T(8,128)(2,1)} %get-tuple-element.56), channel_id=1, source_target_pairs={{0,1},{1,2},{2,3},{3,0},{4,5},{5,6},{6,7},{7,4},{8,9},{9,10},{10,1... | collective-permute-start | bytes 798728 | tf_op jit(solution)/shard_map/ppermute | solution.py:28
  135.1 27.7 %collective-permute-start.26 = (s16[65,16,128]{2,1,0:T(8,128)(2,1)}, s16[65,16,128]{2,1,0:T(8,128)(2,1)}, u32[]{:S(2)}, u32[]{:S(2)}) collective-permute-start(s16[65,16,128]{2,1,0:T(8,128)(2,1)} %get-tuple-element.57), channel_id=1, source_target_pairs={{0,2},{1,3},{2,0},{3,1},{4,6},{5,7},{6,4},{7,5},{8,10},{9,11},{10,... | collective-permute-start | bytes 798728 | tf_op jit(solution)/shard_map/ppermute | solution.py:28
  136.8 26.1 %collective-permute-start.27 = (s16[65,16,128]{2,1,0:T(8,128)(2,1)}, s16[65,16,128]{2,1,0:T(8,128)(2,1)S(1)}, u32[]{:S(2)}, u32[]{:S(2)}) collective-permute-start(s16[65,16,128]{2,1,0:T(8,128)(2,1)} %get-tuple-element.58), channel_id=1, source_target_pairs={{0,3},{1,0},{2,1},{3,2},{4,7},{5,4},{6,5},{7,6},{8,11},{9,8},{10,9... | collective-permute-start | bytes 798728 | tf_op jit(solution)/shard_map/ppermute | solution.py:28
  153.0 8.7 %copy-start.19 = (s32[1,4,16,8]{2,3,1,0:T(8,128)S(1)}, s32[1,4,16,8]{2,3,1,0:T(8,128)}, u32[]{:S(2)}) copy-start(s32[1,4,16,8]{2,3,1,0:T(8,128)} %copy.66) | copy-start | bytes 6148
  158.2 7.8 %collective-permute-start.16 = (s16[65,16,128]{2,1,0:T(8,128)(2,1)}, s16[65,16,128]{2,1,0:T(8,128)(2,1)S(1)}, u32[]{:S(2)}, u32[]{:S(2)}) collective-permute-start(s16[65,16,128]{2,1,0:T(8,128)(2,1)} %get-tuple-element.44), channel_id=1, source_target_pairs={{0,4},{1,5},{2,6},{3,7},{4,8},{5,9},{6,10},{7,11},{8,12},{9,13},{1... | collective-permute-start | bytes 798728 | tf_op jit(solution)/shard_map/ppermute | solution.py:28
  158.2 10.9 %collective-permute-start.17 = (s16[65,16,128]{2,1,0:T(8,128)(2,1)}, s16[65,16,128]{2,1,0:T(8,128)(2,1)S(1)}, u32[]{:S(2)}, u32[]{:S(2)}) collective-permute-start(s16[65,16,128]{2,1,0:T(8,128)(2,1)} %get-tuple-element.45), channel_id=1, source_target_pairs={{0,8},{1,9},{2,10},{3,11},{4,12},{5,13},{6,14},{7,15},{8,0},{9,1},... | collective-permute-start | bytes 798728 | tf_op jit(solution)/shard_map/ppermute | solution.py:28
  161.7 8.1 %copy-start.14 = (s16[65,16,128]{2,1,0:T(8,128)(2,1)}, s16[65,16,128]{2,1,0:T(8,128)(2,1)S(1)}, u32[]{:S(2)}) copy-start(s16[65,16,128]{2,1,0:T(8,128)(2,1)S(1)} %collective-permute-done.25.refs_5_) | copy-start | bytes 798724
  161.7 8.1 %collective-permute-start.18 = (s16[65,16,128]{2,1,0:T(8,128)(2,1)}, s16[65,16,128]{2,1,0:T(8,128)(2,1)S(1)}, u32[]{:S(2)}, u32[]{:S(2)}) collective-permute-start(s16[65,16,128]{2,1,0:T(8,128)(2,1)} %get-tuple-element.46), channel_id=1, source_target_pairs={{0,12},{1,13},{2,14},{3,15},{4,0},{5,1},{6,2},{7,3},{8,4},{9,5},{1... | collective-permute-start | bytes 798728 | tf_op jit(solution)/shard_map/ppermute | solution.py:28
  162.9 6.9 %copy-start.15 = (s16[65,16,128]{2,1,0:T(8,128)(2,1)}, s16[65,16,128]{2,1,0:T(8,128)(2,1)S(1)}, u32[]{:S(2)}) copy-start(s16[65,16,128]{2,1,0:T(8,128)(2,1)S(1)} %collective-permute-done.27.refs_7_) | copy-start | bytes 798724
  166.0 3.8 %copy-start.16 = (s16[65,16,128]{2,1,0:T(8,128)(2,1)}, s16[65,16,128]{2,1,0:T(8,128)(2,1)S(1)}, u32[]{:S(2)}) copy-start(s16[65,16,128]{2,1,0:T(8,128)(2,1)S(1)} %collective-permute-done.16.refs_1_) | copy-start | bytes 798724
  169.1 0.7 copy-start.17
  169.8 0.7 copy-start.18
  183.1 2.9 %collective-permute-start.28 = (f32[4,16,4,8,128]{4,3,2,1,0:T(8,128)}, f32[4,16,4,8,128]{4,3,2,1,0:T(8,128)S(1)}, u32[]{:S(2)}, u32[]{:S(2)}) collective-permute-start(f32[4,16,4,8,128]{4,3,2,1,0:T(8,128)} %get-tuple-element.61), channel_id=1, source_target_pairs={{0,16},{16,0},{32,48},{48,32},{64,80},{80,64},{96,112},{112,96},{1... | collective-permute-start | bytes 3145736 | tf_op jit(solution)/shard_map/ppermute | solution.py:23
  187.2 12.2 %collective-permute-start.29 = (f32[16,4,8,128]{3,2,1,0:T(8,128)S(1)}, f32[16,4,8,128]{3,2,1,0:T(8,128)S(1)}, u32[]{:S(2)}, u32[]{:S(2)}) collective-permute-start(f32[16,4,8,128]{3,2,1,0:T(8,128)S(1)} %get-tuple-element.72), channel_id=1, source_target_pairs={{0,32},{16,48},{32,64},{48,80},{64,96},{80,112},{96,0},{112,16},{1... | collective-permute-start | bytes 786440 | tf_op jit(solution)/shard_map/ppermute | solution.py:23
  189.2 14.8 %collective-permute-start.30 = (f32[16,4,8,128]{3,2,1,0:T(8,128)S(1)}, f32[16,4,8,128]{3,2,1,0:T(8,128)S(1)}, u32[]{:S(2)}, u32[]{:S(2)}) collective-permute-start(f32[16,4,8,128]{3,2,1,0:T(8,128)S(1)} %get-tuple-element.74), channel_id=1, source_target_pairs={{0,64},{16,80},{32,96},{48,112},{64,0},{80,16},{96,32},{112,48},{1... | collective-permute-start | bytes 786440 | tf_op jit(solution)/shard_map/ppermute | solution.py:23
  192.1 11.9 %collective-permute-start.31 = (f32[16,4,8,128]{3,2,1,0:T(8,128)S(1)}, f32[16,4,8,128]{3,2,1,0:T(8,128)S(1)}, u32[]{:S(2)}, u32[]{:S(2)}) collective-permute-start(f32[16,4,8,128]{3,2,1,0:T(8,128)S(1)} %get-tuple-element.73), channel_id=1, source_target_pairs={{0,96},{16,112},{32,0},{48,16},{64,32},{80,48},{96,64},{112,80},{1... | collective-permute-start | bytes 786440 | tf_op jit(solution)/shard_map/ppermute | solution.py:23
  192.1 18.7 %all-to-all-start = ((bf16[16,2,64,128]{3,2,1,0:T(8,128)(2,1)}), bf16[16,2,64,128]{3,2,1,0:T(8,128)(2,1)S(1)}, u32[]{:S(2)}, u32[]{:S(2)}) async-start(bf16[16,2,64,128]{3,2,1,0:T(8,128)(2,1)} %get-tuple-element.59), calls=%async_computation | async-start | bytes 1048576 | tf_op jit(solution)/shard_map/all_to_all | solution.py:610
  210.7 3.5 %copy-start.5 = (bf16[16,2,64,128]{3,2,1,0:T(8,128)(2,1)}, bf16[16,2,64,128]{3,2,1,0:T(8,128)(2,1)S(1)}, u32[]{:S(2)}) copy-start(bf16[16,2,64,128]{3,2,1,0:T(8,128)(2,1)S(1)} %all-to-all-done.x_ref) | copy-start | bytes 1572868
  210.7 12.2 %all-to-all-start.1 = ((f32[16,4,8,128]{3,2,1,0:T(8,128)}), f32[16,4,8,128]{3,2,1,0:T(8,128)S(1)}, u32[]{:S(2)}, u32[]{:S(2)}) async-start(f32[16,4,8,128]{3,2,1,0:T(8,128)} %fusion.10), calls=%async_computation.1 | async-start | bytes 524288 | tf_op jit(solution)/shard_map/all_to_all | solution.py:612
  222.9 0.7 copy-start.7

commit v4 on v3

--- a/solution.py
+++ b/solution.py
@@ -218,7 +218,10 @@
             scratch_shapes=[pltpu.VMEM((NCOL, 128), jnp.float32)]
             + [pltpu.VMEM((KAP * B, 128), jnp.float32)] * 2,
         ),
-        out_shape=[jax.ShapeDtypeStruct((257, 16, 128), jnp.int16)] * 2,
+        out_shape=[
+            (pltpu.HBM if j == 0 else jax.ShapeDtypeStruct)((257, 16, 128), jnp.int16),
+            jax.ShapeDtypeStruct((257, 16, 128), jnp.int16),
+        ],
         compiler_params=pltpu.CompilerParams(vmem_limit_bytes=20 * 1024 * 1024),
     )(
         idx,
@@ -281,7 +284,8 @@
             scratch_shapes=[pltpu.VMEM((NCOL, 128), jnp.float32)]
             + [pltpu.VMEM((KAP * B, 128), jnp.float32)] * 2,
         ),
-        out_shape=[jax.ShapeDtypeStruct((129, 16, 128), jnp.int16)] * 4,
+        out_shape=[pltpu.HBM((129, 16, 128), jnp.int16)]
+        + [jax.ShapeDtypeStruct((129, 16, 128), jnp.int16)] * 3,
         compiler_params=pltpu.CompilerParams(vmem_limit_bytes=20 * 1024 * 1024),
     )(
         idx,
@@ -379,7 +383,8 @@
                     parts[qh * 4 + d][c * 4 + sp].astype(jnp.float32) * scales[d] for d in range(4)
                 ]
                 total = (terms[0] + terms[1]) + (terms[2] + terms[3])
-                out_ref[c, qh, sp * 16:(sp + 1) * 16, :] = total.astype(jnp.bfloat16)
+                row = qh * B + sp * 16
+                out_ref[c, row:row + 16, :] = total.astype(jnp.bfloat16)
         return carry
 
     lax.fori_loop(0, NCOL, one, 0)
@@ -388,20 +393,20 @@
 def coarse_kernel(tgt_ref, at_ref, *refs):
     parts, (p0_ref, p1_ref, p2_ref, p3_ref) = refs[:8], refs[8:12]
     x_ref, keep_ref, send_ref, acc_ref, scale_ref = refs[12:]
-    dx = pl.program_id(0)
+    dy = pl.program_id(0)
     low = low_lanes(8)
     low_x = low_lanes(B)
     my_x, my_y, my_z, my_core = at_ref[0], at_ref[1], at_ref[2], at_ref[3]
 
-    @pl.when(dx == 0)
+    @pl.when(dy == 0)
     def _():
         acc_ref[...] = jnp.zeros_like(acc_ref)
         decode(parts, x_ref, scale_ref)
 
-    for dy, p_ref in enumerate((p0_ref, p1_ref, p2_ref, p3_ref)):
+    for dx, p_ref in enumerate((p0_ref, p1_ref, p2_ref, p3_ref)):
         c = lax.rem(my_y - dy + 4, 4) * 4 + lax.rem(my_x - dx + 4, 4)
         for qh in range(2):
-            x = x_ref[c, qh]
+            x = x_ref[c, qh * B:(qh + 1) * B, :]
             none = jnp.zeros_like(x)
             lhs = jnp.concatenate([jnp.where(low_x, x, none), jnp.where(low_x, none, x)], axis=0)
             rhs = p_ref[0, qh * 2 * B:(qh + 1) * 2 * B, :]
@@ -421,7 +426,7 @@
                 for at, total in zip(ats, sums):
                     acc_ref[at] = total
 
-    @pl.when(dx == 3)
+    @pl.when(dy == 3)
     def _():
         for flip, out_ref in ((1, send_ref), (0, keep_ref)):
             core = lax.rem(my_core + flip, 2)
@@ -451,7 +456,7 @@
             in_specs=[pl.BlockSpec((65, 16, 128), lambda dx, tgt, at: (0, 0, 0))] * 8
             + [pl.BlockSpec((1, 4 * B + 16, KP * B), lambda dx, tgt, at: (dx, 0, 0))] * 4,
             out_specs=[
-                pl.BlockSpec((NCOL, 2, B, 128), lambda dx, tgt, at: (0, 0, 0, 0)), out, out
+                pl.BlockSpec((NCOL, 3 * B, 128), lambda dx, tgt, at: (0, 0, 0)), out, out
             ],
             scratch_shapes=[
                 pltpu.VMEM((NCB * KC + 1, 8, 128), jnp.float32),
@@ -459,7 +464,7 @@
             ],
         ),
         out_shape=[
-            jax.ShapeDtypeStruct((NCOL, 2, B, 128), jnp.bfloat16),
+            jax.ShapeDtypeStruct((NCOL, 3 * B, 128), jnp.bfloat16),
             jax.ShapeDtypeStruct(shape, jnp.float32),
             jax.ShapeDtypeStruct(shape, jnp.float32),
         ],
@@ -467,12 +472,30 @@
     )(tgt, at, *parts, *ps)
 
 
-def ap_out_kernel(x_ref, out_ref, turn_ref):
+def layout_kernel(x_ref, ap_ref, coarse_ref, turn_ref, wide_ref, flat_ref):
+    for tp in range(KC // 2):
+        rows = []
+        for bg in range(8):
+            total = None
+            for ih in range(2):
+                for part in range(2):
+                    r0 = 2 * B + part * 32 + tp * 8
+                    term = x_ref[bg * 2 + ih, r0:r0 + 8, :].astype(jnp.float32)
+                    total = term if total is None else total + term
+            rows.append(total)
+        wide_ref[...] = jnp.concatenate(rows, axis=0).T
+        for lo in range(2):
+            even = wide_ref[pl.ds(lo * B, 32, stride=2), :]
+            odd = wide_ref[pl.ds(lo * B + 1, 32, stride=2), :]
+            flat_ref[pl.ds(tp * 2 + lo, 32, stride=8), :] = jnp.concatenate([even, odd], axis=1)
+    for h in range(32):
+        coarse_ref[:, h * 128:(h + 1) * 128] = flat_ref[h * 8:(h + 1) * 8, :]
     for ih in range(2):
         for qh in range(2):
             for s in range(KAP):
+                r0 = qh * B + s * 8
                 m = jnp.concatenate(
-                    [x_ref[bg * 2 + ih, qh, s * 8:(s + 1) * 8, :] for bg in range(8)], axis=0
+                    [x_ref[bg * 2 + ih, r0:r0 + 8, :] for bg in range(8)], axis=0
                 )
                 t = m.astype(jnp.float32).T
                 for lo in range(2):
@@ -481,42 +504,25 @@
             for lo in range(2):
                 for h in range(32):
                     tile = turn_ref[lo, h * 8:(h + 1) * 8, :]
-                    out_ref[ih * 4 + qh * 2 + lo, :, h * 128:(h + 1) * 128] = tile.astype(jnp.bfloat16)
-
-
-def ap_layout(x):
+                    ap_ref[ih * 4 + qh * 2 + lo, :, h * 128:(h + 1) * 128] = tile.astype(jnp.bfloat16)
+
+
+def layout(x):
     vmem = pl.BlockSpec(memory_space=pltpu.VMEM)
     return pl.pallas_call(
-        ap_out_kernel,
+        layout_kernel,
         in_specs=[vmem],
-        out_specs=vmem,
-        scratch_shapes=[pltpu.VMEM((2, 256, 128), jnp.float32)],
-        out_shape=jax.ShapeDtypeStruct((8, KAP, B * B), jnp.bfloat16),
-        name="ap_layout",
-    )(x)
-
-
-def coarse_out_kernel(x_ref, out_ref, turn_ref, flat_ref):
-    for tp in range(KC // 2):
-        m = jnp.concatenate([x_ref[bg * 2, tp] + x_ref[bg * 2 + 1, tp] for bg in range(8)], axis=0)
-        turn_ref[...] = m.T
-        for lo in range(2):
-            even = turn_ref[pl.ds(lo * B, 32, stride=2), :]
-            odd = turn_ref[pl.ds(lo * B + 1, 32, stride=2), :]
-            flat_ref[pl.ds(tp * 2 + lo, 32, stride=8), :] = jnp.concatenate([even, odd], axis=1)
-    for h in range(32):
-        out_ref[:, h * 128:(h + 1) * 128] = flat_ref[h * 8:(h + 1) * 8, :]
-
-
-def coarse_layout(x):
-    vmem = pl.BlockSpec(memory_space=pltpu.VMEM)
-    return pl.pallas_call(
-        coarse_out_kernel,
-        in_specs=[vmem],
-        out_specs=vmem,
-        scratch_shapes=[pltpu.VMEM((128, B), jnp.float32), pltpu.VMEM((256, 128), jnp.float32)],
-        out_shape=jax.ShapeDtypeStruct((KC, B * B), jnp.float32),
-        name="coarse_layout",
+        out_specs=[vmem, vmem],
+        scratch_shapes=[
+            pltpu.VMEM((2, 256, 128), jnp.float32),
+            pltpu.VMEM((128, B), jnp.float32),
+            pltpu.VMEM((256, 128), jnp.float32),
+        ],
+        out_shape=[
+            jax.ShapeDtypeStruct((8, KAP, B * B), jnp.bfloat16),
+            jax.ShapeDtypeStruct((KC, B * B), jnp.float32),
+        ],
+        name="layout",
     )(x)
 
 
@@ -557,11 +563,7 @@
     parts = [by_z[0], partner]
     for part in by_z[1:]:
         parts += [part, along_row(part, 0, 1)]
-    same = lax.dynamic_index_in_dim(halves, half, 0, keepdims=False)
-    diff = lax.dynamic_index_in_dim(halves, 1 - half, 0, keepdims=False)
-    by_x = [same, along_col(diff, 1, 0), along_col(same, 2, 0), along_col(diff, 3, 0)]
-    by_x = jnp.stack(by_x)
-    ps = [by_x] + [along_col(by_x, 0, d) for d in (1, 2, 3)]
+    by_y = [halves] + [along_col(halves, 0, d) for d in (1, 2, 3)]
 
     a = spread(a_blocks[:, 0]).reshape(4, 2, NCOL, B, KA * B)
 
@@ -574,18 +576,6 @@
     equal = picked[:, :, None, :] == ap_index[:, None, :, None]
     ids = place[:, :, None, None] * KP + jnp.arange(KP, dtype=jnp.int32)
     idx = jnp.min(jnp.where(equal, ids, NK * KP), axis=3).reshape(-1)
-
-    cols_p = jnp.stack([p[:, 4 * B:4 * B + 4, :KP] for p in ps]).reshape(NCOL, 16)
-    cc = jnp.arange(NCOL, dtype=jnp.int32)
-    where = ((y - cc // 4) % 4) * 4 + (x - cc % 4) % 4
-    cols_i = pick_rows(cols_p, where).reshape(NCOL, 4, KP)
-    slots = lax.dynamic_index_in_dim(
-        ap_index.reshape(2, 4, NCOL, KAP), half, 0, keepdims=False
-    ).transpose(1, 0, 2)
-    targets = pick_rows(coarse_index, cols_i)
-    hit = targets[:, :, :, None, :] == slots[:, :, None, :, None]
-    slot = cols_i[:, :, :, None, None] * KC + jnp.arange(KC, dtype=jnp.int32)
-    tgt = jnp.min(jnp.where(hit, slot, NCB * KC), axis=4).reshape(-1)
 
     x1, x3 = x_products(1, idx, at, a, dup)
     got_x1, got_x3 = along_col(x1, 1, 0), along_col(x3, 3, 0)
@@ -600,6 +590,23 @@
     s1 = middle(y_middle_kernel, at, [ya[0], *got_ya, yb[0], *got_yb])
     x_last = [along_col(s1[d], d, 0) for d in (1, 2, 3)]
 
+    by_y = jnp.stack(by_y)
+    same = lax.dynamic_index_in_dim(by_y, half, 1, keepdims=False)
+    diff = lax.dynamic_index_in_dim(by_y, 1 - half, 1, keepdims=False)
+    ps = [same, along_col(diff, 1, 0), along_col(same, 2, 0), along_col(diff, 3, 0)]
+
+    cols_p = jnp.stack([p[:, 4 * B:4 * B + 4, :KP] for p in ps]).reshape(NCOL, 16)
+    cc = jnp.arange(NCOL, dtype=jnp.int32)
+    where = ((x - cc % 4) % 4) * 4 + (y - cc // 4) % 4
+    cols_i = pick_rows(cols_p, where).reshape(NCOL, 4, KP)
+    slots = lax.dynamic_index_in_dim(
+        ap_index.reshape(2, 4, NCOL, KAP), half, 0, keepdims=False
+    ).transpose(1, 0, 2)
+    targets = pick_rows(coarse_index, cols_i)
+    hit = targets[:, :, :, None, :] == slots[:, :, None, :, None]
+    slot = cols_i[:, :, :, None, None] * KC + jnp.arange(KC, dtype=jnp.int32)
+    tgt = jnp.min(jnp.where(hit, slot, NCB * KC), axis=4).reshape(-1)
+
     apt, keep, send = coarse_terms(tgt, at, [s0[0], *y_last, s1[0], *x_last], ps)
     got = along_row(send, 0, 1)
     sums = [keep[d] + got[d] for d in range(4)]
@@ -607,10 +614,15 @@
     moved = [along_row(sums[d], d, 0) for d in (1, 2, 3)]
     for part in moved:
         coarse = coarse + part
-    back = lax.all_to_all(apt, "col", 0, 0, tiled=True)
-    ap_out = ap_layout(back).reshape(8, 1, KAP, B * B)
-    coarse = lax.all_to_all(coarse, "col", 0, 0, tiled=True)
-    coarse_out = coarse_layout(coarse).reshape(1, KC, B * B)
+    high = lax.reduce_precision(coarse, exponent_bits=8, mantissa_bits=7)
+    pair = jnp.concatenate(
+        [v.astype(jnp.bfloat16).reshape(NCOL, 32, 128) for v in (high, coarse - high)], axis=1
+    )
+    both = lax.dynamic_update_slice(apt, pair, (0, 2 * B, 0))
+    both = lax.all_to_all(both, "col", 0, 0, tiled=True)
+    ap_out, coarse_out = layout(both)
+    ap_out = ap_out.reshape(8, 1, KAP, B * B)
+    coarse_out = coarse_out.reshape(1, KC, B * B)
     return ap_out, coarse_out
 
 

time: 227 us -> 236 us (1.040)
  blocking collectives: 0 us -> 17.8 us
  starting transfers between devices: 54.2 us -> 39.8 us
  waiting for transfers between devices: 82.6 us -> 87 us
    all_to_all x0 -> x1, blocking collectives: none -> 17.8 us  [step(): both = lax.all_to_all(both, 'col', 0, 0, tiled=True)]
    all_to_all x2 -> x0, waiting for transfers between devices: 11.2 us -> none  [the longest x1 6.21 us: step(): coarse = lax.all_to_all(coarse, 'col', 0, 0, tiled=True)]
    all_to_all x2 -> x0, starting transfers between devices: 10.9 us -> none  [the longest x1 7.38 us: step(): back = lax.all_to_all(apt, 'col', 0, 0, tiled=True)]
    ppermute x21, waiting for transfers between devices: 55 us -> 64.4 us  [along_col(): return lax.ppermute(v, 'col', pairs)]
    ppermute x11, waiting for transfers between devices: 16.4 us -> 22.6 us  [along_row(): return lax.ppermute(v, 'row', pairs)]
    ppermute x21, starting transfers between devices: 31.2 us -> 27.7 us  [along_col(): return lax.ppermute(v, 'col', pairs)]
    unnamed x48 -> x34, local copies, waits for them, and re-layouts: 7.08 us -> 7.33 us
  transfers between devices with their start and end apart: 34 -> 32, of which waited for: 15 -> 14; matrix products, arithmetic and copies ran while one was open for 5% -> 4% of each run, Pallas kernels for 23% -> 22%
where the time goes in v4:
time: 236 us; the launch traced here: 234 us
  waiting for transfers between devices  87 us (37%)
  Pallas kernels  67 us (28%)
  starting transfers between devices  39.8 us (17%)
  blocking collectives  17.8 us (8%)
  local copies, waits for them, and re-layouts  16.9 us (7%)
  other arithmetic  4.08 us (2%)
    ppermute x21, waiting for transfers between devices, along_col(): return lax.ppermute(v, 'col', pairs)  64.4 us
    ppermute x21, starting transfers between devices, along_col(): return lax.ppermute(v, 'col', pairs)  27.7 us
    ppermute x11, waiting for transfers between devices, along_row(): return lax.ppermute(v, 'row', pairs)  22.6 us
    all_to_all x1, blocking collectives, step(): both = lax.all_to_all(both, 'col', 0, 0, tiled=True)  17.8 us
    pallas_call x2, Pallas kernels, y_products(): pl.pallas_call(lambda *refs: y_product_kernel(part, *refs), grid_spec=plt...  14.7 us
    pallas_call x2, Pallas kernels, x_products(): pl.pallas_call(lambda *refs: x_product_kernel(j, *refs), grid_spec=pltpu....  13.3 us
    pallas_call x1, Pallas kernels, coarse_terms(): pl.pallas_call(coarse_kernel, grid_spec=pltpu.PrefetchScalarGridSpec(num_...  12.6 us
    ppermute x11, starting transfers between devices, along_row(): return lax.ppermute(v, 'row', pairs)  12.2 us
  transfers between devices with their start and end apart: 32, of which 14 were waited for; matrix products, arithmetic and copies ran while one was open for 4% of the time, Pallas kernels for 22%

profile of v4, /device:TPU:0, one launch (start us, length us, event | category | flops | bytes accessed | tf_op | source)
XLA Modules:
  0.0 234.2 jit_solution(11494120944392017077)
XLA Ops:
  0.6 1.4 reshape_squeeze.3
  2.4 0.3 reshape.302
  2.9 2.1 collective-permute-start
  5.0 3.6 %collective-permute-start.1 = (bf16[528,256]{1,0:T(8,128)(2,1)S(1)}, bf16[528,256]{1,0:T(8,128)(2,1)S(1)}, u32[]{:S(2)}, u32[]{:S(2)}) collective-permute-start(bf16[528,256]{1,0:T(8,128)(2,1)S(1)} %fusion.3.refs_0_), channel_id=1, source_target_pairs={{0,64},{16,80},{32,96},{48,112},{64,0},{80,16},{96,32},{112,48},{1... | collective-permute-start | bytes 811016 | tf_op jit(solution)/shard_map/ppermute | solution.py:23
  8.6 1.0 collective-permute-start.2
  9.6 0.4 reshape_reshape_squeeze.3
  10.0 0.4 fusion.44
  11.7 1.9 collective-permute-done.refs_2_
  13.6 7.0 %collective-permute-done.1.refs_4_ = bf16[528,256]{1,0:T(8,128)(2,1)S(1)} collective-permute-done((bf16[528,256]{1,0:T(8,128)(2,1)S(1)}, bf16[528,256]{1,0:T(8,128)(2,1)S(1)}, u32[]{:S(2)}, u32[]{:S(2)}) %collective-permute-start.1) | collective-permute-done | bytes 270368 | tf_op jit(solution)/shard_map/ppermute | solution.py:23
  20.5 0.5 collective-permute-start.11
  21.1 8.4 %spread.1 = bf16[128,64,256]{2,1,0:T(8,128)(2,1)} custom-call(bf16[128,4,4096]{2,1,0:T(4,128)(2,1)} %bitcast.101), custom_call_target="tpu_custom_call" | custom-call | tf_op jit(solution)/shard_map/spread/pallas_call | solution.py:59
  29.5 1.6 collective-permute-start.3
  31.2 2.9 %collective-permute-start.4 = (bf16[2,272,256]{2,1,0:T(8,128)(2,1)S(1)}, bf16[2,272,256]{2,1,0:T(8,128)(2,1)}, u32[]{:S(2)}, u32[]{:S(2)}) collective-permute-start(bf16[2,272,256]{2,1,0:T(8,128)(2,1)S(1)} %pad_maximum_fusion.1), channel_id=1, source_target_pairs={{0,8},{1,9},{2,10},{3,11},{4,12},{5,13},{6,14},{7,15},{8,0},{9,1},... | collective-permute-start | bytes 835592 | tf_op jit(solution)/shard_map/ppermute | solution.py:28
  34.1 1.3 collective-permute-start.5
  35.4 4.9 %table.1 = (bf16[257,64,128]{2,1,0:T(8,128)(2,1)}, f32[64,128]{1,0:T(8,128)S(1)}) custom-call(bf16[528,256]{1,0:T(8,128)(2,1)S(1)} %fusion.3.refs_0_, bf16[528,256]{1,0:T(8,128)(2,1)S(1)} %collective-permute-done.9.refs_1_, bf16[528,256]{1,0:T(8,128)(2,1)S(1)} %collective-permute-done.refs_2_, bf16[528,256]{1,0:T(8,128)(2,1)S(1)} %collective-permute-done.10.refs_3_, ...), custom_call_target="tpu_custom_call" | custom-call | tf_op jit(solution)/shard_map/table/pallas_call | solution.py:92
  40.9 2.2 copy-done
  43.1 7.1 %shard_map.81 = (s16[129,16,128]{2,1,0:T(8,128)(2,1)}, s16[129,16,128]{2,1,0:T(8,128)(2,1)S(1)}, s16[129,16,128]{2,1,0:T(8,128)(2,1)S(1)}, s16[129,16,128]{2,1,0:T(8,128)(2,1)S(1)}) custom-call(s32[4096]{0:T(1024)S(1)} %reshape.306.refs_0_, s32[4]{0:T(128)S(1)} %pad_add_fusion.refs_1_.at_ref, bf16[4,2,16,64,256]{4,3,2,1,0:T(8,128)(2,1)} %bitcast.97, ...), custom_call_target="tpu_custom_call" | custom-call | tf_op jit(solution)/shard_map/pallas_call | solution.py:272
  50.1 0.7 collective-permute-start.22
  50.8 0.8 collective-permute-start.23
  51.6 1.9 collective-permute-start.24
  53.5 2.2 copy-done.1
  55.7 7.7 %shard_map.80 = (s16[129,16,128]{2,1,0:T(8,128)(2,1)}, s16[129,16,128]{2,1,0:T(8,128)(2,1)}, s16[129,16,128]{2,1,0:T(8,128)(2,1)}, s16[129,16,128]{2,1,0:T(8,128)(2,1)}) custom-call(s32[4096]{0:T(1024)S(1)} %reshape.306.refs_0_, s32[4]{0:T(128)S(1)} %pad_add_fusion.refs_1_.at_ref, bf16[4,2,16,64,256]{4,3,2,1,0:T(8,128)(2,1)} %bitcast.98, ...), custom_call_target="tpu_custom_call" | custom-call | tf_op jit(solution)/shard_map/pallas_call | solution.py:272
  63.4 0.7 collective-permute-start.19
  64.1 1.2 pad_maximum_fusion
  65.3 1.1 dynamic-slice_bitcast_fusion.1
  66.4 2.8 %collective-permute-start.8 = (bf16[4,272,256]{2,1,0:T(8,128)(2,1)}, bf16[4,272,256]{2,1,0:T(8,128)(2,1)}, u32[]{:S(2)}, u32[]{:S(2)}) collective-permute-start(bf16[4,272,256]{2,1,0:T(8,128)(2,1)} %get-tuple-element.82), channel_id=1, source_target_pairs={{0,3},{1,0},{2,1},{3,2},{4,7},{5,4},{6,5},{7,6},{8,11},{9,8},{10,9... | collective-permute-start | bytes 1671176 | tf_op jit(solution)/shard_map/ppermute | solution.py:28
  69.1 8.4 %collective-permute-done.22.refs_5_ = s16[129,16,128]{2,1,0:T(8,128)(2,1)S(1)} collective-permute-done((s16[129,16,128]{2,1,0:T(8,128)(2,1)S(1)}, s16[129,16,128]{2,1,0:T(8,128)(2,1)S(1)}, u32[]{:S(2)}, u32[]{:S(2)}) %collective-permute-start.22) | collective-permute-done | bytes 528416 | tf_op jit(solution)/shard_map/ppermute | solution.py:28
  77.8 0.7 collective-permute-done.24.refs_7_
  78.5 3.0 %collective-permute-start.7 = (bf16[4,272,256]{2,1,0:T(8,128)(2,1)}, bf16[4,272,256]{2,1,0:T(8,128)(2,1)}, u32[]{:S(2)}, u32[]{:S(2)}) collective-permute-start(bf16[4,272,256]{2,1,0:T(8,128)(2,1)} %get-tuple-element.81.refs_8_), channel_id=1, source_target_pairs={{0,2},{1,3},{2,0},{3,1},{4,6},{5,7},{6,4},{7,5},{8,10},{9,11},{10,... | collective-permute-start | bytes 1671176 | tf_op jit(solution)/shard_map/ppermute | solution.py:28
  81.6 2.2 copy-done.2
  83.8 6.2 %shard_map.78 = (s16[257,16,128]{2,1,0:T(8,128)(2,1)S(1)}, s16[257,16,128]{2,1,0:T(8,128)(2,1)S(1)}) custom-call(s32[4096]{0:T(1024)S(1)} %reshape.306.refs_0_, s32[4]{0:T(128)S(1)} %pad_add_fusion.refs_1_.at_ref, bf16[4,2,16,64,256]{4,3,2,1,0:T(8,128)(2,1)} %bitcast.99, bf16[257,64,128]{2,1,0:T(8,128)(2,1)S(1)} %copy-done.2), custom_call_target="tpu_custom_call" | custom-call | tf_op jit(solution)/shard_map/pallas_call | solution.py:205
  89.9 7.1 %shard_map.77 = (s16[257,16,128]{2,1,0:T(8,128)(2,1)}, s16[257,16,128]{2,1,0:T(8,128)(2,1)S(1)}) custom-call(s32[4096]{0:T(1024)S(1)} %reshape.306.refs_0_, s32[4]{0:T(128)S(1)} %pad_add_fusion.refs_1_.at_ref, bf16[4,2,16,64,256]{4,3,2,1,0:T(8,128)(2,1)} %bitcast.100, bf16[257,64,128]{2,1,0:T(8,128)(2,1)S(1)} %copy-done.2), custom_call_target="tpu_custom_call" | custom-call | tf_op jit(solution)/shard_map/pallas_call | solution.py:205
  97.1 1.9 collective-permute-done.19.refs_1_
  99.0 1.5 collective-permute-start.6
  100.5 0.7 slice_bitcast_fusion.3
  101.2 1.5 collective-permute-start.13
  102.7 1.7 collective-permute-start.15
  104.5 5.2 %shard_map.82 = (s16[65,16,128]{2,1,0:T(8,128)(2,1)}, s16[65,16,128]{2,1,0:T(8,128)(2,1)}, s16[65,16,128]{2,1,0:T(8,128)(2,1)}, s16[65,16,128]{2,1,0:T(8,128)(2,1)}) custom-call(s32[4]{0:T(128)} %copy-done.3, s16[129,16,128]{2,1,0:T(8,128)(2,1)} %get-tuple-element.49.refs_0_, s16[129,16,128]{2,1,0:T(8,128)(2,1)} %collective-permute-done.19.refs_1_, ...), custom_call_target="tpu_custom_call" | custom-call | tf_op jit(solution)/shard_map/pallas_call | solution.py:362
  109.7 1.6 collective-permute-start.14
  111.3 0.7 slice_bitcast_fusion
  112.0 0.7 slice_bitcast_fusion.1
  112.7 3.4 %collective-permute-done.6.refs_9_ = bf16[4,272,256]{2,1,0:T(8,128)(2,1)} collective-permute-done((bf16[4,272,256]{2,1,0:T(8,128)(2,1)}, bf16[4,272,256]{2,1,0:T(8,128)(2,1)}, u32[]{:S(2)}, u32[]{:S(2)}) %collective-permute-start.6) | collective-permute-done | bytes 557088 | tf_op jit(solution)/shard_map/ppermute | solution.py:28
  116.0 1.8 collective-permute-start.26
  117.9 0.7 slice_bitcast_fusion.2
  119.3 40.9 %collective-permute-done.13.m1 = s16[257,16,128]{2,1,0:T(8,128)(2,1)} collective-permute-done((s16[257,16,128]{2,1,0:T(8,128)(2,1)S(1)}, s16[257,16,128]{2,1,0:T(8,128)(2,1)}, u32[]{:S(2)}, u32[]{:S(2)}) %collective-permute-start.13) | collective-permute-done | bytes 1052704 | tf_op jit(solution)/shard_map/ppermute | solution.py:28
  160.1 2.1 collective-permute-done.14.m2
  162.2 5.2 %shard_map.79 = (s16[65,16,128]{2,1,0:T(8,128)(2,1)}, s16[65,16,128]{2,1,0:T(8,128)(2,1)}, s16[65,16,128]{2,1,0:T(8,128)(2,1)}, s16[65,16,128]{2,1,0:T(8,128)(2,1)}) custom-call(s32[4]{0:T(128)} %copy-done.3, s16[257,16,128]{2,1,0:T(8,128)(2,1)} %get-tuple-element.41.m0, s16[257,16,128]{2,1,0:T(8,128)(2,1)} %collective-permute-done.13.m1, ...), custom_call_target="tpu_custom_call" | custom-call | tf_op jit(solution)/shard_map/pallas_call | solution.py:362
  167.4 2.7 %collective-permute-start.17 = (s16[65,16,128]{2,1,0:T(8,128)(2,1)}, s16[65,16,128]{2,1,0:T(8,128)(2,1)S(1)}, u32[]{:S(2)}, u32[]{:S(2)}) collective-permute-start(s16[65,16,128]{2,1,0:T(8,128)(2,1)} %get-tuple-element.47), channel_id=1, source_target_pairs={{0,8},{1,9},{2,10},{3,11},{4,12},{5,13},{6,14},{7,15},{8,0},{9,1},... | collective-permute-start | bytes 798728 | tf_op jit(solution)/shard_map/ppermute | solution.py:28
  170.1 1.0 collective-permute-start.18
  171.5 0.8 reshape.305.tgt_ref
  172.3 6.3 %collective-permute-done.16.refs_1_ = s16[65,16,128]{2,1,0:T(8,128)(2,1)S(1)} collective-permute-done((s16[65,16,128]{2,1,0:T(8,128)(2,1)}, s16[65,16,128]{2,1,0:T(8,128)(2,1)S(1)}, u32[]{:S(2)}, u32[]{:S(2)}) %collective-permute-start.16) | collective-permute-done | bytes 266272 | tf_op jit(solution)/shard_map/ppermute | solution.py:28
  178.6 0.7 collective-permute-done.18.refs_3_
  179.4 0.6 copy-done.12
  180.0 12.6 %coarse_terms.1 = (bf16[16,192,128]{2,1,0:T(8,128)(2,1)}, f32[4,16,4,8,128]{4,3,2,1,0:T(8,128)}, f32[4,16,4,8,128]{4,3,2,1,0:T(8,128)}) custom-call(s32[2048]{0:T(1024)} %reshape.305.tgt_ref, s32[4]{0:T(128)} %copy-done.3, s16[65,16,128]{2,1,0:T(8,128)(2,1)} %get-tuple-element.45.refs_0_, s16[65,16,128]{2,1,0:T(8,128)(2,1)} %copy-done.10, ...), custom_call_target="tpu_custom_call" | custom-call | tf_op jit(solution)/shard_map/coarse_terms/pallas_call | solution.py:451
  192.6 2.9 %collective-permute-done.28 = f32[4,16,4,8,128]{4,3,2,1,0:T(8,128)S(1)} collective-permute-done((f32[4,16,4,8,128]{4,3,2,1,0:T(8,128)}, f32[4,16,4,8,128]{4,3,2,1,0:T(8,128)S(1)}, u32[]{:S(2)}, u32[]{:S(2)}) %collective-permute-start.28) | collective-permute-done | bytes 1048608 | tf_op jit(solution)/shard_map/ppermute | solution.py:23
  195.5 1.2 fusion.7
  196.8 1.3 collective-permute-start.29
  198.1 2.4 %collective-permute-start.30 = (f32[16,4,8,128]{3,2,1,0:T(8,128)S(1)}, f32[16,4,8,128]{3,2,1,0:T(8,128)S(1)}, u32[]{:S(2)}, u32[]{:S(2)}) collective-permute-start(f32[16,4,8,128]{3,2,1,0:T(8,128)S(1)} %get-tuple-element.80), channel_id=1, source_target_pairs={{0,64},{16,80},{32,96},{48,112},{64,0},{80,16},{96,32},{112,48},{1... | collective-permute-start | bytes 786440 | tf_op jit(solution)/shard_map/ppermute | solution.py:23
  200.4 1.3 collective-permute-start.31
  201.7 5.1 %collective-permute-done.29 = f32[16,4,8,128]{3,2,1,0:T(8,128)S(1)} collective-permute-done((f32[16,4,8,128]{3,2,1,0:T(8,128)S(1)}, f32[16,4,8,128]{3,2,1,0:T(8,128)S(1)}, u32[]{:S(2)}, u32[]{:S(2)}) %collective-permute-start.29) | collective-permute-done | bytes 262176 | tf_op jit(solution)/shard_map/ppermute | solution.py:23
  206.8 5.5 %collective-permute-done.30 = f32[16,4,8,128]{3,2,1,0:T(8,128)S(1)} collective-permute-done((f32[16,4,8,128]{3,2,1,0:T(8,128)S(1)}, f32[16,4,8,128]{3,2,1,0:T(8,128)S(1)}, u32[]{:S(2)}, u32[]{:S(2)}) %collective-permute-start.30) | collective-permute-done | bytes 262176 | tf_op jit(solution)/shard_map/ppermute | solution.py:23
  212.6 1.1 fusion.17
  213.8 17.8 %all_to_all.5.x_ref = bf16[16,192,128]{2,1,0:T(8,128)(2,1)} all-to-all(bf16[16,192,128]{2,1,0:T(8,128)(2,1)S(1)} %maximum_dynamic-update-slice_fusion), channel_id=1, replica_groups=mesh['row'=8,'col'=16] {'col'}, dimensions={0} | all-to-all | bytes 1572864 | tf_op jit(solution)/shard_map/all_to_all | solution.py:622
  231.6 2.6 %layout.1 = (bf16[8,8,4096]{2,1,0:T(8,128)(2,1)}, f32[8,4096]{1,0:T(8,128)}) custom-call(bf16[16,192,128]{2,1,0:T(8,128)(2,1)} %all_to_all.5.x_ref), custom_call_target="tpu_custom_call" | custom-call | tf_op jit(solution)/shard_map/layout/pallas_call | solution.py:512
  (94 shorter events, 4.2 us)
Async XLA Ops:
  2.1 0.7 copy-start.14
  2.1 7.5 %copy-start.4 = (bf16[8,1,4,4096]{3,2,1,0:T(4,128)(2,1)S(1)}, bf16[8,1,4,4096]{3,2,1,0:T(4,128)(2,1)}, u32[]{:S(2)}) copy-start(bf16[8,1,4,4096]{3,2,1,0:T(4,128)(2,1)} %param.8) | copy-start | bytes 786436
  2.9 10.7 %collective-permute-start = (bf16[528,256]{1,0:T(8,128)(2,1)S(1)}, bf16[528,256]{1,0:T(8,128)(2,1)S(1)}, u32[]{:S(2)}, u32[]{:S(2)}) collective-permute-start(bf16[528,256]{1,0:T(8,128)(2,1)S(1)} %fusion.3.refs_0_), channel_id=1, source_target_pairs={{0,32},{16,48},{32,64},{48,80},{64,96},{80,112},{96,0},{112,16},{1... | collective-permute-start | bytes 811016 | tf_op jit(solution)/shard_map/ppermute | solution.py:23
  5.0 15.6 %collective-permute-start.1 = (bf16[528,256]{1,0:T(8,128)(2,1)S(1)}, bf16[528,256]{1,0:T(8,128)(2,1)S(1)}, u32[]{:S(2)}, u32[]{:S(2)}) collective-permute-start(bf16[528,256]{1,0:T(8,128)(2,1)S(1)} %fusion.3.refs_0_), channel_id=1, source_target_pairs={{0,64},{16,80},{32,96},{48,112},{64,0},{80,16},{96,32},{112,48},{1... | collective-permute-start | bytes 811016 | tf_op jit(solution)/shard_map/ppermute | solution.py:23
  8.6 12.0 %collective-permute-start.2 = (bf16[528,256]{1,0:T(8,128)(2,1)S(1)}, bf16[528,256]{1,0:T(8,128)(2,1)S(1)}, u32[]{:S(2)}, u32[]{:S(2)}) collective-permute-start(bf16[528,256]{1,0:T(8,128)(2,1)S(1)} %fusion.3.refs_0_), channel_id=1, source_target_pairs={{0,96},{16,112},{32,0},{48,16},{64,32},{80,48},{96,64},{112,80},{1... | collective-permute-start | bytes 811016 | tf_op jit(solution)/shard_map/ppermute | solution.py:23
  9.6 21.6 %collective-permute-start.9 = (bf16[528,256]{1,0:T(8,128)(2,1)S(1)}, bf16[528,256]{1,0:T(8,128)(2,1)S(1)}, u32[]{:S(2)}, u32[]{:S(2)}) collective-permute-start(bf16[528,256]{1,0:T(8,128)(2,1)S(1)} %fusion.3.refs_0_), channel_id=1, source_target_pairs={{0,16},{16,0},{32,48},{48,32},{64,80},{80,64},{96,112},{112,96},{1... | collective-permute-start | bytes 811016 | tf_op jit(solution)/shard_map/ppermute | solution.py:23
  10.8 0.8 copy-start.15
  20.5 13.5 %collective-permute-start.10 = (bf16[528,256]{1,0:T(8,128)(2,1)S(1)}, bf16[528,256]{1,0:T(8,128)(2,1)S(1)}, u32[]{:S(2)}, u32[]{:S(2)}) collective-permute-start(bf16[528,256]{1,0:T(8,128)(2,1)S(1)} %collective-permute-done.refs_2_), channel_id=1, source_target_pairs={{0,16},{16,0},{32,48},{48,32},{64,80},{80,64},{96,112},{112,96},{1... | collective-permute-start | bytes 811016 | tf_op jit(solution)/shard_map/ppermute | solution.py:23
  20.5 14.9 %collective-permute-start.11 = (bf16[528,256]{1,0:T(8,128)(2,1)S(1)}, bf16[528,256]{1,0:T(8,128)(2,1)S(1)}, u32[]{:S(2)}, u32[]{:S(2)}) collective-permute-start(bf16[528,256]{1,0:T(8,128)(2,1)S(1)} %collective-permute-done.1.refs_4_), channel_id=1, source_target_pairs={{0,16},{16,0},{32,48},{48,32},{64,80},{80,64},{96,112},{112,96},{1... | collective-permute-start | bytes 811016 | tf_op jit(solution)/shard_map/ppermute | solution.py:23
  21.1 14.4 %collective-permute-start.12 = (bf16[528,256]{1,0:T(8,128)(2,1)S(1)}, bf16[528,256]{1,0:T(8,128)(2,1)S(1)}, u32[]{:S(2)}, u32[]{:S(2)}) collective-permute-start(bf16[528,256]{1,0:T(8,128)(2,1)S(1)} %collective-permute-done.2.refs_6_), channel_id=1, source_target_pairs={{0,16},{16,0},{32,48},{48,32},{64,80},{80,64},{96,112},{112,96},{1... | collective-permute-start | bytes 811016 | tf_op jit(solution)/shard_map/ppermute | solution.py:23
  21.1 68.8 %copy-start.3 = (s32[4]{0:T(128)}, s32[4]{0:T(128)S(1)}, u32[]{:S(2)}) copy-start(s32[4]{0:T(128)S(1)} %pad_add_fusion.refs_1_.at_ref) | copy-start | bytes 52
  29.5 11.0 %copy-start.13 = (s32[128,8]{0,1:T(8,128)S(1)}, s32[128,8]{0,1:T(8,128)}, u32[]{:S(2)}) copy-start(s32[128,8]{0,1:T(8,128)} %param.10) | copy-start | bytes 12292
  29.5 22.1 %collective-permute-start.3 = (bf16[2,272,256]{2,1,0:T(8,128)(2,1)S(1)}, bf16[2,272,256]{2,1,0:T(8,128)(2,1)S(1)}, u32[]{:S(2)}, u32[]{:S(2)}) collective-permute-start(bf16[2,272,256]{2,1,0:T(8,128)(2,1)S(1)} %pad_maximum_fusion.1), channel_id=1, source_target_pairs={{0,4},{1,5},{2,6},{3,7},{4,8},{5,9},{6,10},{7,11},{8,12},{9,13},{1... | collective-permute-start | bytes 835592 | tf_op jit(solution)/shard_map/ppermute | solution.py:28
  31.2 32.2 %collective-permute-start.4 = (bf16[2,272,256]{2,1,0:T(8,128)(2,1)S(1)}, bf16[2,272,256]{2,1,0:T(8,128)(2,1)}, u32[]{:S(2)}, u32[]{:S(2)}) collective-permute-start(bf16[2,272,256]{2,1,0:T(8,128)(2,1)S(1)} %pad_maximum_fusion.1), channel_id=1, source_target_pairs={{0,8},{1,9},{2,10},{3,11},{4,12},{5,13},{6,14},{7,15},{8,0},{9,1},... | collective-permute-start | bytes 835592 | tf_op jit(solution)/shard_map/ppermute | solution.py:28
  34.1 30.0 %collective-permute-start.5 = (bf16[2,272,256]{2,1,0:T(8,128)(2,1)S(1)}, bf16[2,272,256]{2,1,0:T(8,128)(2,1)}, u32[]{:S(2)}, u32[]{:S(2)}) collective-permute-start(bf16[2,272,256]{2,1,0:T(8,128)(2,1)S(1)} %pad_maximum_fusion.1), channel_id=1, source_target_pairs={{0,12},{1,13},{2,14},{3,15},{4,0},{5,1},{6,2},{7,3},{8,4},{9,5},{1... | collective-permute-start | bytes 835592 | tf_op jit(solution)/shard_map/ppermute | solution.py:28
  40.9 2.2 copy-start
  50.1 27.4 %collective-permute-start.22 = (s16[129,16,128]{2,1,0:T(8,128)(2,1)S(1)}, s16[129,16,128]{2,1,0:T(8,128)(2,1)S(1)}, u32[]{:S(2)}, u32[]{:S(2)}) collective-permute-start(s16[129,16,128]{2,1,0:T(8,128)(2,1)S(1)} %get-tuple-element.54), channel_id=1, source_target_pairs={{0,4},{1,5},{2,6},{3,7},{4,8},{5,9},{6,10},{7,11},{8,12},{9,13},{1... | collective-permute-start | bytes 1585160 | tf_op jit(solution)/shard_map/ppermute | solution.py:28
  50.8 26.7 %collective-permute-start.23 = (s16[129,16,128]{2,1,0:T(8,128)(2,1)S(1)}, s16[129,16,128]{2,1,0:T(8,128)(2,1)S(1)}, u32[]{:S(2)}, u32[]{:S(2)}) collective-permute-start(s16[129,16,128]{2,1,0:T(8,128)(2,1)S(1)} %get-tuple-element.55), channel_id=1, source_target_pairs={{0,8},{1,9},{2,10},{3,11},{4,12},{5,13},{6,14},{7,15},{8,0},{9,1},... | collective-permute-start | bytes 1585160 | tf_op jit(solution)/shard_map/ppermute | solution.py:28
  51.6 26.9 %collective-permute-start.24 = (s16[129,16,128]{2,1,0:T(8,128)(2,1)S(1)}, s16[129,16,128]{2,1,0:T(8,128)(2,1)}, u32[]{:S(2)}, u32[]{:S(2)}) collective-permute-start(s16[129,16,128]{2,1,0:T(8,128)(2,1)S(1)} %get-tuple-element.56), channel_id=1, source_target_pairs={{0,12},{1,13},{2,14},{3,15},{4,0},{5,1},{6,2},{7,3},{8,4},{9,5},{1... | collective-permute-start | bytes 1585160 | tf_op jit(solution)/shard_map/ppermute | solution.py:28
  53.5 2.2 copy-start.1
  63.4 35.7 %collective-permute-start.19 = (s16[129,16,128]{2,1,0:T(8,128)(2,1)}, s16[129,16,128]{2,1,0:T(8,128)(2,1)}, u32[]{:S(2)}, u32[]{:S(2)}) collective-permute-start(s16[129,16,128]{2,1,0:T(8,128)(2,1)} %get-tuple-element.50), channel_id=1, source_target_pairs={{0,4},{1,5},{2,6},{3,7},{4,8},{5,9},{6,10},{7,11},{8,12},{9,13},{1... | collective-permute-start | bytes 1585160 | tf_op jit(solution)/shard_map/ppermute | solution.py:28
  66.4 43.3 %collective-permute-start.8 = (bf16[4,272,256]{2,1,0:T(8,128)(2,1)}, bf16[4,272,256]{2,1,0:T(8,128)(2,1)}, u32[]{:S(2)}, u32[]{:S(2)}) collective-permute-start(bf16[4,272,256]{2,1,0:T(8,128)(2,1)} %get-tuple-element.82), channel_id=1, source_target_pairs={{0,3},{1,0},{2,1},{3,2},{4,7},{5,4},{6,5},{7,6},{8,11},{9,8},{10,9... | collective-permute-start | bytes 1671176 | tf_op jit(solution)/shard_map/ppermute | solution.py:28
  77.6 4.0 %copy-start.6 = (s16[129,16,128]{2,1,0:T(8,128)(2,1)}, s16[129,16,128]{2,1,0:T(8,128)(2,1)S(1)}, u32[]{:S(2)}) copy-start(s16[129,16,128]{2,1,0:T(8,128)(2,1)S(1)} %collective-permute-done.22.refs_5_) | copy-start | bytes 1585156
  77.6 23.6 %collective-permute-start.20 = (s16[129,16,128]{2,1,0:T(8,128)(2,1)}, s16[129,16,128]{2,1,0:T(8,128)(2,1)}, u32[]{:S(2)}, u32[]{:S(2)}) collective-permute-start(s16[129,16,128]{2,1,0:T(8,128)(2,1)} %get-tuple-element.51), channel_id=1, source_target_pairs={{0,8},{1,9},{2,10},{3,11},{4,12},{5,13},{6,14},{7,15},{8,0},{9,1},... | collective-permute-start | bytes 1585160 | tf_op jit(solution)/shard_map/ppermute | solution.py:28
  77.6 4.0 %copy-start.7 = (s16[129,16,128]{2,1,0:T(8,128)(2,1)}, s16[129,16,128]{2,1,0:T(8,128)(2,1)S(1)}, u32[]{:S(2)}) copy-start(s16[129,16,128]{2,1,0:T(8,128)(2,1)S(1)} %collective-permute-done.23.refs_6_) | copy-start | bytes 1585156
  77.6 25.1 %collective-permute-start.21 = (s16[129,16,128]{2,1,0:T(8,128)(2,1)}, s16[129,16,128]{2,1,0:T(8,128)(2,1)}, u32[]{:S(2)}, u32[]{:S(2)}) collective-permute-start(s16[129,16,128]{2,1,0:T(8,128)(2,1)} %get-tuple-element.52), channel_id=1, source_target_pairs={{0,12},{1,13},{2,14},{3,15},{4,0},{5,1},{6,2},{7,3},{8,4},{9,5},{1... | collective-permute-start | bytes 1585160 | tf_op jit(solution)/shard_map/ppermute | solution.py:28
  78.5 33.5 %collective-permute-start.7 = (bf16[4,272,256]{2,1,0:T(8,128)(2,1)}, bf16[4,272,256]{2,1,0:T(8,128)(2,1)}, u32[]{:S(2)}, u32[]{:S(2)}) collective-permute-start(bf16[4,272,256]{2,1,0:T(8,128)(2,1)} %get-tuple-element.81.refs_8_), channel_id=1, source_target_pairs={{0,2},{1,3},{2,0},{3,1},{4,6},{5,7},{6,4},{7,5},{8,10},{9,11},{10,... | collective-permute-start | bytes 1671176 | tf_op jit(solution)/shard_map/ppermute | solution.py:28
  81.6 2.2 copy-start.2
  99.0 17.0 %collective-permute-start.6 = (bf16[4,272,256]{2,1,0:T(8,128)(2,1)}, bf16[4,272,256]{2,1,0:T(8,128)(2,1)}, u32[]{:S(2)}, u32[]{:S(2)}) collective-permute-start(bf16[4,272,256]{2,1,0:T(8,128)(2,1)} %get-tuple-element.82), channel_id=1, source_target_pairs={{0,1},{1,2},{2,3},{3,0},{4,5},{5,6},{6,7},{7,4},{8,9},{9,10},{10,1... | collective-permute-start | bytes 1671176 | tf_op jit(solution)/shard_map/ppermute | solution.py:28
  101.2 58.9 %collective-permute-start.13 = (s16[257,16,128]{2,1,0:T(8,128)(2,1)S(1)}, s16[257,16,128]{2,1,0:T(8,128)(2,1)}, u32[]{:S(2)}, u32[]{:S(2)}) collective-permute-start(s16[257,16,128]{2,1,0:T(8,128)(2,1)S(1)} %get-tuple-element.42), channel_id=1, source_target_pairs={{0,1},{1,2},{2,3},{3,0},{4,5},{5,6},{6,7},{7,4},{8,9},{9,10},{10,1... | collective-permute-start | bytes 3158024 | tf_op jit(solution)/shard_map/ppermute | solution.py:28
  102.7 57.4 %collective-permute-start.15 = (s16[257,16,128]{2,1,0:T(8,128)(2,1)S(1)}, s16[257,16,128]{2,1,0:T(8,128)(2,1)}, u32[]{:S(2)}, u32[]{:S(2)}) collective-permute-start(s16[257,16,128]{2,1,0:T(8,128)(2,1)S(1)} %get-tuple-element.44), channel_id=1, source_target_pairs={{0,3},{1,0},{2,1},{3,2},{4,7},{5,4},{6,5},{7,6},{8,11},{9,8},{10,9... | collective-permute-start | bytes 3158024 | tf_op jit(solution)/shard_map/ppermute | solution.py:28
  104.5 14.5 %copy-start.16 = (s32[128,8]{0,1:T(8,128)S(1)}, s32[128,8]{0,1:T(8,128)}, u32[]{:S(2)}) copy-start(s32[128,8]{0,1:T(8,128)} %param.11) | copy-start | bytes 12292
  109.7 52.5 %collective-permute-start.14 = (s16[257,16,128]{2,1,0:T(8,128)(2,1)S(1)}, s16[257,16,128]{2,1,0:T(8,128)(2,1)}, u32[]{:S(2)}, u32[]{:S(2)}) collective-permute-start(s16[257,16,128]{2,1,0:T(8,128)(2,1)S(1)} %get-tuple-element.43), channel_id=1, source_target_pairs={{0,2},{1,3},{2,0},{3,1},{4,6},{5,7},{6,4},{7,5},{8,10},{9,11},{10,... | collective-permute-start | bytes 3158024 | tf_op jit(solution)/shard_map/ppermute | solution.py:28
  112.0 58.1 %collective-permute-start.25 = (s16[65,16,128]{2,1,0:T(8,128)(2,1)}, s16[65,16,128]{2,1,0:T(8,128)(2,1)S(1)}, u32[]{:S(2)}, u32[]{:S(2)}) collective-permute-start(s16[65,16,128]{2,1,0:T(8,128)(2,1)} %get-tuple-element.58), channel_id=1, source_target_pairs={{0,1},{1,2},{2,3},{3,0},{4,5},{5,6},{6,7},{7,4},{8,9},{9,10},{10,1... | collective-permute-start | bytes 798728 | tf_op jit(solution)/shard_map/ppermute | solution.py:28
  116.0 56.2 %collective-permute-start.26 = (s16[65,16,128]{2,1,0:T(8,128)(2,1)}, s16[65,16,128]{2,1,0:T(8,128)(2,1)}, u32[]{:S(2)}, u32[]{:S(2)}) collective-permute-start(s16[65,16,128]{2,1,0:T(8,128)(2,1)} %get-tuple-element.59), channel_id=1, source_target_pairs={{0,2},{1,3},{2,0},{3,1},{4,6},{5,7},{6,4},{7,5},{8,10},{9,11},{10,... | collective-permute-start | bytes 798728 | tf_op jit(solution)/shard_map/ppermute | solution.py:28
  160.1 12.1 %collective-permute-start.27 = (s16[65,16,128]{2,1,0:T(8,128)(2,1)}, s16[65,16,128]{2,1,0:T(8,128)(2,1)S(1)}, u32[]{:S(2)}, u32[]{:S(2)}) collective-permute-start(s16[65,16,128]{2,1,0:T(8,128)(2,1)} %get-tuple-element.60), channel_id=1, source_target_pairs={{0,3},{1,0},{2,1},{3,2},{4,7},{5,4},{6,5},{7,6},{8,11},{9,8},{10,9... | collective-permute-start | bytes 798728 | tf_op jit(solution)/shard_map/ppermute | solution.py:28
  167.4 11.2 %collective-permute-start.16 = (s16[65,16,128]{2,1,0:T(8,128)(2,1)}, s16[65,16,128]{2,1,0:T(8,128)(2,1)S(1)}, u32[]{:S(2)}, u32[]{:S(2)}) collective-permute-start(s16[65,16,128]{2,1,0:T(8,128)(2,1)} %get-tuple-element.46), channel_id=1, source_target_pairs={{0,4},{1,5},{2,6},{3,7},{4,8},{5,9},{6,10},{7,11},{8,12},{9,13},{1... | collective-permute-start | bytes 798728 | tf_op jit(solution)/shard_map/ppermute | solution.py:28
  167.4 11.2 %collective-permute-start.17 = (s16[65,16,128]{2,1,0:T(8,128)(2,1)}, s16[65,16,128]{2,1,0:T(8,128)(2,1)S(1)}, u32[]{:S(2)}, u32[]{:S(2)}) collective-permute-start(s16[65,16,128]{2,1,0:T(8,128)(2,1)} %get-tuple-element.47), channel_id=1, source_target_pairs={{0,8},{1,9},{2,10},{3,11},{4,12},{5,13},{6,14},{7,15},{8,0},{9,1},... | collective-permute-start | bytes 798728 | tf_op jit(solution)/shard_map/ppermute | solution.py:28
  170.1 9.2 %copy-start.8 = (s16[65,16,128]{2,1,0:T(8,128)(2,1)}, s16[65,16,128]{2,1,0:T(8,128)(2,1)S(1)}, u32[]{:S(2)}) copy-start(s16[65,16,128]{2,1,0:T(8,128)(2,1)S(1)} %collective-permute-done.25.refs_5_) | copy-start | bytes 798724
  170.1 9.2 %collective-permute-start.18 = (s16[65,16,128]{2,1,0:T(8,128)(2,1)}, s16[65,16,128]{2,1,0:T(8,128)(2,1)S(1)}, u32[]{:S(2)}, u32[]{:S(2)}) collective-permute-start(s16[65,16,128]{2,1,0:T(8,128)(2,1)} %get-tuple-element.48), channel_id=1, source_target_pairs={{0,12},{1,13},{2,14},{3,15},{4,0},{5,1},{6,2},{7,3},{8,4},{9,5},{1... | collective-permute-start | bytes 798728 | tf_op jit(solution)/shard_map/ppermute | solution.py:28
  172.3 7.0 %copy-start.9 = (s16[65,16,128]{2,1,0:T(8,128)(2,1)}, s16[65,16,128]{2,1,0:T(8,128)(2,1)S(1)}, u32[]{:S(2)}) copy-start(s16[65,16,128]{2,1,0:T(8,128)(2,1)S(1)} %collective-permute-done.27.refs_7_) | copy-start | bytes 798724
  178.6 0.7 copy-start.10
  178.6 0.8 copy-start.11
  179.3 0.7 copy-start.12
  192.6 2.9 %collective-permute-start.28 = (f32[4,16,4,8,128]{4,3,2,1,0:T(8,128)}, f32[4,16,4,8,128]{4,3,2,1,0:T(8,128)S(1)}, u32[]{:S(2)}, u32[]{:S(2)}) collective-permute-start(f32[4,16,4,8,128]{4,3,2,1,0:T(8,128)} %get-tuple-element.63), channel_id=1, source_target_pairs={{0,16},{16,0},{32,48},{48,32},{64,80},{80,64},{96,112},{112,96},{1... | collective-permute-start | bytes 3145736 | tf_op jit(solution)/shard_map/ppermute | solution.py:23
  196.7 17.0 %copy-start.5 = (bf16[16,192,128]{2,1,0:T(8,128)(2,1)S(1)}, bf16[16,192,128]{2,1,0:T(8,128)(2,1)}, u32[]{:S(2)}) copy-start(bf16[16,192,128]{2,1,0:T(8,128)(2,1)} %get-tuple-element.61) | copy-start | bytes 2359300
  196.8 10.1 %collective-permute-start.29 = (f32[16,4,8,128]{3,2,1,0:T(8,128)S(1)}, f32[16,4,8,128]{3,2,1,0:T(8,128)S(1)}, u32[]{:S(2)}, u32[]{:S(2)}) collective-permute-start(f32[16,4,8,128]{3,2,1,0:T(8,128)S(1)} %get-tuple-element.78), channel_id=1, source_target_pairs={{0,32},{16,48},{32,64},{48,80},{64,96},{80,112},{96,0},{112,16},{1... | collective-permute-start | bytes 786440 | tf_op jit(solution)/shard_map/ppermute | solution.py:23
  198.1 14.3 %collective-permute-start.30 = (f32[16,4,8,128]{3,2,1,0:T(8,128)S(1)}, f32[16,4,8,128]{3,2,1,0:T(8,128)S(1)}, u32[]{:S(2)}, u32[]{:S(2)}) collective-permute-start(f32[16,4,8,128]{3,2,1,0:T(8,128)S(1)} %get-tuple-element.80), channel_id=1, source_target_pairs={{0,64},{16,80},{32,96},{48,112},{64,0},{80,16},{96,32},{112,48},{1... | collective-permute-start | bytes 786440 | tf_op jit(solution)/shard_map/ppermute | solution.py:23
  200.4 12.2 %collective-permute-start.31 = (f32[16,4,8,128]{3,2,1,0:T(8,128)S(1)}, f32[16,4,8,128]{3,2,1,0:T(8,128)S(1)}, u32[]{:S(2)}, u32[]{:S(2)}) collective-permute-start(f32[16,4,8,128]{3,2,1,0:T(8,128)S(1)} %get-tuple-element.79), channel_id=1, source_target_pairs={{0,96},{16,112},{32,0},{48,16},{64,32},{80,48},{96,64},{112,80},{1... | collective-permute-start | bytes 786440 | tf_op jit(solution)/shard_map/ppermute | solution.py:23

commit v5 on v4

--- a/solution.py
+++ b/solution.py
@@ -371,72 +371,85 @@
     )(at, *parts)
 
 
-def decode(parts, out_ref, scale_ref):
+def decode(parts, out_ref, first_row, scale_ref):
     for n, m in enumerate(parts):
         scale_ref[n] = jnp.exp2(m[64].astype(jnp.float32) - FULL)
 
     def one(c, carry):
-        for qh in range(2):
-            scales = [scale_ref[qh * 4 + d, pl.ds(c, 1), :] for d in range(4)]
-            for sp in range(4):
-                terms = [
-                    parts[qh * 4 + d][c * 4 + sp].astype(jnp.float32) * scales[d] for d in range(4)
-                ]
-                total = (terms[0] + terms[1]) + (terms[2] + terms[3])
-                row = qh * B + sp * 16
-                out_ref[c, row:row + 16, :] = total.astype(jnp.bfloat16)
+        scales = [scale_ref[d, pl.ds(c, 1), :] for d in range(4)]
+        for sp in range(4):
+            terms = [parts[d][c * 4 + sp].astype(jnp.float32) * scales[d] for d in range(4)]
+            total = (terms[0] + terms[1]) + (terms[2] + terms[3])
+            row = first_row + sp * 16
+            out_ref[c, row:row + 16, :] = total.astype(jnp.bfloat16)
         return carry
 
-    lax.fori_loop(0, NCOL, one, 0)
-
-
-def coarse_kernel(tgt_ref, at_ref, *refs):
-    parts, (p0_ref, p1_ref, p2_ref, p3_ref) = refs[:8], refs[8:12]
-    x_ref, keep_ref, send_ref, acc_ref, scale_ref = refs[12:]
+    lax.fori_loop(0, NCOL, one, 0, unroll=2)
+
+
+def add_terms(qh, tgt_ref, at_ref, x_ref, p_refs, acc_ref):
     dy = pl.program_id(0)
     low = low_lanes(8)
     low_x = low_lanes(B)
-    my_x, my_y, my_z, my_core = at_ref[0], at_ref[1], at_ref[2], at_ref[3]
-
-    @pl.when(dy == 0)
+    for dx, p_ref in enumerate(p_refs):
+        c = lax.rem(at_ref[1] - dy + 4, 4) * 4 + lax.rem(at_ref[0] - dx + 4, 4)
+        x = x_ref[c, qh * B:(qh + 1) * B, :]
+        none = jnp.zeros_like(x)
+        lhs = jnp.concatenate([jnp.where(low_x, x, none), jnp.where(low_x, none, x)], axis=0)
+        rhs = p_ref[0]
+        res = lax.dot_general(
+            lhs, rhs, (((1,), (0,)), ((), ())), preferred_element_type=jnp.float32
+        )
+        for lo in range(2):
+            ats, sums = [], []
+            for m in range(KP):
+                for s in range(KAP):
+                    at = tgt_ref[(((c * 2 + qh) * 2 + lo) * KP + m) * KAP + s]
+                    rows = (lo * KAP + s) * 8
+                    tile = res[rows:rows + 8, (m // 2) * 128:(m // 2) * 128 + 128]
+                    keep = low if m % 2 == 0 else jnp.logical_not(low)
+                    ats.append(at)
+                    sums.append(acc_ref[at] + jnp.where(keep, tile, 0.0))
+            for at, total in zip(ats, sums):
+                acc_ref[at] = total
+
+
+def first_coarse_kernel(tgt_ref, at_ref, *refs):
+    parts, p_refs, (x_ref, acc_ref, scale_ref) = refs[:4], refs[4:8], refs[8:]
+
+    @pl.when(pl.program_id(0) == 0)
     def _():
         acc_ref[...] = jnp.zeros_like(acc_ref)
-        decode(parts, x_ref, scale_ref)
-
-    for dx, p_ref in enumerate((p0_ref, p1_ref, p2_ref, p3_ref)):
-        c = lax.rem(my_y - dy + 4, 4) * 4 + lax.rem(my_x - dx + 4, 4)
-        for qh in range(2):
-            x = x_ref[c, qh * B:(qh + 1) * B, :]
-            none = jnp.zeros_like(x)
-            lhs = jnp.concatenate([jnp.where(low_x, x, none), jnp.where(low_x, none, x)], axis=0)
-            rhs = p_ref[0, qh * 2 * B:(qh + 1) * 2 * B, :]
-            res = lax.dot_general(
-                lhs, rhs, (((1,), (0,)), ((), ())), preferred_element_type=jnp.float32
-            )
-            for lo in range(2):
-                ats, sums = [], []
-                for m in range(KP):
-                    for s in range(KAP):
-                        at = tgt_ref[(((c * 2 + qh) * 2 + lo) * KP + m) * KAP + s]
-                        rows = (lo * KAP + s) * 8
-                        tile = res[rows:rows + 8, (m // 2) * 128:(m // 2) * 128 + 128]
-                        keep = low if m % 2 == 0 else jnp.logical_not(low)
-                        ats.append(at)
-                        sums.append(acc_ref[at] + jnp.where(keep, tile, 0.0))
-                for at, total in zip(ats, sums):
-                    acc_ref[at] = total
-
-    @pl.when(dy == 3)
+        decode(parts, x_ref, 0, scale_ref)
+
+    add_terms(0, tgt_ref, at_ref, x_ref, p_refs, acc_ref)
+
+
+def second_coarse_kernel(tgt_ref, at_ref, *refs):
+    parts, p_refs, (x0_ref, before_ref) = refs[:4], refs[4:8], refs[8:10]
+    x_ref, keep_ref, send_ref, acc_ref, scale_ref = refs[10:]
+    low = low_lanes(8)
+
+    @pl.when(pl.program_id(0) == 0)
+    def _():
+        acc_ref[...] = jnp.zeros_like(acc_ref)
+        decode(parts, x_ref, B, scale_ref)
+        x_ref[:, 0:B, :] = x0_ref[...]
+
+    add_terms(1, tgt_ref, at_ref, x_ref, p_refs, acc_ref)
+
+    @pl.when(pl.program_id(0) == 3)
     def _():
         for flip, out_ref in ((1, send_ref), (0, keep_ref)):
-            core = lax.rem(my_core + flip, 2)
+            core = lax.rem(at_ref[3] + flip, 2)
             for d in range(4):
-                first = (lax.rem(my_z + d, 4) * 2 + core) * NCOL
+                first = (lax.rem(at_ref[2] + d, 4) * 2 + core) * NCOL
 
                 def fold(col, carry):
                     for tp in range(KC // 2):
-                        t0 = acc_ref[(first + col) * KC + 2 * tp]
-                        t1 = acc_ref[(first + col) * KC + 2 * tp + 1]
+                        at = (first + col) * KC + 2 * tp
+                        t0 = acc_ref[at] + before_ref[at]
+                        t1 = acc_ref[at + 1] + before_ref[at + 1]
                         t0 = t0 + pltpu.roll(t0, B, 1)
                         t1 = t1 + pltpu.roll(t1, B, 1)
                         out_ref[d, col, tp] = jnp.where(low, t0, t1)
@@ -445,22 +458,54 @@
                 lax.fori_loop(0, NCOL, fold, 0, unroll=4)
 
 
-def coarse_terms(tgt, at, parts, ps):
-    shape = (4, NCOL, KC // 2, 8, 128)
-    out = pl.BlockSpec(shape, lambda dx, tgt, at: (0, 0, 0, 0, 0))
-    return pl.pallas_call(
-        coarse_kernel,
+def coarse_specs(qh):
+    whole = pl.BlockSpec((65, 16, 128), lambda dy, tgt, at: (0, 0, 0))
+    return [whole] * 4 + [
+        pl.BlockSpec((1, 2 * B, KP * B), lambda dy, tgt, at: (dy, qh, 0))
+    ] * 4
+
+
+def first_coarse(tgt, at, parts, ps):
+    return pl.pallas_call(
+        first_coarse_kernel,
         grid_spec=pltpu.PrefetchScalarGridSpec(
             num_scalar_prefetch=2,
             grid=(4,),
-            in_specs=[pl.BlockSpec((65, 16, 128), lambda dx, tgt, at: (0, 0, 0))] * 8
-            + [pl.BlockSpec((1, 4 * B + 16, KP * B), lambda dx, tgt, at: (dx, 0, 0))] * 4,
+            in_specs=coarse_specs(0),
             out_specs=[
-                pl.BlockSpec((NCOL, 3 * B, 128), lambda dx, tgt, at: (0, 0, 0)), out, out
+                pl.BlockSpec((NCOL, B, 128), lambda dy, tgt, at: (0, 0, 0)),
+                pl.BlockSpec((NCB * KC + 1, 8, 128), lambda dy, tgt, at: (0, 0, 0)),
+            ],
+            scratch_shapes=[pltpu.VMEM((4, NCOL, 128), jnp.float32)],
+        ),
+        out_shape=[
+            jax.ShapeDtypeStruct((NCOL, B, 128), jnp.bfloat16),
+            jax.ShapeDtypeStruct((NCB * KC + 1, 8, 128), jnp.float32),
+        ],
+        name="first_coarse",
+        compiler_params=pltpu.CompilerParams(vmem_limit_bytes=32 * 1024 * 1024),
+    )(tgt, at, *parts, *ps)
+
+
+def second_coarse(tgt, at, parts, ps, x0, before):
+    shape = (4, NCOL, KC // 2, 8, 128)
+    out = pl.BlockSpec(shape, lambda dy, tgt, at: (0, 0, 0, 0, 0))
+    return pl.pallas_call(
+        second_coarse_kernel,
+        grid_spec=pltpu.PrefetchScalarGridSpec(
+            num_scalar_prefetch=2,
+            grid=(4,),
+            in_specs=coarse_specs(1)
+            + [
+                pl.BlockSpec((NCOL, B, 128), lambda dy, tgt, at: (0, 0, 0)),
+                pl.BlockSpec(memory_space=pltpu.VMEM),
+            ],
+            out_specs=[
+                pl.BlockSpec((NCOL, 3 * B, 128), lambda dy, tgt, at: (0, 0, 0)), out, out
             ],
             scratch_shapes=[
                 pltpu.VMEM((NCB * KC + 1, 8, 128), jnp.float32),
-                pltpu.VMEM((8, NCOL, 128), jnp.float32),
+                pltpu.VMEM((4, NCOL, 128), jnp.float32),
             ],
         ),
         out_shape=[
@@ -468,8 +513,9 @@
             jax.ShapeDtypeStruct(shape, jnp.float32),
             jax.ShapeDtypeStruct(shape, jnp.float32),
         ],
-        name="coarse_terms",
-    )(tgt, at, *parts, *ps)
+        name="second_coarse",
+        compiler_params=pltpu.CompilerParams(vmem_limit_bytes=32 * 1024 * 1024),
+    )(tgt, at, *parts, *ps, x0, pltpu.with_memory_space_constraint(before, pltpu.VMEM))
 
 
 def layout_kernel(x_ref, ap_ref, coarse_ref, turn_ref, wide_ref, flat_ref):
@@ -588,7 +634,8 @@
     s0 = middle(x_middle_kernel, at, [x0, got_x1, got_x2, got_x3])
     y_last = [along_col(s0[d], 0, d) for d in (1, 2, 3)]
     s1 = middle(y_middle_kernel, at, [ya[0], *got_ya, yb[0], *got_yb])
-    x_last = [along_col(s1[d], d, 0) for d in (1, 2, 3)]
+    far = along_col(s1[2], 2, 0)
+    x_last = [along_col(s1[1], 1, 0), far, along_col(s1[3], 3, 0)]
 
     by_y = jnp.stack(by_y)
     same = lax.dynamic_index_in_dim(by_y, half, 1, keepdims=False)
@@ -607,7 +654,8 @@
     slot = cols_i[:, :, :, None, None] * KC + jnp.arange(KC, dtype=jnp.int32)
     tgt = jnp.min(jnp.where(hit, slot, NCB * KC), axis=4).reshape(-1)
 
-    apt, keep, send = coarse_terms(tgt, at, [s0[0], *y_last, s1[0], *x_last], ps)
+    x0, before = first_coarse(tgt, at, [s0[0], *y_last], ps)
+    apt, keep, send = second_coarse(tgt, at, [s1[0], *x_last], ps, x0, before)
     got = along_row(send, 0, 1)
     sums = [keep[d] + got[d] for d in range(4)]
     coarse = sums[0]

time: 236 us -> 240 us (1.017)
  waiting for transfers between devices: 87 us -> 93.6 us
  local copies, waits for them, and re-layouts: 16.9 us -> 13.5 us
    ppermute x21, waiting for transfers between devices: 64.4 us -> 68.5 us  [along_col(): return lax.ppermute(v, 'col', pairs)]
    ppermute x21, starting transfers between devices: 27.7 us -> 30.6 us  [along_col(): return lax.ppermute(v, 'col', pairs)]
    another operation x4, local copies, waits for them, and re-layouts: 2.8 us -> 0.02 us  [step(): jnp.stack([p[:, 4 * B:4 * B + 4, :KP] for p in ps]).reshape(NCOL, 16)]
    ppermute x11, waiting for transfers between devices: 22.6 us -> 25.2 us  [along_row(): return lax.ppermute(v, 'row', pairs)]
    pallas_call x1 -> x2, Pallas kernels: 12.6 us -> 11.4 us  [the longest x1 6.93 us: second_coarse(): pl.pallas_call(second_coarse_kernel, grid_spec=pltpu.PrefetchScalarGridSp...]
    unnamed x34 -> x28, local copies, waits for them, and re-layouts: 7.33 us -> 7.6 us
  transfers between devices with their start and end apart: 32 -> 32, of which waited for: 14 -> 12; matrix products, arithmetic and copies ran while one was open for 4% -> 3% of each run, Pallas kernels for 22% -> 24%
where the time goes in v5:
time: 240 us; the launch traced here: 239 us
  waiting for transfers between devices  93.6 us (39%)
  Pallas kernels  67.1 us (28%)
  starting transfers between devices  41.6 us (17%)
  blocking collectives  19 us (8%)
  local copies, waits for them, and re-layouts  13.5 us (6%)
  other arithmetic  2.78 us (1%)
    ppermute x21, waiting for transfers between devices, along_col(): return lax.ppermute(v, 'col', pairs)  68.5 us
    ppermute x21, starting transfers between devices, along_col(): return lax.ppermute(v, 'col', pairs)  30.6 us
    ppermute x11, waiting for transfers between devices, along_row(): return lax.ppermute(v, 'row', pairs)  25.2 us
    all_to_all x1, blocking collectives, step(): both = lax.all_to_all(both, 'col', 0, 0, tiled=True)  19 us
    pallas_call x2, Pallas kernels, x_products(): pl.pallas_call(lambda *refs: x_product_kernel(j, *refs), grid_spec=pltpu....  14.8 us
    pallas_call x2, Pallas kernels, y_products(): pl.pallas_call(lambda *refs: y_product_kernel(part, *refs), grid_spec=plt...  14.6 us
    ppermute x11, starting transfers between devices, along_row(): return lax.ppermute(v, 'row', pairs)  11 us
    pallas_call x2, Pallas kernels, middle(): pl.pallas_call(kernel, in_specs=[pl.BlockSpec(memory_space=pltpu.SMEM)] +...  10.4 us
  transfers between devices with their start and end apart: 32, of which 12 were waited for; matrix products, arithmetic and copies ran while one was open for 3% of the time, Pallas kernels for 24%

profile of v5, /device:TPU:0, one launch (start us, length us, event | category | flops | bytes accessed | tf_op | source)
XLA Modules:
  0.0 239.4 jit_solution(12151008379743247220)
XLA Ops:
  0.6 0.7 convert_bitcast_fusion
  1.4 1.4 reshape_squeeze.3
  2.9 0.3 copy.61
  3.2 0.3 reshape.302
  3.5 2.1 collective-permute-start
  5.6 3.6 %collective-permute-start.1 = (bf16[528,256]{1,0:T(8,128)(2,1)S(1)}, bf16[528,256]{1,0:T(8,128)(2,1)S(1)}, u32[]{:S(2)}, u32[]{:S(2)}) collective-permute-start(bf16[528,256]{1,0:T(8,128)(2,1)S(1)} %fusion.3.refs_0_), channel_id=1, source_target_pairs={{0,64},{16,80},{32,96},{48,112},{64,0},{80,16},{96,32},{112,48},{1... | collective-permute-start | bytes 811016 | tf_op jit(solution)/shard_map/ppermute | solution.py:23
  9.2 1.0 collective-permute-start.2
  10.3 0.4 reshape_reshape_squeeze.3
  10.9 0.4 fusion.44
  12.4 1.8 collective-permute-done.refs_2_
  14.2 7.0 %collective-permute-done.1.refs_4_ = bf16[528,256]{1,0:T(8,128)(2,1)S(1)} collective-permute-done((bf16[528,256]{1,0:T(8,128)(2,1)S(1)}, bf16[528,256]{1,0:T(8,128)(2,1)S(1)}, u32[]{:S(2)}, u32[]{:S(2)}) %collective-permute-start.1) | collective-permute-done | bytes 270368 | tf_op jit(solution)/shard_map/ppermute | solution.py:23
  21.2 0.5 collective-permute-start.11
  21.8 8.4 %spread.1 = bf16[128,64,256]{2,1,0:T(8,128)(2,1)} custom-call(bf16[128,4,4096]{2,1,0:T(4,128)(2,1)} %bitcast.101), custom_call_target="tpu_custom_call" | custom-call | tf_op jit(solution)/shard_map/spread/pallas_call | solution.py:59
  30.2 3.1 %collective-permute-start.5 = (bf16[2,272,256]{2,1,0:T(8,128)(2,1)S(1)}, bf16[2,272,256]{2,1,0:T(8,128)(2,1)}, u32[]{:S(2)}, u32[]{:S(2)}) collective-permute-start(bf16[2,272,256]{2,1,0:T(8,128)(2,1)S(1)} %pad_maximum_fusion.1), channel_id=1, source_target_pairs={{0,12},{1,13},{2,14},{3,15},{4,0},{5,1},{6,2},{7,3},{8,4},{9,5},{1... | collective-permute-start | bytes 835592 | tf_op jit(solution)/shard_map/ppermute | solution.py:28
  33.3 0.6 collective-permute-start.4
  33.9 1.0 collective-permute-start.3
  34.9 4.9 %table.1 = (bf16[257,64,128]{2,1,0:T(8,128)(2,1)}, f32[64,128]{1,0:T(8,128)S(1)}) custom-call(bf16[528,256]{1,0:T(8,128)(2,1)S(1)} %fusion.3.refs_0_, bf16[528,256]{1,0:T(8,128)(2,1)S(1)} %collective-permute-done.9.refs_1_, bf16[528,256]{1,0:T(8,128)(2,1)S(1)} %collective-permute-done.refs_2_, bf16[528,256]{1,0:T(8,128)(2,1)S(1)} %collective-permute-done.10.refs_3_, ...), custom_call_target="tpu_custom_call" | custom-call | tf_op jit(solution)/shard_map/table/pallas_call | solution.py:92
  40.1 0.2 reshape.306.refs_0_
  40.3 2.2 copy-done
  42.5 7.2 %shard_map.77 = (s16[129,16,128]{2,1,0:T(8,128)(2,1)}, s16[129,16,128]{2,1,0:T(8,128)(2,1)S(1)}, s16[129,16,128]{2,1,0:T(8,128)(2,1)S(1)}, s16[129,16,128]{2,1,0:T(8,128)(2,1)S(1)}) custom-call(s32[4096]{0:T(1024)S(1)} %reshape.306.refs_0_, s32[4]{0:T(128)S(1)} %pad_add_fusion.refs_1_.at_ref, bf16[4,2,16,64,256]{4,3,2,1,0:T(8,128)(2,1)} %bitcast.97, ...), custom_call_target="tpu_custom_call" | custom-call | tf_op jit(solution)/shard_map/pallas_call | solution.py:272
  49.7 1.9 collective-permute-start.13
  51.6 1.8 collective-permute-start.14
  53.4 0.9 collective-permute-start.15
  54.3 1.3 pad_maximum_fusion
  55.5 0.9 dynamic-slice_bitcast_fusion.1
  56.4 2.8 %collective-permute-start.8 = (bf16[4,272,256]{2,1,0:T(8,128)(2,1)}, bf16[4,272,256]{2,1,0:T(8,128)(2,1)S(1)}, u32[]{:S(2)}, u32[]{:S(2)}) collective-permute-start(bf16[4,272,256]{2,1,0:T(8,128)(2,1)} %get-tuple-element.86), channel_id=1, source_target_pairs={{0,3},{1,0},{2,1},{3,2},{4,7},{5,4},{6,5},{7,6},{8,11},{9,8},{10,9... | collective-permute-start | bytes 1671176 | tf_op jit(solution)/shard_map/ppermute | solution.py:28
  59.2 2.2 copy-done.1
  61.4 7.5 %shard_map.78 = (s16[129,16,128]{2,1,0:T(8,128)(2,1)}, s16[129,16,128]{2,1,0:T(8,128)(2,1)}, s16[129,16,128]{2,1,0:T(8,128)(2,1)}, s16[129,16,128]{2,1,0:T(8,128)(2,1)S(1)}) custom-call(s32[4096]{0:T(1024)S(1)} %reshape.306.refs_0_, s32[4]{0:T(128)S(1)} %pad_add_fusion.refs_1_.at_ref, bf16[4,2,16,64,256]{4,3,2,1,0:T(8,128)(2,1)} %bitcast.98, ...), custom_call_target="tpu_custom_call" | custom-call | tf_op jit(solution)/shard_map/pallas_call | solution.py:272
  68.8 1.2 collective-permute-start.16
  70.0 1.7 collective-permute-start.17
  71.7 6.0 %collective-permute-done.14.refs_2_ = s16[129,16,128]{2,1,0:T(8,128)(2,1)} collective-permute-done((s16[129,16,128]{2,1,0:T(8,128)(2,1)S(1)}, s16[129,16,128]{2,1,0:T(8,128)(2,1)}, u32[]{:S(2)}, u32[]{:S(2)}) %collective-permute-start.14) | collective-permute-done | bytes 528416 | tf_op jit(solution)/shard_map/ppermute | solution.py:28
  77.9 0.2 collective-permute-done.15.refs_3_
  78.1 3.0 %collective-permute-start.7 = (bf16[4,272,256]{2,1,0:T(8,128)(2,1)S(1)}, bf16[4,272,256]{2,1,0:T(8,128)(2,1)S(1)}, u32[]{:S(2)}, u32[]{:S(2)}) collective-permute-start(bf16[4,272,256]{2,1,0:T(8,128)(2,1)S(1)} %get-tuple-element.85.refs_4_), channel_id=1, source_target_pairs={{0,2},{1,3},{2,0},{3,1},{4,6},{5,7},{6,4},{7,5},{8,10},{9,11},{10,... | collective-permute-start | bytes 1671176 | tf_op jit(solution)/shard_map/ppermute | solution.py:28
  81.2 2.2 copy-done.2
  83.4 7.4 %shard_map.80 = (s16[257,16,128]{2,1,0:T(8,128)(2,1)}, s16[257,16,128]{2,1,0:T(8,128)(2,1)}) custom-call(s32[4096]{0:T(1024)S(1)} %reshape.306.refs_0_, s32[4]{0:T(128)S(1)} %pad_add_fusion.refs_1_.at_ref, bf16[4,2,16,64,256]{4,3,2,1,0:T(8,128)(2,1)} %bitcast.99, bf16[257,64,128]{2,1,0:T(8,128)(2,1)S(1)} %copy-done.2), custom_call_target="tpu_custom_call" | custom-call | tf_op jit(solution)/shard_map/pallas_call | solution.py:205
  90.8 7.4 %shard_map.81 = (s16[257,16,128]{2,1,0:T(8,128)(2,1)}, s16[257,16,128]{2,1,0:T(8,128)(2,1)}) custom-call(s32[4096]{0:T(1024)S(1)} %reshape.306.refs_0_, s32[4]{0:T(128)S(1)} %pad_add_fusion.refs_1_.at_ref, bf16[4,2,16,64,256]{4,3,2,1,0:T(8,128)(2,1)} %bitcast.100, bf16[257,64,128]{2,1,0:T(8,128)(2,1)S(1)} %copy-done.2), custom_call_target="tpu_custom_call" | custom-call | tf_op jit(solution)/shard_map/pallas_call | solution.py:205
  98.2 0.6 collective-permute-start.22
  99.0 3.0 %collective-permute-start.23 = (s16[257,16,128]{2,1,0:T(8,128)(2,1)}, s16[257,16,128]{2,1,0:T(8,128)(2,1)}, u32[]{:S(2)}, u32[]{:S(2)}) collective-permute-start(s16[257,16,128]{2,1,0:T(8,128)(2,1)} %get-tuple-element.57), channel_id=1, source_target_pairs={{0,2},{1,3},{2,0},{3,1},{4,6},{5,7},{6,4},{7,5},{8,10},{9,11},{10,... | collective-permute-start | bytes 3158024 | tf_op jit(solution)/shard_map/ppermute | solution.py:28
  102.0 1.1 collective-permute-start.24
  103.2 1.0 collective-permute-start.6
  104.1 5.2 %shard_map.79 = (s16[65,16,128]{2,1,0:T(8,128)(2,1)}, s16[65,16,128]{2,1,0:T(8,128)(2,1)}, s16[65,16,128]{2,1,0:T(8,128)(2,1)}, s16[65,16,128]{2,1,0:T(8,128)(2,1)}) custom-call(s32[4]{0:T(128)} %copy-done.5, s16[129,16,128]{2,1,0:T(8,128)(2,1)} %get-tuple-element.43.refs_0_, s16[129,16,128]{2,1,0:T(8,128)(2,1)} %collective-permute-done.13.refs_1_, ...), custom_call_target="tpu_custom_call" | custom-call | tf_op jit(solution)/shard_map/pallas_call | solution.py:362
  109.3 0.7 collective-permute-start.19
  110.0 50.8 %collective-permute-done.6.refs_5_ = bf16[4,272,256]{2,1,0:T(8,128)(2,1)S(1)} collective-permute-done((bf16[4,272,256]{2,1,0:T(8,128)(2,1)}, bf16[4,272,256]{2,1,0:T(8,128)(2,1)S(1)}, u32[]{:S(2)}, u32[]{:S(2)}) %collective-permute-start.6) | collective-permute-done | bytes 557088 | tf_op jit(solution)/shard_map/ppermute | solution.py:28
  161.2 1.5 collective-permute-start.21
  162.8 5.2 %shard_map.82 = (s16[65,16,128]{2,1,0:T(8,128)(2,1)}, s16[65,16,128]{2,1,0:T(8,128)(2,1)}, s16[65,16,128]{2,1,0:T(8,128)(2,1)}, s16[65,16,128]{2,1,0:T(8,128)(2,1)}) custom-call(s32[4]{0:T(128)} %copy-done.5, s16[257,16,128]{2,1,0:T(8,128)(2,1)} %get-tuple-element.55.m0, s16[257,16,128]{2,1,0:T(8,128)(2,1)} %collective-permute-done.22.m1, ...), custom_call_target="tpu_custom_call" | custom-call | tf_op jit(solution)/shard_map/pallas_call | solution.py:362
  168.0 2.0 collective-permute-start.25
  170.0 0.3 convolution_convert_fusion
  170.3 2.2 collective-permute-start.26
  172.5 5.5 %collective-permute-done.25.refs_1_ = s16[65,16,128]{2,1,0:T(8,128)(2,1)S(1)} collective-permute-done((s16[65,16,128]{2,1,0:T(8,128)(2,1)}, s16[65,16,128]{2,1,0:T(8,128)(2,1)S(1)}, u32[]{:S(2)}, u32[]{:S(2)}) %collective-permute-start.25) | collective-permute-done | bytes 266272 | tf_op jit(solution)/shard_map/ppermute | solution.py:28
  178.1 0.6 collective-permute-start.27
  178.6 0.2 select_reduce_fusion
  179.2 1.8 collective-permute-done.26.refs_2_
  181.0 3.8 %collective-permute-done.27.refs_3_ = s16[65,16,128]{2,1,0:T(8,128)(2,1)} collective-permute-done((s16[65,16,128]{2,1,0:T(8,128)(2,1)}, s16[65,16,128]{2,1,0:T(8,128)(2,1)}, u32[]{:S(2)}, u32[]{:S(2)}) %collective-permute-start.27) | collective-permute-done | bytes 266272 | tf_op jit(solution)/shard_map/ppermute | solution.py:28
  184.8 1.0 copy-done.4
  185.8 4.5 %first_coarse.1 = (bf16[16,64,128]{2,1,0:T(8,128)(2,1)S(1)}, f32[1025,8,128]{2,1,0:T(8,128)S(1)}) custom-call(s32[2048]{0:T(1024)S(1)} %reshape.305.tgt_ref, s32[4]{0:T(128)S(1)} %copy-done.6, s16[65,16,128]{2,1,0:T(8,128)(2,1)S(1)} %copy-done.4, s16[65,16,128]{2,1,0:T(8,128)(2,1)S(1)} %collective-permute-done.25.refs_1_, ...), custom_call_target="tpu_custom_call" | custom-call | tf_op jit(solution)/shard_map/first_coarse/pallas_call | solution.py:469
  190.3 6.9 %second_coarse.1 = (bf16[16,192,128]{2,1,0:T(8,128)(2,1)S(1)}, f32[4,16,4,8,128]{4,3,2,1,0:T(8,128)S(1)}, f32[4,16,4,8,128]{4,3,2,1,0:T(8,128)S(1)}) custom-call(s32[2048]{0:T(1024)S(1)} %reshape.305.tgt_ref, s32[4]{0:T(128)S(1)} %copy-done.6, s16[65,16,128]{2,1,0:T(8,128)(2,1)S(1)} %copy-done.3, s16[65,16,128]{2,1,0:T(8,128)(2,1)S(1)} %collective-permute-done.19.refs_1_, ...), custom_call_target="tpu_custom_call" | custom-call | tf_op jit(solution)/shard_map/second_coarse/pallas_call | solution.py:493
  197.3 2.6 %collective-permute-done.28 = f32[4,16,4,8,128]{4,3,2,1,0:T(8,128)S(1)} collective-permute-done((f32[4,16,4,8,128]{4,3,2,1,0:T(8,128)S(1)}, f32[4,16,4,8,128]{4,3,2,1,0:T(8,128)S(1)}, u32[]{:S(2)}, u32[]{:S(2)}) %collective-permute-start.28) | collective-permute-done | bytes 1048608 | tf_op jit(solution)/shard_map/ppermute | solution.py:23
  200.1 2.3 collective-permute-start.31
  202.4 1.1 collective-permute-start.30
  203.5 0.4 collective-permute-start.29
  203.8 10.0 %collective-permute-done.31 = f32[16,4,8,128]{3,2,1,0:T(8,128)S(1)} collective-permute-done((f32[16,4,8,128]{3,2,1,0:T(8,128)S(1)}, f32[16,4,8,128]{3,2,1,0:T(8,128)S(1)}, u32[]{:S(2)}, u32[]{:S(2)}) %collective-permute-start.31) | collective-permute-done | bytes 262176 | tf_op jit(solution)/shard_map/ppermute | solution.py:23
  213.9 3.7 %collective-permute-done.29 = f32[16,4,8,128]{3,2,1,0:T(8,128)S(1)} collective-permute-done((f32[16,4,8,128]{3,2,1,0:T(8,128)S(1)}, f32[16,4,8,128]{3,2,1,0:T(8,128)S(1)}, u32[]{:S(2)}, u32[]{:S(2)}) %collective-permute-start.29) | collective-permute-done | bytes 262176 | tf_op jit(solution)/shard_map/ppermute | solution.py:23
  217.8 19.0 %all_to_all.5.x_ref = bf16[16,192,128]{2,1,0:T(8,128)(2,1)} all-to-all(bf16[16,192,128]{2,1,0:T(8,128)(2,1)S(1)} %maximum_dynamic-update-slice_fusion), channel_id=1, replica_groups=mesh['row'=8,'col'=16] {'col'}, dimensions={0} | all-to-all | bytes 1572864 | tf_op jit(solution)/shard_map/all_to_all | solution.py:670
  236.8 2.6 %layout.1 = (bf16[8,8,4096]{2,1,0:T(8,128)(2,1)}, f32[8,4096]{1,0:T(8,128)}) custom-call(bf16[16,192,128]{2,1,0:T(8,128)(2,1)} %all_to_all.5.x_ref), custom_call_target="tpu_custom_call" | custom-call | tf_op jit(solution)/shard_map/layout/pallas_call | solution.py:558
  (89 shorter events, 3.3 us)
Async XLA Ops:
  2.8 7.4 %copy-start.11 = (s32[8,1,4]{0,2,1:T(4,128)S(1)}, s32[8,1,4]{0,2,1:T(4,128)}, u32[]{:S(2)}) copy-start(s32[8,1,4]{0,2,1:T(4,128)} %param.9) | copy-start | bytes 388
  2.8 7.4 %copy-start.7 = (bf16[8,1,4,4096]{3,2,1,0:T(4,128)(2,1)S(1)}, bf16[8,1,4,4096]{3,2,1,0:T(4,128)(2,1)}, u32[]{:S(2)}) copy-start(bf16[8,1,4,4096]{3,2,1,0:T(4,128)(2,1)} %param.8) | copy-start | bytes 786436
  3.5 10.7 %collective-permute-start = (bf16[528,256]{1,0:T(8,128)(2,1)S(1)}, bf16[528,256]{1,0:T(8,128)(2,1)S(1)}, u32[]{:S(2)}, u32[]{:S(2)}) collective-permute-start(bf16[528,256]{1,0:T(8,128)(2,1)S(1)} %fusion.3.refs_0_), channel_id=1, source_target_pairs={{0,32},{16,48},{32,64},{48,80},{64,96},{80,112},{96,0},{112,16},{1... | collective-permute-start | bytes 811016 | tf_op jit(solution)/shard_map/ppermute | solution.py:23
  5.6 15.6 %collective-permute-start.1 = (bf16[528,256]{1,0:T(8,128)(2,1)S(1)}, bf16[528,256]{1,0:T(8,128)(2,1)S(1)}, u32[]{:S(2)}, u32[]{:S(2)}) collective-permute-start(bf16[528,256]{1,0:T(8,128)(2,1)S(1)} %fusion.3.refs_0_), channel_id=1, source_target_pairs={{0,64},{16,80},{32,96},{48,112},{64,0},{80,16},{96,32},{112,48},{1... | collective-permute-start | bytes 811016 | tf_op jit(solution)/shard_map/ppermute | solution.py:23
  9.2 12.0 %collective-permute-start.2 = (bf16[528,256]{1,0:T(8,128)(2,1)S(1)}, bf16[528,256]{1,0:T(8,128)(2,1)S(1)}, u32[]{:S(2)}, u32[]{:S(2)}) collective-permute-start(bf16[528,256]{1,0:T(8,128)(2,1)S(1)} %fusion.3.refs_0_), channel_id=1, source_target_pairs={{0,96},{16,112},{32,0},{48,16},{64,32},{80,48},{96,64},{112,80},{1... | collective-permute-start | bytes 811016 | tf_op jit(solution)/shard_map/ppermute | solution.py:23
  10.2 23.0 %collective-permute-start.9 = (bf16[528,256]{1,0:T(8,128)(2,1)S(1)}, bf16[528,256]{1,0:T(8,128)(2,1)S(1)}, u32[]{:S(2)}, u32[]{:S(2)}) collective-permute-start(bf16[528,256]{1,0:T(8,128)(2,1)S(1)} %fusion.3.refs_0_), channel_id=1, source_target_pairs={{0,16},{16,0},{32,48},{48,32},{64,80},{80,64},{96,112},{112,96},{1... | collective-permute-start | bytes 811016 | tf_op jit(solution)/shard_map/ppermute | solution.py:23
  11.7 0.7 copy-start.12
  21.2 12.7 %collective-permute-start.10 = (bf16[528,256]{1,0:T(8,128)(2,1)S(1)}, bf16[528,256]{1,0:T(8,128)(2,1)S(1)}, u32[]{:S(2)}, u32[]{:S(2)}) collective-permute-start(bf16[528,256]{1,0:T(8,128)(2,1)S(1)} %collective-permute-done.refs_2_), channel_id=1, source_target_pairs={{0,16},{16,0},{32,48},{48,32},{64,80},{80,64},{96,112},{112,96},{1... | collective-permute-start | bytes 811016 | tf_op jit(solution)/shard_map/ppermute | solution.py:23
  21.2 13.7 %collective-permute-start.11 = (bf16[528,256]{1,0:T(8,128)(2,1)S(1)}, bf16[528,256]{1,0:T(8,128)(2,1)S(1)}, u32[]{:S(2)}, u32[]{:S(2)}) collective-permute-start(bf16[528,256]{1,0:T(8,128)(2,1)S(1)} %collective-permute-done.1.refs_4_), channel_id=1, source_target_pairs={{0,16},{16,0},{32,48},{48,32},{64,80},{80,64},{96,112},{112,96},{1... | collective-permute-start | bytes 811016 | tf_op jit(solution)/shard_map/ppermute | solution.py:23
  21.7 13.1 %collective-permute-start.12 = (bf16[528,256]{1,0:T(8,128)(2,1)S(1)}, bf16[528,256]{1,0:T(8,128)(2,1)S(1)}, u32[]{:S(2)}, u32[]{:S(2)}) collective-permute-start(bf16[528,256]{1,0:T(8,128)(2,1)S(1)} %collective-permute-done.2.refs_6_), channel_id=1, source_target_pairs={{0,16},{16,0},{32,48},{48,32},{64,80},{80,64},{96,112},{112,96},{1... | collective-permute-start | bytes 811016 | tf_op jit(solution)/shard_map/ppermute | solution.py:23
  21.8 69.0 %copy-start.5 = (s32[4]{0:T(128)}, s32[4]{0:T(128)S(1)}, u32[]{:S(2)}) copy-start(s32[4]{0:T(128)S(1)} %pad_add_fusion.refs_1_.at_ref) | copy-start | bytes 52
  30.2 9.7 %copy-start.10 = (s32[128,8]{0,1:T(8,128)S(1)}, s32[128,8]{0,1:T(8,128)}, u32[]{:S(2)}) copy-start(s32[128,8]{0,1:T(8,128)} %param.10) | copy-start | bytes 12292
  30.2 23.2 %collective-permute-start.5 = (bf16[2,272,256]{2,1,0:T(8,128)(2,1)S(1)}, bf16[2,272,256]{2,1,0:T(8,128)(2,1)}, u32[]{:S(2)}, u32[]{:S(2)}) collective-permute-start(bf16[2,272,256]{2,1,0:T(8,128)(2,1)S(1)} %pad_maximum_fusion.1), channel_id=1, source_target_pairs={{0,12},{1,13},{2,14},{3,15},{4,0},{5,1},{6,2},{7,3},{8,4},{9,5},{1... | collective-permute-start | bytes 835592 | tf_op jit(solution)/shard_map/ppermute | solution.py:28
  33.3 21.0 %collective-permute-start.4 = (bf16[2,272,256]{2,1,0:T(8,128)(2,1)S(1)}, bf16[2,272,256]{2,1,0:T(8,128)(2,1)}, u32[]{:S(2)}, u32[]{:S(2)}) collective-permute-start(bf16[2,272,256]{2,1,0:T(8,128)(2,1)S(1)} %pad_maximum_fusion.1), channel_id=1, source_target_pairs={{0,8},{1,9},{2,10},{3,11},{4,12},{5,13},{6,14},{7,15},{8,0},{9,1},... | collective-permute-start | bytes 835592 | tf_op jit(solution)/shard_map/ppermute | solution.py:28
  33.9 20.4 %collective-permute-start.3 = (bf16[2,272,256]{2,1,0:T(8,128)(2,1)S(1)}, bf16[2,272,256]{2,1,0:T(8,128)(2,1)}, u32[]{:S(2)}, u32[]{:S(2)}) collective-permute-start(bf16[2,272,256]{2,1,0:T(8,128)(2,1)S(1)} %pad_maximum_fusion.1), channel_id=1, source_target_pairs={{0,4},{1,5},{2,6},{3,7},{4,8},{5,9},{6,10},{7,11},{8,12},{9,13},{1... | collective-permute-start | bytes 835592 | tf_op jit(solution)/shard_map/ppermute | solution.py:28
  40.3 2.2 copy-start
  49.7 20.3 %collective-permute-start.13 = (s16[129,16,128]{2,1,0:T(8,128)(2,1)S(1)}, s16[129,16,128]{2,1,0:T(8,128)(2,1)}, u32[]{:S(2)}, u32[]{:S(2)}) collective-permute-start(s16[129,16,128]{2,1,0:T(8,128)(2,1)S(1)} %get-tuple-element.44), channel_id=1, source_target_pairs={{0,4},{1,5},{2,6},{3,7},{4,8},{5,9},{6,10},{7,11},{8,12},{9,13},{1... | collective-permute-start | bytes 1585160 | tf_op jit(solution)/shard_map/ppermute | solution.py:28
  51.6 26.2 %collective-permute-start.14 = (s16[129,16,128]{2,1,0:T(8,128)(2,1)S(1)}, s16[129,16,128]{2,1,0:T(8,128)(2,1)}, u32[]{:S(2)}, u32[]{:S(2)}) collective-permute-start(s16[129,16,128]{2,1,0:T(8,128)(2,1)S(1)} %get-tuple-element.45), channel_id=1, source_target_pairs={{0,8},{1,9},{2,10},{3,11},{4,12},{5,13},{6,14},{7,15},{8,0},{9,1},... | collective-permute-start | bytes 1585160 | tf_op jit(solution)/shard_map/ppermute | solution.py:28
  53.4 24.7 %collective-permute-start.15 = (s16[129,16,128]{2,1,0:T(8,128)(2,1)S(1)}, s16[129,16,128]{2,1,0:T(8,128)(2,1)}, u32[]{:S(2)}, u32[]{:S(2)}) collective-permute-start(s16[129,16,128]{2,1,0:T(8,128)(2,1)S(1)} %get-tuple-element.46), channel_id=1, source_target_pairs={{0,12},{1,13},{2,14},{3,15},{4,0},{5,1},{6,2},{7,3},{8,4},{9,5},{1... | collective-permute-start | bytes 1585160 | tf_op jit(solution)/shard_map/ppermute | solution.py:28
  56.4 46.7 %collective-permute-start.8 = (bf16[4,272,256]{2,1,0:T(8,128)(2,1)}, bf16[4,272,256]{2,1,0:T(8,128)(2,1)S(1)}, u32[]{:S(2)}, u32[]{:S(2)}) collective-permute-start(bf16[4,272,256]{2,1,0:T(8,128)(2,1)} %get-tuple-element.86), channel_id=1, source_target_pairs={{0,3},{1,0},{2,1},{3,2},{4,7},{5,4},{6,5},{7,6},{8,11},{9,8},{10,9... | collective-permute-start | bytes 1671176 | tf_op jit(solution)/shard_map/ppermute | solution.py:28
  59.2 2.2 copy-start.1
  68.8 29.4 %collective-permute-start.16 = (s16[129,16,128]{2,1,0:T(8,128)(2,1)}, s16[129,16,128]{2,1,0:T(8,128)(2,1)}, u32[]{:S(2)}, u32[]{:S(2)}) collective-permute-start(s16[129,16,128]{2,1,0:T(8,128)(2,1)} %get-tuple-element.48), channel_id=1, source_target_pairs={{0,4},{1,5},{2,6},{3,7},{4,8},{5,9},{6,10},{7,11},{8,12},{9,13},{1... | collective-permute-start | bytes 1585160 | tf_op jit(solution)/shard_map/ppermute | solution.py:28
  70.0 29.0 %collective-permute-start.17 = (s16[129,16,128]{2,1,0:T(8,128)(2,1)}, s16[129,16,128]{2,1,0:T(8,128)(2,1)S(1)}, u32[]{:S(2)}, u32[]{:S(2)}) collective-permute-start(s16[129,16,128]{2,1,0:T(8,128)(2,1)} %get-tuple-element.49), channel_id=1, source_target_pairs={{0,8},{1,9},{2,10},{3,11},{4,12},{5,13},{6,14},{7,15},{8,0},{9,1},... | collective-permute-start | bytes 1585160 | tf_op jit(solution)/shard_map/ppermute | solution.py:28
  77.7 24.3 %collective-permute-start.18 = (s16[129,16,128]{2,1,0:T(8,128)(2,1)S(1)}, s16[129,16,128]{2,1,0:T(8,128)(2,1)S(1)}, u32[]{:S(2)}, u32[]{:S(2)}) collective-permute-start(s16[129,16,128]{2,1,0:T(8,128)(2,1)S(1)} %get-tuple-element.50), channel_id=1, source_target_pairs={{0,12},{1,13},{2,14},{3,15},{4,0},{5,1},{6,2},{7,3},{8,4},{9,5},{1... | collective-permute-start | bytes 1585160 | tf_op jit(solution)/shard_map/ppermute | solution.py:28
  78.1 31.2 %collective-permute-start.7 = (bf16[4,272,256]{2,1,0:T(8,128)(2,1)S(1)}, bf16[4,272,256]{2,1,0:T(8,128)(2,1)S(1)}, u32[]{:S(2)}, u32[]{:S(2)}) collective-permute-start(bf16[4,272,256]{2,1,0:T(8,128)(2,1)S(1)} %get-tuple-element.85.refs_4_), channel_id=1, source_target_pairs={{0,2},{1,3},{2,0},{3,1},{4,6},{5,7},{6,4},{7,5},{8,10},{9,11},{10,... | collective-permute-start | bytes 1671176 | tf_op jit(solution)/shard_map/ppermute | solution.py:28
  81.2 2.2 copy-start.2
  98.2 63.0 %collective-permute-start.22 = (s16[257,16,128]{2,1,0:T(8,128)(2,1)}, s16[257,16,128]{2,1,0:T(8,128)(2,1)}, u32[]{:S(2)}, u32[]{:S(2)}) collective-permute-start(s16[257,16,128]{2,1,0:T(8,128)(2,1)} %get-tuple-element.56), channel_id=1, source_target_pairs={{0,1},{1,2},{2,3},{3,0},{4,5},{5,6},{6,7},{7,4},{8,9},{9,10},{10,1... | collective-permute-start | bytes 3158024 | tf_op jit(solution)/shard_map/ppermute | solution.py:28
  99.0 4.2 %copy-start.8 = (s16[129,16,128]{2,1,0:T(8,128)(2,1)}, s16[129,16,128]{2,1,0:T(8,128)(2,1)S(1)}, u32[]{:S(2)}) copy-start(s16[129,16,128]{2,1,0:T(8,128)(2,1)S(1)} %collective-permute-done.17.refs_6_) | copy-start | bytes 1585156
  99.0 63.7 %collective-permute-start.23 = (s16[257,16,128]{2,1,0:T(8,128)(2,1)}, s16[257,16,128]{2,1,0:T(8,128)(2,1)}, u32[]{:S(2)}, u32[]{:S(2)}) collective-permute-start(s16[257,16,128]{2,1,0:T(8,128)(2,1)} %get-tuple-element.57), channel_id=1, source_target_pairs={{0,2},{1,3},{2,0},{3,1},{4,6},{5,7},{6,4},{7,5},{8,10},{9,11},{10,... | collective-permute-start | bytes 3158024 | tf_op jit(solution)/shard_map/ppermute | solution.py:28
  102.0 1.1 copy-start.9
  102.0 60.7 %collective-permute-start.24 = (s16[257,16,128]{2,1,0:T(8,128)(2,1)}, s16[257,16,128]{2,1,0:T(8,128)(2,1)}, u32[]{:S(2)}, u32[]{:S(2)}) collective-permute-start(s16[257,16,128]{2,1,0:T(8,128)(2,1)} %get-tuple-element.58), channel_id=1, source_target_pairs={{0,3},{1,0},{2,1},{3,2},{4,7},{5,4},{6,5},{7,6},{8,11},{9,8},{10,9... | collective-permute-start | bytes 3158024 | tf_op jit(solution)/shard_map/ppermute | solution.py:28
  103.2 57.7 %collective-permute-start.6 = (bf16[4,272,256]{2,1,0:T(8,128)(2,1)}, bf16[4,272,256]{2,1,0:T(8,128)(2,1)S(1)}, u32[]{:S(2)}, u32[]{:S(2)}) collective-permute-start(bf16[4,272,256]{2,1,0:T(8,128)(2,1)} %get-tuple-element.86), channel_id=1, source_target_pairs={{0,1},{1,2},{2,3},{3,0},{4,5},{5,6},{6,7},{7,4},{8,9},{9,10},{10,1... | collective-permute-start | bytes 1671176 | tf_op jit(solution)/shard_map/ppermute | solution.py:28
  109.3 80.9 %collective-permute-start.19 = (s16[65,16,128]{2,1,0:T(8,128)(2,1)}, s16[65,16,128]{2,1,0:T(8,128)(2,1)S(1)}, u32[]{:S(2)}, u32[]{:S(2)}) collective-permute-start(s16[65,16,128]{2,1,0:T(8,128)(2,1)} %get-tuple-element.52), channel_id=1, source_target_pairs={{0,1},{1,2},{2,3},{3,0},{4,5},{5,6},{6,7},{7,4},{8,9},{9,10},{10,1... | collective-permute-start | bytes 798728 | tf_op jit(solution)/shard_map/ppermute | solution.py:28
  160.8 29.4 %collective-permute-start.20 = (s16[65,16,128]{2,1,0:T(8,128)(2,1)}, s16[65,16,128]{2,1,0:T(8,128)(2,1)S(1)}, u32[]{:S(2)}, u32[]{:S(2)}) collective-permute-start(s16[65,16,128]{2,1,0:T(8,128)(2,1)} %get-tuple-element.53), channel_id=1, source_target_pairs={{0,2},{1,3},{2,0},{3,1},{4,6},{5,7},{6,4},{7,5},{8,10},{9,11},{10,... | collective-permute-start | bytes 798728 | tf_op jit(solution)/shard_map/ppermute | solution.py:28
  161.2 29.0 %collective-permute-start.21 = (s16[65,16,128]{2,1,0:T(8,128)(2,1)}, s16[65,16,128]{2,1,0:T(8,128)(2,1)S(1)}, u32[]{:S(2)}, u32[]{:S(2)}) collective-permute-start(s16[65,16,128]{2,1,0:T(8,128)(2,1)} %get-tuple-element.54), channel_id=1, source_target_pairs={{0,3},{1,0},{2,1},{3,2},{4,7},{5,4},{6,5},{7,6},{8,11},{9,8},{10,9... | collective-permute-start | bytes 798728 | tf_op jit(solution)/shard_map/ppermute | solution.py:28
  162.7 7.3 %copy-start.13 = (s32[128,8]{0,1:T(8,128)S(1)}, s32[128,8]{0,1:T(8,128)}, u32[]{:S(2)}) copy-start(s32[128,8]{0,1:T(8,128)} %param.11) | copy-start | bytes 12292
  162.7 22.1 %copy-start.6 = (s32[4]{0:T(128)S(1)}, s32[4]{0:T(128)}, u32[]{:S(2)}) copy-start(s32[4]{0:T(128)} %copy-done.5) | copy-start | bytes 52
  168.0 10.1 %collective-permute-start.25 = (s16[65,16,128]{2,1,0:T(8,128)(2,1)}, s16[65,16,128]{2,1,0:T(8,128)(2,1)S(1)}, u32[]{:S(2)}, u32[]{:S(2)}) collective-permute-start(s16[65,16,128]{2,1,0:T(8,128)(2,1)} %get-tuple-element.60), channel_id=1, source_target_pairs={{0,4},{1,5},{2,6},{3,7},{4,8},{5,9},{6,10},{7,11},{8,12},{9,13},{1... | collective-permute-start | bytes 798728 | tf_op jit(solution)/shard_map/ppermute | solution.py:28
  170.3 10.7 %collective-permute-start.26 = (s16[65,16,128]{2,1,0:T(8,128)(2,1)}, s16[65,16,128]{2,1,0:T(8,128)(2,1)}, u32[]{:S(2)}, u32[]{:S(2)}) collective-permute-start(s16[65,16,128]{2,1,0:T(8,128)(2,1)} %get-tuple-element.61), channel_id=1, source_target_pairs={{0,8},{1,9},{2,10},{3,11},{4,12},{5,13},{6,14},{7,15},{8,0},{9,1},... | collective-permute-start | bytes 798728 | tf_op jit(solution)/shard_map/ppermute | solution.py:28
  178.1 6.7 %collective-permute-start.27 = (s16[65,16,128]{2,1,0:T(8,128)(2,1)}, s16[65,16,128]{2,1,0:T(8,128)(2,1)}, u32[]{:S(2)}, u32[]{:S(2)}) collective-permute-start(s16[65,16,128]{2,1,0:T(8,128)(2,1)} %get-tuple-element.62), channel_id=1, source_target_pairs={{0,12},{1,13},{2,14},{3,15},{4,0},{5,1},{6,2},{7,3},{8,4},{9,5},{1... | collective-permute-start | bytes 798728 | tf_op jit(solution)/shard_map/ppermute | solution.py:28
  184.8 1.0 copy-start.4
  185.8 4.5 %copy-start.3 = (s16[65,16,128]{2,1,0:T(8,128)(2,1)S(1)}, s16[65,16,128]{2,1,0:T(8,128)(2,1)}, u32[]{:S(2)}) copy-start(s16[65,16,128]{2,1,0:T(8,128)(2,1)} %get-tuple-element.51.refs_0_) | copy-start | bytes 798724
  197.2 2.7 %collective-permute-start.28 = (f32[4,16,4,8,128]{4,3,2,1,0:T(8,128)S(1)}, f32[4,16,4,8,128]{4,3,2,1,0:T(8,128)S(1)}, u32[]{:S(2)}, u32[]{:S(2)}) collective-permute-start(f32[4,16,4,8,128]{4,3,2,1,0:T(8,128)S(1)} %get-tuple-element.67), channel_id=1, source_target_pairs={{0,16},{16,0},{32,48},{48,32},{64,80},{80,64},{96,112},{112,96},{1... | collective-permute-start | bytes 3145736 | tf_op jit(solution)/shard_map/ppermute | solution.py:23
  200.1 13.8 %collective-permute-start.31 = (f32[16,4,8,128]{3,2,1,0:T(8,128)S(1)}, f32[16,4,8,128]{3,2,1,0:T(8,128)S(1)}, u32[]{:S(2)}, u32[]{:S(2)}) collective-permute-start(f32[16,4,8,128]{3,2,1,0:T(8,128)S(1)} %get-tuple-element.83), channel_id=1, source_target_pairs={{0,96},{16,112},{32,0},{48,16},{64,32},{80,48},{96,64},{112,80},{1... | collective-permute-start | bytes 786440 | tf_op jit(solution)/shard_map/ppermute | solution.py:23
  202.4 11.5 %collective-permute-start.30 = (f32[16,4,8,128]{3,2,1,0:T(8,128)S(1)}, f32[16,4,8,128]{3,2,1,0:T(8,128)S(1)}, u32[]{:S(2)}, u32[]{:S(2)}) collective-permute-start(f32[16,4,8,128]{3,2,1,0:T(8,128)S(1)} %get-tuple-element.84), channel_id=1, source_target_pairs={{0,64},{16,80},{32,96},{48,112},{64,0},{80,16},{96,32},{112,48},{1... | collective-permute-start | bytes 786440 | tf_op jit(solution)/shard_map/ppermute | solution.py:23
  203.5 14.1 %collective-permute-start.29 = (f32[16,4,8,128]{3,2,1,0:T(8,128)S(1)}, f32[16,4,8,128]{3,2,1,0:T(8,128)S(1)}, u32[]{:S(2)}, u32[]{:S(2)}) collective-permute-start(f32[16,4,8,128]{3,2,1,0:T(8,128)S(1)} %get-tuple-element.82), channel_id=1, source_target_pairs={{0,32},{16,48},{32,64},{48,80},{64,96},{80,112},{96,0},{112,16},{1... | collective-permute-start | bytes 786440 | tf_op jit(solution)/shard_map/ppermute | solution.py:23

commit v6 on v5

--- a/solution.py
+++ b/solution.py
@@ -94,7 +94,7 @@
         in_specs=[whole] * 8,
         out_specs=[whole, whole],
         out_shape=[
-            pltpu.HBM((NK * KP + 1, B, 128), jnp.bfloat16),
+            pltpu.VMEM((NK * KP + 1, B, 128), jnp.bfloat16),
             jax.ShapeDtypeStruct((NK, 128), jnp.float32),
         ],
         name="table",
@@ -131,10 +131,10 @@
     for s in range(KAP):
         pieces = []
         for lo in range(2):
-            base = (first_row + lo * NCOL) * (KA * KAP)
+            row = first_row + lo * NCOL
             for ep in range(2):
-                first = dup_ref[idx_ref[base + (2 * ep) * KAP + s]]
-                second = dup_ref[idx_ref[base + (2 * ep + 1) * KAP + s]]
+                first = dup_ref[idx_ref[(2 * ep) * KAP + s, row]]
+                second = dup_ref[idx_ref[(2 * ep + 1) * KAP + s, row]]
                 pieces.append(jnp.where(low, first, second))
         rows.append(jnp.concatenate(pieces, axis=1))
     return jnp.concatenate(rows, axis=0)
@@ -587,10 +587,11 @@
 def step(a_blocks, a_index, p_blocks, p_index, ap_index, coarse_index):
     row = lax.axis_index("row")
     col = lax.axis_index("col")
-    z, core = row // 2, row % 2
-    y, x = col // 4, col % 4
+    z, core = row >> 1, row & 1
+    y, x = col >> 2, col & 3
     at = jnp.stack([x, y, z, core]).astype(jnp.int32)
-    half = x % 2
+    half = x & 1
+    other_half = 1 - half
 
     own = p_blocks[:, 0].reshape(8, KP, B, B)
     pt = own.transpose(0, 3, 1, 2).reshape(8 * B, KP * B)
@@ -605,7 +606,9 @@
             for h in range(2)
         ]
     )
-    *by_z, halves = lax.optimization_barrier((*by_z, halves))
+    *by_z, halves, half, other_half = lax.optimization_barrier(
+        (*by_z, halves, half, other_half)
+    )
     parts = [by_z[0], partner]
     for part in by_z[1:]:
         parts += [part, along_row(part, 0, 1)]
@@ -614,14 +617,15 @@
     a = spread(a_blocks[:, 0]).reshape(4, 2, NCOL, B, KA * B)
 
     a_idx = a_index[:, 0]
-    from_row = a_idx // 8
-    place = ((z - from_row // 2) % 4) * 2 + (core + from_row) % 2
-    place = place * 8 + a_idx % 8
+    from_row = a_idx >> 3
+    place = ((z - (from_row >> 1)) & 3) * 2 + ((core + from_row) & 1)
+    place = place * 8 + (a_idx & 7)
     dup, cols_k = table(parts)
     picked = pick_rows(cols_k[:, :KP], place)
     equal = picked[:, :, None, :] == ap_index[:, None, :, None]
     ids = place[:, :, None, None] * KP + jnp.arange(KP, dtype=jnp.int32)
-    idx = jnp.min(jnp.where(equal, ids, NK * KP), axis=3).reshape(-1)
+    idx = jnp.min(jnp.where(equal, ids, NK * KP), axis=3)
+    idx = idx.transpose(1, 2, 0).reshape(KA * KAP, 128)
 
     x1, x3 = x_products(1, idx, at, a, dup)
     got_x1, got_x3 = along_col(x1, 1, 0), along_col(x3, 3, 0)
@@ -638,16 +642,16 @@
     x_last = [along_col(s1[1], 1, 0), far, along_col(s1[3], 3, 0)]
 
     by_y = jnp.stack(by_y)
-    same = lax.dynamic_index_in_dim(by_y, half, 1, keepdims=False)
-    diff = lax.dynamic_index_in_dim(by_y, 1 - half, 1, keepdims=False)
+    same = lax.dynamic_index_in_dim(by_y, half, 1, keepdims=False, allow_negative_indices=False)
+    diff = lax.dynamic_index_in_dim(by_y, other_half, 1, keepdims=False, allow_negative_indices=False)
     ps = [same, along_col(diff, 1, 0), along_col(same, 2, 0), along_col(diff, 3, 0)]
 
     cols_p = jnp.stack([p[:, 4 * B:4 * B + 4, :KP] for p in ps]).reshape(NCOL, 16)
     cc = jnp.arange(NCOL, dtype=jnp.int32)
-    where = ((x - cc % 4) % 4) * 4 + (y - cc // 4) % 4
+    where = ((x - (cc & 3)) & 3) * 4 + ((y - (cc >> 2)) & 3)
     cols_i = pick_rows(cols_p, where).reshape(NCOL, 4, KP)
     slots = lax.dynamic_index_in_dim(
-        ap_index.reshape(2, 4, NCOL, KAP), half, 0, keepdims=False
+        ap_index.reshape(2, 4, NCOL, KAP), half, 0, keepdims=False, allow_negative_indices=False
     ).transpose(1, 0, 2)
     targets = pick_rows(coarse_index, cols_i)
     hit = targets[:, :, :, None, :] == slots[:, :, None, :, None]

time: 240 us -> 236 us (0.983)
  local copies, waits for them, and re-layouts: 13.5 us -> 9.63 us
  waiting for transfers between devices: 93.6 us -> 96.4 us
    unnamed x28, local copies, waits for them, and re-layouts: 7.6 us -> 4.07 us
    ppermute x21, waiting for transfers between devices: 68.5 us -> 71.3 us  [along_col(): return lax.ppermute(v, 'col', pairs)]
  transfers between devices with their start and end apart: 32 -> 32, of which waited for: 12 -> 10; matrix products, arithmetic and copies ran while one was open for 3% -> 2% of each run, Pallas kernels for 24% -> 24%
where the time goes in v6:
time: 236 us; the launch traced here: 235 us
  waiting for transfers between devices  96.4 us (41%)
  Pallas kernels  65.5 us (28%)
  starting transfers between devices  41.2 us (17%)
  blocking collectives  19.1 us (8%)
  local copies, waits for them, and re-layouts  9.63 us (4%)
    ppermute x21, waiting for transfers between devices, along_col(): return lax.ppermute(v, 'col', pairs)  71.3 us
    ppermute x21, starting transfers between devices, along_col(): return lax.ppermute(v, 'col', pairs)  30.2 us
    ppermute x11, waiting for transfers between devices, along_row(): return lax.ppermute(v, 'row', pairs)  25.2 us
    all_to_all x1, blocking collectives, step(): both = lax.all_to_all(both, 'col', 0, 0, tiled=True)  19.1 us
    pallas_call x2, Pallas kernels, y_products(): pl.pallas_call(lambda *refs: y_product_kernel(part, *refs), grid_spec=plt...  14.9 us
    pallas_call x2, Pallas kernels, x_products(): pl.pallas_call(lambda *refs: x_product_kernel(j, *refs), grid_spec=pltpu....  14.8 us
    ppermute x11, starting transfers between devices, along_row(): return lax.ppermute(v, 'row', pairs)  11 us
    pallas_call x2, Pallas kernels, middle(): pl.pallas_call(kernel, in_specs=[pl.BlockSpec(memory_space=pltpu.SMEM)] +...  10.5 us
  transfers between devices with their start and end apart: 32, of which 10 were waited for; matrix products, arithmetic and copies ran while one was open for 2% of the time, Pallas kernels for 24%

profile of v6, /device:TPU:0, one launch (start us, length us, event | category | flops | bytes accessed | tf_op | source)
XLA Modules:
  0.0 235.1 jit_solution(1126218361100459870)
XLA Ops:
  0.6 0.7 convert_bitcast_fusion
  1.4 1.4 reshape_squeeze.3
  2.9 0.3 copy.61
  3.2 0.3 reshape.136
  3.5 2.1 collective-permute-start
  5.6 3.6 %collective-permute-start.1 = (bf16[528,256]{1,0:T(8,128)(2,1)S(1)}, bf16[528,256]{1,0:T(8,128)(2,1)S(1)}, u32[]{:S(2)}, u32[]{:S(2)}) collective-permute-start(bf16[528,256]{1,0:T(8,128)(2,1)S(1)} %fusion.3.refs_0_), channel_id=1, source_target_pairs={{0,64},{16,80},{32,96},{48,112},{64,0},{80,16},{96,32},{112,48},{1... | collective-permute-start | bytes 811016 | tf_op jit(solution)/shard_map/ppermute | solution.py:23
  9.2 1.0 collective-permute-start.2
  10.3 0.4 reshape_reshape_squeeze.3
  10.9 0.4 fusion.26
  11.2 0.2 copy.63
  11.5 0.2 squeeze.17
  11.8 0.2 copy.65
  12.0 0.2 squeeze.18
  12.4 1.9 collective-permute-done.refs_2_
  14.2 7.0 %collective-permute-done.1.refs_4_ = bf16[528,256]{1,0:T(8,128)(2,1)S(1)} collective-permute-done((bf16[528,256]{1,0:T(8,128)(2,1)S(1)}, bf16[528,256]{1,0:T(8,128)(2,1)S(1)}, u32[]{:S(2)}, u32[]{:S(2)}) %collective-permute-start.1) | collective-permute-done | bytes 270368 | tf_op jit(solution)/shard_map/ppermute | solution.py:23
  21.2 0.5 collective-permute-start.11
  21.8 8.4 %spread.1 = bf16[128,64,256]{2,1,0:T(8,128)(2,1)} custom-call(bf16[128,4,4096]{2,1,0:T(4,128)(2,1)} %bitcast.92), custom_call_target="tpu_custom_call" | custom-call | tf_op jit(solution)/shard_map/spread/pallas_call | solution.py:59
  30.2 3.1 %collective-permute-start.5 = (bf16[2,272,256]{2,1,0:T(8,128)(2,1)S(1)}, bf16[2,272,256]{2,1,0:T(8,128)(2,1)S(1)}, u32[]{:S(2)}, u32[]{:S(2)}) collective-permute-start(bf16[2,272,256]{2,1,0:T(8,128)(2,1)S(1)} %pad_maximum_fusion.1), channel_id=1, source_target_pairs={{0,12},{1,13},{2,14},{3,15},{4,0},{5,1},{6,2},{7,3},{8,4},{9,5},{1... | collective-permute-start | bytes 835592 | tf_op jit(solution)/shard_map/ppermute | solution.py:28
  33.3 0.6 collective-permute-start.4
  33.9 1.0 collective-permute-start.3
  34.9 2.9 %table.1 = (bf16[257,64,128]{2,1,0:T(8,128)(2,1)S(1)}, f32[64,128]{1,0:T(8,128)S(1)}) custom-call(bf16[528,256]{1,0:T(8,128)(2,1)S(1)} %fusion.3.refs_0_, bf16[528,256]{1,0:T(8,128)(2,1)S(1)} %collective-permute-done.9.refs_1_, bf16[528,256]{1,0:T(8,128)(2,1)S(1)} %collective-permute-done.refs_2_, bf16[528,256]{1,0:T(8,128)(2,1)S(1)} %collective-permute-done.10.refs_3_, ...), custom_call_target="tpu_custom_call" | custom-call | tf_op jit(solution)/shard_map/table/pallas_call | solution.py:92
  38.0 7.5 %shard_map.77 = (s16[129,16,128]{2,1,0:T(8,128)(2,1)}, s16[129,16,128]{2,1,0:T(8,128)(2,1)S(1)}, s16[129,16,128]{2,1,0:T(8,128)(2,1)S(1)}, s16[129,16,128]{2,1,0:T(8,128)(2,1)S(1)}) custom-call(s32[32,128]{1,0:T(8,128)S(1)} %bitcast.84, s32[4]{0:T(128)S(1)} %pad_add_fusion.refs_1_.at_ref, bf16[4,2,16,64,256]{4,3,2,1,0:T(8,128)(2,1)} %bitcast.88, ...), custom_call_target="tpu_custom_call" | custom-call | tf_op jit(solution)/shard_map/pallas_call | solution.py:272
  45.5 1.9 collective-permute-start.13
  47.4 1.8 collective-permute-start.14
  49.2 0.8 collective-permute-start.15
  50.2 0.9 dynamic-slice_bitcast_fusion.1
  51.1 2.8 %collective-permute-start.8 = (bf16[4,272,256]{2,1,0:T(8,128)(2,1)}, bf16[4,272,256]{2,1,0:T(8,128)(2,1)S(1)}, u32[]{:S(2)}, u32[]{:S(2)}) collective-permute-start(bf16[4,272,256]{2,1,0:T(8,128)(2,1)} %get-tuple-element.90), channel_id=1, source_target_pairs={{0,3},{1,0},{2,1},{3,2},{4,7},{5,4},{6,5},{7,6},{8,11},{9,8},{10,9... | collective-permute-start | bytes 1671176 | tf_op jit(solution)/shard_map/ppermute | solution.py:28
  53.9 7.3 %shard_map.78 = (s16[129,16,128]{2,1,0:T(8,128)(2,1)}, s16[129,16,128]{2,1,0:T(8,128)(2,1)}, s16[129,16,128]{2,1,0:T(8,128)(2,1)S(1)}, s16[129,16,128]{2,1,0:T(8,128)(2,1)S(1)}) custom-call(s32[32,128]{1,0:T(8,128)S(1)} %bitcast.85, s32[4]{0:T(128)S(1)} %pad_add_fusion.refs_1_.at_ref, bf16[4,2,16,64,256]{4,3,2,1,0:T(8,128)(2,1)} %bitcast.89, ...), custom_call_target="tpu_custom_call" | custom-call | tf_op jit(solution)/shard_map/pallas_call | solution.py:272
  61.2 1.2 collective-permute-start.16
  62.4 1.7 collective-permute-start.17
  64.1 9.3 %collective-permute-done.14.refs_2_ = s16[129,16,128]{2,1,0:T(8,128)(2,1)S(1)} collective-permute-done((s16[129,16,128]{2,1,0:T(8,128)(2,1)S(1)}, s16[129,16,128]{2,1,0:T(8,128)(2,1)S(1)}, u32[]{:S(2)}, u32[]{:S(2)}) %collective-permute-start.14) | collective-permute-done | bytes 528416 | tf_op jit(solution)/shard_map/ppermute | solution.py:28
  73.5 0.8 copy-done.8
  74.4 3.3 %collective-permute-start.7 = (bf16[4,272,256]{2,1,0:T(8,128)(2,1)S(1)}, bf16[4,272,256]{2,1,0:T(8,128)(2,1)S(1)}, u32[]{:S(2)}, u32[]{:S(2)}) collective-permute-start(bf16[4,272,256]{2,1,0:T(8,128)(2,1)S(1)} %get-tuple-element.89.refs_4_), channel_id=1, source_target_pairs={{0,2},{1,3},{2,0},{3,1},{4,6},{5,7},{6,4},{7,5},{8,10},{9,11},{10,... | collective-permute-start | bytes 1671176 | tf_op jit(solution)/shard_map/ppermute | solution.py:28
  77.7 2.2 copy-done.1
  79.9 7.4 %shard_map.80 = (s16[257,16,128]{2,1,0:T(8,128)(2,1)}, s16[257,16,128]{2,1,0:T(8,128)(2,1)}) custom-call(s32[32,128]{1,0:T(8,128)S(1)} %bitcast.86, s32[4]{0:T(128)S(1)} %pad_add_fusion.refs_1_.at_ref, bf16[4,2,16,64,256]{4,3,2,1,0:T(8,128)(2,1)} %bitcast.90, bf16[257,64,128]{2,1,0:T(8,128)(2,1)S(1)} %copy-done.1), custom_call_target="tpu_custom_call" | custom-call | tf_op jit(solution)/shard_map/pallas_call | solution.py:205
  87.3 7.4 %shard_map.81 = (s16[257,16,128]{2,1,0:T(8,128)(2,1)}, s16[257,16,128]{2,1,0:T(8,128)(2,1)}) custom-call(s32[32,128]{1,0:T(8,128)S(1)} %bitcast.87, s32[4]{0:T(128)S(1)} %pad_add_fusion.refs_1_.at_ref, bf16[4,2,16,64,256]{4,3,2,1,0:T(8,128)(2,1)} %bitcast.91, bf16[257,64,128]{2,1,0:T(8,128)(2,1)S(1)} %copy-done.1), custom_call_target="tpu_custom_call" | custom-call | tf_op jit(solution)/shard_map/pallas_call | solution.py:205
  94.7 0.6 collective-permute-start.22
  95.3 2.7 %collective-permute-start.23 = (s16[257,16,128]{2,1,0:T(8,128)(2,1)}, s16[257,16,128]{2,1,0:T(8,128)(2,1)}, u32[]{:S(2)}, u32[]{:S(2)}) collective-permute-start(s16[257,16,128]{2,1,0:T(8,128)(2,1)} %get-tuple-element.61), channel_id=1, source_target_pairs={{0,2},{1,3},{2,0},{3,1},{4,6},{5,7},{6,4},{7,5},{8,10},{9,11},{10,... | collective-permute-start | bytes 3158024 | tf_op jit(solution)/shard_map/ppermute | solution.py:28
  98.0 1.1 collective-permute-start.24
  99.2 0.9 collective-permute-start.6
  100.1 5.2 %shard_map.79 = (s16[65,16,128]{2,1,0:T(8,128)(2,1)}, s16[65,16,128]{2,1,0:T(8,128)(2,1)}, s16[65,16,128]{2,1,0:T(8,128)(2,1)}, s16[65,16,128]{2,1,0:T(8,128)(2,1)}) custom-call(s32[4]{0:T(128)} %copy-done.4, s16[129,16,128]{2,1,0:T(8,128)(2,1)} %get-tuple-element.47.refs_0_, s16[129,16,128]{2,1,0:T(8,128)(2,1)} %copy-done.7, ...), custom_call_target="tpu_custom_call" | custom-call | tf_op jit(solution)/shard_map/pallas_call | solution.py:362
  105.3 0.9 collective-permute-start.19
  106.2 51.2 %collective-permute-done.6.refs_5_ = bf16[4,272,256]{2,1,0:T(8,128)(2,1)S(1)} collective-permute-done((bf16[4,272,256]{2,1,0:T(8,128)(2,1)}, bf16[4,272,256]{2,1,0:T(8,128)(2,1)S(1)}, u32[]{:S(2)}, u32[]{:S(2)}) %collective-permute-start.6) | collective-permute-done | bytes 557088 | tf_op jit(solution)/shard_map/ppermute | solution.py:28
  157.7 1.5 collective-permute-start.21
  159.3 5.3 %shard_map.82 = (s16[65,16,128]{2,1,0:T(8,128)(2,1)}, s16[65,16,128]{2,1,0:T(8,128)(2,1)}, s16[65,16,128]{2,1,0:T(8,128)(2,1)}, s16[65,16,128]{2,1,0:T(8,128)(2,1)}) custom-call(s32[4]{0:T(128)} %copy-done.4, s16[257,16,128]{2,1,0:T(8,128)(2,1)} %get-tuple-element.59.m0, s16[257,16,128]{2,1,0:T(8,128)(2,1)} %collective-permute-done.22.m1, ...), custom_call_target="tpu_custom_call" | custom-call | tf_op jit(solution)/shard_map/pallas_call | solution.py:362
  164.6 2.0 collective-permute-start.25
  166.6 0.3 convolution_convert_fusion
  166.9 1.7 collective-permute-start.26
  168.6 5.1 %collective-permute-done.25.refs_1_ = s16[65,16,128]{2,1,0:T(8,128)(2,1)S(1)} collective-permute-done((s16[65,16,128]{2,1,0:T(8,128)(2,1)}, s16[65,16,128]{2,1,0:T(8,128)(2,1)S(1)}, u32[]{:S(2)}, u32[]{:S(2)}) %collective-permute-start.25) | collective-permute-done | bytes 266272 | tf_op jit(solution)/shard_map/ppermute | solution.py:28
  173.7 0.6 collective-permute-start.27
  174.3 0.2 select_reduce_fusion
  174.9 1.8 collective-permute-done.26.refs_2_
  176.7 3.8 %collective-permute-done.27.refs_3_ = s16[65,16,128]{2,1,0:T(8,128)(2,1)} collective-permute-done((s16[65,16,128]{2,1,0:T(8,128)(2,1)}, s16[65,16,128]{2,1,0:T(8,128)(2,1)}, u32[]{:S(2)}, u32[]{:S(2)}) %collective-permute-start.27) | collective-permute-done | bytes 266272 | tf_op jit(solution)/shard_map/ppermute | solution.py:28
  180.5 1.0 copy-done.3
  181.4 4.5 %first_coarse.1 = (bf16[16,64,128]{2,1,0:T(8,128)(2,1)S(1)}, f32[1025,8,128]{2,1,0:T(8,128)S(1)}) custom-call(s32[2048]{0:T(1024)S(1)} %reshape.139.tgt_ref, s32[4]{0:T(128)S(1)} %copy-done.5, s16[65,16,128]{2,1,0:T(8,128)(2,1)S(1)} %copy-done.3, s16[65,16,128]{2,1,0:T(8,128)(2,1)S(1)} %collective-permute-done.25.refs_1_, ...), custom_call_target="tpu_custom_call" | custom-call | tf_op jit(solution)/shard_map/first_coarse/pallas_call | solution.py:469
  185.9 6.9 %second_coarse.1 = (bf16[16,192,128]{2,1,0:T(8,128)(2,1)S(1)}, f32[4,16,4,8,128]{4,3,2,1,0:T(8,128)S(1)}, f32[4,16,4,8,128]{4,3,2,1,0:T(8,128)S(1)}) custom-call(s32[2048]{0:T(1024)S(1)} %reshape.139.tgt_ref, s32[4]{0:T(128)S(1)} %copy-done.5, s16[65,16,128]{2,1,0:T(8,128)(2,1)S(1)} %copy-done.2, s16[65,16,128]{2,1,0:T(8,128)(2,1)S(1)} %collective-permute-done.19.refs_1_, ...), custom_call_target="tpu_custom_call" | custom-call | tf_op jit(solution)/shard_map/second_coarse/pallas_call | solution.py:493
  193.0 2.6 %collective-permute-done.28 = f32[4,16,4,8,128]{4,3,2,1,0:T(8,128)S(1)} collective-permute-done((f32[4,16,4,8,128]{4,3,2,1,0:T(8,128)S(1)}, f32[4,16,4,8,128]{4,3,2,1,0:T(8,128)S(1)}, u32[]{:S(2)}, u32[]{:S(2)}) %collective-permute-start.28) | collective-permute-done | bytes 1048608 | tf_op jit(solution)/shard_map/ppermute | solution.py:23
  195.8 2.2 collective-permute-start.31
  198.0 1.1 collective-permute-start.30
  199.1 0.4 collective-permute-start.29
  199.5 10.0 %collective-permute-done.31 = f32[16,4,8,128]{3,2,1,0:T(8,128)S(1)} collective-permute-done((f32[16,4,8,128]{3,2,1,0:T(8,128)S(1)}, f32[16,4,8,128]{3,2,1,0:T(8,128)S(1)}, u32[]{:S(2)}, u32[]{:S(2)}) %collective-permute-start.31) | collective-permute-done | bytes 262176 | tf_op jit(solution)/shard_map/ppermute | solution.py:23
  209.5 3.7 %collective-permute-done.29 = f32[16,4,8,128]{3,2,1,0:T(8,128)S(1)} collective-permute-done((f32[16,4,8,128]{3,2,1,0:T(8,128)S(1)}, f32[16,4,8,128]{3,2,1,0:T(8,128)S(1)}, u32[]{:S(2)}, u32[]{:S(2)}) %collective-permute-start.29) | collective-permute-done | bytes 262176 | tf_op jit(solution)/shard_map/ppermute | solution.py:23
  213.4 19.1 %all_to_all.5.x_ref = bf16[16,192,128]{2,1,0:T(8,128)(2,1)} all-to-all(bf16[16,192,128]{2,1,0:T(8,128)(2,1)S(1)} %maximum_dynamic-update-slice_fusion), channel_id=1, replica_groups=mesh['row'=8,'col'=16] {'col'}, dimensions={0} | all-to-all | bytes 1572864 | tf_op jit(solution)/shard_map/all_to_all | solution.py:674
  232.4 2.6 %layout.1 = (bf16[8,8,4096]{2,1,0:T(8,128)(2,1)}, f32[8,4096]{1,0:T(8,128)}) custom-call(bf16[16,192,128]{2,1,0:T(8,128)(2,1)} %all_to_all.5.x_ref), custom_call_target="tpu_custom_call" | custom-call | tf_op jit(solution)/shard_map/layout/pallas_call | solution.py:558
  (87 shorter events, 2.3 us)
Async XLA Ops:
  2.8 7.4 %copy-start.11 = (s32[8,1,4]{0,2,1:T(4,128)S(1)}, s32[8,1,4]{0,2,1:T(4,128)}, u32[]{:S(2)}) copy-start(s32[8,1,4]{0,2,1:T(4,128)} %param.9) | copy-start | bytes 388
  2.8 7.4 %copy-start.6 = (bf16[8,1,4,4096]{3,2,1,0:T(4,128)(2,1)S(1)}, bf16[8,1,4,4096]{3,2,1,0:T(4,128)(2,1)}, u32[]{:S(2)}) copy-start(bf16[8,1,4,4096]{3,2,1,0:T(4,128)(2,1)} %param.8) | copy-start | bytes 786436
  3.5 10.7 %collective-permute-start = (bf16[528,256]{1,0:T(8,128)(2,1)S(1)}, bf16[528,256]{1,0:T(8,128)(2,1)S(1)}, u32[]{:S(2)}, u32[]{:S(2)}) collective-permute-start(bf16[528,256]{1,0:T(8,128)(2,1)S(1)} %fusion.3.refs_0_), channel_id=1, source_target_pairs={{0,32},{16,48},{32,64},{48,80},{64,96},{80,112},{96,0},{112,16},{1... | collective-permute-start | bytes 811016 | tf_op jit(solution)/shard_map/ppermute | solution.py:23
  5.6 15.6 %collective-permute-start.1 = (bf16[528,256]{1,0:T(8,128)(2,1)S(1)}, bf16[528,256]{1,0:T(8,128)(2,1)S(1)}, u32[]{:S(2)}, u32[]{:S(2)}) collective-permute-start(bf16[528,256]{1,0:T(8,128)(2,1)S(1)} %fusion.3.refs_0_), channel_id=1, source_target_pairs={{0,64},{16,80},{32,96},{48,112},{64,0},{80,16},{96,32},{112,48},{1... | collective-permute-start | bytes 811016 | tf_op jit(solution)/shard_map/ppermute | solution.py:23
  9.2 12.0 %collective-permute-start.2 = (bf16[528,256]{1,0:T(8,128)(2,1)S(1)}, bf16[528,256]{1,0:T(8,128)(2,1)S(1)}, u32[]{:S(2)}, u32[]{:S(2)}) collective-permute-start(bf16[528,256]{1,0:T(8,128)(2,1)S(1)} %fusion.3.refs_0_), channel_id=1, source_target_pairs={{0,96},{16,112},{32,0},{48,16},{64,32},{80,48},{96,64},{112,80},{1... | collective-permute-start | bytes 811016 | tf_op jit(solution)/shard_map/ppermute | solution.py:23
  10.2 23.0 %collective-permute-start.9 = (bf16[528,256]{1,0:T(8,128)(2,1)S(1)}, bf16[528,256]{1,0:T(8,128)(2,1)S(1)}, u32[]{:S(2)}, u32[]{:S(2)}) collective-permute-start(bf16[528,256]{1,0:T(8,128)(2,1)S(1)} %fusion.3.refs_0_), channel_id=1, source_target_pairs={{0,16},{16,0},{32,48},{48,32},{64,80},{80,64},{96,112},{112,96},{1... | collective-permute-start | bytes 811016 | tf_op jit(solution)/shard_map/ppermute | solution.py:23
  11.7 0.7 copy-start.12
  21.2 12.7 %collective-permute-start.10 = (bf16[528,256]{1,0:T(8,128)(2,1)S(1)}, bf16[528,256]{1,0:T(8,128)(2,1)S(1)}, u32[]{:S(2)}, u32[]{:S(2)}) collective-permute-start(bf16[528,256]{1,0:T(8,128)(2,1)S(1)} %collective-permute-done.refs_2_), channel_id=1, source_target_pairs={{0,16},{16,0},{32,48},{48,32},{64,80},{80,64},{96,112},{112,96},{1... | collective-permute-start | bytes 811016 | tf_op jit(solution)/shard_map/ppermute | solution.py:23
  21.2 13.7 %collective-permute-start.11 = (bf16[528,256]{1,0:T(8,128)(2,1)S(1)}, bf16[528,256]{1,0:T(8,128)(2,1)S(1)}, u32[]{:S(2)}, u32[]{:S(2)}) collective-permute-start(bf16[528,256]{1,0:T(8,128)(2,1)S(1)} %collective-permute-done.1.refs_4_), channel_id=1, source_target_pairs={{0,16},{16,0},{32,48},{48,32},{64,80},{80,64},{96,112},{112,96},{1... | collective-permute-start | bytes 811016 | tf_op jit(solution)/shard_map/ppermute | solution.py:23
  21.7 13.1 %collective-permute-start.12 = (bf16[528,256]{1,0:T(8,128)(2,1)S(1)}, bf16[528,256]{1,0:T(8,128)(2,1)S(1)}, u32[]{:S(2)}, u32[]{:S(2)}) collective-permute-start(bf16[528,256]{1,0:T(8,128)(2,1)S(1)} %collective-permute-done.2.refs_6_), channel_id=1, source_target_pairs={{0,16},{16,0},{32,48},{48,32},{64,80},{80,64},{96,112},{112,96},{1... | collective-permute-start | bytes 811016 | tf_op jit(solution)/shard_map/ppermute | solution.py:23
  21.8 65.5 %copy-start.4 = (s32[4]{0:T(128)}, s32[4]{0:T(128)S(1)}, u32[]{:S(2)}) copy-start(s32[4]{0:T(128)S(1)} %pad_add_fusion.refs_1_.at_ref) | copy-start | bytes 52
  30.2 7.8 %copy-start.10 = (s32[128,8]{0,1:T(8,128)S(1)}, s32[128,8]{0,1:T(8,128)}, u32[]{:S(2)}) copy-start(s32[128,8]{0,1:T(8,128)} %param.10) | copy-start | bytes 12292
  30.2 19.1 %collective-permute-start.5 = (bf16[2,272,256]{2,1,0:T(8,128)(2,1)S(1)}, bf16[2,272,256]{2,1,0:T(8,128)(2,1)S(1)}, u32[]{:S(2)}, u32[]{:S(2)}) collective-permute-start(bf16[2,272,256]{2,1,0:T(8,128)(2,1)S(1)} %pad_maximum_fusion.1), channel_id=1, source_target_pairs={{0,12},{1,13},{2,14},{3,15},{4,0},{5,1},{6,2},{7,3},{8,4},{9,5},{1... | collective-permute-start | bytes 835592 | tf_op jit(solution)/shard_map/ppermute | solution.py:28
  33.3 16.8 %collective-permute-start.4 = (bf16[2,272,256]{2,1,0:T(8,128)(2,1)S(1)}, bf16[2,272,256]{2,1,0:T(8,128)(2,1)S(1)}, u32[]{:S(2)}, u32[]{:S(2)}) collective-permute-start(bf16[2,272,256]{2,1,0:T(8,128)(2,1)S(1)} %pad_maximum_fusion.1), channel_id=1, source_target_pairs={{0,8},{1,9},{2,10},{3,11},{4,12},{5,13},{6,14},{7,15},{8,0},{9,1},... | collective-permute-start | bytes 835592 | tf_op jit(solution)/shard_map/ppermute | solution.py:28
  33.9 16.2 %collective-permute-start.3 = (bf16[2,272,256]{2,1,0:T(8,128)(2,1)S(1)}, bf16[2,272,256]{2,1,0:T(8,128)(2,1)S(1)}, u32[]{:S(2)}, u32[]{:S(2)}) collective-permute-start(bf16[2,272,256]{2,1,0:T(8,128)(2,1)S(1)} %pad_maximum_fusion.1), channel_id=1, source_target_pairs={{0,4},{1,5},{2,6},{3,7},{4,8},{5,9},{6,10},{7,11},{8,12},{9,13},{1... | collective-permute-start | bytes 835592 | tf_op jit(solution)/shard_map/ppermute | solution.py:28
  37.7 16.2 %copy-start = (bf16[257,64,128]{2,1,0:T(8,128)(2,1)}, bf16[257,64,128]{2,1,0:T(8,128)(2,1)S(1)}, u32[]{:S(2)}) copy-start(bf16[257,64,128]{2,1,0:T(8,128)(2,1)S(1)} %get-tuple-element.46.refs_3_) | copy-start | bytes 12632068
  45.5 16.9 %collective-permute-start.13 = (s16[129,16,128]{2,1,0:T(8,128)(2,1)S(1)}, s16[129,16,128]{2,1,0:T(8,128)(2,1)S(1)}, u32[]{:S(2)}, u32[]{:S(2)}) collective-permute-start(s16[129,16,128]{2,1,0:T(8,128)(2,1)S(1)} %get-tuple-element.48), channel_id=1, source_target_pairs={{0,4},{1,5},{2,6},{3,7},{4,8},{5,9},{6,10},{7,11},{8,12},{9,13},{1... | collective-permute-start | bytes 1585160 | tf_op jit(solution)/shard_map/ppermute | solution.py:28
  47.4 26.1 %collective-permute-start.14 = (s16[129,16,128]{2,1,0:T(8,128)(2,1)S(1)}, s16[129,16,128]{2,1,0:T(8,128)(2,1)S(1)}, u32[]{:S(2)}, u32[]{:S(2)}) collective-permute-start(s16[129,16,128]{2,1,0:T(8,128)(2,1)S(1)} %get-tuple-element.49), channel_id=1, source_target_pairs={{0,8},{1,9},{2,10},{3,11},{4,12},{5,13},{6,14},{7,15},{8,0},{9,1},... | collective-permute-start | bytes 1585160 | tf_op jit(solution)/shard_map/ppermute | solution.py:28
  49.2 25.2 %collective-permute-start.15 = (s16[129,16,128]{2,1,0:T(8,128)(2,1)S(1)}, s16[129,16,128]{2,1,0:T(8,128)(2,1)}, u32[]{:S(2)}, u32[]{:S(2)}) collective-permute-start(s16[129,16,128]{2,1,0:T(8,128)(2,1)S(1)} %get-tuple-element.50), channel_id=1, source_target_pairs={{0,12},{1,13},{2,14},{3,15},{4,0},{5,1},{6,2},{7,3},{8,4},{9,5},{1... | collective-permute-start | bytes 1585160 | tf_op jit(solution)/shard_map/ppermute | solution.py:28
  51.1 48.0 %collective-permute-start.8 = (bf16[4,272,256]{2,1,0:T(8,128)(2,1)}, bf16[4,272,256]{2,1,0:T(8,128)(2,1)S(1)}, u32[]{:S(2)}, u32[]{:S(2)}) collective-permute-start(bf16[4,272,256]{2,1,0:T(8,128)(2,1)} %get-tuple-element.90), channel_id=1, source_target_pairs={{0,3},{1,0},{2,1},{3,2},{4,7},{5,4},{6,5},{7,6},{8,11},{9,8},{10,9... | collective-permute-start | bytes 1671176 | tf_op jit(solution)/shard_map/ppermute | solution.py:28
  61.2 33.5 %collective-permute-start.16 = (s16[129,16,128]{2,1,0:T(8,128)(2,1)}, s16[129,16,128]{2,1,0:T(8,128)(2,1)}, u32[]{:S(2)}, u32[]{:S(2)}) collective-permute-start(s16[129,16,128]{2,1,0:T(8,128)(2,1)} %get-tuple-element.52), channel_id=1, source_target_pairs={{0,4},{1,5},{2,6},{3,7},{4,8},{5,9},{6,10},{7,11},{8,12},{9,13},{1... | collective-permute-start | bytes 1585160 | tf_op jit(solution)/shard_map/ppermute | solution.py:28
  62.4 11.1 %copy-start.7 = (s16[129,16,128]{2,1,0:T(8,128)(2,1)}, s16[129,16,128]{2,1,0:T(8,128)(2,1)S(1)}, u32[]{:S(2)}) copy-start(s16[129,16,128]{2,1,0:T(8,128)(2,1)S(1)} %collective-permute-done.13.refs_1_) | copy-start | bytes 1585156
  62.4 32.9 %collective-permute-start.17 = (s16[129,16,128]{2,1,0:T(8,128)(2,1)S(1)}, s16[129,16,128]{2,1,0:T(8,128)(2,1)}, u32[]{:S(2)}, u32[]{:S(2)}) collective-permute-start(s16[129,16,128]{2,1,0:T(8,128)(2,1)S(1)} %get-tuple-element.53), channel_id=1, source_target_pairs={{0,8},{1,9},{2,10},{3,11},{4,12},{5,13},{6,14},{7,15},{8,0},{9,1},... | collective-permute-start | bytes 1585160 | tf_op jit(solution)/shard_map/ppermute | solution.py:28
  73.5 0.8 copy-start.8
  74.3 23.8 %collective-permute-start.18 = (s16[129,16,128]{2,1,0:T(8,128)(2,1)S(1)}, s16[129,16,128]{2,1,0:T(8,128)(2,1)S(1)}, u32[]{:S(2)}, u32[]{:S(2)}) collective-permute-start(s16[129,16,128]{2,1,0:T(8,128)(2,1)S(1)} %get-tuple-element.54), channel_id=1, source_target_pairs={{0,12},{1,13},{2,14},{3,15},{4,0},{5,1},{6,2},{7,3},{8,4},{9,5},{1... | collective-permute-start | bytes 1585160 | tf_op jit(solution)/shard_map/ppermute | solution.py:28
  74.4 30.9 %collective-permute-start.7 = (bf16[4,272,256]{2,1,0:T(8,128)(2,1)S(1)}, bf16[4,272,256]{2,1,0:T(8,128)(2,1)S(1)}, u32[]{:S(2)}, u32[]{:S(2)}) collective-permute-start(bf16[4,272,256]{2,1,0:T(8,128)(2,1)S(1)} %get-tuple-element.89.refs_4_), channel_id=1, source_target_pairs={{0,2},{1,3},{2,0},{3,1},{4,6},{5,7},{6,4},{7,5},{8,10},{9,11},{10,... | collective-permute-start | bytes 1671176 | tf_op jit(solution)/shard_map/ppermute | solution.py:28
  77.7 2.2 copy-start.1
  94.7 63.0 %collective-permute-start.22 = (s16[257,16,128]{2,1,0:T(8,128)(2,1)}, s16[257,16,128]{2,1,0:T(8,128)(2,1)}, u32[]{:S(2)}, u32[]{:S(2)}) collective-permute-start(s16[257,16,128]{2,1,0:T(8,128)(2,1)} %get-tuple-element.60), channel_id=1, source_target_pairs={{0,1},{1,2},{2,3},{3,0},{4,5},{5,6},{6,7},{7,4},{8,9},{9,10},{10,1... | collective-permute-start | bytes 3158024 | tf_op jit(solution)/shard_map/ppermute | solution.py:28
  95.3 63.9 %collective-permute-start.23 = (s16[257,16,128]{2,1,0:T(8,128)(2,1)}, s16[257,16,128]{2,1,0:T(8,128)(2,1)}, u32[]{:S(2)}, u32[]{:S(2)}) collective-permute-start(s16[257,16,128]{2,1,0:T(8,128)(2,1)} %get-tuple-element.61), channel_id=1, source_target_pairs={{0,2},{1,3},{2,0},{3,1},{4,6},{5,7},{6,4},{7,5},{8,10},{9,11},{10,... | collective-permute-start | bytes 3158024 | tf_op jit(solution)/shard_map/ppermute | solution.py:28
  98.0 2.0 copy-start.9
  98.0 61.2 %collective-permute-start.24 = (s16[257,16,128]{2,1,0:T(8,128)(2,1)}, s16[257,16,128]{2,1,0:T(8,128)(2,1)}, u32[]{:S(2)}, u32[]{:S(2)}) collective-permute-start(s16[257,16,128]{2,1,0:T(8,128)(2,1)} %get-tuple-element.62), channel_id=1, source_target_pairs={{0,3},{1,0},{2,1},{3,2},{4,7},{5,4},{6,5},{7,6},{8,11},{9,8},{10,9... | collective-permute-start | bytes 3158024 | tf_op jit(solution)/shard_map/ppermute | solution.py:28
  99.2 58.2 %collective-permute-start.6 = (bf16[4,272,256]{2,1,0:T(8,128)(2,1)}, bf16[4,272,256]{2,1,0:T(8,128)(2,1)S(1)}, u32[]{:S(2)}, u32[]{:S(2)}) collective-permute-start(bf16[4,272,256]{2,1,0:T(8,128)(2,1)} %get-tuple-element.90), channel_id=1, source_target_pairs={{0,1},{1,2},{2,3},{3,0},{4,5},{5,6},{6,7},{7,4},{8,9},{9,10},{10,1... | collective-permute-start | bytes 1671176 | tf_op jit(solution)/shard_map/ppermute | solution.py:28
  105.3 80.6 %collective-permute-start.19 = (s16[65,16,128]{2,1,0:T(8,128)(2,1)}, s16[65,16,128]{2,1,0:T(8,128)(2,1)S(1)}, u32[]{:S(2)}, u32[]{:S(2)}) collective-permute-start(s16[65,16,128]{2,1,0:T(8,128)(2,1)} %get-tuple-element.56), channel_id=1, source_target_pairs={{0,1},{1,2},{2,3},{3,0},{4,5},{5,6},{6,7},{7,4},{8,9},{9,10},{10,1... | collective-permute-start | bytes 798728 | tf_op jit(solution)/shard_map/ppermute | solution.py:28
  157.3 28.6 %collective-permute-start.20 = (s16[65,16,128]{2,1,0:T(8,128)(2,1)}, s16[65,16,128]{2,1,0:T(8,128)(2,1)S(1)}, u32[]{:S(2)}, u32[]{:S(2)}) collective-permute-start(s16[65,16,128]{2,1,0:T(8,128)(2,1)} %get-tuple-element.57), channel_id=1, source_target_pairs={{0,2},{1,3},{2,0},{3,1},{4,6},{5,7},{6,4},{7,5},{8,10},{9,11},{10,... | collective-permute-start | bytes 798728 | tf_op jit(solution)/shard_map/ppermute | solution.py:28
  157.7 28.2 %collective-permute-start.21 = (s16[65,16,128]{2,1,0:T(8,128)(2,1)}, s16[65,16,128]{2,1,0:T(8,128)(2,1)S(1)}, u32[]{:S(2)}, u32[]{:S(2)}) collective-permute-start(s16[65,16,128]{2,1,0:T(8,128)(2,1)} %get-tuple-element.58), channel_id=1, source_target_pairs={{0,3},{1,0},{2,1},{3,2},{4,7},{5,4},{6,5},{7,6},{8,11},{9,8},{10,9... | collective-permute-start | bytes 798728 | tf_op jit(solution)/shard_map/ppermute | solution.py:28
  159.3 7.3 %copy-start.13 = (s32[128,8]{0,1:T(8,128)S(1)}, s32[128,8]{0,1:T(8,128)}, u32[]{:S(2)}) copy-start(s32[128,8]{0,1:T(8,128)} %param.11) | copy-start | bytes 12292
  159.3 21.2 %copy-start.5 = (s32[4]{0:T(128)S(1)}, s32[4]{0:T(128)}, u32[]{:S(2)}) copy-start(s32[4]{0:T(128)} %copy-done.4) | copy-start | bytes 52
  164.6 9.2 %collective-permute-start.25 = (s16[65,16,128]{2,1,0:T(8,128)(2,1)}, s16[65,16,128]{2,1,0:T(8,128)(2,1)S(1)}, u32[]{:S(2)}, u32[]{:S(2)}) collective-permute-start(s16[65,16,128]{2,1,0:T(8,128)(2,1)} %get-tuple-element.64), channel_id=1, source_target_pairs={{0,4},{1,5},{2,6},{3,7},{4,8},{5,9},{6,10},{7,11},{8,12},{9,13},{1... | collective-permute-start | bytes 798728 | tf_op jit(solution)/shard_map/ppermute | solution.py:28
  166.9 9.8 %collective-permute-start.26 = (s16[65,16,128]{2,1,0:T(8,128)(2,1)}, s16[65,16,128]{2,1,0:T(8,128)(2,1)}, u32[]{:S(2)}, u32[]{:S(2)}) collective-permute-start(s16[65,16,128]{2,1,0:T(8,128)(2,1)} %get-tuple-element.65), channel_id=1, source_target_pairs={{0,8},{1,9},{2,10},{3,11},{4,12},{5,13},{6,14},{7,15},{8,0},{9,1},... | collective-permute-start | bytes 798728 | tf_op jit(solution)/shard_map/ppermute | solution.py:28
  173.7 6.7 %collective-permute-start.27 = (s16[65,16,128]{2,1,0:T(8,128)(2,1)}, s16[65,16,128]{2,1,0:T(8,128)(2,1)}, u32[]{:S(2)}, u32[]{:S(2)}) collective-permute-start(s16[65,16,128]{2,1,0:T(8,128)(2,1)} %get-tuple-element.66), channel_id=1, source_target_pairs={{0,12},{1,13},{2,14},{3,15},{4,0},{5,1},{6,2},{7,3},{8,4},{9,5},{1... | collective-permute-start | bytes 798728 | tf_op jit(solution)/shard_map/ppermute | solution.py:28
  180.5 1.0 copy-start.3
  181.4 4.5 %copy-start.2 = (s16[65,16,128]{2,1,0:T(8,128)(2,1)S(1)}, s16[65,16,128]{2,1,0:T(8,128)(2,1)}, u32[]{:S(2)}) copy-start(s16[65,16,128]{2,1,0:T(8,128)(2,1)} %get-tuple-element.55.refs_0_) | copy-start | bytes 798724
  192.9 2.7 %collective-permute-start.28 = (f32[4,16,4,8,128]{4,3,2,1,0:T(8,128)S(1)}, f32[4,16,4,8,128]{4,3,2,1,0:T(8,128)S(1)}, u32[]{:S(2)}, u32[]{:S(2)}) collective-permute-start(f32[4,16,4,8,128]{4,3,2,1,0:T(8,128)S(1)} %get-tuple-element.71), channel_id=1, source_target_pairs={{0,16},{16,0},{32,48},{48,32},{64,80},{80,64},{96,112},{112,96},{1... | collective-permute-start | bytes 3145736 | tf_op jit(solution)/shard_map/ppermute | solution.py:23
  195.8 13.7 %collective-permute-start.31 = (f32[16,4,8,128]{3,2,1,0:T(8,128)S(1)}, f32[16,4,8,128]{3,2,1,0:T(8,128)S(1)}, u32[]{:S(2)}, u32[]{:S(2)}) collective-permute-start(f32[16,4,8,128]{3,2,1,0:T(8,128)S(1)} %get-tuple-element.87), channel_id=1, source_target_pairs={{0,96},{16,112},{32,0},{48,16},{64,32},{80,48},{96,64},{112,80},{1... | collective-permute-start | bytes 786440 | tf_op jit(solution)/shard_map/ppermute | solution.py:23
  198.0 11.5 %collective-permute-start.30 = (f32[16,4,8,128]{3,2,1,0:T(8,128)S(1)}, f32[16,4,8,128]{3,2,1,0:T(8,128)S(1)}, u32[]{:S(2)}, u32[]{:S(2)}) collective-permute-start(f32[16,4,8,128]{3,2,1,0:T(8,128)S(1)} %get-tuple-element.88), channel_id=1, source_target_pairs={{0,64},{16,80},{32,96},{48,112},{64,0},{80,16},{96,32},{112,48},{1... | collective-permute-start | bytes 786440 | tf_op jit(solution)/shard_map/ppermute | solution.py:23
  199.1 14.1 %collective-permute-start.29 = (f32[16,4,8,128]{3,2,1,0:T(8,128)S(1)}, f32[16,4,8,128]{3,2,1,0:T(8,128)S(1)}, u32[]{:S(2)}, u32[]{:S(2)}) collective-permute-start(f32[16,4,8,128]{3,2,1,0:T(8,128)S(1)} %get-tuple-element.86), channel_id=1, source_target_pairs={{0,32},{16,48},{32,64},{48,80},{64,96},{80,112},{96,0},{112,16},{1... | collective-permute-start | bytes 786440 | tf_op jit(solution)/shard_map/ppermute | solution.py:23

commit v7 on v6

--- a/solution.py
+++ b/solution.py
@@ -62,7 +62,7 @@
         in_specs=[pl.BlockSpec((16, KA, B * B), lambda g: (g, 0, 0))],
         out_specs=pl.BlockSpec((16, B, KA * B), lambda g: (g, 0, 0)),
         scratch_shapes=[pltpu.VMEM((4, 128, 128), jnp.float32)],
-        out_shape=pltpu.HBM((128, B, KA * B), jnp.bfloat16),
+        out_shape=pltpu.VMEM((128, B, KA * B), jnp.bfloat16),
         name="spread",
         compiler_params=pltpu.CompilerParams(vmem_limit_bytes=8 * 1024 * 1024),
     )(pltpu.with_memory_space_constraint(a, pltpu.HBM))
@@ -226,7 +226,7 @@
     )(
         idx,
         at,
-        pltpu.with_memory_space_constraint(a, pltpu.HBM),
+        pltpu.with_memory_space_constraint(a, pltpu.VMEM),
         pltpu.with_memory_space_constraint(dup, pltpu.VMEM),
     )
 
@@ -290,7 +290,7 @@
     )(
         idx,
         at,
-        pltpu.with_memory_space_constraint(a, pltpu.HBM),
+        pltpu.with_memory_space_constraint(a, pltpu.VMEM),
         pltpu.with_memory_space_constraint(dup, pltpu.VMEM),
     )
 

time: 236 us -> 236 us (level)
  waiting for transfers between devices: 96.4 us -> 103 us
  Pallas kernels: 65.5 us -> 59.7 us
    ppermute x21, waiting for transfers between devices: 71.3 us -> 77.4 us  [along_col(): return lax.ppermute(v, 'col', pairs)]
    unnamed x28 -> x32, local copies, waits for them, and re-layouts: 4.07 us -> 6.23 us
  transfers between devices with their start and end apart: 32 -> 32, of which waited for: 10 -> 11; matrix products, arithmetic and copies ran while one was open for 2% -> 2% of each run, Pallas kernels for 24% -> 21%
where the time goes in v7:
time: 236 us; the launch traced here: 235 us
  waiting for transfers between devices  103 us (44%)
  Pallas kernels  59.7 us (25%)
  starting transfers between devices  39.2 us (17%)
  blocking collectives  18.5 us (8%)
  local copies, waits for them, and re-layouts  11.8 us (5%)
    ppermute x21, waiting for transfers between devices, along_col(): return lax.ppermute(v, 'col', pairs)  77.4 us
    ppermute x21, starting transfers between devices, along_col(): return lax.ppermute(v, 'col', pairs)  28.2 us
    ppermute x11, waiting for transfers between devices, along_row(): return lax.ppermute(v, 'row', pairs)  25.2 us
    all_to_all x1, blocking collectives, step(): both = lax.all_to_all(both, 'col', 0, 0, tiled=True)  18.5 us
    pallas_call x2, Pallas kernels, x_products(): pl.pallas_call(lambda *refs: x_product_kernel(j, *refs), grid_spec=pltpu....  13 us
    pallas_call x2, Pallas kernels, y_products(): pl.pallas_call(lambda *refs: y_product_kernel(part, *refs), grid_spec=plt...  12.5 us
    ppermute x11, starting transfers between devices, along_row(): return lax.ppermute(v, 'row', pairs)  11 us
    pallas_call x2, Pallas kernels, middle(): pl.pallas_call(kernel, in_specs=[pl.BlockSpec(memory_space=pltpu.SMEM)] +...  10.4 us
  transfers between devices with their start and end apart: 32, of which 11 were waited for; matrix products, arithmetic and copies ran while one was open for 2% of the time, Pallas kernels for 21%

profile of v7, /device:TPU:0, one launch (start us, length us, event | category | flops | bytes accessed | tf_op | source)
XLA Modules:
  0.0 235.1 jit_solution(6194917279029654173)
XLA Ops:
  0.6 0.7 convert_bitcast_fusion
  1.4 1.4 reshape_squeeze.3
  2.9 0.3 copy.61
  3.2 0.3 reshape.136
  3.5 2.1 collective-permute-start
  5.6 3.6 %collective-permute-start.1 = (bf16[528,256]{1,0:T(8,128)(2,1)S(1)}, bf16[528,256]{1,0:T(8,128)(2,1)S(1)}, u32[]{:S(2)}, u32[]{:S(2)}) collective-permute-start(bf16[528,256]{1,0:T(8,128)(2,1)S(1)} %fusion.3.refs_0_), channel_id=1, source_target_pairs={{0,64},{16,80},{32,96},{48,112},{64,0},{80,16},{96,32},{112,48},{1... | collective-permute-start | bytes 811016 | tf_op jit(solution)/shard_map/ppermute | solution.py:23
  9.2 1.0 collective-permute-start.2
  10.3 0.4 reshape_reshape_squeeze.3
  10.9 0.4 fusion.26
  11.2 0.2 copy.63
  11.5 0.2 squeeze.17
  11.8 0.2 copy.65
  12.0 0.2 squeeze.18
  12.4 1.9 collective-permute-done.refs_2_
  14.2 7.0 %collective-permute-done.1.refs_4_ = bf16[528,256]{1,0:T(8,128)(2,1)S(1)} collective-permute-done((bf16[528,256]{1,0:T(8,128)(2,1)S(1)}, bf16[528,256]{1,0:T(8,128)(2,1)S(1)}, u32[]{:S(2)}, u32[]{:S(2)}) %collective-permute-start.1) | collective-permute-done | bytes 270368 | tf_op jit(solution)/shard_map/ppermute | solution.py:23
  21.2 0.5 collective-permute-start.11
  21.8 6.9 %spread.1 = bf16[128,64,256]{2,1,0:T(8,128)(2,1)S(1)} custom-call(bf16[128,4,4096]{2,1,0:T(4,128)(2,1)} %bitcast.92), custom_call_target="tpu_custom_call" | custom-call | tf_op jit(solution)/shard_map/spread/pallas_call | solution.py:59
  28.7 3.1 %collective-permute-start.5 = (bf16[2,272,256]{2,1,0:T(8,128)(2,1)S(1)}, bf16[2,272,256]{2,1,0:T(8,128)(2,1)S(1)}, u32[]{:S(2)}, u32[]{:S(2)}) collective-permute-start(bf16[2,272,256]{2,1,0:T(8,128)(2,1)S(1)} %pad_maximum_fusion.1), channel_id=1, source_target_pairs={{0,12},{1,13},{2,14},{3,15},{4,0},{5,1},{6,2},{7,3},{8,4},{9,5},{1... | collective-permute-start | bytes 835592 | tf_op jit(solution)/shard_map/ppermute | solution.py:28
  31.8 0.6 collective-permute-start.4
  32.4 1.0 collective-permute-start.3
  33.4 2.9 %table.1 = (bf16[257,64,128]{2,1,0:T(8,128)(2,1)S(1)}, f32[64,128]{1,0:T(8,128)S(1)}) custom-call(bf16[528,256]{1,0:T(8,128)(2,1)S(1)} %fusion.3.refs_0_, bf16[528,256]{1,0:T(8,128)(2,1)S(1)} %collective-permute-done.9.refs_1_, bf16[528,256]{1,0:T(8,128)(2,1)S(1)} %collective-permute-done.refs_2_, bf16[528,256]{1,0:T(8,128)(2,1)S(1)} %collective-permute-done.10.refs_3_, ...), custom_call_target="tpu_custom_call" | custom-call | tf_op jit(solution)/shard_map/table/pallas_call | solution.py:92
  36.5 6.1 %shard_map.77 = (s16[129,16,128]{2,1,0:T(8,128)(2,1)}, s16[129,16,128]{2,1,0:T(8,128)(2,1)S(1)}, s16[129,16,128]{2,1,0:T(8,128)(2,1)S(1)}, s16[129,16,128]{2,1,0:T(8,128)(2,1)S(1)}) custom-call(s32[32,128]{1,0:T(8,128)S(1)} %bitcast.88, s32[4]{0:T(128)S(1)} %pad_add_fusion.refs_1_.at_ref, bf16[4,2,16,64,256]{4,3,2,1,0:T(8,128)(2,1)S(1)} %bitcast.84, ...), custom_call_target="tpu_custom_call" | custom-call | tf_op jit(solution)/shard_map/pallas_call | solution.py:272
  42.6 1.9 collective-permute-start.13
  44.5 1.8 collective-permute-start.14
  46.4 1.7 collective-permute-start.15
  48.3 0.9 dynamic-slice_bitcast_fusion.1
  49.2 2.8 %collective-permute-start.8 = (bf16[4,272,256]{2,1,0:T(8,128)(2,1)}, bf16[4,272,256]{2,1,0:T(8,128)(2,1)S(1)}, u32[]{:S(2)}, u32[]{:S(2)}) collective-permute-start(bf16[4,272,256]{2,1,0:T(8,128)(2,1)} %get-tuple-element.90), channel_id=1, source_target_pairs={{0,3},{1,0},{2,1},{3,2},{4,7},{5,4},{6,5},{7,6},{8,11},{9,8},{10,9... | collective-permute-start | bytes 1671176 | tf_op jit(solution)/shard_map/ppermute | solution.py:28
  52.0 6.4 %shard_map.78 = (s16[129,16,128]{2,1,0:T(8,128)(2,1)}, s16[129,16,128]{2,1,0:T(8,128)(2,1)}, s16[129,16,128]{2,1,0:T(8,128)(2,1)S(1)}, s16[129,16,128]{2,1,0:T(8,128)(2,1)S(1)}) custom-call(s32[32,128]{1,0:T(8,128)S(1)} %bitcast.89, s32[4]{0:T(128)S(1)} %pad_add_fusion.refs_1_.at_ref, bf16[4,2,16,64,256]{4,3,2,1,0:T(8,128)(2,1)S(1)} %bitcast.85, ...), custom_call_target="tpu_custom_call" | custom-call | tf_op jit(solution)/shard_map/pallas_call | solution.py:272
  58.3 0.2 collective-permute-start.16
  58.6 1.5 collective-permute-done.13.refs_1_
  60.1 0.9 collective-permute-start.17
  61.0 10.5 %collective-permute-done.14.refs_2_ = s16[129,16,128]{2,1,0:T(8,128)(2,1)S(1)} collective-permute-done((s16[129,16,128]{2,1,0:T(8,128)(2,1)S(1)}, s16[129,16,128]{2,1,0:T(8,128)(2,1)S(1)}, u32[]{:S(2)}, u32[]{:S(2)}) %collective-permute-start.14) | collective-permute-done | bytes 528416 | tf_op jit(solution)/shard_map/ppermute | solution.py:28
  71.5 0.8 copy-done.10
  72.4 3.3 %collective-permute-start.7 = (bf16[4,272,256]{2,1,0:T(8,128)(2,1)S(1)}, bf16[4,272,256]{2,1,0:T(8,128)(2,1)S(1)}, u32[]{:S(2)}, u32[]{:S(2)}) collective-permute-start(bf16[4,272,256]{2,1,0:T(8,128)(2,1)S(1)} %get-tuple-element.89.refs_4_), channel_id=1, source_target_pairs={{0,2},{1,3},{2,0},{3,1},{4,6},{5,7},{6,4},{7,5},{8,10},{9,11},{10,... | collective-permute-start | bytes 1671176 | tf_op jit(solution)/shard_map/ppermute | solution.py:28
  75.7 2.2 copy-done.1
  77.9 2.2 copy-done.3
  80.1 6.5 %shard_map.80 = (s16[257,16,128]{2,1,0:T(8,128)(2,1)}, s16[257,16,128]{2,1,0:T(8,128)(2,1)}) custom-call(s32[32,128]{1,0:T(8,128)S(1)} %bitcast.90, s32[4]{0:T(128)S(1)} %pad_add_fusion.refs_1_.at_ref, bf16[4,2,16,64,256]{4,3,2,1,0:T(8,128)(2,1)S(1)} %bitcast.86, bf16[257,64,128]{2,1,0:T(8,128)(2,1)S(1)} %copy-done.3), custom_call_target="tpu_custom_call" | custom-call | tf_op jit(solution)/shard_map/pallas_call | solution.py:205
  86.6 6.5 %shard_map.81 = (s16[257,16,128]{2,1,0:T(8,128)(2,1)}, s16[257,16,128]{2,1,0:T(8,128)(2,1)}) custom-call(s32[32,128]{1,0:T(8,128)S(1)} %bitcast.91, s32[4]{0:T(128)S(1)} %pad_add_fusion.refs_1_.at_ref, bf16[4,2,16,64,256]{4,3,2,1,0:T(8,128)(2,1)S(1)} %bitcast.87, bf16[257,64,128]{2,1,0:T(8,128)(2,1)S(1)} %copy-done.3), custom_call_target="tpu_custom_call" | custom-call | tf_op jit(solution)/shard_map/pallas_call | solution.py:205
  93.2 0.6 collective-permute-start.22
  93.7 2.8 %collective-permute-start.23 = (s16[257,16,128]{2,1,0:T(8,128)(2,1)}, s16[257,16,128]{2,1,0:T(8,128)(2,1)}, u32[]{:S(2)}, u32[]{:S(2)}) collective-permute-start(s16[257,16,128]{2,1,0:T(8,128)(2,1)} %get-tuple-element.61), channel_id=1, source_target_pairs={{0,2},{1,3},{2,0},{3,1},{4,6},{5,7},{6,4},{7,5},{8,10},{9,11},{10,... | collective-permute-start | bytes 3158024 | tf_op jit(solution)/shard_map/ppermute | solution.py:28
  96.6 1.1 collective-permute-start.24
  97.7 0.9 collective-permute-start.6
  98.6 5.2 %shard_map.79 = (s16[65,16,128]{2,1,0:T(8,128)(2,1)}, s16[65,16,128]{2,1,0:T(8,128)(2,1)}, s16[65,16,128]{2,1,0:T(8,128)(2,1)}, s16[65,16,128]{2,1,0:T(8,128)(2,1)}) custom-call(s32[4]{0:T(128)} %copy-done.6, s16[129,16,128]{2,1,0:T(8,128)(2,1)} %get-tuple-element.47.refs_0_, s16[129,16,128]{2,1,0:T(8,128)(2,1)} %copy-done.9, ...), custom_call_target="tpu_custom_call" | custom-call | tf_op jit(solution)/shard_map/pallas_call | solution.py:362
  103.8 0.7 collective-permute-start.19
  104.6 50.7 %collective-permute-done.6.refs_5_ = bf16[4,272,256]{2,1,0:T(8,128)(2,1)S(1)} collective-permute-done((bf16[4,272,256]{2,1,0:T(8,128)(2,1)}, bf16[4,272,256]{2,1,0:T(8,128)(2,1)S(1)}, u32[]{:S(2)}, u32[]{:S(2)}) %collective-permute-start.6) | collective-permute-done | bytes 557088 | tf_op jit(solution)/shard_map/ppermute | solution.py:28
  155.7 1.9 collective-permute-start.21
  157.7 5.2 %shard_map.82 = (s16[65,16,128]{2,1,0:T(8,128)(2,1)}, s16[65,16,128]{2,1,0:T(8,128)(2,1)}, s16[65,16,128]{2,1,0:T(8,128)(2,1)}, s16[65,16,128]{2,1,0:T(8,128)(2,1)}) custom-call(s32[4]{0:T(128)} %copy-done.6, s16[257,16,128]{2,1,0:T(8,128)(2,1)} %get-tuple-element.59.m0, s16[257,16,128]{2,1,0:T(8,128)(2,1)} %collective-permute-done.22.m1, ...), custom_call_target="tpu_custom_call" | custom-call | tf_op jit(solution)/shard_map/pallas_call | solution.py:362
  162.9 2.0 collective-permute-start.25
  165.0 0.3 convolution_convert_fusion
  165.3 0.8 collective-permute-start.26
  166.1 8.3 %collective-permute-done.25.refs_1_ = s16[65,16,128]{2,1,0:T(8,128)(2,1)S(1)} collective-permute-done((s16[65,16,128]{2,1,0:T(8,128)(2,1)}, s16[65,16,128]{2,1,0:T(8,128)(2,1)S(1)}, u32[]{:S(2)}, u32[]{:S(2)}) %collective-permute-start.25) | collective-permute-done | bytes 266272 | tf_op jit(solution)/shard_map/ppermute | solution.py:28
  174.3 0.2 select_reduce_fusion
  174.9 6.2 %collective-permute-done.27.refs_3_ = s16[65,16,128]{2,1,0:T(8,128)(2,1)} collective-permute-done((s16[65,16,128]{2,1,0:T(8,128)(2,1)}, s16[65,16,128]{2,1,0:T(8,128)(2,1)}, u32[]{:S(2)}, u32[]{:S(2)}) %collective-permute-start.27) | collective-permute-done | bytes 266272 | tf_op jit(solution)/shard_map/ppermute | solution.py:28
  181.1 1.0 copy-done.5
  182.0 4.5 %first_coarse.1 = (bf16[16,64,128]{2,1,0:T(8,128)(2,1)S(1)}, f32[1025,8,128]{2,1,0:T(8,128)S(1)}) custom-call(s32[2048]{0:T(1024)S(1)} %reshape.139.tgt_ref, s32[4]{0:T(128)S(1)} %copy-done.7, s16[65,16,128]{2,1,0:T(8,128)(2,1)S(1)} %copy-done.5, s16[65,16,128]{2,1,0:T(8,128)(2,1)S(1)} %collective-permute-done.25.refs_1_, ...), custom_call_target="tpu_custom_call" | custom-call | tf_op jit(solution)/shard_map/first_coarse/pallas_call | solution.py:469
  186.5 6.9 %second_coarse.1 = (bf16[16,192,128]{2,1,0:T(8,128)(2,1)S(1)}, f32[4,16,4,8,128]{4,3,2,1,0:T(8,128)S(1)}, f32[4,16,4,8,128]{4,3,2,1,0:T(8,128)S(1)}) custom-call(s32[2048]{0:T(1024)S(1)} %reshape.139.tgt_ref, s32[4]{0:T(128)S(1)} %copy-done.7, s16[65,16,128]{2,1,0:T(8,128)(2,1)S(1)} %copy-done.4, s16[65,16,128]{2,1,0:T(8,128)(2,1)S(1)} %collective-permute-done.19.refs_1_, ...), custom_call_target="tpu_custom_call" | custom-call | tf_op jit(solution)/shard_map/second_coarse/pallas_call | solution.py:493
  193.6 2.6 %collective-permute-done.28 = f32[4,16,4,8,128]{4,3,2,1,0:T(8,128)S(1)} collective-permute-done((f32[4,16,4,8,128]{4,3,2,1,0:T(8,128)S(1)}, f32[4,16,4,8,128]{4,3,2,1,0:T(8,128)S(1)}, u32[]{:S(2)}, u32[]{:S(2)}) %collective-permute-start.28) | collective-permute-done | bytes 1048608 | tf_op jit(solution)/shard_map/ppermute | solution.py:23
  196.4 2.2 collective-permute-start.31
  198.6 1.1 collective-permute-start.30
  199.7 0.4 collective-permute-start.29
  200.1 10.0 %collective-permute-done.31 = f32[16,4,8,128]{3,2,1,0:T(8,128)S(1)} collective-permute-done((f32[16,4,8,128]{3,2,1,0:T(8,128)S(1)}, f32[16,4,8,128]{3,2,1,0:T(8,128)S(1)}, u32[]{:S(2)}, u32[]{:S(2)}) %collective-permute-start.31) | collective-permute-done | bytes 262176 | tf_op jit(solution)/shard_map/ppermute | solution.py:23
  210.1 3.7 %collective-permute-done.29 = f32[16,4,8,128]{3,2,1,0:T(8,128)S(1)} collective-permute-done((f32[16,4,8,128]{3,2,1,0:T(8,128)S(1)}, f32[16,4,8,128]{3,2,1,0:T(8,128)S(1)}, u32[]{:S(2)}, u32[]{:S(2)}) %collective-permute-start.29) | collective-permute-done | bytes 262176 | tf_op jit(solution)/shard_map/ppermute | solution.py:23
  214.0 18.5 %all_to_all.5.x_ref = bf16[16,192,128]{2,1,0:T(8,128)(2,1)} all-to-all(bf16[16,192,128]{2,1,0:T(8,128)(2,1)S(1)} %maximum_dynamic-update-slice_fusion), channel_id=1, replica_groups=mesh['row'=8,'col'=16] {'col'}, dimensions={0} | all-to-all | bytes 1572864 | tf_op jit(solution)/shard_map/all_to_all | solution.py:674
  232.5 2.6 %layout.1 = (bf16[8,8,4096]{2,1,0:T(8,128)(2,1)}, f32[8,4096]{1,0:T(8,128)}) custom-call(bf16[16,192,128]{2,1,0:T(8,128)(2,1)} %all_to_all.5.x_ref), custom_call_target="tpu_custom_call" | custom-call | tf_op jit(solution)/shard_map/layout/pallas_call | solution.py:558
  (91 shorter events, 2.4 us)
Async XLA Ops:
  2.8 7.4 %copy-start.13 = (s32[8,1,4]{0,2,1:T(4,128)S(1)}, s32[8,1,4]{0,2,1:T(4,128)}, u32[]{:S(2)}) copy-start(s32[8,1,4]{0,2,1:T(4,128)} %param.9) | copy-start | bytes 388
  2.8 7.4 %copy-start.8 = (bf16[8,1,4,4096]{3,2,1,0:T(4,128)(2,1)S(1)}, bf16[8,1,4,4096]{3,2,1,0:T(4,128)(2,1)}, u32[]{:S(2)}) copy-start(bf16[8,1,4,4096]{3,2,1,0:T(4,128)(2,1)} %param.8) | copy-start | bytes 786436
  3.5 10.7 %collective-permute-start = (bf16[528,256]{1,0:T(8,128)(2,1)S(1)}, bf16[528,256]{1,0:T(8,128)(2,1)S(1)}, u32[]{:S(2)}, u32[]{:S(2)}) collective-permute-start(bf16[528,256]{1,0:T(8,128)(2,1)S(1)} %fusion.3.refs_0_), channel_id=1, source_target_pairs={{0,32},{16,48},{32,64},{48,80},{64,96},{80,112},{96,0},{112,16},{1... | collective-permute-start | bytes 811016 | tf_op jit(solution)/shard_map/ppermute | solution.py:23
  5.6 15.6 %collective-permute-start.1 = (bf16[528,256]{1,0:T(8,128)(2,1)S(1)}, bf16[528,256]{1,0:T(8,128)(2,1)S(1)}, u32[]{:S(2)}, u32[]{:S(2)}) collective-permute-start(bf16[528,256]{1,0:T(8,128)(2,1)S(1)} %fusion.3.refs_0_), channel_id=1, source_target_pairs={{0,64},{16,80},{32,96},{48,112},{64,0},{80,16},{96,32},{112,48},{1... | collective-permute-start | bytes 811016 | tf_op jit(solution)/shard_map/ppermute | solution.py:23
  9.2 12.0 %collective-permute-start.2 = (bf16[528,256]{1,0:T(8,128)(2,1)S(1)}, bf16[528,256]{1,0:T(8,128)(2,1)S(1)}, u32[]{:S(2)}, u32[]{:S(2)}) collective-permute-start(bf16[528,256]{1,0:T(8,128)(2,1)S(1)} %fusion.3.refs_0_), channel_id=1, source_target_pairs={{0,96},{16,112},{32,0},{48,16},{64,32},{80,48},{96,64},{112,80},{1... | collective-permute-start | bytes 811016 | tf_op jit(solution)/shard_map/ppermute | solution.py:23
  10.2 21.6 %collective-permute-start.9 = (bf16[528,256]{1,0:T(8,128)(2,1)S(1)}, bf16[528,256]{1,0:T(8,128)(2,1)S(1)}, u32[]{:S(2)}, u32[]{:S(2)}) collective-permute-start(bf16[528,256]{1,0:T(8,128)(2,1)S(1)} %fusion.3.refs_0_), channel_id=1, source_target_pairs={{0,16},{16,0},{32,48},{48,32},{64,80},{80,64},{96,112},{112,96},{1... | collective-permute-start | bytes 811016 | tf_op jit(solution)/shard_map/ppermute | solution.py:23
  11.7 0.7 copy-start.14
  21.2 11.2 %collective-permute-start.10 = (bf16[528,256]{1,0:T(8,128)(2,1)S(1)}, bf16[528,256]{1,0:T(8,128)(2,1)S(1)}, u32[]{:S(2)}, u32[]{:S(2)}) collective-permute-start(bf16[528,256]{1,0:T(8,128)(2,1)S(1)} %collective-permute-done.refs_2_), channel_id=1, source_target_pairs={{0,16},{16,0},{32,48},{48,32},{64,80},{80,64},{96,112},{112,96},{1... | collective-permute-start | bytes 811016 | tf_op jit(solution)/shard_map/ppermute | solution.py:23
  21.2 12.2 %collective-permute-start.11 = (bf16[528,256]{1,0:T(8,128)(2,1)S(1)}, bf16[528,256]{1,0:T(8,128)(2,1)S(1)}, u32[]{:S(2)}, u32[]{:S(2)}) collective-permute-start(bf16[528,256]{1,0:T(8,128)(2,1)S(1)} %collective-permute-done.1.refs_4_), channel_id=1, source_target_pairs={{0,16},{16,0},{32,48},{48,32},{64,80},{80,64},{96,112},{112,96},{1... | collective-permute-start | bytes 811016 | tf_op jit(solution)/shard_map/ppermute | solution.py:23
  21.7 11.7 %collective-permute-start.12 = (bf16[528,256]{1,0:T(8,128)(2,1)S(1)}, bf16[528,256]{1,0:T(8,128)(2,1)S(1)}, u32[]{:S(2)}, u32[]{:S(2)}) collective-permute-start(bf16[528,256]{1,0:T(8,128)(2,1)S(1)} %collective-permute-done.2.refs_6_), channel_id=1, source_target_pairs={{0,16},{16,0},{32,48},{48,32},{64,80},{80,64},{96,112},{112,96},{1... | collective-permute-start | bytes 811016 | tf_op jit(solution)/shard_map/ppermute | solution.py:23
  21.8 64.8 %copy-start.6 = (s32[4]{0:T(128)}, s32[4]{0:T(128)S(1)}, u32[]{:S(2)}) copy-start(s32[4]{0:T(128)S(1)} %pad_add_fusion.refs_1_.at_ref) | copy-start | bytes 52
  28.7 23.3 %copy-start = (bf16[128,64,256]{2,1,0:T(8,128)(2,1)}, bf16[128,64,256]{2,1,0:T(8,128)(2,1)S(1)}, u32[]{:S(2)}) copy-start(bf16[128,64,256]{2,1,0:T(8,128)(2,1)S(1)} %spread.1) | copy-start | bytes 12582916
  28.7 7.8 %copy-start.12 = (s32[128,8]{0,1:T(8,128)S(1)}, s32[128,8]{0,1:T(8,128)}, u32[]{:S(2)}) copy-start(s32[128,8]{0,1:T(8,128)} %param.10) | copy-start | bytes 12292
  28.7 17.7 %collective-permute-start.5 = (bf16[2,272,256]{2,1,0:T(8,128)(2,1)S(1)}, bf16[2,272,256]{2,1,0:T(8,128)(2,1)S(1)}, u32[]{:S(2)}, u32[]{:S(2)}) collective-permute-start(bf16[2,272,256]{2,1,0:T(8,128)(2,1)S(1)} %pad_maximum_fusion.1), channel_id=1, source_target_pairs={{0,12},{1,13},{2,14},{3,15},{4,0},{5,1},{6,2},{7,3},{8,4},{9,5},{1... | collective-permute-start | bytes 835592 | tf_op jit(solution)/shard_map/ppermute | solution.py:28
  31.8 16.2 %collective-permute-start.4 = (bf16[2,272,256]{2,1,0:T(8,128)(2,1)S(1)}, bf16[2,272,256]{2,1,0:T(8,128)(2,1)S(1)}, u32[]{:S(2)}, u32[]{:S(2)}) collective-permute-start(bf16[2,272,256]{2,1,0:T(8,128)(2,1)S(1)} %pad_maximum_fusion.1), channel_id=1, source_target_pairs={{0,8},{1,9},{2,10},{3,11},{4,12},{5,13},{6,14},{7,15},{8,0},{9,1},... | collective-permute-start | bytes 835592 | tf_op jit(solution)/shard_map/ppermute | solution.py:28
  32.4 15.7 %collective-permute-start.3 = (bf16[2,272,256]{2,1,0:T(8,128)(2,1)S(1)}, bf16[2,272,256]{2,1,0:T(8,128)(2,1)S(1)}, u32[]{:S(2)}, u32[]{:S(2)}) collective-permute-start(bf16[2,272,256]{2,1,0:T(8,128)(2,1)S(1)} %pad_maximum_fusion.1), channel_id=1, source_target_pairs={{0,4},{1,5},{2,6},{3,7},{4,8},{5,9},{6,10},{7,11},{8,12},{9,13},{1... | collective-permute-start | bytes 835592 | tf_op jit(solution)/shard_map/ppermute | solution.py:28
  36.3 15.7 %copy-start.2 = (bf16[257,64,128]{2,1,0:T(8,128)(2,1)}, bf16[257,64,128]{2,1,0:T(8,128)(2,1)S(1)}, u32[]{:S(2)}) copy-start(bf16[257,64,128]{2,1,0:T(8,128)(2,1)S(1)} %get-tuple-element.46.refs_3_) | copy-start | bytes 12632068
  42.6 17.4 %collective-permute-start.13 = (s16[129,16,128]{2,1,0:T(8,128)(2,1)S(1)}, s16[129,16,128]{2,1,0:T(8,128)(2,1)S(1)}, u32[]{:S(2)}, u32[]{:S(2)}) collective-permute-start(s16[129,16,128]{2,1,0:T(8,128)(2,1)S(1)} %get-tuple-element.48), channel_id=1, source_target_pairs={{0,4},{1,5},{2,6},{3,7},{4,8},{5,9},{6,10},{7,11},{8,12},{9,13},{1... | collective-permute-start | bytes 1585160 | tf_op jit(solution)/shard_map/ppermute | solution.py:28
  44.5 27.0 %collective-permute-start.14 = (s16[129,16,128]{2,1,0:T(8,128)(2,1)S(1)}, s16[129,16,128]{2,1,0:T(8,128)(2,1)S(1)}, u32[]{:S(2)}, u32[]{:S(2)}) collective-permute-start(s16[129,16,128]{2,1,0:T(8,128)(2,1)S(1)} %get-tuple-element.49), channel_id=1, source_target_pairs={{0,8},{1,9},{2,10},{3,11},{4,12},{5,13},{6,14},{7,15},{8,0},{9,1},... | collective-permute-start | bytes 1585160 | tf_op jit(solution)/shard_map/ppermute | solution.py:28
  46.4 26.1 %collective-permute-start.15 = (s16[129,16,128]{2,1,0:T(8,128)(2,1)S(1)}, s16[129,16,128]{2,1,0:T(8,128)(2,1)}, u32[]{:S(2)}, u32[]{:S(2)}) collective-permute-start(s16[129,16,128]{2,1,0:T(8,128)(2,1)S(1)} %get-tuple-element.50), channel_id=1, source_target_pairs={{0,12},{1,13},{2,14},{3,15},{4,0},{5,1},{6,2},{7,3},{8,4},{9,5},{1... | collective-permute-start | bytes 1585160 | tf_op jit(solution)/shard_map/ppermute | solution.py:28
  49.2 48.5 %collective-permute-start.8 = (bf16[4,272,256]{2,1,0:T(8,128)(2,1)}, bf16[4,272,256]{2,1,0:T(8,128)(2,1)S(1)}, u32[]{:S(2)}, u32[]{:S(2)}) collective-permute-start(bf16[4,272,256]{2,1,0:T(8,128)(2,1)} %get-tuple-element.90), channel_id=1, source_target_pairs={{0,3},{1,0},{2,1},{3,2},{4,7},{5,4},{6,5},{7,6},{8,11},{9,8},{10,9... | collective-permute-start | bytes 1671176 | tf_op jit(solution)/shard_map/ppermute | solution.py:28
  58.3 34.8 %collective-permute-start.16 = (s16[129,16,128]{2,1,0:T(8,128)(2,1)}, s16[129,16,128]{2,1,0:T(8,128)(2,1)}, u32[]{:S(2)}, u32[]{:S(2)}) collective-permute-start(s16[129,16,128]{2,1,0:T(8,128)(2,1)} %get-tuple-element.52), channel_id=1, source_target_pairs={{0,4},{1,5},{2,6},{3,7},{4,8},{5,9},{6,10},{7,11},{8,12},{9,13},{1... | collective-permute-start | bytes 1585160 | tf_op jit(solution)/shard_map/ppermute | solution.py:28
  60.1 11.5 %copy-start.9 = (s16[129,16,128]{2,1,0:T(8,128)(2,1)}, s16[129,16,128]{2,1,0:T(8,128)(2,1)S(1)}, u32[]{:S(2)}) copy-start(s16[129,16,128]{2,1,0:T(8,128)(2,1)S(1)} %collective-permute-done.13.refs_1_) | copy-start | bytes 1585156
  60.1 33.6 %collective-permute-start.17 = (s16[129,16,128]{2,1,0:T(8,128)(2,1)S(1)}, s16[129,16,128]{2,1,0:T(8,128)(2,1)}, u32[]{:S(2)}, u32[]{:S(2)}) collective-permute-start(s16[129,16,128]{2,1,0:T(8,128)(2,1)S(1)} %get-tuple-element.53), channel_id=1, source_target_pairs={{0,8},{1,9},{2,10},{3,11},{4,12},{5,13},{6,14},{7,15},{8,0},{9,1},... | collective-permute-start | bytes 1585160 | tf_op jit(solution)/shard_map/ppermute | solution.py:28
  71.5 0.8 copy-start.10
  72.3 24.3 %collective-permute-start.18 = (s16[129,16,128]{2,1,0:T(8,128)(2,1)S(1)}, s16[129,16,128]{2,1,0:T(8,128)(2,1)S(1)}, u32[]{:S(2)}, u32[]{:S(2)}) collective-permute-start(s16[129,16,128]{2,1,0:T(8,128)(2,1)S(1)} %get-tuple-element.54), channel_id=1, source_target_pairs={{0,12},{1,13},{2,14},{3,15},{4,0},{5,1},{6,2},{7,3},{8,4},{9,5},{1... | collective-permute-start | bytes 1585160 | tf_op jit(solution)/shard_map/ppermute | solution.py:28
  72.4 31.4 %collective-permute-start.7 = (bf16[4,272,256]{2,1,0:T(8,128)(2,1)S(1)}, bf16[4,272,256]{2,1,0:T(8,128)(2,1)S(1)}, u32[]{:S(2)}, u32[]{:S(2)}) collective-permute-start(bf16[4,272,256]{2,1,0:T(8,128)(2,1)S(1)} %get-tuple-element.89.refs_4_), channel_id=1, source_target_pairs={{0,2},{1,3},{2,0},{3,1},{4,6},{5,7},{6,4},{7,5},{8,10},{9,11},{10,... | collective-permute-start | bytes 1671176 | tf_op jit(solution)/shard_map/ppermute | solution.py:28
  75.7 2.2 copy-start.1
  77.9 2.2 copy-start.3
  93.2 62.6 %collective-permute-start.22 = (s16[257,16,128]{2,1,0:T(8,128)(2,1)}, s16[257,16,128]{2,1,0:T(8,128)(2,1)}, u32[]{:S(2)}, u32[]{:S(2)}) collective-permute-start(s16[257,16,128]{2,1,0:T(8,128)(2,1)} %get-tuple-element.60), channel_id=1, source_target_pairs={{0,1},{1,2},{2,3},{3,0},{4,5},{5,6},{6,7},{7,4},{8,9},{9,10},{10,1... | collective-permute-start | bytes 3158024 | tf_op jit(solution)/shard_map/ppermute | solution.py:28
  93.7 63.9 %collective-permute-start.23 = (s16[257,16,128]{2,1,0:T(8,128)(2,1)}, s16[257,16,128]{2,1,0:T(8,128)(2,1)}, u32[]{:S(2)}, u32[]{:S(2)}) collective-permute-start(s16[257,16,128]{2,1,0:T(8,128)(2,1)} %get-tuple-element.61), channel_id=1, source_target_pairs={{0,2},{1,3},{2,0},{3,1},{4,6},{5,7},{6,4},{7,5},{8,10},{9,11},{10,... | collective-permute-start | bytes 3158024 | tf_op jit(solution)/shard_map/ppermute | solution.py:28
  96.6 2.0 copy-start.11
  96.6 61.1 %collective-permute-start.24 = (s16[257,16,128]{2,1,0:T(8,128)(2,1)}, s16[257,16,128]{2,1,0:T(8,128)(2,1)}, u32[]{:S(2)}, u32[]{:S(2)}) collective-permute-start(s16[257,16,128]{2,1,0:T(8,128)(2,1)} %get-tuple-element.62), channel_id=1, source_target_pairs={{0,3},{1,0},{2,1},{3,2},{4,7},{5,4},{6,5},{7,6},{8,11},{9,8},{10,9... | collective-permute-start | bytes 3158024 | tf_op jit(solution)/shard_map/ppermute | solution.py:28
  97.7 57.6 %collective-permute-start.6 = (bf16[4,272,256]{2,1,0:T(8,128)(2,1)}, bf16[4,272,256]{2,1,0:T(8,128)(2,1)S(1)}, u32[]{:S(2)}, u32[]{:S(2)}) collective-permute-start(bf16[4,272,256]{2,1,0:T(8,128)(2,1)} %get-tuple-element.90), channel_id=1, source_target_pairs={{0,1},{1,2},{2,3},{3,0},{4,5},{5,6},{6,7},{7,4},{8,9},{9,10},{10,1... | collective-permute-start | bytes 1671176 | tf_op jit(solution)/shard_map/ppermute | solution.py:28
  103.8 82.7 %collective-permute-start.19 = (s16[65,16,128]{2,1,0:T(8,128)(2,1)}, s16[65,16,128]{2,1,0:T(8,128)(2,1)S(1)}, u32[]{:S(2)}, u32[]{:S(2)}) collective-permute-start(s16[65,16,128]{2,1,0:T(8,128)(2,1)} %get-tuple-element.56), channel_id=1, source_target_pairs={{0,1},{1,2},{2,3},{3,0},{4,5},{5,6},{6,7},{7,4},{8,9},{9,10},{10,1... | collective-permute-start | bytes 798728 | tf_op jit(solution)/shard_map/ppermute | solution.py:28
  155.3 31.2 %collective-permute-start.20 = (s16[65,16,128]{2,1,0:T(8,128)(2,1)}, s16[65,16,128]{2,1,0:T(8,128)(2,1)S(1)}, u32[]{:S(2)}, u32[]{:S(2)}) collective-permute-start(s16[65,16,128]{2,1,0:T(8,128)(2,1)} %get-tuple-element.57), channel_id=1, source_target_pairs={{0,2},{1,3},{2,0},{3,1},{4,6},{5,7},{6,4},{7,5},{8,10},{9,11},{10,... | collective-permute-start | bytes 798728 | tf_op jit(solution)/shard_map/ppermute | solution.py:28
  155.7 30.8 %collective-permute-start.21 = (s16[65,16,128]{2,1,0:T(8,128)(2,1)}, s16[65,16,128]{2,1,0:T(8,128)(2,1)S(1)}, u32[]{:S(2)}, u32[]{:S(2)}) collective-permute-start(s16[65,16,128]{2,1,0:T(8,128)(2,1)} %get-tuple-element.58), channel_id=1, source_target_pairs={{0,3},{1,0},{2,1},{3,2},{4,7},{5,4},{6,5},{7,6},{8,11},{9,8},{10,9... | collective-permute-start | bytes 798728 | tf_op jit(solution)/shard_map/ppermute | solution.py:28
  157.7 7.3 %copy-start.15 = (s32[128,8]{0,1:T(8,128)S(1)}, s32[128,8]{0,1:T(8,128)}, u32[]{:S(2)}) copy-start(s32[128,8]{0,1:T(8,128)} %param.11) | copy-start | bytes 12292
  157.7 23.4 %copy-start.7 = (s32[4]{0:T(128)S(1)}, s32[4]{0:T(128)}, u32[]{:S(2)}) copy-start(s32[4]{0:T(128)} %copy-done.6) | copy-start | bytes 52
  162.9 11.4 %collective-permute-start.25 = (s16[65,16,128]{2,1,0:T(8,128)(2,1)}, s16[65,16,128]{2,1,0:T(8,128)(2,1)S(1)}, u32[]{:S(2)}, u32[]{:S(2)}) collective-permute-start(s16[65,16,128]{2,1,0:T(8,128)(2,1)} %get-tuple-element.64), channel_id=1, source_target_pairs={{0,4},{1,5},{2,6},{3,7},{4,8},{5,9},{6,10},{7,11},{8,12},{9,13},{1... | collective-permute-start | bytes 798728 | tf_op jit(solution)/shard_map/ppermute | solution.py:28
  165.3 9.6 %collective-permute-start.26 = (s16[65,16,128]{2,1,0:T(8,128)(2,1)}, s16[65,16,128]{2,1,0:T(8,128)(2,1)}, u32[]{:S(2)}, u32[]{:S(2)}) collective-permute-start(s16[65,16,128]{2,1,0:T(8,128)(2,1)} %get-tuple-element.65), channel_id=1, source_target_pairs={{0,8},{1,9},{2,10},{3,11},{4,12},{5,13},{6,14},{7,15},{8,0},{9,1},... | collective-permute-start | bytes 798728 | tf_op jit(solution)/shard_map/ppermute | solution.py:28
  174.3 6.7 %collective-permute-start.27 = (s16[65,16,128]{2,1,0:T(8,128)(2,1)}, s16[65,16,128]{2,1,0:T(8,128)(2,1)}, u32[]{:S(2)}, u32[]{:S(2)}) collective-permute-start(s16[65,16,128]{2,1,0:T(8,128)(2,1)} %get-tuple-element.66), channel_id=1, source_target_pairs={{0,12},{1,13},{2,14},{3,15},{4,0},{5,1},{6,2},{7,3},{8,4},{9,5},{1... | collective-permute-start | bytes 798728 | tf_op jit(solution)/shard_map/ppermute | solution.py:28
  181.1 1.0 copy-start.5
  182.0 4.5 %copy-start.4 = (s16[65,16,128]{2,1,0:T(8,128)(2,1)S(1)}, s16[65,16,128]{2,1,0:T(8,128)(2,1)}, u32[]{:S(2)}) copy-start(s16[65,16,128]{2,1,0:T(8,128)(2,1)} %get-tuple-element.55.refs_0_) | copy-start | bytes 798724
  193.5 2.7 %collective-permute-start.28 = (f32[4,16,4,8,128]{4,3,2,1,0:T(8,128)S(1)}, f32[4,16,4,8,128]{4,3,2,1,0:T(8,128)S(1)}, u32[]{:S(2)}, u32[]{:S(2)}) collective-permute-start(f32[4,16,4,8,128]{4,3,2,1,0:T(8,128)S(1)} %get-tuple-element.71), channel_id=1, source_target_pairs={{0,16},{16,0},{32,48},{48,32},{64,80},{80,64},{96,112},{112,96},{1... | collective-permute-start | bytes 3145736 | tf_op jit(solution)/shard_map/ppermute | solution.py:23
  196.4 13.7 %collective-permute-start.31 = (f32[16,4,8,128]{3,2,1,0:T(8,128)S(1)}, f32[16,4,8,128]{3,2,1,0:T(8,128)S(1)}, u32[]{:S(2)}, u32[]{:S(2)}) collective-permute-start(f32[16,4,8,128]{3,2,1,0:T(8,128)S(1)} %get-tuple-element.87), channel_id=1, source_target_pairs={{0,96},{16,112},{32,0},{48,16},{64,32},{80,48},{96,64},{112,80},{1... | collective-permute-start | bytes 786440 | tf_op jit(solution)/shard_map/ppermute | solution.py:23
  198.6 11.5 %collective-permute-start.30 = (f32[16,4,8,128]{3,2,1,0:T(8,128)S(1)}, f32[16,4,8,128]{3,2,1,0:T(8,128)S(1)}, u32[]{:S(2)}, u32[]{:S(2)}) collective-permute-start(f32[16,4,8,128]{3,2,1,0:T(8,128)S(1)} %get-tuple-element.88), channel_id=1, source_target_pairs={{0,64},{16,80},{32,96},{48,112},{64,0},{80,16},{96,32},{112,48},{1... | collective-permute-start | bytes 786440 | tf_op jit(solution)/shard_map/ppermute | solution.py:23
  199.7 14.1 %collective-permute-start.29 = (f32[16,4,8,128]{3,2,1,0:T(8,128)S(1)}, f32[16,4,8,128]{3,2,1,0:T(8,128)S(1)}, u32[]{:S(2)}, u32[]{:S(2)}) collective-permute-start(f32[16,4,8,128]{3,2,1,0:T(8,128)S(1)} %get-tuple-element.86), channel_id=1, source_target_pairs={{0,32},{16,48},{32,64},{48,80},{64,96},{80,112},{96,0},{112,16},{1... | collective-permute-start | bytes 786440 | tf_op jit(solution)/shard_map/ppermute | solution.py:23
